TPU v7x, 32 devices: a whole 2x2x4 slice. The times are simulated.
32 devices in a mesh: dp: 2 (over x), row: 4 (over z), col: 4 (over y, core).
Axes of the slice: x: 2, y: 2, z: 4, core: 2. Of those that a mesh axis runs over, the one named last changes fastest.
Arguments:
- tokens: bfloat16 [4096, 2048], P(('dp', 'row'), 'col'), may hold values from -6 to 6
- segment_ids: int32 [2, 2048], P('dp'), may hold values from 0 to 2, never falling along the last dimension, each value on 1 to 1024 neighbouring positions
- ln_gain: float32 [2048], P('col'), may hold values from 0.1 to 1.9
- ln_bias: float32 [2048], P('col'), may hold values from -3 to 3
- qkv_weight: bfloat16 [2048, 16, 3, 128], P('col', 'row'), may hold values from -0.125 to 0.125
- qkv_bias: float32 [16, 3, 128], P(('row', 'col')), may hold values from -3 to 3
- out_weight: bfloat16 [2048, 2048], P('row', 'col'), may hold values from -1 to 1
- fc1_weight: bfloat16 [2048, 8192], P('col', 'row'), may hold values from -0.125 to 0.125
- fc1_bias: float32 [8192], P(('row', 'col')), may hold values from -3 to 3
- fc2_weight: bfloat16 [8192, 2048], P('row', 'col'), may hold values from -0.0625 to 0.0625
- out_bias: float32 [2048], P('col'), may hold values from -3 to 3
- out_grad: bfloat16 [4096, 2048], P(('dp', 'row'), 'col'), may hold values from -6 to 6
Outputs:
- out: bfloat16 [4096, 2048], P(('dp', 'row'), 'col')
- tokens_grad: float32 [4096, 2048], P(('dp', 'row'), 'col')
- ln_gain_grad: float32 [2048], P('col')
- ln_bias_grad: float32 [2048], P('col')
- qkv_weight_grad: float32 [2048, 16, 3, 128], P('col', 'row')
- qkv_bias_grad: float32 [16, 3, 128], P(('row', 'col'))
- out_weight_grad: float32 [2048, 2048], P('row', 'col')
- fc1_weight_grad: float32 [2048, 8192], P('col', 'row')
- fc1_bias_grad: float32 [8192], P(('row', 'col'))
- fc2_weight_grad: float32 [8192, 2048], P('row', 'col')
- out_bias_grad: float32 [2048], P('col')
Inputs may be any that keep to these rules, and one draw needn't show every extreme that they name: `segment_ids`: in each row the ids run 0 to 2 without falling, each sequence of 1 to 1024 tokens, and some row holds one of exactly 1024.
All inputs are finite; a program needn't handle non-finite values.
Results may differ from a plain program's by a relative error of at most 0.013.
Values may be sent and summed in bfloat16 or wider, within the bound.
No kernel may reach another device: no remote copies, remote signals or barrier semaphores. Data moves between devices by JAX's collectives and lax.ppermute only.
A program may use at most 256 MiB of HBM per device.

v0:
```python
import math

import jax
import jax.numpy as jnp
from jax import lax
from jax.sharding import PartitionSpec as P

HEAD_DIM = 64
ROT = 32
SEGS = 3


epsilon = 1e-05


def positions(seg_row):
    length_all = seg_row.shape[0]
    labels = jnp.arange(SEGS, dtype=jnp.int32)
    onehot = (seg_row[:, None] == labels[None, :]).astype(jnp.int32)
    counts = jnp.sum(onehot, axis=0)
    starts = jnp.cumsum(counts) - counts
    offset_of = jnp.sum(onehot * starts[None, :], axis=1)
    return jnp.arange(length_all, dtype=jnp.int32) - offset_of


def rope_tables(pos_row):
    half_rot = ROT // 2
    inverse = jnp.exp(jnp.arange(half_rot, dtype=jnp.float32) * (-2.0 * math.log(10000.0) / ROT))
    angles = pos_row.astype(jnp.float32)[:, None] * inverse[None, :]
    return (jnp.cos(angles), jnp.sin(angles))


def rotate(values, cosine_table, sine_table):
    half_rot = ROT // 2
    front_half = values[..., :half_rot]
    back_half = values[..., half_rot:ROT]
    cosine_b = cosine_table[:, None, :]
    sine_b = sine_table[:, None, :]
    return jnp.concatenate(
        [
            front_half * cosine_b - back_half * sine_b,
            back_half * cosine_b + front_half * sine_b,
            values[..., ROT:],
        ],
        axis=-1,
    )


def gelu(values):
    return (
        0.5
        * values
        * (1.0 + jnp.tanh(0.7978845608028654 * (values + 0.044715 * values * values * values)))
    )


def block_scores(query_block, key_rows, seg_row, begin_row, score_scale):
    count = query_block.shape[0]
    span = key_rows.shape[0]
    row_ids = begin_row + jnp.arange(count, dtype=jnp.int32)
    col_ids = jnp.arange(span, dtype=jnp.int32)
    visible = (col_ids[None, :] <= row_ids[:, None]) & (
        seg_row[:span][None, :] == seg_row[begin_row : begin_row + count][:, None]
    )
    scores = (
        jnp.einsum("qhd,khd->hqk", query_block, key_rows, preferred_element_type=jnp.float32)
        * score_scale
    )
    return jnp.where(visible[None], scores, -1000000000.0)


def local(
    tokens,
    segment_ids,
    ln_gain,
    ln_bias,
    qkv_weight,
    qkv_bias,
    out_weight,
    fc1_weight,
    fc1_bias,
    fc2_weight,
    out_bias,
    out_grad,
):
    col_count = lax.axis_size("col")
    local_rows, local_width = tokens.shape
    full_width = local_width * col_count
    pair_dim = qkv_weight.shape[3]
    token_f = tokens.astype(jnp.float32)
    ln_sums = lax.psum((jnp.sum(token_f, axis=1), jnp.sum(token_f * token_f, axis=1)), "col")
    row_mean = ln_sums[0] / full_width
    variance = ln_sums[1] / full_width - row_mean * row_mean
    inv_std = lax.rsqrt(variance + epsilon)
    centred = (token_f - row_mean[:, None]) * inv_std[:, None]
    normed = (centred * ln_gain + ln_bias).astype(jnp.bfloat16)
    normed_rows = lax.all_gather(normed, "row", axis=0, tiled=True)
    group_rows = normed_rows.shape[0]
    proj_part = jnp.dot(
        normed_rows, qkv_weight.reshape(local_width, -1), preferred_element_type=jnp.float32
    ).reshape(group_rows, col_count, -1)
    up_part = jnp.dot(normed_rows, fc1_weight, preferred_element_type=jnp.float32).reshape(
        group_rows, col_count, -1
    )
    proj_sum, up_sum = (
        lax.psum_scatter(proj_part, "col", scatter_dimension=1, tiled=True),
        lax.psum_scatter(up_part, "col", scatter_dimension=1, tiled=True),
    )
    proj_sum = proj_sum.reshape(group_rows, -1)
    up_sum = up_sum.reshape(group_rows, -1)
    pair_local = qkv_bias.shape[0]
    projected = proj_sum.reshape(group_rows, pair_local, 3, pair_dim) + qkv_bias[None]
    queries = projected[:, :, 0, :].reshape(group_rows, -1, HEAD_DIM)
    key_vals = projected[:, :, 1, :].reshape(group_rows, -1, HEAD_DIM)
    value_vals = projected[:, :, 2, :].reshape(group_rows, -1, HEAD_DIM)
    seg_row = segment_ids[0]
    cosine_table, sine_table = rope_tables(positions(seg_row))
    q_rot = rotate(queries, cosine_table, sine_table).astype(jnp.bfloat16)
    k_rot = rotate(key_vals, cosine_table, sine_table).astype(jnp.bfloat16)
    v_low = value_vals.astype(jnp.bfloat16)
    up_pre = up_sum + fc1_bias
    activation = gelu(up_pre).astype(jnp.bfloat16)
    block = min(512, group_rows)
    score_scale = 1.0 / math.sqrt(HEAD_DIM)
    block_outs = []
    block_lse = []
    for begin_row in range(0, group_rows, block):
        end_row = begin_row + block
        scores = block_scores(
            q_rot[begin_row:end_row], k_rot[:end_row], seg_row, begin_row, score_scale
        )
        row_top = jnp.max(scores, axis=-1, keepdims=True)
        shifted = jnp.exp(scores - row_top)
        row_sum = jnp.sum(shifted, axis=-1, keepdims=True)
        attn_prob = (shifted / row_sum).astype(jnp.bfloat16)
        block_outs.append(
            jnp.einsum(
                "hqk,khd->qhd", attn_prob, v_low[:end_row], preferred_element_type=jnp.float32
            )
        )
        block_lse.append(row_top + jnp.log(row_sum))
    attn_low = jnp.concatenate(block_outs, axis=0).reshape(group_rows, -1).astype(jnp.bfloat16)
    attn_rows, act_rows = (
        lax.all_gather(attn_low, "col", axis=1, tiled=True),
        lax.all_gather(activation, "col", axis=1, tiled=True),
    )
    mixed = lax.psum_scatter(
        (
            jnp.dot(attn_rows, out_weight, preferred_element_type=jnp.float32)
            + jnp.dot(act_rows, fc2_weight, preferred_element_type=jnp.float32)
        ).astype(jnp.bfloat16),
        "row",
        scatter_dimension=0,
        tiled=True,
    ).astype(jnp.float32)
    out = (token_f + mixed + out_bias).astype(jnp.bfloat16)
    cot_rows = lax.all_gather(out_grad, "row", axis=0, tiled=True)
    out_weight_grad = jnp.einsum(
        "tk,td->kd", attn_rows, cot_rows, preferred_element_type=jnp.float32
    )
    fc2_weight_grad = jnp.einsum(
        "tk,td->kd", act_rows, cot_rows, preferred_element_type=jnp.float32
    )
    out_bias_grad = jnp.sum(cot_rows.astype(jnp.float32), axis=0)
    back_attn = jnp.einsum(
        "td,kd->tk", cot_rows, out_weight, preferred_element_type=jnp.float32
    ).reshape(group_rows, col_count, -1)
    back_act = jnp.einsum(
        "td,kd->tk", cot_rows, fc2_weight, preferred_element_type=jnp.float32
    ).reshape(group_rows, col_count, -1)
    d_attn, d_act = (
        lax.psum_scatter(back_attn, "col", scatter_dimension=1, tiled=True),
        lax.psum_scatter(back_act, "col", scatter_dimension=1, tiled=True),
    )
    d_attn_low = d_attn.reshape(group_rows, -1, HEAD_DIM).astype(jnp.bfloat16)
    _, gelu_back = jax.vjp(gelu, up_pre)
    d_up = gelu_back(d_act.reshape(group_rows, -1))[0].astype(jnp.bfloat16)
    fc1_bias_grad = jnp.sum(d_up.astype(jnp.float32), axis=0)
    d_query_parts = []
    d_key_rot = jnp.zeros(k_rot.shape, jnp.float32)
    d_value = jnp.zeros(v_low.shape, jnp.float32)
    for block_index, begin_row in enumerate(range(0, group_rows, block)):
        end_row = begin_row + block
        scores = block_scores(
            q_rot[begin_row:end_row], k_rot[:end_row], seg_row, begin_row, score_scale
        )
        attn_prob = jnp.exp(scores - block_lse[block_index])
        prob_low = attn_prob.astype(jnp.bfloat16)
        grad_block = d_attn_low[begin_row:end_row]
        d_prob = jnp.einsum(
            "qhd,khd->hqk", grad_block, v_low[:end_row], preferred_element_type=jnp.float32
        )
        d_score = (
            attn_prob * (d_prob - jnp.sum(attn_prob * d_prob, axis=-1, keepdims=True))
        ).astype(jnp.bfloat16)
        d_query_parts.append(
            jnp.einsum("hqk,khd->qhd", d_score, k_rot[:end_row], preferred_element_type=jnp.float32)
            * score_scale
        )
        key_update = (
            jnp.einsum(
                "hqk,qhd->khd",
                d_score,
                q_rot[begin_row:end_row],
                preferred_element_type=jnp.float32,
            )
            * score_scale
        )
        d_key_rot = d_key_rot.at[:end_row].add(key_update)
        d_value = d_value.at[:end_row].add(
            jnp.einsum("hqk,qhd->khd", prob_low, grad_block, preferred_element_type=jnp.float32)
        )
    d_query_rot = jnp.concatenate(d_query_parts, axis=0)
    _, rotate_back = jax.vjp(lambda values: rotate(values, cosine_table, sine_table), queries)
    d_query = rotate_back(d_query_rot)[0]
    d_key = rotate_back(d_key_rot)[0]
    d_proj = jnp.stack(
        [
            d_query.reshape(group_rows, pair_local, pair_dim),
            d_key.reshape(group_rows, pair_local, pair_dim),
            d_value.reshape(group_rows, pair_local, pair_dim),
        ],
        axis=2,
    ).astype(jnp.bfloat16)
    qkv_bias_grad = jnp.sum(d_proj.astype(jnp.float32), axis=0)
    d_proj_rows, d_up_rows = (
        lax.all_gather(d_proj.reshape(group_rows, 1, -1), "col", axis=1, tiled=True),
        lax.all_gather(d_up.reshape(group_rows, 1, -1), "col", axis=1, tiled=True),
    )
    d_proj_flat = d_proj_rows.reshape(group_rows, -1)
    d_up_flat = d_up_rows.reshape(group_rows, -1)
    qkv_weight_grad = jnp.einsum(
        "tk,tj->kj", normed_rows, d_proj_flat, preferred_element_type=jnp.float32
    ).reshape(qkv_weight.shape)
    fc1_weight_grad = jnp.einsum(
        "tk,tj->kj", normed_rows, d_up_flat, preferred_element_type=jnp.float32
    )
    qkv_flat = qkv_weight.reshape(local_width, -1)
    proj_part = d_proj_flat
    up_part = d_up_flat
    d_normed = lax.psum_scatter(
        (
            jnp.einsum("tj,kj->tk", proj_part, qkv_flat, preferred_element_type=jnp.float32)
            + jnp.einsum("tj,kj->tk", up_part, fc1_weight, preferred_element_type=jnp.float32)
        ).astype(jnp.bfloat16),
        "row",
        scatter_dimension=0,
        tiled=True,
    ).astype(jnp.float32)
    d_hat = d_normed * ln_gain
    back_sums = lax.psum((jnp.sum(d_hat, axis=1), jnp.sum(d_hat * centred, axis=1)), "col")
    tokens_grad = out_grad.astype(jnp.float32) + inv_std[:, None] * (
        d_hat - back_sums[0][:, None] / full_width - centred * (back_sums[1][:, None] / full_width)
    )
    vector_sums = lax.psum(
        (jnp.sum(d_normed * centred, axis=0), jnp.sum(d_normed, axis=0)), ("dp", "row")
    )
    weight_totals = (
        lax.psum(qkv_weight_grad.astype(jnp.bfloat16), "dp").astype(jnp.float32),
        lax.psum(out_weight_grad.astype(jnp.bfloat16), "dp").astype(jnp.float32),
        lax.psum(fc1_weight_grad.astype(jnp.bfloat16), "dp").astype(jnp.float32),
        lax.psum(fc2_weight_grad.astype(jnp.bfloat16), "dp").astype(jnp.float32),
        lax.psum(qkv_bias_grad.astype(jnp.bfloat16), "dp").astype(jnp.float32),
        lax.psum(fc1_bias_grad.astype(jnp.bfloat16), "dp").astype(jnp.float32),
        lax.psum(out_bias_grad.astype(jnp.bfloat16), "dp").astype(jnp.float32),
    )
    return (
        out,
        tokens_grad,
        vector_sums[0],
        vector_sums[1],
        weight_totals[0],
        weight_totals[4],
        weight_totals[1],
        weight_totals[2],
        weight_totals[5],
        weight_totals[3],
        weight_totals[6],
    )


def solution(mesh):
    return jax.shard_map(
        local,
        mesh=mesh,
        in_specs=(
            P(("dp", "row"), "col"),
            P("dp", None),
            P("col"),
            P("col"),
            P("col", "row", None, None),
            P(("row", "col"), None, None),
            P("row", "col"),
            P("col", "row"),
            P(("row", "col")),
            P("row", "col"),
            P("col"),
            P(("dp", "row"), "col"),
        ),
        out_specs=(
            P(("dp", "row"), "col"),
            P(("dp", "row"), "col"),
            P("col"),
            P("col"),
            P("col", "row", None, None),
            P(("row", "col"), None, None),
            P("row", "col"),
            P("col", "row"),
            P(("row", "col")),
            P("row", "col"),
            P("col"),
        ),
        check_vma=False,
    )
```

profile of v0, /device:TPU:0, one launch (start us, length us, event | category | flops | bytes accessed | tf_op | source)
XLA Modules:
  0.0 969.1 jit_solution(9875291804322905900)
XLA Ops:
  9.3 8.4 all-reduce.10
  20.5 37.5 %all-gather.13.cloned.1.call-done = bf16[2048,512]{1,0:T(8,128)(2,1)} async-done(((bf16[512,512]{1,0:T(8,128)(2,1)}), bf16[2048,512]{1,0:T(8,128)(2,1)}) %all-gather.13.cloned.1.call-update) | async-done | bytes 2097168 | tf_op jit(solution)/shard_map/all_gather | solution.py:157
  66.8 37.8 %all-gather.7.cloned.1.call-done = bf16[2048,512]{1,0:T(8,128)(2,1)} async-done(((bf16[512,512]{1,0:T(8,128)(2,1)}), bf16[2048,512]{1,0:T(8,128)(2,1)}) %all-gather.7.cloned.1.call-update) | async-done | bytes 2097168 | tf_op jit(solution)/shard_map/all_gather | solution.py:97
  104.6 11.5 %fusion.55 = f32[2048,4,384]{2,0,1:T(8,128)} fusion(bf16[4,384,512]{2,1,0:T(8,128)(2,1)} %bitcast.204, bf16[2048,512]{1,0:T(8,128)(2,1)} %all-gather.7.cloned.1.call-done), kind=kOutput, calls=%fused_computation.81 | convolution fusion | flops 3221225472 | bytes 16252928 | tf_op jit(solution)/shard_map/dot_general | solution.py:99
  116.2 10.1 %fusion.130 = f32[2048,2048]{0,1:T(8,128)} fusion(bf16[2048,512]{1,0:T(8,128)(2,1)} %all-gather.7.cloned.1.call-done, bf16[512,2048]{1,0:T(8,128)(2,1)S(1)} %copy-done), kind=kOutput, calls=%fused_computation.212 | convolution fusion | flops 4294967296 | bytes 20971520 | tf_op jit(solution)/shard_map/dot_general | solution.py:102
  126.3 16.4 %copy.70 = f32[2048,4,512]{2,0,1:T(8,128)} copy(f32[2048,4,512]{0,2,1:T(8,128)} %bitcast.184) | data formatting | bytes 33554432 | tf_op jit(solution)/shard_map/reshape | solution.py:102
  143.1 12.5 %fusion.134 = f32[2048,2048]{0,1:T(8,128)} fusion(bf16[2048,512]{1,0:T(8,128)(2,1)} %all-gather.13.cloned.1.call-done, bf16[2048,512]{1,0:T(8,128)(2,1)} %param.41), kind=kOutput, calls=%fused_computation.216 | convolution fusion | flops 4294967296 | bytes 20971520 | tf_op jit(solution)/shard_map/td,kd->tk/dot_general | solution.py:168
  155.6 18.0 %copy.76 = f32[2048,4,512]{2,0,1:T(8,128)} copy(f32[2048,4,512]{0,2,1:T(8,128)} %bitcast.185) | data formatting | bytes 33554432 | tf_op jit(solution)/shard_map/reshape | solution.py:170
  182.6 70.8 %reduce-scatter.7.cloned.1.call-done = f32[2048,1,384]{2,0,1:T(8,128)} async-done(((f32[2048,4,384]{2,0,1:T(8,128)}), f32[2048,1,384]{2,0,1:T(8,128)}) %reduce-scatter.7.cloned.1.call-update) | async-done | bytes 3145744 | tf_op jit(solution)/shard_map/reduce_scatter | solution.py:106
  307.1 73.8 %reduce-scatter.9.cloned.1.call-done = f32[2048,1,512]{2,0,1:T(8,128)} async-done(((f32[2048,4,512]{2,0,1:T(8,128)}), f32[2048,1,512]{2,0,1:T(8,128)}) %reduce-scatter.9.cloned.1.call-update) | async-done | bytes 4194320 | tf_op jit(solution)/shard_map/reduce_scatter | solution.py:107
  380.9 127.5 %reduce-scatter.15.cloned.1.call-done = f32[2048,1,512]{2,0,1:T(8,128)} async-done(((f32[2048,4,512]{2,0,1:T(8,128)}), f32[2048,1,512]{2,0,1:T(8,128)}) %reduce-scatter.15.cloned.1.call-update) | async-done | bytes 4194320 | tf_op jit(solution)/shard_map/reduce_scatter | solution.py:173
  532.3 24.1 %all-gather.15.cloned.1.call-done = bf16[2048,4,384]{2,0,1:T(8,128)(2,1)} async-done(((bf16[2048,1,384]{2,0,1:T(8,128)(2,1)}), bf16[2048,4,384]{2,0,1:T(8,128)(2,1)}) %all-gather.15.cloned.1.call-update) | async-done | bytes 6291472 | tf_op jit(solution)/shard_map/all_gather | solution.py:227
  556.4 8.7 copy.75
  565.1 9.7 %fusion.133 = f32[2048,512]{1,0:T(8,128)} fusion(bf16[2048,1536]{0,1:T(8,128)(2,1)} %bitcast.191, bf16[512,1536]{0,1:T(8,128)(2,1)} %bitcast.205), kind=kOutput, calls=%fused_computation.215 | convolution fusion | flops 3221225472 | bytes 12058624 | tf_op jit(solution)/shard_map/tj,kj->tk/dot_general | solution.py:243
  574.8 42.0 %all-gather.17.cloned.1.call-done = bf16[2048,4,512]{2,0,1:T(8,128)(2,1)} async-done(((bf16[2048,1,512]{2,0,1:T(8,128)(2,1)}), bf16[2048,4,512]{2,0,1:T(8,128)(2,1)}) %all-gather.17.cloned.1.call-update) | async-done | bytes 8388624 | tf_op jit(solution)/shard_map/all_gather | solution.py:228
  616.8 11.7 %copy.77 = bf16[2048,4,512]{0,2,1:T(8,128)(2,1)} copy(bf16[2048,4,512]{2,0,1:T(8,128)(2,1)} %all-gather.17.cloned.1.call-done) | data formatting | bytes 16777216 | tf_op jit(solution)/shard_map/all_gather | solution.py:228
  628.5 11.5 %add_convert_fusion = bf16[2048,512]{1,0:T(8,128)(2,1)} fusion(f32[2048,512]{1,0:T(8,128)} %fusion.133, bf16[2048,2048]{0,1:T(8,128)(2,1)} %bitcast.187, bf16[512,2048]{1,0:T(8,128)(2,1)S(1)} %copy-done), kind=kOutput, calls=%fused_computation.43 | convolution fusion | flops 4297064448 | bytes 16777216 | tf_op jit(solution)/shard_map/tj,kj->tk/dot_general | solution.py:244
  640.1 37.2 %all-gather.11.cloned.1.call-done = bf16[2048,2048]{1,0:T(8,128)(2,1)} async-done(((bf16[2048,512]{1,0:T(8,128)(2,1)}), bf16[2048,2048]{1,0:T(8,128)(2,1)}) %all-gather.11.cloned.1.call-update) | async-done | bytes 8388624 | tf_op jit(solution)/shard_map/all_gather | solution.py:145
  677.3 10.5 %fusion.131 = f32[2048,512]{1,0:T(8,128)} fusion(bf16[2048,2048]{1,0:T(8,128)(2,1)} %all-gather.11.cloned.1.call-done, bf16[2048,512]{1,0:T(8,128)(2,1)} %param.41), kind=kOutput, calls=%fused_computation.213 | convolution fusion | flops 4294967296 | bytes 14680064 | tf_op jit(solution)/shard_map/dot_general | solution.py:150
  687.8 14.1 %all-gather.9.cloned.1.call-done = bf16[2048,512]{0,1:T(8,128)(2,1)} async-done(((bf16[2048,128]{0,1:T(8,128)(2,1)}), bf16[2048,512]{0,1:T(8,128)(2,1)}) %all-gather.9.cloned.1.call-update) | async-done | bytes 2097168 | tf_op jit(solution)/shard_map/all_gather | solution.py:144
  718.7 7.6 convolution_convert_fusion.1
  750.0 21.0 %all-reduce.8 = (f32[512]{0:T(512)}, f32[512]{0:T(512)}) all-reduce(f32[512]{0:T(512)S(1)} %get-tuple-element.178, f32[512]{0:T(512)S(1)} %get-tuple-element.181), channel_id=1, replica_groups=mesh['dp'=2,'row'=4,'col'=4] {'dp','row'}, use_global_device_ids=true, to_apply=%region_30.31 | all-reduce | flops 1024 | bytes 8192 | tf_op jit(solution)/shard_map/psum | solution.py:255
  777.3 17.0 %reduce-scatter.11.cloned.1.call-done = bf16[512,512]{1,0:T(8,128)(2,1)} async-done(((bf16[2048,512]{1,0:T(8,128)(2,1)}), bf16[512,512]{1,0:T(8,128)(2,1)}) %reduce-scatter.11.cloned.1.call-update) | async-done | bytes 524304 | tf_op jit(solution)/shard_map/reduce_scatter | solution.py:147
  797.1 153.4 %all-reduce.15.cloned.1.call-done = (bf16[512,4,3,128]{3,0,2,1:T(8,128)(2,1)}, bf16[512,512]{1,0:T(8,128)(2,1)}, bf16[512,2048]{1,0:T(8,128)(2,1)}, bf16[2048,512]{1,0:T(8,128)(2,1)}) async-done(((bf16[512,4,3,128]{3,0,2,1:T(8,128)(2,1)}, bf16[512,512]{1,0:T(8,128)(2,1)}, bf16[512,2048]{1,0:T(8,128)(2,1)}, bf16[2048,512]{1,0:T(8,128)(2,1)}), (bf16[512,4,3,128]{3,0,2,1:T(8,128)(2,1)}, ...) | async-done | bytes 6291472 | tf_op jit(solution)/shard_map/psum | solution.py:259
  (271 shorter events, 160.8 us)
Async XLA Ops:
  7.2 109.0 %copy-start = (bf16[512,2048]{1,0:T(8,128)(2,1)S(1)}, bf16[512,2048]{1,0:T(8,128)(2,1)}, u32[]{:S(2)}) copy-start(bf16[512,2048]{1,0:T(8,128)(2,1)} %param.39) | copy-start | bytes 6291460
  7.2 50.8 %all-gather.13.cloned.1.call-start = ((), (), s32[]{:S(2)}) async-start(), calls=%async_computation.12 | async-start | bytes 2621440 | tf_op jit(solution)/shard_map/all_gather | solution.py:157
  7.9 96.7 %all-gather.7.cloned.1.call-start = ((), (), s32[]{:S(2)}) async-start(), calls=%async_computation.6 | async-start | bytes 2621440 | tf_op jit(solution)/shard_map/all_gather | solution.py:97
  20.4 160.1 %reduce-scatter.13.cloned.1.call-start = ((), (), s32[]{:S(2)}) async-start(), calls=%async_computation.13 | async-start | bytes 5242880 | tf_op jit(solution)/shard_map/reduce_scatter | solution.py:172
  63.0 190.4 %reduce-scatter.7.cloned.1.call-start = ((), (), s32[]{:S(2)}) async-start(), calls=%async_computation.7 | async-start | bytes 15728640 | tf_op jit(solution)/shard_map/reduce_scatter | solution.py:106
  116.1 264.8 %reduce-scatter.9.cloned.1.call-start = ((), (), s32[]{:S(2)}) async-start(), calls=%async_computation.9 | async-start | bytes 20971520 | tf_op jit(solution)/shard_map/reduce_scatter | solution.py:107
  142.8 365.6 %reduce-scatter.15.cloned.1.call-start = ((), (), s32[]{:S(2)}) async-start(), calls=%async_computation.15 | async-start | bytes 20971520 | tf_op jit(solution)/shard_map/reduce_scatter | solution.py:173
  173.6 382.8 %all-gather.15.cloned.1.call-start = ((), (), s32[]{:S(2)}) async-start(), calls=%async_computation.14 | async-start | bytes 7864320 | tf_op jit(solution)/shard_map/all_gather | solution.py:227
  176.9 84.8 %copy-start.20 = (f32[2048,16]{0,1:T(8,128)}, f32[2048,16]{0,1:T(8,128)S(1)}, u32[]{:S(2)}) copy-start(f32[2048,16]{0,1:T(8,128)S(1)} %get-tuple-element.221) | copy-start | bytes 393220
  176.9 84.8 %copy-start.22 = (f32[2048,16]{0,1:T(8,128)}, f32[2048,16]{0,1:T(8,128)S(1)}, u32[]{:S(2)}) copy-start(f32[2048,16]{0,1:T(8,128)S(1)} %get-tuple-element.222) | copy-start | bytes 393220
  182.6 80.4 %copy-start.38 = (bf16[512,1,128]{0,2,1:T(8,128)(2,1)}, bf16[512,1,128]{0,2,1:T(8,128)(2,1)S(1)}, u32[]{:S(2)}) copy-start(bf16[512,1,128]{0,2,1:T(8,128)(2,1)S(1)} %get-tuple-element.217) | copy-start | bytes 393220
  267.5 31.2 %copy-start.3 = (f32[2,512,1024]{2,1,0:T(8,128)}, f32[2,512,1024]{2,1,0:T(8,128)S(1)}, u32[]{:S(2)}) copy-start(f32[2,512,1024]{2,1,0:T(8,128)S(1)} %get-tuple-element.232) | copy-start | bytes 12582916
  270.2 29.9 %copy-start.2 = (f32[2,512,1536]{2,1,0:T(8,128)}, f32[2,512,1536]{2,1,0:T(8,128)S(1)}, u32[]{:S(2)}) copy-start(f32[2,512,1536]{2,1,0:T(8,128)S(1)} %get-tuple-element.234) | copy-start | bytes 18874372
  274.4 27.1 %copy-start.1 = (f32[2,512,2048]{2,1,0:T(8,128)}, f32[2,512,2048]{2,1,0:T(8,128)S(1)}, u32[]{:S(2)}) copy-start(f32[2,512,2048]{2,1,0:T(8,128)S(1)} %get-tuple-element.236) | copy-start | bytes 25165828
  303.1 205.4 %copy-start.54 = (f32[512]{0:T(512)S(1)}, f32[512]{0:T(512)}, u32[]{:S(2)}) copy-start(f32[512]{0:T(512)} %param.40) | copy-start | bytes 6148
  307.0 309.8 %all-gather.17.cloned.1.call-start = ((), (), s32[]{:S(2)}) async-start(), calls=%async_computation.16 | async-start | bytes 10485760 | tf_op jit(solution)/shard_map/all_gather | solution.py:228
  515.6 161.7 %all-gather.11.cloned.1.call-start = ((), (), s32[]{:S(2)}) async-start(), calls=%async_computation.10 | async-start | bytes 10485760 | tf_op jit(solution)/shard_map/all_gather | solution.py:145
  521.2 180.7 %all-gather.9.cloned.1.call-start = ((), (), s32[]{:S(2)}) async-start(), calls=%async_computation.8 | async-start | bytes 2621440 | tf_op jit(solution)/shard_map/all_gather | solution.py:144
  532.3 216.1 %reduce-scatter.17.cloned.1.call-start = ((), (), s32[]{:S(2)}) async-start(), calls=%async_computation.17 | async-start | bytes 2621440 | tf_op jit(solution)/shard_map/reduce_scatter | solution.py:241
  640.0 61.8 %copy-start.26 = (bf16[512,512]{1,0:T(8,128)(2,1)S(1)}, bf16[512,512]{1,0:T(8,128)(2,1)}, u32[]{:S(2)}) copy-start(bf16[512,512]{1,0:T(8,128)(2,1)} %param.38) | copy-start | bytes 1572868
  640.0 154.2 %reduce-scatter.11.cloned.1.call-start = ((), (), s32[]{:S(2)}) async-start(), calls=%async_computation.11 | async-start | bytes 2621440 | tf_op jit(solution)/shard_map/reduce_scatter | solution.py:147
  707.3 243.2 %all-reduce.15.cloned.1.call-start = ((), (), s32[]{:S(2)}) async-start(), calls=%async_computation.18 | async-start | bytes 12582912 | tf_op jit(solution)/shard_map/psum | solution.py:259
  734.1 60.2 %copy-start.29 = (bf16[512,512]{1,0:T(8,128)(2,1)S(1)}, bf16[512,512]{1,0:T(8,128)(2,1)}, u32[]{:S(2)}) copy-start(bf16[512,512]{1,0:T(8,128)(2,1)} %param.43) | copy-start | bytes 1572868
  734.1 60.2 %copy-start.55 = (f32[512]{0:T(512)S(1)}, f32[512]{0:T(512)}, u32[]{:S(2)}) copy-start(f32[512]{0:T(512)} %param.42) | copy-start | bytes 6148
  (55 other events, 267.7 us)
Sparse Core Ops, SparseCore 0:
  9.6 48.3 all-gather.12
  60.1 44.4 all-gather.6
  107.7 43.3 reduce-scatter.12
  153.6 99.7 reduce-scatter.6
  255.8 125.0 reduce-scatter.8
  383.4 125.0 reduce-scatter.14
  510.0 46.3 all-gather.14
  558.5 58.2 all-gather.16
  619.0 58.2 all-gather.10
  679.2 22.5 all-gather.8
  704.7 43.6 reduce-scatter.16
  751.1 43.1 reduce-scatter.10
  798.0 152.4 all-reduce.14
where the time goes:
time: 977 us; the launch traced here: 969 us
  waiting for transfers between devices  638 us (65%)
  matrix products  137 us (14%)
  local copies, waits for them, and re-layouts  76.5 us (8%)
  other arithmetic  61.1 us (6%)
  blocking collectives  40.6 us (4%)
  between operations  15.3 us (2%)
    psum x1, waiting for transfers between devices, local(): lax.psum(qkv_weight_grad.astype(jnp.bfloat16), 'dp').astype(jnp.float32)  153 us
    reduce_scatter x1, waiting for transfers between devices, local(): lax.psum_scatter(back_act, 'col', scatter_dimension=1, tiled=True)  128 us
    reduce_scatter x1, waiting for transfers between devices, local(): lax.psum_scatter(up_part, 'col', scatter_dimension=1, tiled=True)  73.8 us
    reduce_scatter x1, waiting for transfers between devices, local(): lax.psum_scatter(proj_part, 'col', scatter_dimension=1, tiled=True)  70.8 us
    all_gather x1, waiting for transfers between devices, local(): lax.all_gather(d_up.reshape(group_rows, 1, -1), 'col', axis=1, tiled=True)  42 us
    all_gather x1, waiting for transfers between devices, local(): normed_rows = lax.all_gather(normed, 'row', axis=0, tiled=True)  37.8 us
    all_gather x1, waiting for transfers between devices, local(): cot_rows = lax.all_gather(out_grad, 'row', axis=0, tiled=True)  37.5 us
    all_gather x1, waiting for transfers between devices, local(): lax.all_gather(activation, 'col', axis=1, tiled=True)  37.2 us
  transfers between devices with their start and end apart: 13, of which 12 were waited for; matrix products, arithmetic and copies ran while one was open for 27% of the time, Pallas kernels for 0%

commit v1 on v0

v1 whole, which is shorter than its diff:
```python
import math

import jax
import jax.numpy as jnp
from jax import lax
from jax.experimental import pallas as pl
from jax.experimental.pallas import tpu as pltpu
from jax.sharding import PartitionSpec as P


HEAD_DIM = 64
ROT = 32
SEGS = 3
LONGEST = 1024


epsilon = 1e-05
f32 = jnp.float32
bf16 = jnp.bfloat16
NN = (((1,), (0,)), ((), ()))
NT = (((1,), (1,)), ((), ()))
TN = (((0,), (0,)), ((), ()))


def mul(left, right, dims=NN):
    return lax.dot_general(left, right, dims, preferred_element_type=f32)


ROW, COL, DP = "row", "col", "dp"


def params():
    return pltpu.CompilerParams(vmem_limit_bytes=56 * 1024 * 1024)


def cost(flops, bytes_accessed, transcendentals=0):
    return pl.CostEstimate(
        flops=int(flops), bytes_accessed=int(bytes_accessed), transcendentals=int(transcendentals)
    )


def positions(seg_row):
    length_all = seg_row.shape[0]
    labels = jnp.arange(SEGS, dtype=jnp.int32)
    onehot = (seg_row[:, None] == labels[None, :]).astype(jnp.int32)
    counts = jnp.sum(onehot, axis=0)
    starts = jnp.cumsum(counts) - counts
    offset_of = jnp.sum(onehot * starts[None, :], axis=1)
    return jnp.arange(length_all, dtype=jnp.int32) - offset_of


def rope_tables(pos_row, width):
    half_rot = ROT // 2
    lane = jnp.arange(width, dtype=jnp.int32) % HEAD_DIM
    inverse = jnp.exp((lane % half_rot).astype(f32) * (-2.0 * math.log(10000.0) / ROT))
    angles = pos_row.astype(f32)[:, None] * inverse[None, :]
    cosine, sine = jnp.cos(angles), jnp.sin(angles)
    keep = jnp.where(lane < ROT, cosine, 1.0)
    from_high = jnp.where(lane < half_rot, -sine, 0.0)
    from_low = jnp.where((lane >= half_rot) & (lane < ROT), sine, 0.0)
    return keep, from_high, from_low


def turn(value, keep, from_high, from_low):
    half_rot = ROT // 2
    width = value.shape[-1]
    return (
        value * keep
        + pltpu.roll(value, width - half_rot, 1) * from_high
        + pltpu.roll(value, half_rot, 1) * from_low
    )


def gelu(values):
    return (
        0.5
        * values
        * (1.0 + jnp.tanh(0.7978845608028654 * (values + 0.044715 * values * values * values)))
    )


def gelu_slope(values):
    inner = jnp.tanh(0.7978845608028654 * (values + 0.044715 * values * values * values))
    return 0.5 * (1.0 + inner) + 0.5 * values * (1.0 - inner * inner) * (
        0.7978845608028654 * (1.0 + 3.0 * 0.044715 * values * values)
    )


def swap_bits(value, axis, bit):
    count = lax.axis_size(axis)
    return lax.ppermute(value, axis, [(place, place ^ bit) for place in range(count)])


def all_bits(axis):
    bits = []
    bit = 1
    while bit < lax.axis_size(axis):
        bits.append(bit)
        bit *= 2
    return bits


def total_over(value, axes):
    for axis in axes:
        for bit in all_bits(axis):
            value = value + swap_bits(value, axis, bit)
    return value


def stack_blocks(items):
    shape = items[0][0].shape[1:]

    def kernel(*refs):
        out_ref = refs[-1]
        for place, (_, index) in enumerate(items):
            out_ref[place] = refs[place][index]

    return pl.pallas_call(
        kernel,
        out_shape=jax.ShapeDtypeStruct((len(items),) + shape, items[0][0].dtype),
        compiler_params=params(),
        cost_estimate=cost(0, 4 * len(items) * math.prod(shape)),
    )(*[item for item, _ in items])


def pack_in(places, fc1_weight, qkv_flat):
    width, rows = fc1_weight.shape[1] // 4, fc1_weight.shape[0]
    small = qkv_flat.shape[1] // 4

    def kernel(places_ref, *refs):
        for place in range(3):
            refs[6 + place][:, :width] = refs[place][...]
            refs[6 + place][:, width:] = refs[3 + place][...]

    def at(place):
        return lambda step, s: (0, s[place])

    whole = pl.BlockSpec((rows, width + small), lambda step, s: (0, 0))
    shape = jax.ShapeDtypeStruct((rows, width + small), bf16)
    return pl.pallas_call(
        kernel,
        grid_spec=pltpu.PrefetchScalarGridSpec(
            num_scalar_prefetch=1,
            grid=(1,),
            in_specs=[pl.BlockSpec((rows, width), at(i)) for i in range(3)]
            + [pl.BlockSpec((rows, small), at(i)) for i in range(3)],
            out_specs=[whole] * 3,
        ),
        out_shape=[shape] * 3,
        compiler_params=params(),
        cost_estimate=cost(0, 3 * 4 * rows * (width + small)),
    )(places, fc1_weight, fc1_weight, fc1_weight, qkv_flat, qkv_flat, qkv_flat)


def pack_out(places, fc2_weight, out_weight):
    tall, cols = fc2_weight.shape[0] // 4, fc2_weight.shape[1]
    small = out_weight.shape[0] // 4

    def kernel(places_ref, *refs):
        for place in range(3):
            refs[6 + place][:tall] = refs[place][...]
            refs[6 + place][tall:] = refs[3 + place][...]

    def at(place):
        return lambda step, s: (s[place], 0)

    whole = pl.BlockSpec((tall + small, cols), lambda step, s: (0, 0))
    shape = jax.ShapeDtypeStruct((tall + small, cols), bf16)
    return pl.pallas_call(
        kernel,
        grid_spec=pltpu.PrefetchScalarGridSpec(
            num_scalar_prefetch=1,
            grid=(1,),
            in_specs=[pl.BlockSpec((tall, cols), at(i)) for i in range(3)]
            + [pl.BlockSpec((small, cols), at(i)) for i in range(3)],
            out_specs=[whole] * 3,
        ),
        out_shape=[shape] * 3,
        compiler_params=params(),
        cost_estimate=cost(0, 3 * 4 * cols * (tall + small)),
    )(places, fc2_weight, fc2_weight, fc2_weight, out_weight, out_weight, out_weight)


def forward_step(xs, ws, fc1_bias, qkv_bias, tables):
    rows, width = xs[0].shape
    hidden = fc1_bias.shape[1]
    pair = qkv_bias.shape[1] // 3
    block = 512

    def kernel(*refs):
        x_refs, w_refs = refs[:4], refs[4:8]
        fb, qb, keep, high, low = refs[8:13]
        up_o, act_o, q_o, k_o, v_o = refs[13:]
        total = mul(x_refs[0][...], w_refs[0][...])
        for x_ref, w_ref in zip(x_refs[1:], w_refs[1:]):
            total = total + mul(x_ref[...], w_ref[...])
        up = total[:, :hidden] + fb[...]
        up_o[...] = up
        act_o[...] = gelu(up).astype(bf16)
        qkv = total[:, hidden:] + qb[...]
        q_o[...] = turn(qkv[:, :pair], keep[...], high[...], low[...]).astype(bf16)
        k_o[...] = turn(qkv[:, pair : 2 * pair], keep[...], high[...], low[...]).astype(bf16)
        v_o[...] = qkv[:, 2 * pair :].astype(bf16)

    def rowed(cols):
        return pl.BlockSpec((block, cols), lambda i: (i, 0))

    def fixed(array):
        return pl.BlockSpec(array.shape, lambda i: (0, 0))

    return pl.pallas_call(
        kernel,
        grid=(rows // block,),
        in_specs=[rowed(width)] * 4
        + [fixed(w) for w in ws]
        + [fixed(fc1_bias), fixed(qkv_bias)]
        + [rowed(pair)] * 3,
        out_specs=[rowed(hidden), rowed(hidden), rowed(pair), rowed(pair), rowed(pair)],
        out_shape=[
            jax.ShapeDtypeStruct((rows, hidden), f32),
            jax.ShapeDtypeStruct((rows, hidden), bf16),
        ]
        + [jax.ShapeDtypeStruct((rows, pair), bf16)] * 3,
        compiler_params=params(),
        cost_estimate=cost(
            8 * rows * width * (hidden + 3 * pair), 8 * rows * width + 10 * rows * hidden
        ),
    )(*xs, *ws, fc1_bias, qkv_bias, *tables)


def slope_step(gs, ws, up_pre):
    rows, width = gs[0].shape
    hidden = up_pre.shape[1]
    pair = ws[0].shape[0] - hidden
    block = 512

    def kernel(*refs):
        g_refs, w_refs, up = refs[:4], refs[4:8], refs[8]
        dup_o, dattn_o, bias_o = refs[9:]
        total = mul(g_refs[0][...], w_refs[0][...], NT)
        for g_ref, w_ref in zip(g_refs[1:], w_refs[1:]):
            total = total + mul(g_ref[...], w_ref[...], NT)
        d_up = (total[:, :hidden] * gelu_slope(up[...])).astype(bf16)
        dup_o[...] = d_up
        dattn_o[...] = total[:, hidden:].astype(bf16)

        @pl.when(pl.program_id(0) == 0)
        def _():
            bias_o[...] = jnp.zeros_like(bias_o)

        bias_o[...] += jnp.sum(d_up.astype(f32), axis=0, keepdims=True)

    def rowed(cols):
        return pl.BlockSpec((block, cols), lambda i: (i, 0))

    def fixed(shape):
        return pl.BlockSpec(shape, lambda i: (0, 0))

    return pl.pallas_call(
        kernel,
        grid=(rows // block,),
        in_specs=[rowed(width)] * 4 + [fixed(w.shape) for w in ws] + [rowed(hidden)],
        out_specs=[rowed(hidden), rowed(pair), fixed((1, hidden))],
        out_shape=[
            jax.ShapeDtypeStruct((rows, hidden), bf16),
            jax.ShapeDtypeStruct((rows, pair), bf16),
            jax.ShapeDtypeStruct((1, hidden), f32),
        ],
        compiler_params=params(),
        cost_estimate=cost(
            8 * rows * width * (hidden + pair), 8 * rows * width + 6 * rows * hidden
        ),
    )(*gs, *ws, up_pre)


def spread(hidden_vals, pair_vals, ws, received, transposed):
    rows, hidden = hidden_vals.shape
    pair = pair_vals.shape[1]
    width = ws[0].shape[0] if transposed else ws[0].shape[1]
    block = min(1024, rows)
    extra = len(received)

    def kernel(*refs):
        a, b = refs[0][...], refs[1][...]
        w_refs, got, outs = refs[2:4], refs[4 : 4 + extra], refs[4 + extra :]
        for place in range(2):
            w = w_refs[place]
            if transposed:
                total = mul(a, w[:, :hidden], NT) + mul(b, w[:, hidden:], NT)
            else:
                total = mul(a, w[:hidden], NN) + mul(b, w[hidden:], NN)
            if extra:
                total = total + got[place][...].astype(f32)
            outs[place][...] = total.astype(bf16)

    def rowed(cols):
        return pl.BlockSpec((block, cols), lambda i: (i, 0))

    return pl.pallas_call(
        kernel,
        grid=(rows // block,),
        in_specs=[rowed(hidden), rowed(pair)]
        + [pl.BlockSpec(w.shape, lambda i: (0, 0)) for w in ws]
        + [rowed(width)] * extra,
        out_specs=[rowed(width)] * 2,
        out_shape=[jax.ShapeDtypeStruct((rows, width), bf16)] * 2,
        compiler_params=params(),
        cost_estimate=cost(
            4 * rows * width * (hidden + pair), 2 * rows * (hidden + pair + (2 + extra) * width)
        ),
    )(hidden_vals, pair_vals, *ws, *received)


def grad_blocks(half, fixed_side, moving, fixed_left):
    rows, cols = fixed_side.shape
    width = moving[0].shape[1]
    out_rows, out_cols = (cols, width) if fixed_left else (width, cols)
    block = min(1024, rows)
    steps = rows // block
    cut = out_rows // 2

    def kernel(half_ref, *refs):
        keep_o, send_o, total = refs[5:]
        step = pl.program_id(0)
        side = refs[0][...]
        for place in range(4):
            other = refs[1 + place][...]
            part = mul(side, other, TN) if fixed_left else mul(other, side, TN)

            @pl.when(step == 0)
            def _():
                total[place] = part

            @pl.when(step > 0)
            def _():
                total[place] += part

        @pl.when(step == steps - 1)
        def _():
            mine = pl.multiple_of(half_ref[0] * cut, cut)
            theirs = pl.multiple_of((1 - half_ref[0]) * cut, cut)
            for place in range(4):
                keep_o[place] = total[place, pl.ds(mine, cut)].astype(bf16)
                send_o[place] = total[place, pl.ds(theirs, cut)].astype(bf16)

    def rowed(n):
        return pl.BlockSpec((block, n), lambda i, s: (i, 0))

    whole = pl.BlockSpec((4, cut, out_cols), lambda i, s: (0, 0, 0))
    return pl.pallas_call(
        kernel,
        grid_spec=pltpu.PrefetchScalarGridSpec(
            num_scalar_prefetch=1,
            grid=(steps,),
            in_specs=[rowed(cols)] + [rowed(width)] * 4,
            out_specs=[whole] * 2,
            scratch_shapes=[pltpu.VMEM((4, out_rows, out_cols), f32)],
        ),
        out_shape=[jax.ShapeDtypeStruct((4, cut, out_cols), bf16)] * 2,
        compiler_params=params(),
        cost_estimate=cost(8 * rows * cols * width, 2 * rows * (cols + 4 * width)),
    )(half, fixed_side, *moving)


def add_halves(keep, received):
    shape = (2,) + keep.shape[1:]

    def kernel(keep_ref, received_ref, near_o, far_o):
        near_o[...] = (keep_ref[:2].astype(f32) + received_ref[:2].astype(f32)).astype(bf16)
        far_o[...] = (keep_ref[2:].astype(f32) + received_ref[2:].astype(f32)).astype(bf16)

    return pl.pallas_call(
        kernel,
        out_shape=[jax.ShapeDtypeStruct(shape, bf16)] * 2,
        compiler_params=params(),
        cost_estimate=cost(keep.size, 6 * keep.size),
    )(keep, received)


def lay_out(places, mine, theirs, by_rows):
    _, cut, cols = mine.shape

    def kernel(places_ref, mine_ref, theirs_ref, out_ref):
        half = pl.program_id(0)

        def fill(source):
            for place in range(4):
                spot = places_ref[place]
                value = source[place].astype(f32)
                if by_rows:
                    out_ref[spot, 0] = value
                else:
                    out_ref[:, pl.ds(pl.multiple_of(spot * cols, 128), cols)] = value

        @pl.when(half == places_ref[4])
        def _():
            fill(mine_ref)

        @pl.when(half != places_ref[4])
        def _():
            fill(theirs_ref)

    if by_rows:
        shape = (4, 2, cut, cols)
        out_spec = pl.BlockSpec((4, 1, cut, cols), lambda h, s: (0, h, 0, 0))
    else:
        shape = (2 * cut, 4 * cols)
        out_spec = pl.BlockSpec((cut, 4 * cols), lambda h, s: (h, 0))
    part = pl.BlockSpec((4, cut, cols), lambda h, s: (0, 0, 0))
    result = pl.pallas_call(
        kernel,
        grid_spec=pltpu.PrefetchScalarGridSpec(
            num_scalar_prefetch=1, grid=(2,), in_specs=[part, part], out_specs=out_spec
        ),
        out_shape=jax.ShapeDtypeStruct(shape, f32),
        compiler_params=params(),
        cost_estimate=cost(0, 12 * mine.size),
    )(places, mine, theirs)
    return result.reshape(8 * cut, cols) if by_rows else result


def pick(same, first, second):
    def kernel(same_ref, first_ref, second_ref, own_o, other_o):
        @pl.when(same_ref[0] == 1)
        def _():
            own_o[...] = first_ref[...]
            other_o[...] = second_ref[...]

        @pl.when(same_ref[0] != 1)
        def _():
            own_o[...] = second_ref[...]
            other_o[...] = first_ref[...]

    whole = pl.BlockSpec(first.shape, lambda i, s: (0, 0))
    return pl.pallas_call(
        kernel,
        grid_spec=pltpu.PrefetchScalarGridSpec(
            num_scalar_prefetch=1, grid=(1,), in_specs=[whole] * 2, out_specs=[whole] * 2
        ),
        out_shape=[jax.ShapeDtypeStruct(first.shape, first.dtype)] * 2,
        compiler_params=params(),
        cost_estimate=cost(0, 8 * first.size),
    )(same, first, second)


def attend(lowest, q_rot, k_rot, v_low, begin):
    rows, pair = q_rot.shape
    block = 256
    steps = rows // block
    heads = pair // HEAD_DIM
    scale = 1.0 / math.sqrt(HEAD_DIM)

    def kernel(lowest_ref, q_ref, k_ref, v_ref, begin_ref, o_ref, of_ref, lse_ref, v_turned):
        step = pl.program_id(0)

        @pl.when(step == 0)
        def _():
            v_turned[...] = v_ref[...].T

        lane = lax.broadcasted_iota(jnp.int32, (block, pair), 1) // HEAD_DIM
        query = q_ref[...] * jnp.asarray(scale, bf16)
        zero = jnp.zeros_like(query)
        q_heads = [jnp.where(lane == head, query, zero) for head in range(heads)]
        begins = begin_ref[...]
        own = step * block + lax.broadcasted_iota(jnp.int32, (block, block), 1)
        key_at = lax.broadcasted_iota(jnp.int32, (block, block), 0)

        def body(place, carry):
            at = pl.multiple_of(place * block, block)
            keys = k_ref[pl.ds(at, block), :]
            index = key_at + at
            seen = (index <= own) & (index >= begins)
            new = []
            for head in range(heads):
                top, total, out = carry[head]
                score = jnp.where(seen, mul(keys, q_heads[head], NT), -1000000000.0)
                new_top = jnp.maximum(top, jnp.max(score, axis=0, keepdims=True))
                shifted = jnp.exp(score - new_top)
                fade = jnp.exp(top - new_top)
                values = v_turned[head * HEAD_DIM : (head + 1) * HEAD_DIM, pl.ds(at, block)]
                new.append(
                    (
                        new_top,
                        total * fade + jnp.sum(shifted, axis=0, keepdims=True),
                        out * fade + mul(values, shifted.astype(bf16)),
                    )
                )
            return tuple(new)

        initial = (
            jnp.full((1, block), -1000000000.0, f32),
            jnp.zeros((1, block), f32),
            jnp.zeros((HEAD_DIM, block), f32),
        )
        result = lax.fori_loop(lowest_ref[step], step + 1, body, (initial,) * heads)
        out = jnp.concatenate([out / total for _, total, out in result], axis=0).T
        o_ref[...] = out.astype(bf16)
        of_ref[...] = out
        for head in range(heads):
            top, total, _ = result[head]
            lse_ref[head : head + 1, :] = top + jnp.log(total)

    def rowed(cols):
        return pl.BlockSpec((block, cols), lambda i, s: (i, 0))

    whole = pl.BlockSpec((rows, pair), lambda i, s: (0, 0))
    along = lambda n: pl.BlockSpec((n, block), lambda i, s: (0, i))
    return pl.pallas_call(
        kernel,
        grid_spec=pltpu.PrefetchScalarGridSpec(
            num_scalar_prefetch=1,
            grid=(steps,),
            in_specs=[rowed(pair), whole, whole, along(1)],
            out_specs=[rowed(pair), rowed(pair), along(heads)],
            scratch_shapes=[pltpu.VMEM((pair, rows), bf16)],
        ),
        out_shape=[
            jax.ShapeDtypeStruct((rows, pair), bf16),
            jax.ShapeDtypeStruct((rows, pair), f32),
            jax.ShapeDtypeStruct((heads, rows), f32),
        ],
        compiler_params=params(),
        cost_estimate=cost(4 * rows * LONGEST * pair, 12 * rows * pair, rows * LONGEST),
    )(lowest, q_rot, k_rot, v_low, begin)


def attend_back(lowest, q_rot, k_rot, v_low, begin, d_attn, out_full, lse, tables):
    rows, pair = q_rot.shape
    block = 256
    steps = rows // block
    heads = pair // HEAD_DIM
    scale = 1.0 / math.sqrt(HEAD_DIM)

    def kernel(lowest_ref, q_ref, k_ref, v_ref, begin_ref, do_ref, of_ref, lse_ref,
               keep_ref, high_ref, low_ref, grad_ref, bias_ref, k_turned, dk, dv):
        step = pl.program_id(0)

        @pl.when(step == 0)
        def _():
            k_turned[...] = k_ref[...].T
            dk[...] = jnp.zeros_like(dk)
            dv[...] = jnp.zeros_like(dv)
            bias_ref[...] = jnp.zeros_like(bias_ref)

        lane = lax.broadcasted_iota(jnp.int32, (block, pair), 1) // HEAD_DIM
        query = q_ref[...] * jnp.asarray(scale, bf16)
        grads = do_ref[...]
        zero = jnp.zeros_like(query)
        q_heads = [jnp.where(lane == head, query, zero) for head in range(heads)]
        d_heads = [jnp.where(lane == head, grads, zero) for head in range(heads)]
        product = (grads.astype(f32) * of_ref[...]).T
        dots = [
            jnp.sum(product[head * HEAD_DIM : (head + 1) * HEAD_DIM], axis=0, keepdims=True)
            for head in range(heads)
        ]
        lses = [lse_ref[head : head + 1, :] for head in range(heads)]
        begins = begin_ref[...]
        own = step * block + lax.broadcasted_iota(jnp.int32, (block, block), 1)
        key_at = lax.broadcasted_iota(jnp.int32, (block, block), 0)

        def body(place, carry):
            at = pl.multiple_of(place * block, block)
            keys = k_ref[pl.ds(at, block), :]
            values = v_ref[pl.ds(at, block), :]
            index = key_at + at
            seen = (index <= own) & (index >= begins)
            new, d_key, d_value = [], None, None
            for head in range(heads):
                score = jnp.where(seen, mul(keys, q_heads[head], NT), -1000000000.0)
                prob = jnp.exp(score - lses[head])
                d_prob = mul(values, d_heads[head], NT)
                d_score = (prob * (d_prob - dots[head])).astype(bf16)
                value_part = mul(prob.astype(bf16), d_heads[head])
                key_part = mul(d_score, q_heads[head])
                d_value = value_part if d_value is None else d_value + value_part
                d_key = key_part if d_key is None else d_key + key_part
                turned = k_turned[head * HEAD_DIM : (head + 1) * HEAD_DIM, pl.ds(at, block)]
                new.append(carry[head] + mul(turned, d_score))
            dv[pl.ds(at, block), :] += d_value
            dk[pl.ds(at, block), :] += d_key
            return tuple(new)

        result = lax.fori_loop(
            lowest_ref[step], step + 1, body, (jnp.zeros((HEAD_DIM, block), f32),) * heads
        )
        d_query = jnp.concatenate(result, axis=0).T * scale
        here = pl.ds(pl.multiple_of(step * block, block), block)
        grad_ref[here, :pair] = turn(
            d_query, keep_ref[here, :], -high_ref[here, :], -low_ref[here, :]
        ).astype(bf16)

        @pl.when(step == steps - 1)
        def _():
            def finish(place, carry):
                spot = pl.ds(pl.multiple_of(place * block, block), block)
                d_key = turn(dk[spot, :], keep_ref[spot, :], -high_ref[spot, :], -low_ref[spot, :])
                grad_ref[spot, pair : 2 * pair] = d_key.astype(bf16)
                grad_ref[spot, 2 * pair :] = dv[spot, :].astype(bf16)
                bias_ref[...] += jnp.sum(grad_ref[spot, :].astype(f32), axis=0, keepdims=True)
                return carry

            lax.fori_loop(0, steps, finish, 0)

    def rowed(cols):
        return pl.BlockSpec((block, cols), lambda i, s: (i, 0))

    def fixed(shape):
        return pl.BlockSpec(shape, lambda i, s: (0, 0))

    along = lambda n: pl.BlockSpec((n, block), lambda i, s: (0, i))
    whole = fixed((rows, pair))
    return pl.pallas_call(
        kernel,
        grid_spec=pltpu.PrefetchScalarGridSpec(
            num_scalar_prefetch=1,
            grid=(steps,),
            in_specs=[rowed(pair), whole, whole, along(1), rowed(pair), rowed(pair), along(heads)]
            + [whole] * 3,
            out_specs=[fixed((rows, 3 * pair)), fixed((1, 3 * pair))],
            scratch_shapes=[
                pltpu.VMEM((pair, rows), bf16),
                pltpu.VMEM((rows, pair), f32),
                pltpu.VMEM((rows, pair), f32),
            ],
        ),
        out_shape=[
            jax.ShapeDtypeStruct((rows, 3 * pair), bf16),
            jax.ShapeDtypeStruct((1, 3 * pair), f32),
        ],
        compiler_params=params(),
        cost_estimate=cost(10 * rows * LONGEST * pair, 16 * rows * pair, rows * LONGEST),
    )(lowest, q_rot, k_rot, v_low, begin, d_attn, out_full, lse, *tables)


def after(value, *earlier):
    return lax.optimization_barrier((value,) + earlier)[0]


def step(
    tokens,
    segment_ids,
    ln_gain,
    ln_bias,
    qkv_weight,
    qkv_bias,
    out_weight,
    fc1_weight,
    fc1_bias,
    fc2_weight,
    out_bias,
    out_grad,
):
    col_index = lax.axis_index(COL)
    dp_index = lax.axis_index(DP)
    _, local_width = tokens.shape
    full_width = local_width * lax.axis_size(COL)
    group_rows = segment_ids.shape[1]
    pair_dim = qkv_weight.shape[3]

    half = (dp_index & 1).astype(jnp.int32)
    far_block = (1 - (col_index >> 1)) * 2 + half
    packs = jnp.stack([col_index, col_index ^ 1, far_block]).astype(jnp.int32)
    places = jnp.stack([col_index, col_index ^ 2, col_index ^ 1, col_index ^ 3, half]).astype(
        jnp.int32
    )
    same = (half == (col_index & 1)).astype(jnp.int32).reshape(1)
    half = half.reshape(1)

    token_f = tokens.astype(f32)
    ln_local = jnp.stack([jnp.sum(token_f, axis=1), jnp.sum(token_f * token_f, axis=1)])
    ln_sums = ln_local + swap_bits(ln_local, COL, 1)
    in_own, in_near, in_far = pack_in(
        packs, fc1_weight, after(qkv_weight, ln_local).reshape(local_width, -1)
    )
    ln_far = swap_bits(after(ln_sums, in_far), COL, 2)
    in_first = swap_bits(after(in_far, ln_far), COL, 2)
    ln_sums = ln_sums + ln_far
    row_mean = ln_sums[0] / full_width
    variance = ln_sums[1] / full_width - row_mean * row_mean
    inv_std = lax.rsqrt(variance + epsilon)
    centred = (token_f - row_mean[:, None]) * inv_std[:, None]
    normed = (centred * ln_gain + ln_bias).astype(bf16)
    normed_0 = lax.all_gather(normed, ROW, axis=0, tiled=True)
    out_own, out_near, out_far = pack_out(packs, fc2_weight, after(out_weight, normed))
    cot_0 = lax.all_gather(after(out_grad, normed), ROW, axis=0, tiled=True)

    in_1 = swap_bits(after(in_near, normed), COL, 1)
    out_1 = swap_bits(out_near, COL, 1)
    in_second = swap_bits(in_first, DP, 1)
    out_first = swap_bits(after(out_far, in_first), COL, 2)
    in_2, in_pass = pick(same, in_first, in_second)
    in_3 = swap_bits(in_pass, COL, 1)
    out_second = swap_bits(after(out_first, in_second), DP, 1)
    out_2, out_pass = pick(same, out_first, out_second)
    out_3 = swap_bits(out_pass, COL, 1)
    in_mats = [in_own, in_1, in_2, in_3]
    out_mats = [out_own, out_1, out_2, out_3]

    pos = positions(segment_ids[0])
    tables = rope_tables(pos, pair_dim)
    start = jnp.arange(group_rows, dtype=jnp.int32) - pos
    lowest = start[::256] // 256
    begin = start.reshape(1, -1)

    normed_2 = swap_bits(after(normed_0, out_first), COL, 2)
    normed_1 = swap_bits(normed_0, COL, 1)
    cot_2 = swap_bits(after(cot_0, normed_2), COL, 2)
    normed_3 = swap_bits(normed_2, COL, 1)
    cot_1 = swap_bits(cot_0, COL, 1)
    normed_all = [normed_0, normed_1, normed_2, normed_3]
    up_pre, activation, q_rot, k_rot, v_low = forward_step(
        normed_all, in_mats, fc1_bias.reshape(1, -1), qkv_bias.reshape(1, -1), tables
    )
    attn_low, attn_full, lse = attend(lowest, q_rot, k_rot, v_low, begin)
    give = spread(activation, attn_low, [out_mats[1], out_mats[3]], [], False)
    got = [swap_bits(give[0], COL, 1), swap_bits(give[1], COL, 1)]
    mix_near, mix_far = spread(
        activation, attn_low, [out_mats[0], out_mats[2]], got, False
    )
    cot_3 = swap_bits(cot_2, COL, 1)
    cot_all = [cot_0, cot_1, cot_2, cot_3]

    def sum_halves(keep, send):
        received = swap_bits(send, DP, 1)
        near, far = add_halves(keep, received)
        for bit in all_bits(DP)[1:]:
            near = (near.astype(f32) + swap_bits(near, DP, bit).astype(f32)).astype(bf16)
            far = (far.astype(f32) + swap_bits(far, DP, bit).astype(f32)).astype(bf16)
        return near, far

    def cross(near, far):
        crossed = swap_bits(far, COL, 2)
        joined = stack_blocks([(near, 1), (crossed, 1)])
        passed = swap_bits(joined, COL, 1)
        mine = stack_blocks([(near, 0), (crossed, 0), (passed, 0), (passed, 1)])
        return crossed, mine

    def finish(mine, theirs, by_rows):
        return lay_out(places, mine, theirs, by_rows)

    fc2_keep, fc2_send = grad_blocks(half, activation, cot_all, True)
    d_up, d_attn, fc1_sums = slope_step(cot_all, out_mats, after(up_pre, fc2_send))
    mix_recv = swap_bits(after(mix_far, cot_2), COL, 2)
    fc2_near, fc2_far = sum_halves(fc2_keep, fc2_send)
    fc1_keep, fc1_send = grad_blocks(half, d_up, normed_all, False)
    d_proj, qkv_sums = attend_back(
        lowest, q_rot, k_rot, v_low, begin, after(d_attn, fc1_send), attn_full, lse, tables
    )
    mix_total = (mix_near.astype(f32) + mix_recv.astype(f32)).astype(bf16)
    mixed = lax.psum_scatter(mix_total, ROW, scatter_dimension=0, tiled=True).astype(f32)
    fc2_crossed, fc2_mine = cross(fc2_near, after(fc2_far, mix_total))
    give = spread(d_up, d_proj, [in_mats[1], in_mats[3]], [], True)
    got = [swap_bits(give[0], COL, 1), swap_bits(give[1], COL, 1)]
    fc1_near, fc1_far = sum_halves(fc1_keep, fc1_send)
    fc1_crossed, fc1_mine = cross(fc1_near, after(fc1_far, fc2_crossed))
    qkv_keep, qkv_send = grad_blocks(half, after(d_proj, give[0]), normed_all, False)
    fc2_theirs = swap_bits(after(fc2_mine, fc1_near), DP, 1)
    back_near, back_far = spread(after(d_up, qkv_send), d_proj, [in_mats[0], in_mats[2]], got, True)
    back_recv = swap_bits(after(back_far, fc1_crossed), COL, 2)
    out_keep, out_send = grad_blocks(half, after(attn_low, back_far), cot_all, True)
    qkv_near, qkv_far = sum_halves(qkv_keep, after(qkv_send, fc2_theirs))
    fc1_theirs = swap_bits(after(fc1_mine, qkv_near), DP, 1)
    back_total = (back_near.astype(f32) + back_recv.astype(f32)).astype(bf16)
    d_normed = lax.psum_scatter(
        back_total, ROW, scatter_dimension=0, tiled=True
    ).astype(f32)
    qkv_crossed, qkv_mine = cross(qkv_near, after(qkv_far, back_total))
    wo_near, wo_far = sum_halves(out_keep, after(out_send, fc1_theirs))
    qkv_theirs = swap_bits(after(qkv_mine, wo_near), DP, 1)
    _, wo_mine = cross(wo_near, after(wo_far, qkv_crossed))
    wo_theirs = swap_bits(after(wo_mine, qkv_theirs), DP, 1)
    fc2_weight_grad = finish(fc2_mine, fc2_theirs, True)
    fc1_weight_grad = finish(fc1_mine, fc1_theirs, False)
    qkv_weight_grad = finish(qkv_mine, qkv_theirs, False)
    out_weight_grad = finish(wo_mine, wo_theirs, True)

    out = (token_f + mixed + out_bias).astype(bf16)
    d_hat = d_normed * ln_gain
    back_sums = total_over(
        jnp.stack([jnp.sum(d_hat, axis=1), jnp.sum(d_hat * centred, axis=1)]), (COL,)
    )
    tokens_grad = out_grad.astype(f32) + inv_std[:, None] * (
        d_hat - back_sums[0][:, None] / full_width - centred * (back_sums[1][:, None] / full_width)
    )
    vector_sums = total_over(
        jnp.stack(
            [
                jnp.sum(d_normed * centred, axis=0),
                jnp.sum(d_normed, axis=0),
                jnp.sum(out_grad.astype(f32), axis=0),
            ]
        ),
        (ROW, DP),
    )
    bias_sums = total_over(jnp.concatenate([qkv_sums, fc1_sums], axis=1), (DP,))[0]
    return (
        out,
        tokens_grad,
        vector_sums[0],
        vector_sums[1],
        qkv_weight_grad.reshape(qkv_weight.shape),
        bias_sums[: 3 * pair_dim].reshape(qkv_bias.shape),
        out_weight_grad,
        fc1_weight_grad,
        bias_sums[3 * pair_dim :],
        fc2_weight_grad,
        vector_sums[2],
    )


def solution(mesh):
    return jax.shard_map(
        step,
        mesh=mesh,
        in_specs=(
            P((DP, ROW), COL),
            P(DP, None),
            P(COL),
            P(COL),
            P(COL, ROW, None, None),
            P((ROW, COL), None, None),
            P(ROW, COL),
            P(COL, ROW),
            P((ROW, COL)),
            P(ROW, COL),
            P(COL),
            P((DP, ROW), COL),
        ),
        out_specs=(
            P((DP, ROW), COL),
            P((DP, ROW), COL),
            P(COL),
            P(COL),
            P(COL, ROW, None, None),
            P((ROW, COL), None, None),
            P(ROW, COL),
            P(COL, ROW),
            P((ROW, COL)),
            P(ROW, COL),
            P(COL),
        ),
        check_vma=False,
    )
```

time: 977 us -> 528 us (0.54)
  waiting for transfers between devices: 638 us -> 237 us
  Pallas kernels: 0 us -> 188 us
  matrix products: 137 us -> 0 us
  local copies, waits for them, and re-layouts: 76.5 us -> 25.6 us
  blocking collectives: 40.6 us -> 0 us
  other arithmetic: 61.1 us -> 21.5 us
  starting transfers between devices: 0.92 us -> 39.4 us
    reduce_scatter x6 -> x2, waiting for transfers between devices: 291 us -> 0.01 us  [the longest x1 0.01 us: step(): lax.psum_scatter(back_total, ROW, scatter_dimension=0, tiled=True)]
    pallas_call x0 -> x32, Pallas kernels: none -> 188 us  [the longest x4 36.9 us: grad_blocks(): pl.pallas_call(kernel, grid_spec=pltpu.PrefetchScalarGridSpec(num_scalar_...]
    ppermute x0 -> x44, waiting for transfers between devices: none -> 185 us  [swap_bits(): lax.ppermute(value, axis, [(place, place ^ bit) for place in range(count)])]
    psum x1 -> x0, waiting for transfers between devices: 153 us -> none  [local(): lax.psum(qkv_weight_grad.astype(jnp.bfloat16), 'dp').astype(jnp.float32)]
    all_gather x6 -> x2, waiting for transfers between devices: 193 us -> 52.4 us  [the longest x1 42.8 us: step(): cot_0 = lax.all_gather(after(out_grad, normed), ROW, axis=0, tiled=True)]
    dot_general x36 -> x0, matrix products: 137 us -> none  [the longest x1 12.5 us: local(): jnp.einsum('td,kd->tk', cot_rows, fc2_weight, preferred_element_type=jnp....]
    psum x4 -> x0, blocking collectives: 40.6 us -> none  [the longest x1 21 us: local(): lax.psum((jnp.sum(d_normed * centred, axis=0), jnp.sum(d_normed, axis=0))...]
    ppermute x0 -> x44, starting transfers between devices: none -> 39.3 us  [swap_bits(): lax.ppermute(value, axis, [(place, place ^ bit) for place in range(count)])]
  transfers between devices with their start and end apart: 13 -> 48, of which waited for: 12 -> 20; matrix products, arithmetic and copies ran while one was open for 27% -> 5% of each run, Pallas kernels for 0% -> 36%
where the time goes in v1:
time: 528 us; the launch traced here: 526 us
  waiting for transfers between devices  237 us (45%)
  Pallas kernels  188 us (36%)
  starting transfers between devices  39.4 us (7%)
  local copies, waits for them, and re-layouts  25.6 us (5%)
  other arithmetic  21.5 us (4%)
  between operations  14.1 us (3%)
    ppermute x44, waiting for transfers between devices, swap_bits(): lax.ppermute(value, axis, [(place, place ^ bit) for place in range(count)])  185 us
    all_gather x1, waiting for transfers between devices, step(): cot_0 = lax.all_gather(after(out_grad, normed), ROW, axis=0, tiled=True)  42.8 us
    ppermute x44, starting transfers between devices, swap_bits(): lax.ppermute(value, axis, [(place, place ^ bit) for place in range(count)])  39.3 us
    pallas_call x4, Pallas kernels, grad_blocks(): pl.pallas_call(kernel, grid_spec=pltpu.PrefetchScalarGridSpec(num_scalar_...  36.9 us
    pallas_call x4, Pallas kernels, spread(): pl.pallas_call(kernel, grid=(rows // block,), in_specs=[rowed(hidden), ro...  29.7 us
    pallas_call x1, Pallas kernels, attend_back(): pl.pallas_call(kernel, grid_spec=pltpu.PrefetchScalarGridSpec(num_scalar_...  21.4 us
    pallas_call x8, Pallas kernels, stack_blocks(): pl.pallas_call(kernel, out_shape=jax.ShapeDtypeStruct((len(items),) + sha...  17.1 us
    pallas_call x1, Pallas kernels, attend(): pl.pallas_call(kernel, grid_spec=pltpu.PrefetchScalarGridSpec(num_scalar_...  17.1 us
  transfers between devices with their start and end apart: 48, of which 20 were waited for; matrix products, arithmetic and copies ran while one was open for 5% of the time, Pallas kernels for 36%

profile of v1, /device:TPU:0, one launch (start us, length us, event | category | flops | bytes accessed | tf_op | source)
XLA Modules:
  0.0 526.4 jit_solution(17237996389712855375)
XLA Ops:
  29.0 16.5 %collective-permute-done.3.first_ref = bf16[512,896]{1,0:T(8,128)(2,1)S(1)} collective-permute-done((bf16[512,896]{1,0:T(8,128)(2,1)}, bf16[512,896]{1,0:T(8,128)(2,1)S(1)}, u32[]{:S(2)}, u32[]{:S(2)}) %collective-permute-start.3) | collective-permute-done | bytes 917536 | tf_op jit(solution)/shard_map/ppermute | solution.py:91
  47.3 14.0 %collective-permute-done.4.first_ref = bf16[640,512]{1,0:T(8,128)(2,1)S(1)} collective-permute-done((bf16[640,512]{1,0:T(8,128)(2,1)}, bf16[640,512]{1,0:T(8,128)(2,1)S(1)}, u32[]{:S(2)}, u32[]{:S(2)}) %collective-permute-start.4) | collective-permute-done | bytes 655392 | tf_op jit(solution)/shard_map/ppermute | solution.py:91
  61.3 9.6 %all-gather.3.cloned.1.call-done.refs_0_.refs_1_ = bf16[2048,512]{1,0:T(8,128)(2,1)} async-done(((bf16[512,512]{1,0:T(8,128)(2,1)}), bf16[2048,512]{1,0:T(8,128)(2,1)}) %all-gather.3.cloned.1.call-update) | async-done | bytes 2097168 | tf_op jit(solution)/shard_map/all_gather | solution.py:683
  74.2 42.8 %all-gather.5.cloned.1.call-done.refs_1_.refs_0_ = bf16[2048,512]{1,0:T(8,128)(2,1)} async-done(((bf16[512,512]{1,0:T(8,128)(2,1)}), bf16[2048,512]{1,0:T(8,128)(2,1)}) %all-gather.5.cloned.1.call-update) | async-done | bytes 2097168 | tf_op jit(solution)/shard_map/all_gather | solution.py:685
  125.3 12.1 %collective-permute-done.10.second_ref = bf16[640,512]{1,0:T(8,128)(2,1)} collective-permute-done((bf16[640,512]{1,0:T(8,128)(2,1)S(1)}, bf16[640,512]{1,0:T(8,128)(2,1)}, u32[]{:S(2)}, u32[]{:S(2)}) %collective-permute-start.10) | collective-permute-done | bytes 655392 | tf_op jit(solution)/shard_map/ppermute | solution.py:91
  147.9 17.2 %collective-permute-done.15.refs_3_.refs_2_ = bf16[2048,512]{1,0:T(8,128)(2,1)} collective-permute-done((bf16[2048,512]{1,0:T(8,128)(2,1)}, bf16[2048,512]{1,0:T(8,128)(2,1)}, u32[]{:S(2)}, u32[]{:S(2)}) %collective-permute-start.15) | collective-permute-done | bytes 2097184 | tf_op jit(solution)/shard_map/ppermute | solution.py:91
  165.1 15.6 %shard_map.206 = (f32[2048,512]{1,0:T(8,128)}, bf16[2048,512]{1,0:T(8,128)(2,1)}, bf16[2048,128]{1,0:T(8,128)(2,1)}, bf16[2048,128]{1,0:T(8,128)(2,1)}, bf16[2048,128]{1,0:T(8,128)(2,1)}) custom-call(bf16[2048,512]{1,0:T(8,128)(2,1)} %all-gather.3.cloned.1.call-done.refs_0_.refs_1_, bf16[2048,512]{1,0:T(8,128)(2,1)} %collective-permute-done.2.refs_1_.refs_2_, ...), custom_call_target="tpu_custom_call" | custom-call | flops 7516192768 | bytes 18874368 | tf_op jit(solution)/shard_map/pallas_call | solution.py:211
  180.7 17.1 %shard_map.207 = (bf16[2048,128]{1,0:T(8,128)(2,1)}, f32[2048,128]{1,0:T(8,128)}, f32[2,2048]{1,0:T(2,128)}) custom-call(s32[8]{0:T(128)} %and_select_fusion.lowest_ref, bf16[2048,128]{1,0:T(8,128)(2,1)} %get-tuple-element.99.q_ref, bf16[2048,128]{1,0:T(8,128)(2,1)} %get-tuple-element.100.k_ref, bf16[2048,128]{1,0:T(8,128)(2,1)} %get-tuple-element.101.v_ref, ...), custom_call_target="tpu_custom_call" | custom-call | flops 1073741824 | bytes 3145728 | tf_op jit(solution)/shard_map/pallas_call | solution.py:508
  198.7 6.2 %shard_map.209 = (bf16[2048,512]{1,0:T(8,128)(2,1)}, bf16[2048,512]{1,0:T(8,128)(2,1)}) custom-call(bf16[2048,512]{1,0:T(8,128)(2,1)} %get-tuple-element.98.refs_0_, bf16[2048,128]{1,0:T(8,128)(2,1)} %get-tuple-element.147.refs_1_.refs_0_, bf16[640,512]{1,0:T(8,128)(2,1)} %copy-done.33, bf16[640,512]{1,0:T(8,128)(2,1)} %collective-permute-done.12.refs_3_.refs_7_), custom_call_target="tpu_custom_call" | custom-call | flops 2684354560 | bytes 6815744 | tf_op jit(solution)/shard_map/pallas_call | solution.py:299
  207.5 10.4 %shard_map.211 = (bf16[4,256,512]{2,1,0:T(8,128)(2,1)}, bf16[4,256,512]{2,1,0:T(8,128)(2,1)}) custom-call(s32[1]{0:T(128)} %bitcast.15.half_ref, bf16[2048,512]{1,0:T(8,128)(2,1)} %get-tuple-element.98.refs_0_, bf16[2048,512]{1,0:T(8,128)(2,1)} %all-gather.5.cloned.1.call-done.refs_1_.refs_0_, bf16[2048,512]{1,0:T(8,128)(2,1)} %copy-done.2, ...), custom_call_target="tpu_custom_call" | custom-call | flops 4294967296 | bytes 10485760 | tf_op jit(solution)/shard_map/pallas_call | solution.py:350
  220.8 7.0 %shard_map.210 = (bf16[2048,512]{1,0:T(8,128)(2,1)}, bf16[2048,512]{1,0:T(8,128)(2,1)}) custom-call(bf16[2048,512]{1,0:T(8,128)(2,1)} %get-tuple-element.98.refs_0_, bf16[2048,128]{1,0:T(8,128)(2,1)} %get-tuple-element.147.refs_1_.refs_0_, bf16[640,512]{1,0:T(8,128)(2,1)} %get-tuple-element.103.refs_2_.refs_4_, ...), custom_call_target="tpu_custom_call" | custom-call | flops 2684354560 | bytes 11010048 | tf_op jit(solution)/shard_map/pallas_call | solution.py:299
  229.3 12.9 %shard_map.212 = (bf16[2048,512]{1,0:T(8,128)(2,1)}, bf16[2048,128]{1,0:T(8,128)(2,1)}, f32[1,512]{1,0:T(1,128)}) custom-call(bf16[2048,512]{1,0:T(8,128)(2,1)} %all-gather.5.cloned.1.call-done.refs_1_.refs_0_, bf16[2048,512]{1,0:T(8,128)(2,1)} %copy-done.2, bf16[2048,512]{1,0:T(8,128)(2,1)} %collective-permute-done.15.refs_3_.refs_2_, ...), custom_call_target="tpu_custom_call" | custom-call | flops 5368709120 | bytes 14680064 | tf_op jit(solution)/shard_map/pallas_call | solution.py:259
  242.2 10.5 %shard_map.213 = (bf16[4,256,512]{2,1,0:T(8,128)(2,1)}, bf16[4,256,512]{2,1,0:T(8,128)(2,1)}) custom-call(s32[1]{0:T(128)} %bitcast.15.half_ref, bf16[2048,512]{1,0:T(8,128)(2,1)} %get-tuple-element.128.refs_0_, bf16[2048,512]{1,0:T(8,128)(2,1)} %all-gather.3.cloned.1.call-done.refs_0_.refs_1_, bf16[2048,512]{1,0:T(8,128)(2,1)} %collective-permute-done.2.refs_1_.refs_2_, ...), custom_call_target="tpu_custom_call" | custom-call | flops 4294967296 | bytes 10485760 | tf_op jit(solution)/shard_map/pallas_call | solution.py:350
  252.7 21.4 %shard_map.214 = (bf16[2048,384]{1,0:T(8,128)(2,1)}, f32[1,384]{1,0:T(1,128)}) custom-call(s32[8]{0:T(128)} %and_select_fusion.lowest_ref, bf16[2048,128]{1,0:T(8,128)(2,1)} %get-tuple-element.99.q_ref, bf16[2048,128]{1,0:T(8,128)(2,1)} %get-tuple-element.100.k_ref, bf16[2048,128]{1,0:T(8,128)(2,1)} %get-tuple-element.101.v_ref, ...), custom_call_target="tpu_custom_call" | custom-call | flops 2684354560 | bytes 4194304 | tf_op jit(solution)/shard_map/pallas_call | solution.py:612
  274.1 7.9 %shard_map.215 = (bf16[2048,512]{1,0:T(8,128)(2,1)}, bf16[2048,512]{1,0:T(8,128)(2,1)}) custom-call(bf16[2048,512]{1,0:T(8,128)(2,1)} %get-tuple-element.128.refs_0_, bf16[2048,384]{1,0:T(8,128)(2,1)} %get-tuple-element.126.refs_1_.refs_0_, bf16[512,896]{1,0:T(8,128)(2,1)} %copy-done.30, bf16[512,896]{1,0:T(8,128)(2,1)} %copy-done.31), custom_call_target="tpu_custom_call" | custom-call | flops 3758096384 | bytes 7864320 | tf_op jit(solution)/shard_map/pallas_call | solution.py:299
  290.0 17.8 %collective-permute-done.21.received_ref = bf16[4,256,512]{2,1,0:T(8,128)(2,1)S(1)} collective-permute-done((bf16[4,256,512]{2,1,0:T(8,128)(2,1)}, bf16[4,256,512]{2,1,0:T(8,128)(2,1)S(1)}, u32[]{:S(2)}, u32[]{:S(2)}) %collective-permute-start.21) | collective-permute-done | bytes 1048608 | tf_op jit(solution)/shard_map/ppermute | solution.py:91
  312.0 10.2 %shard_map.216 = (bf16[4,256,384]{2,1,0:T(8,128)(2,1)}, bf16[4,256,384]{2,1,0:T(8,128)(2,1)}) custom-call(s32[1]{0:T(128)} %bitcast.15.half_ref, bf16[2048,384]{1,0:T(8,128)(2,1)} %get-tuple-element.126.refs_1_.refs_0_, bf16[2048,512]{1,0:T(8,128)(2,1)} %all-gather.3.cloned.1.call-done.refs_0_.refs_1_, ...), custom_call_target="tpu_custom_call" | custom-call | flops 3221225472 | bytes 9961472 | tf_op jit(solution)/shard_map/pallas_call | solution.py:350
  322.2 8.6 %shard_map.217 = (bf16[2048,512]{1,0:T(8,128)(2,1)}, bf16[2048,512]{1,0:T(8,128)(2,1)}) custom-call(bf16[2048,512]{1,0:T(8,128)(2,1)} %get-tuple-element.128.refs_0_, bf16[2048,384]{1,0:T(8,128)(2,1)} %get-tuple-element.126.refs_1_.refs_0_, bf16[512,896]{1,0:T(8,128)(2,1)} %get-tuple-element.93.refs_4_.refs_2_, ...), custom_call_target="tpu_custom_call" | custom-call | flops 3758096384 | bytes 12058624 | tf_op jit(solution)/shard_map/pallas_call | solution.py:299
  332.4 45.2 %collective-permute-done.25 = bf16[2048,512]{1,0:T(8,128)(2,1)S(1)} collective-permute-done((bf16[2048,512]{1,0:T(8,128)(2,1)}, bf16[2048,512]{1,0:T(8,128)(2,1)S(1)}, u32[]{:S(2)}, u32[]{:S(2)}) %collective-permute-start.25) | collective-permute-done | bytes 2097184 | tf_op jit(solution)/shard_map/ppermute | solution.py:91
  390.6 23.8 %collective-permute-done.32.theirs_ref = bf16[4,256,512]{2,1,0:T(8,128)(2,1)S(1)} collective-permute-done((bf16[4,256,512]{2,1,0:T(8,128)(2,1)}, bf16[4,256,512]{2,1,0:T(8,128)(2,1)S(1)}, u32[]{:S(2)}, u32[]{:S(2)}) %collective-permute-start.32) | collective-permute-done | bytes 1048608 | tf_op jit(solution)/shard_map/ppermute | solution.py:91
  423.6 9.7 %collective-permute-done.33.received_ref = bf16[4,256,384]{2,1,0:T(8,128)(2,1)S(1)} collective-permute-done((bf16[4,256,384]{2,1,0:T(8,128)(2,1)S(1)}, bf16[4,256,384]{2,1,0:T(8,128)(2,1)S(1)}, u32[]{:S(2)}, u32[]{:S(2)}) %collective-permute-start.33) | collective-permute-done | bytes 786464 | tf_op jit(solution)/shard_map/ppermute | solution.py:91
  439.7 5.8 %shard_map.225 = (bf16[4,64,512]{2,1,0:T(8,128)(2,1)}, bf16[4,64,512]{2,1,0:T(8,128)(2,1)}) custom-call(s32[1]{0:T(128)} %bitcast.15.half_ref, bf16[2048,128]{1,0:T(8,128)(2,1)} %get-tuple-element.147.refs_1_.refs_0_, bf16[2048,512]{1,0:T(8,128)(2,1)} %all-gather.5.cloned.1.call-done.refs_1_.refs_0_, bf16[2048,512]{1,0:T(8,128)(2,1)} %copy-done.2, ...), custom_call_target="tpu_custom_call" | custom-call | flops 1073741824 | bytes 8912896 | tf_op jit(solution)/shard_map/pallas_call | solution.py:350
  450.3 10.2 %collective-permute-done.37.theirs_ref = bf16[4,256,512]{2,1,0:T(8,128)(2,1)S(1)} collective-permute-done((bf16[4,256,512]{2,1,0:T(8,128)(2,1)}, bf16[4,256,512]{2,1,0:T(8,128)(2,1)S(1)}, u32[]{:S(2)}, u32[]{:S(2)}) %collective-permute-start.37) | collective-permute-done | bytes 1048608 | tf_op jit(solution)/shard_map/ppermute | solution.py:91
  484.6 7.1 %collective-permute-done.40 = f32[1,896]{1,0:T(1,128)S(1)} collective-permute-done((f32[1,896]{1,0:T(1,128)S(1)}, f32[1,896]{1,0:T(1,128)S(1)}, u32[]{:S(2)}, u32[]{:S(2)}) %collective-permute-start.40) | collective-permute-done | bytes 3616 | tf_op jit(solution)/shard_map/ppermute | solution.py:91
  (221 shorter events, 152.5 us)
Async XLA Ops:
  7.2 63.7 %all-gather.3.cloned.1.call-start = ((), (), s32[]{:S(2)}) async-start(), calls=%async_computation.2 | async-start | bytes 2621440 | tf_op jit(solution)/shard_map/all_gather | solution.py:683
  23.4 93.6 %all-gather.5.cloned.1.call-start = ((), (), s32[]{:S(2)}) async-start(), calls=%async_computation.3 | async-start | bytes 2621440 | tf_op jit(solution)/shard_map/all_gather | solution.py:685
  23.4 22.1 %collective-permute-start.3 = (bf16[512,896]{1,0:T(8,128)(2,1)}, bf16[512,896]{1,0:T(8,128)(2,1)S(1)}, u32[]{:S(2)}, u32[]{:S(2)}) collective-permute-start(bf16[512,896]{1,0:T(8,128)(2,1)} %get-tuple-element.90), channel_id=1, source_target_pairs={{0,2},{1,3},{2,0},{3,1},{4,6},{5,7},{6,4},{7,5},{8,10},{9,11},{10,... | collective-permute-start | bytes 2752520 | tf_op jit(solution)/shard_map/ppermute | solution.py:91
  25.5 436.5 %reduce-scatter.5.cloned.1.call-start = ((), (), s32[]{:S(2)}) async-start(), calls=%async_computation.5 | async-start | bytes 2621440 | tf_op jit(solution)/shard_map/reduce_scatter | solution.py:764
  70.9 47.5 %collective-permute-start.5 = (bf16[2048,512]{1,0:T(8,128)(2,1)}, bf16[2048,512]{1,0:T(8,128)(2,1)}, u32[]{:S(2)}, u32[]{:S(2)}) collective-permute-start(bf16[2048,512]{1,0:T(8,128)(2,1)} %all-gather.3.cloned.1.call-done.refs_0_.refs_1_), channel_id=1, source_target_pairs={{0,2},{1,3},{2,0},{3,1},{4,6},{5,7},{6,4},{7,5},{8,10},{9,11},{10,... | collective-permute-start | bytes 6291464 | tf_op jit(solution)/shard_map/ppermute | solution.py:91
  72.4 47.6 %collective-permute-start.8 = (bf16[512,896]{1,0:T(8,128)(2,1)S(1)}, bf16[512,896]{1,0:T(8,128)(2,1)S(1)}, u32[]{:S(2)}, u32[]{:S(2)}) collective-permute-start(bf16[512,896]{1,0:T(8,128)(2,1)S(1)} %collective-permute-done.3.first_ref), channel_id=1, source_target_pairs={{0,16},{16,0},{1,17},{17,1},{2,18},{18,2},{3,19},{19,3},{4,20},{20... | collective-permute-start | bytes 2752520 | tf_op jit(solution)/shard_map/ppermute | solution.py:91
  74.2 73.4 %collective-permute-start.2 = (bf16[2048,512]{1,0:T(8,128)(2,1)}, bf16[2048,512]{1,0:T(8,128)(2,1)}, u32[]{:S(2)}, u32[]{:S(2)}) collective-permute-start(bf16[2048,512]{1,0:T(8,128)(2,1)} %all-gather.3.cloned.1.call-done.refs_0_.refs_1_), channel_id=1, source_target_pairs={{0,1},{1,0},{2,3},{3,2},{4,5},{5,4},{6,7},{7,6},{8,9},{9,8},{10,11... | collective-permute-start | bytes 6291464 | tf_op jit(solution)/shard_map/ppermute | solution.py:91
  118.4 46.7 %collective-permute-start.15 = (bf16[2048,512]{1,0:T(8,128)(2,1)}, bf16[2048,512]{1,0:T(8,128)(2,1)}, u32[]{:S(2)}, u32[]{:S(2)}) collective-permute-start(bf16[2048,512]{1,0:T(8,128)(2,1)} %all-gather.5.cloned.1.call-done.refs_1_.refs_0_), channel_id=1, source_target_pairs={{0,2},{1,3},{2,0},{3,1},{4,6},{5,7},{6,4},{7,5},{8,10},{9,11},{10,... | collective-permute-start | bytes 6291464 | tf_op jit(solution)/shard_map/ppermute | solution.py:91
  119.9 45.2 %collective-permute-start.6 = (bf16[2048,512]{1,0:T(8,128)(2,1)}, bf16[2048,512]{1,0:T(8,128)(2,1)}, u32[]{:S(2)}, u32[]{:S(2)}) collective-permute-start(bf16[2048,512]{1,0:T(8,128)(2,1)} %collective-permute-done.5.refs_2_.refs_3_), channel_id=1, source_target_pairs={{0,1},{1,0},{2,3},{3,2},{4,5},{5,4},{6,7},{7,6},{8,9},{9,8},{10,11... | collective-permute-start | bytes 6291464 | tf_op jit(solution)/shard_map/ppermute | solution.py:91
  122.2 23.9 %collective-permute-start.7 = (bf16[512,896]{1,0:T(8,128)(2,1)}, bf16[512,896]{1,0:T(8,128)(2,1)S(1)}, u32[]{:S(2)}, u32[]{:S(2)}) collective-permute-start(bf16[512,896]{1,0:T(8,128)(2,1)} %get-tuple-element.95), channel_id=1, source_target_pairs={{0,1},{1,0},{2,3},{3,2},{4,5},{5,4},{6,7},{7,6},{8,9},{9,8},{10,11... | collective-permute-start | bytes 2752520 | tf_op jit(solution)/shard_map/ppermute | solution.py:91
  146.1 51.7 %collective-permute-start.11 = (bf16[640,512]{1,0:T(8,128)(2,1)}, bf16[640,512]{1,0:T(8,128)(2,1)S(1)}, u32[]{:S(2)}, u32[]{:S(2)}) collective-permute-start(bf16[640,512]{1,0:T(8,128)(2,1)} %get-tuple-element.106), channel_id=1, source_target_pairs={{0,1},{1,0},{2,3},{3,2},{4,5},{5,4},{6,7},{7,6},{8,9},{9,8},{10,11... | collective-permute-start | bytes 1966088 | tf_op jit(solution)/shard_map/ppermute | solution.py:91
  146.6 51.2 %collective-permute-start.12 = (bf16[640,512]{1,0:T(8,128)(2,1)}, bf16[640,512]{1,0:T(8,128)(2,1)}, u32[]{:S(2)}, u32[]{:S(2)}) collective-permute-start(bf16[640,512]{1,0:T(8,128)(2,1)} %get-tuple-element.107), channel_id=1, source_target_pairs={{0,1},{1,0},{2,3},{3,2},{4,5},{5,4},{6,7},{7,6},{8,9},{9,8},{10,11... | collective-permute-start | bytes 1966088 | tf_op jit(solution)/shard_map/ppermute | solution.py:91
  147.6 57.9 %collective-permute-start.17 = (bf16[2048,512]{1,0:T(8,128)(2,1)S(1)}, bf16[2048,512]{1,0:T(8,128)(2,1)S(1)}, u32[]{:S(2)}, u32[]{:S(2)}) collective-permute-start(bf16[2048,512]{1,0:T(8,128)(2,1)S(1)} %copy-done.1), channel_id=1, source_target_pairs={{0,1},{1,0},{2,3},{3,2},{4,5},{5,4},{6,7},{7,6},{8,9},{9,8},{10,11... | collective-permute-start | bytes 6291464 | tf_op jit(solution)/shard_map/ppermute | solution.py:91
  165.1 40.4 %collective-permute-start.18 = (bf16[2048,512]{1,0:T(8,128)(2,1)}, bf16[2048,512]{1,0:T(8,128)(2,1)S(1)}, u32[]{:S(2)}, u32[]{:S(2)}) collective-permute-start(bf16[2048,512]{1,0:T(8,128)(2,1)} %collective-permute-done.15.refs_3_.refs_2_), channel_id=1, source_target_pairs={{0,1},{1,0},{2,3},{3,2},{4,5},{5,4},{6,7},{7,6},{8,9},{9,8},{10,11... | collective-permute-start | bytes 6291464 | tf_op jit(solution)/shard_map/ppermute | solution.py:91
  217.9 66.0 %collective-permute-start.22 = (bf16[4,256,512]{2,1,0:T(8,128)(2,1)}, bf16[4,256,512]{2,1,0:T(8,128)(2,1)S(1)}, u32[]{:S(2)}, u32[]{:S(2)}) collective-permute-start(bf16[4,256,512]{2,1,0:T(8,128)(2,1)} %get-tuple-element.116), channel_id=1, source_target_pairs={{0,16},{16,0},{1,17},{17,1},{2,18},{18,2},{3,19},{19,3},{4,20},{20... | collective-permute-start | bytes 3145736 | tf_op jit(solution)/shard_map/ppermute | solution.py:91
  227.8 59.7 %collective-permute-start.16 = (bf16[2048,512]{1,0:T(8,128)(2,1)}, bf16[2048,512]{1,0:T(8,128)(2,1)S(1)}, u32[]{:S(2)}, u32[]{:S(2)}) collective-permute-start(bf16[2048,512]{1,0:T(8,128)(2,1)} %get-tuple-element.114), channel_id=1, source_target_pairs={{0,2},{1,3},{2,0},{3,1},{4,6},{5,7},{6,4},{7,5},{8,10},{9,11},{10,... | collective-permute-start | bytes 6291464 | tf_op jit(solution)/shard_map/ppermute | solution.py:91
  282.0 40.2 %collective-permute-start.19 = (bf16[2048,512]{1,0:T(8,128)(2,1)}, bf16[2048,512]{1,0:T(8,128)(2,1)}, u32[]{:S(2)}, u32[]{:S(2)}) collective-permute-start(bf16[2048,512]{1,0:T(8,128)(2,1)} %get-tuple-element.125), channel_id=1, source_target_pairs={{0,1},{1,0},{2,3},{3,2},{4,5},{5,4},{6,7},{7,6},{8,9},{9,8},{10,11... | collective-permute-start | bytes 6291464 | tf_op jit(solution)/shard_map/ppermute | solution.py:91
  282.0 40.2 %collective-permute-start.20 = (bf16[2048,512]{1,0:T(8,128)(2,1)}, bf16[2048,512]{1,0:T(8,128)(2,1)}, u32[]{:S(2)}, u32[]{:S(2)}) collective-permute-start(bf16[2048,512]{1,0:T(8,128)(2,1)} %get-tuple-element.129), channel_id=1, source_target_pairs={{0,1},{1,0},{2,3},{3,2},{4,5},{5,4},{6,7},{7,6},{8,9},{9,8},{10,11... | collective-permute-start | bytes 6291464 | tf_op jit(solution)/shard_map/ppermute | solution.py:91
  282.5 25.4 %collective-permute-start.21 = (bf16[4,256,512]{2,1,0:T(8,128)(2,1)}, bf16[4,256,512]{2,1,0:T(8,128)(2,1)S(1)}, u32[]{:S(2)}, u32[]{:S(2)}) collective-permute-start(bf16[4,256,512]{2,1,0:T(8,128)(2,1)} %get-tuple-element.120), channel_id=1, source_target_pairs={{0,16},{16,0},{1,17},{17,1},{2,18},{18,2},{3,19},{19,3},{4,20},{20... | collective-permute-start | bytes 3145736 | tf_op jit(solution)/shard_map/ppermute | solution.py:91
  330.9 46.7 %collective-permute-start.25 = (bf16[2048,512]{1,0:T(8,128)(2,1)}, bf16[2048,512]{1,0:T(8,128)(2,1)S(1)}, u32[]{:S(2)}, u32[]{:S(2)}) collective-permute-start(bf16[2048,512]{1,0:T(8,128)(2,1)} %get-tuple-element.138), channel_id=1, source_target_pairs={{0,2},{1,3},{2,0},{3,1},{4,6},{5,7},{6,4},{7,5},{8,10},{9,11},{10,... | collective-permute-start | bytes 6291464 | tf_op jit(solution)/shard_map/ppermute | solution.py:91
  381.1 92.6 %reduce-scatter.3.cloned.1.call-start = ((), (), s32[]{:S(2)}) async-start(), calls=%async_computation.4 | async-start | bytes 2621440 | tf_op jit(solution)/shard_map/reduce_scatter | solution.py:750
  388.9 25.5 %collective-permute-start.32 = (bf16[4,256,512]{2,1,0:T(8,128)(2,1)}, bf16[4,256,512]{2,1,0:T(8,128)(2,1)S(1)}, u32[]{:S(2)}, u32[]{:S(2)}) collective-permute-start(bf16[4,256,512]{2,1,0:T(8,128)(2,1)} %shard_map.221.mine_ref), channel_id=1, source_target_pairs={{0,16},{16,0},{1,17},{17,1},{2,18},{18,2},{3,19},{19,3},{4,20},{20... | collective-permute-start | bytes 3145736 | tf_op jit(solution)/shard_map/ppermute | solution.py:91
  436.6 23.9 %collective-permute-start.37 = (bf16[4,256,512]{2,1,0:T(8,128)(2,1)}, bf16[4,256,512]{2,1,0:T(8,128)(2,1)S(1)}, u32[]{:S(2)}, u32[]{:S(2)}) collective-permute-start(bf16[4,256,512]{2,1,0:T(8,128)(2,1)} %shard_map.227.mine_ref), channel_id=1, source_target_pairs={{0,16},{16,0},{1,17},{17,1},{2,18},{18,2},{3,19},{19,3},{4,20},{20... | collective-permute-start | bytes 3145736 | tf_op jit(solution)/shard_map/ppermute | solution.py:91
  495.3 24.0 %collective-permute-start.30 = (f32[3,512]{1,0:T(4,128)S(1)}, f32[3,512]{1,0:T(4,128)S(1)}, u32[]{:S(2)}, u32[]{:S(2)}) collective-permute-start(f32[3,512]{1,0:T(4,128)S(1)} %fusion.28), channel_id=1, source_target_pairs={{0,16},{16,0},{1,17},{17,1},{2,18},{18,2},{3,19},{19,3},{4,20},{20... | collective-permute-start | bytes 18440 | tf_op jit(solution)/shard_map/ppermute | solution.py:91
  (59 other events, 715.6 us)
Sparse Core Ops, SparseCore 0:
  23.5 47.3 all-gather.2
  72.5 44.4 all-gather.4
  381.3 43.0 reduce-scatter.4
  426.5 42.8 reduce-scatter.2

commit v2 on v1

--- a/solution.py
+++ b/solution.py
@@ -12,6 +12,8 @@
 ROT = 32
 SEGS = 3
 LONGEST = 1024
+QUERIES = 512
+KEYS = 512
 
 
 epsilon = 1e-05
@@ -107,22 +109,6 @@
     return value
 
 
-def stack_blocks(items):
-    shape = items[0][0].shape[1:]
-
-    def kernel(*refs):
-        out_ref = refs[-1]
-        for place, (_, index) in enumerate(items):
-            out_ref[place] = refs[place][index]
-
-    return pl.pallas_call(
-        kernel,
-        out_shape=jax.ShapeDtypeStruct((len(items),) + shape, items[0][0].dtype),
-        compiler_params=params(),
-        cost_estimate=cost(0, 4 * len(items) * math.prod(shape)),
-    )(*[item for item, _ in items])
-
-
 def pack_in(places, fc1_weight, qkv_flat):
     width, rows = fc1_weight.shape[1] // 4, fc1_weight.shape[0]
     small = qkv_flat.shape[1] // 4
@@ -185,7 +171,7 @@
     rows, width = xs[0].shape
     hidden = fc1_bias.shape[1]
     pair = qkv_bias.shape[1] // 3
-    block = 512
+    block = min(512, rows)
 
     def kernel(*refs):
         x_refs, w_refs = refs[:4], refs[4:8]
@@ -229,17 +215,20 @@
 
 
 def slope_step(gs, ws, up_pre):
-    rows, width = gs[0].shape
+    rows = gs[0].shape[0]
     hidden = up_pre.shape[1]
     pair = ws[0].shape[0] - hidden
-    block = 512
+    block = min(512, rows)
 
     def kernel(*refs):
-        g_refs, w_refs, up = refs[:4], refs[4:8], refs[8]
-        dup_o, dattn_o, bias_o = refs[9:]
-        total = mul(g_refs[0][...], w_refs[0][...], NT)
-        for g_ref, w_ref in zip(g_refs[1:], w_refs[1:]):
-            total = total + mul(g_ref[...], w_ref[...], NT)
+        g_refs, w_refs, up = refs[:6], refs[6:10], refs[10]
+        dup_o, dattn_o, bias_o = refs[11:]
+        cots = blocks_of([ref[...] for ref in g_refs[:3]])
+        cots = cots + blocks_of([ref[...] for ref in g_refs[3:]])
+        total = None
+        for cot, w_ref in zip(cots, w_refs):
+            part = mul(cot, w_ref[...], NT)
+            total = part if total is None else total + part
         d_up = (total[:, :hidden] * gelu_slope(up[...])).astype(bf16)
         dup_o[...] = d_up
         dattn_o[...] = total[:, hidden:].astype(bf16)
@@ -259,7 +248,7 @@
     return pl.pallas_call(
         kernel,
         grid=(rows // block,),
-        in_specs=[rowed(width)] * 4 + [fixed(w.shape) for w in ws] + [rowed(hidden)],
+        in_specs=[rowed(g.shape[1]) for g in gs] + [fixed(w.shape) for w in ws] + [rowed(hidden)],
         out_specs=[rowed(hidden), rowed(pair), fixed((1, hidden))],
         out_shape=[
             jax.ShapeDtypeStruct((rows, hidden), bf16),
@@ -268,155 +257,9 @@
         ],
         compiler_params=params(),
         cost_estimate=cost(
-            8 * rows * width * (hidden + pair), 8 * rows * width + 6 * rows * hidden
+            8 * rows * ws[0].shape[1] * (hidden + pair), 8 * rows * ws[0].shape[1] + 6 * rows * hidden
         ),
     )(*gs, *ws, up_pre)
-
-
-def spread(hidden_vals, pair_vals, ws, received, transposed):
-    rows, hidden = hidden_vals.shape
-    pair = pair_vals.shape[1]
-    width = ws[0].shape[0] if transposed else ws[0].shape[1]
-    block = min(1024, rows)
-    extra = len(received)
-
-    def kernel(*refs):
-        a, b = refs[0][...], refs[1][...]
-        w_refs, got, outs = refs[2:4], refs[4 : 4 + extra], refs[4 + extra :]
-        for place in range(2):
-            w = w_refs[place]
-            if transposed:
-                total = mul(a, w[:, :hidden], NT) + mul(b, w[:, hidden:], NT)
-            else:
-                total = mul(a, w[:hidden], NN) + mul(b, w[hidden:], NN)
-            if extra:
-                total = total + got[place][...].astype(f32)
-            outs[place][...] = total.astype(bf16)
-
-    def rowed(cols):
-        return pl.BlockSpec((block, cols), lambda i: (i, 0))
-
-    return pl.pallas_call(
-        kernel,
-        grid=(rows // block,),
-        in_specs=[rowed(hidden), rowed(pair)]
-        + [pl.BlockSpec(w.shape, lambda i: (0, 0)) for w in ws]
-        + [rowed(width)] * extra,
-        out_specs=[rowed(width)] * 2,
-        out_shape=[jax.ShapeDtypeStruct((rows, width), bf16)] * 2,
-        compiler_params=params(),
-        cost_estimate=cost(
-            4 * rows * width * (hidden + pair), 2 * rows * (hidden + pair + (2 + extra) * width)
-        ),
-    )(hidden_vals, pair_vals, *ws, *received)
-
-
-def grad_blocks(half, fixed_side, moving, fixed_left):
-    rows, cols = fixed_side.shape
-    width = moving[0].shape[1]
-    out_rows, out_cols = (cols, width) if fixed_left else (width, cols)
-    block = min(1024, rows)
-    steps = rows // block
-    cut = out_rows // 2
-
-    def kernel(half_ref, *refs):
-        keep_o, send_o, total = refs[5:]
-        step = pl.program_id(0)
-        side = refs[0][...]
-        for place in range(4):
-            other = refs[1 + place][...]
-            part = mul(side, other, TN) if fixed_left else mul(other, side, TN)
-
-            @pl.when(step == 0)
-            def _():
-                total[place] = part
-
-            @pl.when(step > 0)
-            def _():
-                total[place] += part
-
-        @pl.when(step == steps - 1)
-        def _():
-            mine = pl.multiple_of(half_ref[0] * cut, cut)
-            theirs = pl.multiple_of((1 - half_ref[0]) * cut, cut)
-            for place in range(4):
-                keep_o[place] = total[place, pl.ds(mine, cut)].astype(bf16)
-                send_o[place] = total[place, pl.ds(theirs, cut)].astype(bf16)
-
-    def rowed(n):
-        return pl.BlockSpec((block, n), lambda i, s: (i, 0))
-
-    whole = pl.BlockSpec((4, cut, out_cols), lambda i, s: (0, 0, 0))
-    return pl.pallas_call(
-        kernel,
-        grid_spec=pltpu.PrefetchScalarGridSpec(
-            num_scalar_prefetch=1,
-            grid=(steps,),
-            in_specs=[rowed(cols)] + [rowed(width)] * 4,
-            out_specs=[whole] * 2,
-            scratch_shapes=[pltpu.VMEM((4, out_rows, out_cols), f32)],
-        ),
-        out_shape=[jax.ShapeDtypeStruct((4, cut, out_cols), bf16)] * 2,
-        compiler_params=params(),
-        cost_estimate=cost(8 * rows * cols * width, 2 * rows * (cols + 4 * width)),
-    )(half, fixed_side, *moving)
-
-
-def add_halves(keep, received):
-    shape = (2,) + keep.shape[1:]
-
-    def kernel(keep_ref, received_ref, near_o, far_o):
-        near_o[...] = (keep_ref[:2].astype(f32) + received_ref[:2].astype(f32)).astype(bf16)
-        far_o[...] = (keep_ref[2:].astype(f32) + received_ref[2:].astype(f32)).astype(bf16)
-
-    return pl.pallas_call(
-        kernel,
-        out_shape=[jax.ShapeDtypeStruct(shape, bf16)] * 2,
-        compiler_params=params(),
-        cost_estimate=cost(keep.size, 6 * keep.size),
-    )(keep, received)
-
-
-def lay_out(places, mine, theirs, by_rows):
-    _, cut, cols = mine.shape
-
-    def kernel(places_ref, mine_ref, theirs_ref, out_ref):
-        half = pl.program_id(0)
-
-        def fill(source):
-            for place in range(4):
-                spot = places_ref[place]
-                value = source[place].astype(f32)
-                if by_rows:
-                    out_ref[spot, 0] = value
-                else:
-                    out_ref[:, pl.ds(pl.multiple_of(spot * cols, 128), cols)] = value
-
-        @pl.when(half == places_ref[4])
-        def _():
-            fill(mine_ref)
-
-        @pl.when(half != places_ref[4])
-        def _():
-            fill(theirs_ref)
-
-    if by_rows:
-        shape = (4, 2, cut, cols)
-        out_spec = pl.BlockSpec((4, 1, cut, cols), lambda h, s: (0, h, 0, 0))
-    else:
-        shape = (2 * cut, 4 * cols)
-        out_spec = pl.BlockSpec((cut, 4 * cols), lambda h, s: (h, 0))
-    part = pl.BlockSpec((4, cut, cols), lambda h, s: (0, 0, 0))
-    result = pl.pallas_call(
-        kernel,
-        grid_spec=pltpu.PrefetchScalarGridSpec(
-            num_scalar_prefetch=1, grid=(2,), in_specs=[part, part], out_specs=out_spec
-        ),
-        out_shape=jax.ShapeDtypeStruct(shape, f32),
-        compiler_params=params(),
-        cost_estimate=cost(0, 12 * mine.size),
-    )(places, mine, theirs)
-    return result.reshape(8 * cut, cols) if by_rows else result
 
 
 def pick(same, first, second):
@@ -443,10 +286,201 @@
     )(same, first, second)
 
 
+def spread(sides, near_mats, far_mats, transposed, part):
+    rows, hidden = sides[0][0].shape
+    pair = sides[0][1].shape[1]
+    width = near_mats[0].shape[0] if transposed else near_mats[0].shape[1]
+    block = min(1024, rows)
+    shares = 2 if part else 1
+
+    def kernel(*refs):
+        values = [[refs[0][...], refs[1][...]], [refs[2][...], refs[3][...]]]
+        outs = refs[8:]
+        for place in range(2):
+            total = None
+            for side in range(2):
+                w = refs[4 + 2 * place + side]
+                if transposed:
+                    add = mul(values[side][0], w[:, :hidden], NT) + mul(
+                        values[side][1], w[:, hidden:], NT
+                    )
+                else:
+                    add = mul(values[side][0], w[:hidden]) + mul(values[side][1], w[hidden:])
+                total = add if total is None else total + add
+            total = total.astype(bf16)
+            if part:
+                cut = part // 2
+                for piece in range(block // part):
+                    spot = slice(piece * cut, (piece + 1) * cut)
+                    outs[2 * place][spot] = total[piece * part : piece * part + cut]
+                    outs[2 * place + 1][spot] = total[piece * part + cut : (piece + 1) * part]
+            else:
+                outs[place][...] = total
+
+    def rowed(cols):
+        return pl.BlockSpec((block, cols), lambda i: (i, 0))
+
+    return pl.pallas_call(
+        kernel,
+        grid=(rows // block,),
+        in_specs=[rowed(hidden), rowed(pair)] * 2
+        + [pl.BlockSpec(w.shape, lambda i: (0, 0)) for w in near_mats + far_mats],
+        out_specs=[pl.BlockSpec((block // shares, width), lambda i: (i, 0))] * (2 * shares),
+        out_shape=[jax.ShapeDtypeStruct((rows // shares, width), bf16)] * (2 * shares),
+        compiler_params=params(),
+        cost_estimate=cost(
+            8 * rows * width * (hidden + pair), 4 * rows * (hidden + pair + width)
+        ),
+    )(*sides[0], *sides[1], *near_mats, *far_mats)
+
+
+def blocks_of(values):
+    if len(values) == 2:
+        return values
+    cut = values[2].shape[1] // 2
+    return [
+        jnp.concatenate([values[0], values[2][:, :cut]], axis=1),
+        jnp.concatenate([values[1], values[2][:, cut:]], axis=1),
+    ]
+
+
+def grad_blocks(half, jobs, across):
+    rows = jobs[0][0][0].shape[0]
+    block = min(1024, rows)
+    steps = rows // block
+    sizes = [lefts[0].shape[1] for lefts, _, _ in jobs]
+    out_rows = sum(sizes)
+    _, rights, _ = jobs[0]
+    out_cols = rights[0].shape[1] if len(rights) == 2 else rights[2].shape[1]
+    arrays = [array for lefts, rights, _ in jobs for array in lefts + rights]
+    cut = (out_rows, out_cols // 2) if across else (out_rows // 2, out_cols)
+
+    def kernel(half_ref, *refs):
+        ins, (keep_o, send_o, total) = list(refs[: len(arrays)]), refs[len(arrays) :]
+        step = pl.program_id(0)
+        at = 0
+        for size, (lefts, rights, hidden_left) in zip(sizes, jobs):
+            l0, l1 = [ins.pop(0)[...] for _ in lefts]
+            r0, r1 = blocks_of([ins.pop(0)[...] for _ in rights])
+            if hidden_left:
+                pairs = ((l0, r0), (l1, r0), (l0, r1), (l1, r1))
+            else:
+                pairs = ((l0, r0), (l0, r1), (l1, r0), (l1, r1))
+            spot = slice(at, at + size)
+            for place, (left, right) in enumerate(pairs):
+                piece = mul(left, right, TN)
+
+                @pl.when(step == 0)
+                def _():
+                    total[place, spot] = piece
+
+                @pl.when(step > 0)
+                def _():
+                    total[place, spot] += piece
+
+            at += size
+
+        @pl.when(step == steps - 1)
+        def _():
+            for place in range(4):
+                for out, which in ((keep_o, half_ref[0]), (send_o, 1 - half_ref[0])):
+                    if across:
+                        begin = pl.multiple_of(which * cut[1], cut[1])
+                        out[place] = total[place, :, pl.ds(begin, cut[1])].astype(bf16)
+                    else:
+                        begin = pl.multiple_of(which * cut[0], cut[0])
+                        out[place] = total[place, pl.ds(begin, cut[0])].astype(bf16)
+
+    whole = pl.BlockSpec((4,) + cut, lambda i, s: (0, 0, 0))
+    return pl.pallas_call(
+        kernel,
+        grid_spec=pltpu.PrefetchScalarGridSpec(
+            num_scalar_prefetch=1,
+            grid=(steps,),
+            in_specs=[
+                pl.BlockSpec((block, array.shape[1]), lambda i, s: (i, 0)) for array in arrays
+            ],
+            out_specs=[whole] * 2,
+            scratch_shapes=[pltpu.VMEM((4, out_rows, out_cols), f32)],
+        ),
+        out_shape=[jax.ShapeDtypeStruct((4,) + cut, bf16)] * 2,
+        compiler_params=params(),
+        cost_estimate=cost(8 * rows * out_rows * out_cols, 8 * rows * (out_rows + out_cols)),
+    )(half, *arrays)
+
+
+def add_halves(keep, received):
+    shape = (2,) + keep.shape[1:]
+
+    def kernel(keep_ref, received_ref, near_o, far_o):
+        far_o[...] = (keep_ref[2:].astype(f32) + received_ref[2:].astype(f32)).astype(bf16)
+        near_o[...] = (keep_ref[:2].astype(f32) + received_ref[:2].astype(f32)).astype(bf16)
+
+    return pl.pallas_call(
+        kernel,
+        out_shape=[jax.ShapeDtypeStruct(shape, bf16)] * 2,
+        compiler_params=params(),
+        cost_estimate=cost(keep.size, 6 * keep.size),
+    )(keep, received)
+
+
+def lay_out(places, mine, theirs, kind):
+    _, cut, cols = mine[0].shape
+    hidden = 3 * (cut // 4)
+
+    def kernel(places_ref, *refs):
+        half = pl.program_id(0)
+        outs = refs[4:]
+
+        def fill(sources):
+            for place in range(4):
+                spot = places_ref[place]
+                value = sources[place // 2][place % 2].astype(f32)
+                if kind == 0:
+                    outs[0][spot, 0] = value
+                elif kind == 1:
+                    outs[0][:, pl.ds(pl.multiple_of(spot * cols, 128), cols)] = value
+                else:
+                    outs[0][:, pl.ds(pl.multiple_of(spot * hidden, 128), hidden)] = value[:hidden].T
+                    outs[1][spot] = value[hidden:]
+
+        @pl.when(half == places_ref[4])
+        def _():
+            fill(refs[0:2])
+
+        @pl.when(half != places_ref[4])
+        def _():
+            fill(refs[2:4])
+
+    if kind == 0:
+        shapes = [(4, 2, cut, cols)]
+        out_specs = [pl.BlockSpec((4, 1, cut, cols), lambda h, s: (0, h, 0, 0))]
+    elif kind == 1:
+        shapes = [(2 * cut, 4 * cols)]
+        out_specs = [pl.BlockSpec((cut, 4 * cols), lambda h, s: (h, 0))]
+    else:
+        shapes = [(2 * cols, 4 * hidden), (4, cut - hidden, 2 * cols)]
+        out_specs = [
+            pl.BlockSpec((cols, 4 * hidden), lambda h, s: (h, 0)),
+            pl.BlockSpec((4, cut - hidden, cols), lambda h, s: (0, 0, h)),
+        ]
+    part = pl.BlockSpec((2, cut, cols), lambda h, s: (0, 0, 0))
+    return pl.pallas_call(
+        kernel,
+        grid_spec=pltpu.PrefetchScalarGridSpec(
+            num_scalar_prefetch=1, grid=(2,), in_specs=[part] * 4, out_specs=out_specs
+        ),
+        out_shape=[jax.ShapeDtypeStruct(shape, f32) for shape in shapes],
+        compiler_params=params(),
+        cost_estimate=cost(0, 24 * mine[0].size),
+    )(places, *mine, *theirs)
+
+
 def attend(lowest, q_rot, k_rot, v_low, begin):
     rows, pair = q_rot.shape
-    block = 256
+    block = min(QUERIES, rows)
     steps = rows // block
+    ratio = block // KEYS
     heads = pair // HEAD_DIM
     scale = 1.0 / math.sqrt(HEAD_DIM)
 
@@ -462,12 +496,12 @@
         zero = jnp.zeros_like(query)
         q_heads = [jnp.where(lane == head, query, zero) for head in range(heads)]
         begins = begin_ref[...]
-        own = step * block + lax.broadcasted_iota(jnp.int32, (block, block), 1)
-        key_at = lax.broadcasted_iota(jnp.int32, (block, block), 0)
+        own = step * block + lax.broadcasted_iota(jnp.int32, (KEYS, block), 1)
+        key_at = lax.broadcasted_iota(jnp.int32, (KEYS, block), 0)
 
         def body(place, carry):
-            at = pl.multiple_of(place * block, block)
-            keys = k_ref[pl.ds(at, block), :]
+            at = pl.multiple_of(place * KEYS, KEYS)
+            keys = k_ref[pl.ds(at, KEYS), :]
             index = key_at + at
             seen = (index <= own) & (index >= begins)
             new = []
@@ -477,7 +511,7 @@
                 new_top = jnp.maximum(top, jnp.max(score, axis=0, keepdims=True))
                 shifted = jnp.exp(score - new_top)
                 fade = jnp.exp(top - new_top)
-                values = v_turned[head * HEAD_DIM : (head + 1) * HEAD_DIM, pl.ds(at, block)]
+                values = v_turned[head * HEAD_DIM : (head + 1) * HEAD_DIM, pl.ds(at, KEYS)]
                 new.append(
                     (
                         new_top,
@@ -492,7 +526,7 @@
             jnp.zeros((1, block), f32),
             jnp.zeros((HEAD_DIM, block), f32),
         )
-        result = lax.fori_loop(lowest_ref[step], step + 1, body, (initial,) * heads)
+        result = lax.fori_loop(lowest_ref[step], (step + 1) * ratio, body, (initial,) * heads)
         out = jnp.concatenate([out / total for _, total, out in result], axis=0).T
         o_ref[...] = out.astype(bf16)
         of_ref[...] = out
@@ -526,8 +560,9 @@
 
 def attend_back(lowest, q_rot, k_rot, v_low, begin, d_attn, out_full, lse, tables):
     rows, pair = q_rot.shape
-    block = 256
+    block = min(QUERIES, rows)
     steps = rows // block
+    ratio = block // KEYS
     heads = pair // HEAD_DIM
     scale = 1.0 / math.sqrt(HEAD_DIM)
 
@@ -555,13 +590,13 @@
         ]
         lses = [lse_ref[head : head + 1, :] for head in range(heads)]
         begins = begin_ref[...]
-        own = step * block + lax.broadcasted_iota(jnp.int32, (block, block), 1)
-        key_at = lax.broadcasted_iota(jnp.int32, (block, block), 0)
+        own = step * block + lax.broadcasted_iota(jnp.int32, (KEYS, block), 1)
+        key_at = lax.broadcasted_iota(jnp.int32, (KEYS, block), 0)
 
         def body(place, carry):
-            at = pl.multiple_of(place * block, block)
-            keys = k_ref[pl.ds(at, block), :]
-            values = v_ref[pl.ds(at, block), :]
+            at = pl.multiple_of(place * KEYS, KEYS)
+            keys = k_ref[pl.ds(at, KEYS), :]
+            values = v_ref[pl.ds(at, KEYS), :]
             index = key_at + at
             seen = (index <= own) & (index >= begins)
             new, d_key, d_value = [], None, None
@@ -574,14 +609,14 @@
                 key_part = mul(d_score, q_heads[head])
                 d_value = value_part if d_value is None else d_value + value_part
                 d_key = key_part if d_key is None else d_key + key_part
-                turned = k_turned[head * HEAD_DIM : (head + 1) * HEAD_DIM, pl.ds(at, block)]
+                turned = k_turned[head * HEAD_DIM : (head + 1) * HEAD_DIM, pl.ds(at, KEYS)]
                 new.append(carry[head] + mul(turned, d_score))
-            dv[pl.ds(at, block), :] += d_value
-            dk[pl.ds(at, block), :] += d_key
+            dv[pl.ds(at, KEYS), :] += d_value
+            dk[pl.ds(at, KEYS), :] += d_key
             return tuple(new)
 
         result = lax.fori_loop(
-            lowest_ref[step], step + 1, body, (jnp.zeros((HEAD_DIM, block), f32),) * heads
+            lowest_ref[step], (step + 1) * ratio, body, (jnp.zeros((HEAD_DIM, block), f32),) * heads
         )
         d_query = jnp.concatenate(result, axis=0).T * scale
         here = pl.ds(pl.multiple_of(step * block, block), block)
@@ -652,7 +687,7 @@
 ):
     col_index = lax.axis_index(COL)
     dp_index = lax.axis_index(DP)
-    _, local_width = tokens.shape
+    local_rows, local_width = tokens.shape
     full_width = local_width * lax.axis_size(COL)
     group_rows = segment_ids.shape[1]
     pair_dim = qkv_weight.shape[3]
@@ -660,7 +695,7 @@
     half = (dp_index & 1).astype(jnp.int32)
     far_block = (1 - (col_index >> 1)) * 2 + half
     packs = jnp.stack([col_index, col_index ^ 1, far_block]).astype(jnp.int32)
-    places = jnp.stack([col_index, col_index ^ 2, col_index ^ 1, col_index ^ 3, half]).astype(
+    places = jnp.stack([col_index, col_index ^ 1, col_index ^ 2, col_index ^ 3, half]).astype(
         jnp.int32
     )
     same = (half == (col_index & 1)).astype(jnp.int32).reshape(1)
@@ -669,11 +704,11 @@
     token_f = tokens.astype(f32)
     ln_local = jnp.stack([jnp.sum(token_f, axis=1), jnp.sum(token_f * token_f, axis=1)])
     ln_sums = ln_local + swap_bits(ln_local, COL, 1)
-    in_own, in_near, in_far = pack_in(
-        packs, fc1_weight, after(qkv_weight, ln_local).reshape(local_width, -1)
-    )
-    ln_far = swap_bits(after(ln_sums, in_far), COL, 2)
-    in_first = swap_bits(after(in_far, ln_far), COL, 2)
+    ln_far = swap_bits(ln_sums, COL, 2)
+    cut = local_width // 2
+    tail = out_grad[:, cut:]
+    tail_far = swap_bits(after(tail, ln_far), COL, 2)
+    qkv_flat = after(qkv_weight, ln_sums).reshape(local_width, -1)
     ln_sums = ln_sums + ln_far
     row_mean = ln_sums[0] / full_width
     variance = ln_sums[1] / full_width - row_mean * row_mean
@@ -681,98 +716,120 @@
     centred = (token_f - row_mean[:, None]) * inv_std[:, None]
     normed = (centred * ln_gain + ln_bias).astype(bf16)
     normed_0 = lax.all_gather(normed, ROW, axis=0, tiled=True)
-    out_own, out_near, out_far = pack_out(packs, fc2_weight, after(out_weight, normed))
-    cot_0 = lax.all_gather(after(out_grad, normed), ROW, axis=0, tiled=True)
+    in_own, in_near, in_far = pack_in(packs, fc1_weight, after(qkv_flat, normed))
+    in_first = swap_bits(after(in_far, tail_far), COL, 2)
+    out_own, out_near, out_far = pack_out(packs, fc2_weight, after(out_weight, in_far))
+    cot_0 = lax.all_gather(after(out_grad[:, :cut], normed), ROW, axis=0, tiled=True)
+    cot_b = lax.all_gather(
+        jnp.concatenate([tail, tail_far], axis=1), ROW, axis=0, tiled=True
+    )
+
+    pos = positions(segment_ids[0])
+    tables = rope_tables(pos, pair_dim)
+    start = jnp.arange(group_rows, dtype=jnp.int32) - pos
+    lowest = start[::QUERIES] // KEYS
+    begin = start.reshape(1, -1)
 
     in_1 = swap_bits(after(in_near, normed), COL, 1)
     out_1 = swap_bits(out_near, COL, 1)
     in_second = swap_bits(in_first, DP, 1)
     out_first = swap_bits(after(out_far, in_first), COL, 2)
-    in_2, in_pass = pick(same, in_first, in_second)
+    in_2, in_pass = pick(after(same, *tables), in_first, in_second)
     in_3 = swap_bits(in_pass, COL, 1)
     out_second = swap_bits(after(out_first, in_second), DP, 1)
-    out_2, out_pass = pick(same, out_first, out_second)
+    out_2, out_pass = pick(after(same, in_2), out_first, out_second)
     out_3 = swap_bits(out_pass, COL, 1)
-    in_mats = [in_own, in_1, in_2, in_3]
-    out_mats = [out_own, out_1, out_2, out_3]
-
-    pos = positions(segment_ids[0])
-    tables = rope_tables(pos, pair_dim)
-    start = jnp.arange(group_rows, dtype=jnp.int32) - pos
-    lowest = start[::256] // 256
-    begin = start.reshape(1, -1)
 
     normed_2 = swap_bits(after(normed_0, out_first), COL, 2)
     normed_1 = swap_bits(normed_0, COL, 1)
+    normed_3 = swap_bits(normed_2, COL, 1)
     cot_2 = swap_bits(after(cot_0, normed_2), COL, 2)
-    normed_3 = swap_bits(normed_2, COL, 1)
-    cot_1 = swap_bits(cot_0, COL, 1)
-    normed_all = [normed_0, normed_1, normed_2, normed_3]
-    up_pre, activation, q_rot, k_rot, v_low = forward_step(
-        normed_all, in_mats, fc1_bias.reshape(1, -1), qkv_bias.reshape(1, -1), tables
-    )
-    attn_low, attn_full, lse = attend(lowest, q_rot, k_rot, v_low, begin)
-    give = spread(activation, attn_low, [out_mats[1], out_mats[3]], [], False)
-    got = [swap_bits(give[0], COL, 1), swap_bits(give[1], COL, 1)]
+    up_pre, act, q_rot, k_rot, v_low = forward_step(
+        [normed_0, normed_1, normed_2, normed_3],
+        [in_own, in_1, in_2, in_3],
+        fc1_bias.reshape(1, -1),
+        qkv_bias.reshape(1, -1),
+        tables,
+    )
+    act_1 = swap_bits(act, COL, 1)
+    attn, attn_full, lse = attend(lowest, after(q_rot, act), k_rot, v_low, begin)
+    attn_1 = swap_bits(attn, COL, 1)
+    cots = [cot_0, cot_2, cot_b]
+    cots_1 = [swap_bits(cot_0, COL, 1), swap_bits(cot_2, COL, 1), swap_bits(cot_b, COL, 1)]
+    fc2_keep, fc2_send = grad_blocks(
+        half, [([act, after(act_1, attn)], cots, True)], False
+    )
+    fc2_recv = swap_bits(fc2_send, DP, 1)
+    d_up, d_attn, fc1_sums = slope_step(
+        cots + cots_1, [out_own, out_2, out_1, out_3], after(up_pre, fc2_send)
+    )
+    d_up_1 = swap_bits(d_up, COL, 1)
     mix_near, mix_far = spread(
-        activation, attn_low, [out_mats[0], out_mats[2]], got, False
-    )
-    cot_3 = swap_bits(cot_2, COL, 1)
-    cot_all = [cot_0, cot_1, cot_2, cot_3]
-
-    def sum_halves(keep, send):
-        received = swap_bits(send, DP, 1)
+        [[act, after(attn, d_up)], [act_1, attn_1]],
+        [out_own, out_near],
+        [out_2, out_pass],
+        False,
+        0,
+    )
+    mix_recv = swap_bits(after(mix_far, cot_2), COL, 2)
+
+    def sum_halves(keep, received):
         near, far = add_halves(keep, received)
         for bit in all_bits(DP)[1:]:
             near = (near.astype(f32) + swap_bits(near, DP, bit).astype(f32)).astype(bf16)
             far = (far.astype(f32) + swap_bits(far, DP, bit).astype(f32)).astype(bf16)
         return near, far
 
-    def cross(near, far):
-        crossed = swap_bits(far, COL, 2)
-        joined = stack_blocks([(near, 1), (crossed, 1)])
-        passed = swap_bits(joined, COL, 1)
-        mine = stack_blocks([(near, 0), (crossed, 0), (passed, 0), (passed, 1)])
-        return crossed, mine
-
-    def finish(mine, theirs, by_rows):
-        return lay_out(places, mine, theirs, by_rows)
-
-    fc2_keep, fc2_send = grad_blocks(half, activation, cot_all, True)
-    d_up, d_attn, fc1_sums = slope_step(cot_all, out_mats, after(up_pre, fc2_send))
-    mix_recv = swap_bits(after(mix_far, cot_2), COL, 2)
-    fc2_near, fc2_far = sum_halves(fc2_keep, fc2_send)
-    fc1_keep, fc1_send = grad_blocks(half, d_up, normed_all, False)
+    fc1_keep, fc1_send = grad_blocks(
+        half, [([after(normed_0, mix_far), normed_2], [d_up, d_up_1], False)], False
+    )
+    fc2_near, fc2_far = sum_halves(fc2_keep, after(fc2_recv, mix_far))
+    fc2_near_x = swap_bits(fc2_near, DP, 1)
+    fc1_recv = swap_bits(after(fc1_send, fc2_near_x), DP, 1)
     d_proj, qkv_sums = attend_back(
         lowest, q_rot, k_rot, v_low, begin, after(d_attn, fc1_send), attn_full, lse, tables
     )
+    d_proj_1 = swap_bits(d_proj, COL, 1)
     mix_total = (mix_near.astype(f32) + mix_recv.astype(f32)).astype(bf16)
     mixed = lax.psum_scatter(mix_total, ROW, scatter_dimension=0, tiled=True).astype(f32)
-    fc2_crossed, fc2_mine = cross(fc2_near, after(fc2_far, mix_total))
-    give = spread(d_up, d_proj, [in_mats[1], in_mats[3]], [], True)
-    got = [swap_bits(give[0], COL, 1), swap_bits(give[1], COL, 1)]
-    fc1_near, fc1_far = sum_halves(fc1_keep, fc1_send)
-    fc1_crossed, fc1_mine = cross(fc1_near, after(fc1_far, fc2_crossed))
-    qkv_keep, qkv_send = grad_blocks(half, after(d_proj, give[0]), normed_all, False)
-    fc2_theirs = swap_bits(after(fc2_mine, fc1_near), DP, 1)
-    back_near, back_far = spread(after(d_up, qkv_send), d_proj, [in_mats[0], in_mats[2]], got, True)
-    back_recv = swap_bits(after(back_far, fc1_crossed), COL, 2)
-    out_keep, out_send = grad_blocks(half, after(attn_low, back_far), cot_all, True)
-    qkv_near, qkv_far = sum_halves(qkv_keep, after(qkv_send, fc2_theirs))
-    fc1_theirs = swap_bits(after(fc1_mine, qkv_near), DP, 1)
-    back_total = (back_near.astype(f32) + back_recv.astype(f32)).astype(bf16)
-    d_normed = lax.psum_scatter(
-        back_total, ROW, scatter_dimension=0, tiled=True
-    ).astype(f32)
-    qkv_crossed, qkv_mine = cross(qkv_near, after(qkv_far, back_total))
-    wo_near, wo_far = sum_halves(out_keep, after(out_send, fc1_theirs))
-    qkv_theirs = swap_bits(after(qkv_mine, wo_near), DP, 1)
-    _, wo_mine = cross(wo_near, after(wo_far, qkv_crossed))
-    wo_theirs = swap_bits(after(wo_mine, qkv_theirs), DP, 1)
-    fc2_weight_grad = finish(fc2_mine, fc2_theirs, True)
-    fc1_weight_grad = finish(fc1_mine, fc1_theirs, False)
-    qkv_weight_grad = finish(qkv_mine, qkv_theirs, False)
-    out_weight_grad = finish(wo_mine, wo_theirs, True)
+    fc2_crossed = swap_bits(after(fc2_far, mix_total), COL, 2)
+    fc1_near, fc1_far = sum_halves(fc1_keep, after(fc1_recv, d_proj))
+    fc1_near_x = swap_bits(after(fc1_near, fc1_recv), DP, 1)
+    near_a, near_b, far_a, far_b = spread(
+        [[d_up, d_proj], [d_up_1, d_proj_1]],
+        [in_own, in_near],
+        [in_2, in_pass],
+        True,
+        local_rows,
+    )
+    recv_a = swap_bits(after(far_a, fc2_crossed), COL, 2)
+    recv_b = swap_bits(after(far_b, recv_a), COL, 2)
+    fc2_crossed_x = swap_bits(after(fc2_crossed, fc1_near_x), DP, 1)
+    rest_keep, rest_send = grad_blocks(
+        half,
+        [
+            ([after(d_proj, far_a), d_proj_1], [normed_0, normed_2], True),
+            ([attn, attn_1], cots, True),
+        ],
+        True,
+    )
+    total_a = (near_a.astype(f32) + recv_a.astype(f32)).astype(bf16)
+    d_normed_a = lax.psum_scatter(total_a, ROW, scatter_dimension=0, tiled=True)
+    rest_recv = swap_bits(after(rest_send, fc2_crossed_x), DP, 1)
+    (fc2_weight_grad,) = lay_out(places, [fc2_near, fc2_crossed], [fc2_near_x, fc2_crossed_x], 0)
+    total_b = (near_b.astype(f32) + recv_b.astype(f32)).astype(bf16)
+    d_normed_b = lax.psum_scatter(total_b, ROW, scatter_dimension=0, tiled=True)
+    fc1_crossed = swap_bits(after(fc1_far, total_b), COL, 2)
+    rest_near, rest_far = sum_halves(rest_keep, rest_recv)
+    rest_near_x = swap_bits(after(rest_near, rest_recv), DP, 1)
+    fc1_crossed_x = swap_bits(after(fc1_crossed, rest_near_x), DP, 1)
+    rest_crossed = swap_bits(after(rest_far, fc1_crossed), COL, 2)
+    rest_crossed_x = swap_bits(after(rest_crossed, fc1_crossed_x), DP, 1)
+    d_normed = jnp.concatenate([d_normed_a, d_normed_b], axis=0).astype(f32)
+    (fc1_weight_grad,) = lay_out(places, [fc1_near, fc1_crossed], [fc1_near_x, fc1_crossed_x], 1)
+    qkv_weight_grad, out_weight_grad = lay_out(
+        places, [rest_near, rest_crossed], [rest_near_x, rest_crossed_x], 2
+    )
 
     out = (token_f + mixed + out_bias).astype(bf16)
     d_hat = d_normed * ln_gain
@@ -800,10 +857,10 @@
         vector_sums[1],
         qkv_weight_grad.reshape(qkv_weight.shape),
         bias_sums[: 3 * pair_dim].reshape(qkv_bias.shape),
-        out_weight_grad,
+        out_weight_grad.reshape(out_weight.shape),
         fc1_weight_grad,
         bias_sums[3 * pair_dim :],
-        fc2_weight_grad,
+        fc2_weight_grad.reshape(fc2_weight.shape),
         vector_sums[2],
     )
 

time: 528 us -> 509 us (0.964)
  Pallas kernels: 188 us -> 150 us
  waiting for transfers between devices: 237 us -> 259 us
    ppermute x44 -> x43, waiting for transfers between devices: 185 us -> 259 us  [swap_bits(): lax.ppermute(value, axis, [(place, place ^ bit) for place in range(count)])]
    all_gather x1 -> x2, waiting for transfers between devices: 42.8 us -> 0.01 us  [the longest x1 0.01 us: step(): lax.all_gather(after(out_grad[:, :cut], normed), ROW, axis=0, tiled=True)]
    pallas_call x9 -> x1, Pallas kernels: 30 us -> 13 us  [slope_step(): pl.pallas_call(kernel, grid=(rows // block,), in_specs=[rowed(g.shape[1])...]
    all_gather x1, waiting for transfers between devices: 9.64 us -> 0.01 us  [step(): normed_0 = lax.all_gather(normed, ROW, axis=0, tiled=True)]
    pallas_call x4 -> x2, Pallas kernels: 29.7 us -> 23.8 us  [spread(): pl.pallas_call(kernel, grid=(rows // block,), in_specs=[rowed(hidden), ro...]
    pallas_call x4 -> x3, Pallas kernels: 36.9 us -> 33.7 us  [grad_blocks(): pl.pallas_call(kernel, grid_spec=pltpu.PrefetchScalarGridSpec(num_scalar_...]
    ppermute x44 -> x43, starting transfers between devices: 39.3 us -> 36.5 us  [swap_bits(): lax.ppermute(value, axis, [(place, place ^ bit) for place in range(count)])]
    unnamed x73 -> x83, local copies, waits for them, and re-layouts: 16.4 us -> 14.1 us
  transfers between devices with their start and end apart: 48 -> 49, of which waited for: 20 -> 20; matrix products, arithmetic and copies ran while one was open for 5% -> 6% of each run, Pallas kernels for 36% -> 27%
where the time goes in v2:
time: 509 us
  waiting for transfers between devices  259 us (51%)
  Pallas kernels  150 us (29%)
  starting transfers between devices  36.7 us (7%)
  other arithmetic  24.5 us (5%)
  local copies, waits for them, and re-layouts  23.3 us (5%)
  between operations  14.6 us (3%)
    ppermute x43, waiting for transfers between devices, swap_bits(): lax.ppermute(value, axis, [(place, place ^ bit) for place in range(count)])  259 us
    ppermute x43, starting transfers between devices, swap_bits(): lax.ppermute(value, axis, [(place, place ^ bit) for place in range(count)])  36.5 us
    pallas_call x3, Pallas kernels, grad_blocks(): pl.pallas_call(kernel, grid_spec=pltpu.PrefetchScalarGridSpec(num_scalar_...  33.7 us
    pallas_call x2, Pallas kernels, spread(): pl.pallas_call(kernel, grid=(rows // block,), in_specs=[rowed(hidden), ro...  23.8 us
    pallas_call x1, Pallas kernels, attend_back(): pl.pallas_call(kernel, grid_spec=pltpu.PrefetchScalarGridSpec(num_scalar_...  18.2 us
    pallas_call x1, Pallas kernels, forward_step(): pl.pallas_call(kernel, grid=(rows // block,), in_specs=[rowed(width)] * 4...  15.5 us
    unnamed x83, local copies, waits for them, and re-layouts  14.1 us
    pallas_call x3, Pallas kernels, lay_out(): pl.pallas_call(kernel, grid_spec=pltpu.PrefetchScalarGridSpec(num_scalar_...  13.2 us
  transfers between devices with their start and end apart: 49, of which 20 were waited for; matrix products, arithmetic and copies ran while one was open for 6% of the time, Pallas kernels for 27%

profile of v2, /device:TPU:0, one launch (start us, length us, event | category | flops | bytes accessed | tf_op | source)
XLA Modules:
  0.0 508.8 jit_solution(932892520444541599)
XLA Ops:
  32.0 17.6 %collective-permute-done.4.first_ref = bf16[512,896]{1,0:T(8,128)(2,1)S(1)} collective-permute-done((bf16[512,896]{1,0:T(8,128)(2,1)}, bf16[512,896]{1,0:T(8,128)(2,1)S(1)}, u32[]{:S(2)}, u32[]{:S(2)}) %collective-permute-start.4) | collective-permute-done | bytes 917536 | tf_op jit(solution)/shard_map/ppermute | solution.py:93
  49.9 14.4 %collective-permute-done.5.first_ref = bf16[640,512]{1,0:T(8,128)(2,1)S(1)} collective-permute-done((bf16[640,512]{1,0:T(8,128)(2,1)}, bf16[640,512]{1,0:T(8,128)(2,1)S(1)}, u32[]{:S(2)}, u32[]{:S(2)}) %collective-permute-start.5) | collective-permute-done | bytes 655392 | tf_op jit(solution)/shard_map/ppermute | solution.py:93
  66.6 45.1 %collective-permute-done.6.refs_2_.refs_1_.refs_3_ = bf16[2048,512]{1,0:T(8,128)(2,1)} collective-permute-done((bf16[2048,512]{1,0:T(8,128)(2,1)}, bf16[2048,512]{1,0:T(8,128)(2,1)}, u32[]{:S(2)}, u32[]{:S(2)}) %collective-permute-start.6) | collective-permute-done | bytes 2097184 | tf_op jit(solution)/shard_map/ppermute | solution.py:93
  114.8 6.6 %fusion = (f32[2048,128]{1,0:T(8,128)}, f32[2048,128]{1,0:T(8,128)}, f32[2048,128]{1,0:T(8,128)}) fusion(f32[128]{0:T(128)S(1)} %fusion.22, f32[2048]{0:T(1024)S(1)} %get-tuple-element.218, pred[128]{0:T(512)(128)(4,1)} %get-tuple-element.223, pred[128]{0:T(512)(128)(4,1)} %get-tuple-element.224, pred[128]{0:T(512)(128)(4,1)} %broadcast_compare_fusion.1), kind=kLoop, calls=%fused_computation.12 | loop fusion | flops 1310720 | bytes 3154816 | tf_op jit(solution)/shard_map/jit(_where)/select_n | solution.py:62
  121.7 13.4 %collective-permute-done.9.second_ref = bf16[512,896]{1,0:T(8,128)(2,1)S(1)} collective-permute-done((bf16[512,896]{1,0:T(8,128)(2,1)S(1)}, bf16[512,896]{1,0:T(8,128)(2,1)S(1)}, u32[]{:S(2)}, u32[]{:S(2)}) %collective-permute-start.9) | collective-permute-done | bytes 917536 | tf_op jit(solution)/shard_map/ppermute | solution.py:93
  142.5 15.5 %shard_map.206 = (f32[2048,512]{1,0:T(8,128)}, bf16[2048,512]{1,0:T(8,128)(2,1)}, bf16[2048,128]{1,0:T(8,128)(2,1)}, bf16[2048,128]{1,0:T(8,128)(2,1)}, bf16[2048,128]{1,0:T(8,128)(2,1)}) custom-call(bf16[2048,512]{1,0:T(8,128)(2,1)} %all-gather.4.cloned.1.call-done.refs_0_.refs_2_, bf16[2048,512]{1,0:T(8,128)(2,1)} %collective-permute-done.2.refs_1_, ...), custom_call_target="tpu_custom_call" | custom-call | flops 7516192768 | bytes 18874368 | tf_op jit(solution)/shard_map/pallas_call | solution.py:197
  161.5 22.4 %collective-permute-done.11.refs_3_.refs_1_.refs_7_ = bf16[2048,256]{1,0:T(8,128)(2,1)S(1)} collective-permute-done((bf16[2048,256]{1,0:T(8,128)(2,1)}, bf16[2048,256]{1,0:T(8,128)(2,1)S(1)}, u32[]{:S(2)}, u32[]{:S(2)}) %collective-permute-start.11) | collective-permute-done | bytes 1048608 | tf_op jit(solution)/shard_map/ppermute | solution.py:93
  189.0 12.0 %shard_map.207 = (bf16[2048,128]{1,0:T(8,128)(2,1)}, f32[2048,128]{1,0:T(8,128)}, f32[2,2048]{1,0:T(2,128)}) custom-call(s32[4]{0:T(128)} %and_select_fusion.lowest_ref, bf16[2048,128]{1,0:T(8,128)(2,1)} %get-tuple-element.106.q_ref, bf16[2048,128]{1,0:T(8,128)(2,1)} %get-tuple-element.107.k_ref, bf16[2048,128]{1,0:T(8,128)(2,1)} %get-tuple-element.108.v_ref, ...), custom_call_target="tpu_custom_call" | custom-call | flops 1073741824 | bytes 3145728 | tf_op jit(solution)/shard_map/pallas_call | solution.py:542
  201.0 10.4 %shard_map.209 = (bf16[4,256,512]{2,1,0:T(8,128)(2,1)}, bf16[4,256,512]{2,1,0:T(8,128)(2,1)}) custom-call(s32[1]{0:T(128)} %bitcast.15.half_ref, bf16[2048,512]{1,0:T(8,128)(2,1)} %get-tuple-element.104.refs_0_, bf16[2048,512]{1,0:T(8,128)(2,1)} %collective-permute-done.18.refs_1_.refs_2_, ...), custom_call_target="tpu_custom_call" | custom-call | flops 4294967296 | bytes 16777216 | tf_op jit(solution)/shard_map/pallas_call | solution.py:395
  213.1 13.0 %shard_map.210 = (bf16[2048,512]{1,0:T(8,128)(2,1)}, bf16[2048,128]{1,0:T(8,128)(2,1)}, f32[1,512]{1,0:T(1,128)}) custom-call(bf16[2048,256]{1,0:T(8,128)(2,1)} %all-gather.6.cloned.1.call-done.refs_2_.refs_0_.refs_6_, bf16[2048,256]{1,0:T(8,128)(2,1)} %copy-done.27, bf16[2048,512]{1,0:T(8,128)(2,1)} %all-gather.8.cloned.1.call-done.refs_4_.refs_2_.refs_8_, ...), custom_call_target="tpu_custom_call" | custom-call | flops 5368709120 | bytes 14680064 | tf_op jit(solution)/shard_map/pallas_call | solution.py:248
  232.1 10.4 %shard_map.211 = (bf16[2048,512]{1,0:T(8,128)(2,1)}, bf16[2048,512]{1,0:T(8,128)(2,1)}) custom-call(bf16[2048,512]{1,0:T(8,128)(2,1)} %get-tuple-element.104.refs_0_, bf16[2048,128]{1,0:T(8,128)(2,1)} %get-tuple-element.123.refs_1_.refs_4_, bf16[2048,512]{1,0:T(8,128)(2,1)} %collective-permute-done.18.refs_1_.refs_2_, bf16[2048,128]{1,0:T(8,128)(2,1)} %copy-done.38, ...), custom_call_target="tpu_custom_call" | custom-call | flops 5368709120 | bytes 9437184 | tf_op jit(solution)/shard_map/pallas_call | solution.py:323
  246.8 10.3 %shard_map.212 = (bf16[4,256,512]{2,1,0:T(8,128)(2,1)}, bf16[4,256,512]{2,1,0:T(8,128)(2,1)}) custom-call(s32[1]{0:T(128)} %bitcast.15.half_ref, bf16[2048,512]{1,0:T(8,128)(2,1)} %all-gather.4.cloned.1.call-done.refs_0_.refs_2_, bf16[2048,512]{1,0:T(8,128)(2,1)} %collective-permute-done.6.refs_2_.refs_1_.refs_3_, ...), custom_call_target="tpu_custom_call" | custom-call | flops 4294967296 | bytes 16777216 | tf_op jit(solution)/shard_map/pallas_call | solution.py:395
  257.1 18.2 %shard_map.213 = (bf16[2048,384]{1,0:T(8,128)(2,1)}, f32[1,384]{1,0:T(1,128)}) custom-call(s32[4]{0:T(128)} %and_select_fusion.lowest_ref, bf16[2048,128]{1,0:T(8,128)(2,1)} %get-tuple-element.106.q_ref, bf16[2048,128]{1,0:T(8,128)(2,1)} %get-tuple-element.107.k_ref, bf16[2048,128]{1,0:T(8,128)(2,1)} %get-tuple-element.108.v_ref, ...), custom_call_target="tpu_custom_call" | custom-call | flops 2684354560 | bytes 4194304 | tf_op jit(solution)/shard_map/pallas_call | solution.py:647
  279.0 11.4 %collective-permute-done.20 = bf16[2048,512]{1,0:T(8,128)(2,1)S(1)} collective-permute-done((bf16[2048,512]{1,0:T(8,128)(2,1)}, bf16[2048,512]{1,0:T(8,128)(2,1)S(1)}, u32[]{:S(2)}, u32[]{:S(2)}) %collective-permute-start.20) | collective-permute-done | bytes 2097184 | tf_op jit(solution)/shard_map/ppermute | solution.py:93
  293.8 13.4 %shard_map.214 = (bf16[1024,512]{1,0:T(8,128)(2,1)}, bf16[1024,512]{1,0:T(8,128)(2,1)}, bf16[1024,512]{1,0:T(8,128)(2,1)}, bf16[1024,512]{1,0:T(8,128)(2,1)}) custom-call(bf16[2048,512]{1,0:T(8,128)(2,1)} %get-tuple-element.122.refs_2_.refs_0_, bf16[2048,384]{1,0:T(8,128)(2,1)} %get-tuple-element.144.refs_1_.refs_0_, bf16[2048,512]{1,0:T(8,128)(2,1)} %copy-done.26, ...), custom_call_target="tpu_custom_call" | custom-call | flops 7516192768 | bytes 11534336 | tf_op jit(solution)/shard_map/pallas_call | solution.py:323
  307.8 23.7 %collective-permute-done.25 = bf16[1024,512]{1,0:T(8,128)(2,1)S(1)} collective-permute-done((bf16[1024,512]{1,0:T(8,128)(2,1)}, bf16[1024,512]{1,0:T(8,128)(2,1)S(1)}, u32[]{:S(2)}, u32[]{:S(2)}) %collective-permute-start.25) | collective-permute-done | bytes 1048608 | tf_op jit(solution)/shard_map/ppermute | solution.py:93
  334.8 22.9 %collective-permute-done.26 = bf16[1024,512]{1,0:T(8,128)(2,1)S(1)} collective-permute-done((bf16[1024,512]{1,0:T(8,128)(2,1)}, bf16[1024,512]{1,0:T(8,128)(2,1)S(1)}, u32[]{:S(2)}, u32[]{:S(2)}) %collective-permute-start.26) | collective-permute-done | bytes 1048608 | tf_op jit(solution)/shard_map/ppermute | solution.py:93
  360.6 10.6 %collective-permute-done.32.refs_2_ = bf16[2,256,512]{2,1,0:T(8,128)(2,1)S(1)} collective-permute-done((bf16[2,256,512]{2,1,0:T(8,128)(2,1)S(1)}, bf16[2,256,512]{2,1,0:T(8,128)(2,1)S(1)}, u32[]{:S(2)}, u32[]{:S(2)}) %collective-permute-start.32) | collective-permute-done | bytes 524320 | tf_op jit(solution)/shard_map/ppermute | solution.py:93
  372.7 20.1 %collective-permute-done.33.received_ref = bf16[4,256,512]{2,1,0:T(8,128)(2,1)S(1)} collective-permute-done((bf16[4,256,512]{2,1,0:T(8,128)(2,1)S(1)}, bf16[4,256,512]{2,1,0:T(8,128)(2,1)S(1)}, u32[]{:S(2)}, u32[]{:S(2)}) %collective-permute-start.33) | collective-permute-done | bytes 1048608 | tf_op jit(solution)/shard_map/ppermute | solution.py:93
  397.9 10.7 %collective-permute-done.34.refs_2_ = bf16[2,256,512]{2,1,0:T(8,128)(2,1)S(1)} collective-permute-done((bf16[2,256,512]{2,1,0:T(8,128)(2,1)}, bf16[2,256,512]{2,1,0:T(8,128)(2,1)S(1)}, u32[]{:S(2)}, u32[]{:S(2)}) %collective-permute-start.34) | collective-permute-done | bytes 524320 | tf_op jit(solution)/shard_map/ppermute | solution.py:93
  410.1 13.0 %shard_map.216 = (bf16[4,512,256]{2,1,0:T(8,128)(2,1)}, bf16[4,512,256]{2,1,0:T(8,128)(2,1)}) custom-call(s32[1]{0:T(128)} %bitcast.15.half_ref, bf16[2048,384]{1,0:T(8,128)(2,1)} %get-tuple-element.144.refs_1_.refs_0_, bf16[2048,384]{1,0:T(8,128)(2,1)} %collective-permute-done.22.refs_3_.refs_1_, ...), custom_call_target="tpu_custom_call" | custom-call | flops 4294967296 | bytes 16777216 | tf_op jit(solution)/shard_map/pallas_call | solution.py:395
  424.6 19.1 %collective-permute-done.36.received_ref = bf16[4,512,256]{2,1,0:T(8,128)(2,1)S(1)} collective-permute-done((bf16[4,512,256]{2,1,0:T(8,128)(2,1)}, bf16[4,512,256]{2,1,0:T(8,128)(2,1)S(1)}, u32[]{:S(2)}, u32[]{:S(2)}) %collective-permute-start.36) | collective-permute-done | bytes 1048608 | tf_op jit(solution)/shard_map/ppermute | solution.py:93
  463.8 6.3 %collective-permute-done.40.refs_3_ = bf16[2,256,512]{2,1,0:T(8,128)(2,1)S(1)} collective-permute-done((bf16[2,256,512]{2,1,0:T(8,128)(2,1)S(1)}, bf16[2,256,512]{2,1,0:T(8,128)(2,1)S(1)}, u32[]{:S(2)}, u32[]{:S(2)}) %collective-permute-start.40) | collective-permute-done | bytes 524320 | tf_op jit(solution)/shard_map/ppermute | solution.py:93
  474.2 5.3 %collective-permute-done.42 = f32[1,896]{1,0:T(1,128)S(1)} collective-permute-done((f32[1,896]{1,0:T(1,128)S(1)}, f32[1,896]{1,0:T(1,128)S(1)}, u32[]{:S(2)}, u32[]{:S(2)}) %collective-permute-start.42) | collective-permute-done | bytes 3616 | tf_op jit(solution)/shard_map/ppermute | solution.py:93
  (225 shorter events, 128.4 us)
Async XLA Ops:
  7.2 57.1 %all-gather.4.cloned.1.call-start = ((), (), s32[]{:S(2)}) async-start(), calls=%async_computation.3 | async-start | bytes 2621440 | tf_op jit(solution)/shard_map/all_gather | solution.py:718
  16.6 141.6 %all-gather.6.cloned.1.call-start = ((), (), s32[]{:S(2)}) async-start(), calls=%async_computation.4 | async-start | bytes 1310720 | tf_op jit(solution)/shard_map/all_gather | solution.py:722
  64.3 47.4 %collective-permute-start.6 = (bf16[2048,512]{1,0:T(8,128)(2,1)}, bf16[2048,512]{1,0:T(8,128)(2,1)}, u32[]{:S(2)}, u32[]{:S(2)}) collective-permute-start(bf16[2048,512]{1,0:T(8,128)(2,1)} %all-gather.4.cloned.1.call-done.refs_0_.refs_2_), channel_id=1, source_target_pairs={{0,2},{1,3},{2,0},{3,1},{4,6},{5,7},{6,4},{7,5},{8,10},{9,11},{10,... | collective-permute-start | bytes 6291464 | tf_op jit(solution)/shard_map/ppermute | solution.py:93
  65.7 94.0 %all-gather.8.cloned.1.call-start = ((), (), s32[]{:S(2)}) async-start(), calls=%async_computation.5 | async-start | bytes 2621440 | tf_op jit(solution)/shard_map/all_gather | solution.py:723
  66.6 75.0 %collective-permute-start.2 = (bf16[2048,512]{1,0:T(8,128)(2,1)}, bf16[2048,512]{1,0:T(8,128)(2,1)}, u32[]{:S(2)}, u32[]{:S(2)}) collective-permute-start(bf16[2048,512]{1,0:T(8,128)(2,1)} %all-gather.4.cloned.1.call-done.refs_0_.refs_2_), channel_id=1, source_target_pairs={{0,1},{1,0},{2,3},{3,2},{4,5},{5,4},{6,7},{7,6},{8,9},{9,8},{10,11... | collective-permute-start | bytes 6291464 | tf_op jit(solution)/shard_map/ppermute | solution.py:93
  111.7 29.9 %collective-permute-start.7 = (bf16[2048,512]{1,0:T(8,128)(2,1)}, bf16[2048,512]{1,0:T(8,128)(2,1)}, u32[]{:S(2)}, u32[]{:S(2)}) collective-permute-start(bf16[2048,512]{1,0:T(8,128)(2,1)} %collective-permute-done.6.refs_2_.refs_1_.refs_3_), channel_id=1, source_target_pairs={{0,1},{1,0},{2,3},{3,2},{4,5},{5,4},{6,7},{7,6},{8,9},{9,8},{10,11... | collective-permute-start | bytes 6291464 | tf_op jit(solution)/shard_map/ppermute | solution.py:93
  112.3 22.8 %collective-permute-start.9 = (bf16[512,896]{1,0:T(8,128)(2,1)S(1)}, bf16[512,896]{1,0:T(8,128)(2,1)S(1)}, u32[]{:S(2)}, u32[]{:S(2)}) collective-permute-start(bf16[512,896]{1,0:T(8,128)(2,1)S(1)} %collective-permute-done.4.first_ref), channel_id=1, source_target_pairs={{0,16},{16,0},{1,17},{17,1},{2,18},{18,2},{3,19},{19,3},{4,20},{20... | collective-permute-start | bytes 2752520 | tf_op jit(solution)/shard_map/ppermute | solution.py:93
  114.7 333.6 %reduce-scatter.6.cloned.1.call-start = ((), (), s32[]{:S(2)}) async-start(), calls=%async_computation.7 | async-start | bytes 1310720 | tf_op jit(solution)/shard_map/reduce_scatter | solution.py:817
  158.0 30.0 %collective-permute-start.18 = (bf16[2048,512]{1,0:T(8,128)(2,1)}, bf16[2048,512]{1,0:T(8,128)(2,1)}, u32[]{:S(2)}, u32[]{:S(2)}) collective-permute-start(bf16[2048,512]{1,0:T(8,128)(2,1)} %get-tuple-element.104.refs_0_), channel_id=1, source_target_pairs={{0,1},{1,0},{2,3},{3,2},{4,5},{5,4},{6,7},{7,6},{8,9},{9,8},{10,11... | collective-permute-start | bytes 6291464 | tf_op jit(solution)/shard_map/ppermute | solution.py:93
  158.2 25.6 %collective-permute-start.11 = (bf16[2048,256]{1,0:T(8,128)(2,1)}, bf16[2048,256]{1,0:T(8,128)(2,1)S(1)}, u32[]{:S(2)}, u32[]{:S(2)}) collective-permute-start(bf16[2048,256]{1,0:T(8,128)(2,1)} %all-gather.6.cloned.1.call-done.refs_2_.refs_0_.refs_6_), channel_id=1, source_target_pairs={{0,2},{1,3},{2,0},{3,1},{4,6},{5,7},{6,4},{7,5},{8,10},{9,11},{10,... | collective-permute-start | bytes 3145736 | tf_op jit(solution)/shard_map/ppermute | solution.py:93
  159.7 51.7 %collective-permute-start.14 = (bf16[2048,512]{1,0:T(8,128)(2,1)}, bf16[2048,512]{1,0:T(8,128)(2,1)}, u32[]{:S(2)}, u32[]{:S(2)}) collective-permute-start(bf16[2048,512]{1,0:T(8,128)(2,1)} %all-gather.8.cloned.1.call-done.refs_4_.refs_2_.refs_8_), channel_id=1, source_target_pairs={{0,1},{1,0},{2,3},{3,2},{4,5},{5,4},{6,7},{7,6},{8,9},{9,8},{10,11... | collective-permute-start | bytes 6291464 | tf_op jit(solution)/shard_map/ppermute | solution.py:93
  159.8 24.7 %collective-permute-start.15 = (bf16[640,512]{1,0:T(8,128)(2,1)S(1)}, bf16[640,512]{1,0:T(8,128)(2,1)S(1)}, u32[]{:S(2)}, u32[]{:S(2)}) collective-permute-start(bf16[640,512]{1,0:T(8,128)(2,1)S(1)} %collective-permute-done.5.first_ref), channel_id=1, source_target_pairs={{0,16},{16,0},{1,17},{17,1},{2,18},{18,2},{3,19},{19,3},{4,20},{20... | collective-permute-start | bytes 1966088 | tf_op jit(solution)/shard_map/ppermute | solution.py:93
  161.3 50.0 %collective-permute-start.12 = (bf16[2048,256]{1,0:T(8,128)(2,1)}, bf16[2048,256]{1,0:T(8,128)(2,1)S(1)}, u32[]{:S(2)}, u32[]{:S(2)}) collective-permute-start(bf16[2048,256]{1,0:T(8,128)(2,1)} %all-gather.6.cloned.1.call-done.refs_2_.refs_0_.refs_6_), channel_id=1, source_target_pairs={{0,1},{1,0},{2,3},{3,2},{4,5},{5,4},{6,7},{7,6},{8,9},{9,8},{10,11... | collective-permute-start | bytes 3145736 | tf_op jit(solution)/shard_map/ppermute | solution.py:93
  183.9 27.5 %collective-permute-start.13 = (bf16[2048,256]{1,0:T(8,128)(2,1)S(1)}, bf16[2048,256]{1,0:T(8,128)(2,1)S(1)}, u32[]{:S(2)}, u32[]{:S(2)}) collective-permute-start(bf16[2048,256]{1,0:T(8,128)(2,1)S(1)} %collective-permute-done.11.refs_3_.refs_1_.refs_7_), channel_id=1, source_target_pairs={{0,1},{1,0},{2,3},{3,2},{4,5},{5,4},{6,7},{7,6},{8,9},{9,8},{10,11... | collective-permute-start | bytes 3145736 | tf_op jit(solution)/shard_map/ppermute | solution.py:93
  184.5 26.8 %collective-permute-start.16 = (bf16[640,512]{1,0:T(8,128)(2,1)}, bf16[640,512]{1,0:T(8,128)(2,1)S(1)}, u32[]{:S(2)}, u32[]{:S(2)}) collective-permute-start(bf16[640,512]{1,0:T(8,128)(2,1)} %get-tuple-element.116.refs_5_), channel_id=1, source_target_pairs={{0,1},{1,0},{2,3},{3,2},{4,5},{5,4},{6,7},{7,6},{8,9},{9,8},{10,11... | collective-permute-start | bytes 1966088 | tf_op jit(solution)/shard_map/ppermute | solution.py:93
  188.0 23.4 %collective-permute-start.17 = (bf16[640,512]{1,0:T(8,128)(2,1)}, bf16[640,512]{1,0:T(8,128)(2,1)S(1)}, u32[]{:S(2)}, u32[]{:S(2)}) collective-permute-start(bf16[640,512]{1,0:T(8,128)(2,1)} %get-tuple-element.117.refs_7_), channel_id=1, source_target_pairs={{0,1},{1,0},{2,3},{3,2},{4,5},{5,4},{6,7},{7,6},{8,9},{9,8},{10,11... | collective-permute-start | bytes 1966088 | tf_op jit(solution)/shard_map/ppermute | solution.py:93
  242.5 47.9 %collective-permute-start.20 = (bf16[2048,512]{1,0:T(8,128)(2,1)}, bf16[2048,512]{1,0:T(8,128)(2,1)S(1)}, u32[]{:S(2)}, u32[]{:S(2)}) collective-permute-start(bf16[2048,512]{1,0:T(8,128)(2,1)} %get-tuple-element.126), channel_id=1, source_target_pairs={{0,2},{1,3},{2,0},{3,1},{4,6},{5,7},{6,4},{7,5},{8,10},{9,11},{10,... | collective-permute-start | bytes 6291464 | tf_op jit(solution)/shard_map/ppermute | solution.py:93
  244.0 31.4 %collective-permute-start.23 = (bf16[4,256,512]{2,1,0:T(8,128)(2,1)S(1)}, bf16[4,256,512]{2,1,0:T(8,128)(2,1)S(1)}, u32[]{:S(2)}, u32[]{:S(2)}) collective-permute-start(bf16[4,256,512]{2,1,0:T(8,128)(2,1)S(1)} %copy-done.29), channel_id=1, source_target_pairs={{0,16},{16,0},{1,17},{17,1},{2,18},{18,2},{3,19},{19,3},{4,20},{20... | collective-permute-start | bytes 3145736 | tf_op jit(solution)/shard_map/ppermute | solution.py:93
  307.2 24.3 %collective-permute-start.25 = (bf16[1024,512]{1,0:T(8,128)(2,1)}, bf16[1024,512]{1,0:T(8,128)(2,1)S(1)}, u32[]{:S(2)}, u32[]{:S(2)}) collective-permute-start(bf16[1024,512]{1,0:T(8,128)(2,1)} %get-tuple-element.140), channel_id=1, source_target_pairs={{0,2},{1,3},{2,0},{3,1},{4,6},{5,7},{6,4},{7,5},{8,10},{9,11},{10,... | collective-permute-start | bytes 3145736 | tf_op jit(solution)/shard_map/ppermute | solution.py:93
  334.2 114.1 %reduce-scatter.8.cloned.1.call-start = ((), (), s32[]{:S(2)}) async-start(), calls=%async_computation.8 | async-start | bytes 1310720 | tf_op jit(solution)/shard_map/reduce_scatter | solution.py:821
  334.2 23.5 %collective-permute-start.26 = (bf16[1024,512]{1,0:T(8,128)(2,1)}, bf16[1024,512]{1,0:T(8,128)(2,1)S(1)}, u32[]{:S(2)}, u32[]{:S(2)}) collective-permute-start(bf16[1024,512]{1,0:T(8,128)(2,1)} %get-tuple-element.143), channel_id=1, source_target_pairs={{0,2},{1,3},{2,0},{3,1},{4,6},{5,7},{6,4},{7,5},{8,10},{9,11},{10,... | collective-permute-start | bytes 3145736 | tf_op jit(solution)/shard_map/ppermute | solution.py:93
  359.0 101.7 %reduce-scatter.4.cloned.1.call-start = ((), (), s32[]{:S(2)}) async-start(), calls=%async_computation.6 | async-start | bytes 2621440 | tf_op jit(solution)/shard_map/reduce_scatter | solution.py:794
  371.2 21.6 %collective-permute-start.33 = (bf16[4,256,512]{2,1,0:T(8,128)(2,1)S(1)}, bf16[4,256,512]{2,1,0:T(8,128)(2,1)S(1)}, u32[]{:S(2)}, u32[]{:S(2)}) collective-permute-start(bf16[4,256,512]{2,1,0:T(8,128)(2,1)S(1)} %copy-done.28), channel_id=1, source_target_pairs={{0,16},{16,0},{1,17},{17,1},{2,18},{18,2},{3,19},{19,3},{4,20},{20... | collective-permute-start | bytes 3145736 | tf_op jit(solution)/shard_map/ppermute | solution.py:93
  479.5 21.9 %collective-permute-start.31 = (f32[3,512]{1,0:T(4,128)S(1)}, f32[3,512]{1,0:T(4,128)S(1)}, u32[]{:S(2)}, u32[]{:S(2)}) collective-permute-start(f32[3,512]{1,0:T(4,128)S(1)} %fusion.29), channel_id=1, source_target_pairs={{0,16},{16,0},{1,17},{17,1},{2,18},{18,2},{3,19},{19,3},{4,20},{20... | collective-permute-start | bytes 18440 | tf_op jit(solution)/shard_map/ppermute | solution.py:93
  (65 other events, 997.8 us)
Sparse Core Ops, SparseCore 0:
  16.8 47.3 all-gather.3
  65.8 28.3 all-gather.5
  114.9 43.7 all-gather.7
  334.3 25.3 reduce-scatter.5
  362.4 25.7 reduce-scatter.7
  391.0 42.1 reduce-scatter.3

commit v3 on v2

--- a/solution.py
+++ b/solution.py
@@ -114,9 +114,10 @@
     small = qkv_flat.shape[1] // 4
 
     def kernel(places_ref, *refs):
-        for place in range(3):
-            refs[6 + place][:, :width] = refs[place][...]
-            refs[6 + place][:, width:] = refs[3 + place][...]
+        for place in range(2):
+            refs[5 + place][:, :width] = refs[place][...]
+            refs[5 + place][:, width:] = refs[2 + place][...]
+        refs[7][...] = refs[4][...]
 
     def at(place):
         return lambda step, s: (0, s[place])
@@ -128,14 +129,14 @@
         grid_spec=pltpu.PrefetchScalarGridSpec(
             num_scalar_prefetch=1,
             grid=(1,),
-            in_specs=[pl.BlockSpec((rows, width), at(i)) for i in range(3)]
+            in_specs=[pl.BlockSpec((rows, width), at(i)) for i in range(2)]
             + [pl.BlockSpec((rows, small), at(i)) for i in range(3)],
-            out_specs=[whole] * 3,
-        ),
-        out_shape=[shape] * 3,
+            out_specs=[whole] * 2 + [pl.BlockSpec((rows, small), lambda step, s: (0, 0))],
+        ),
+        out_shape=[shape] * 2 + [jax.ShapeDtypeStruct((rows, small), bf16)],
         compiler_params=params(),
         cost_estimate=cost(0, 3 * 4 * rows * (width + small)),
-    )(places, fc1_weight, fc1_weight, fc1_weight, qkv_flat, qkv_flat, qkv_flat)
+    )(places, fc1_weight, fc1_weight, qkv_flat, qkv_flat, qkv_flat)
 
 
 def pack_out(places, fc2_weight, out_weight):
@@ -168,18 +169,21 @@
 
 
 def forward_step(xs, ws, fc1_bias, qkv_bias, tables):
-    rows, width = xs[0].shape
+    rows, width = xs[0].shape[0], ws[0].shape[0]
     hidden = fc1_bias.shape[1]
     pair = qkv_bias.shape[1] // 3
     block = min(512, rows)
 
     def kernel(*refs):
-        x_refs, w_refs = refs[:4], refs[4:8]
-        fb, qb, keep, high, low = refs[8:13]
-        up_o, act_o, q_o, k_o, v_o = refs[13:]
-        total = mul(x_refs[0][...], w_refs[0][...])
-        for x_ref, w_ref in zip(x_refs[1:], w_refs[1:]):
-            total = total + mul(x_ref[...], w_ref[...])
+        x_refs, w_refs = refs[:8], refs[8:12]
+        fb, qb, keep, high, low = refs[12:17]
+        up_o, act_o, q_o, k_o, v_o = refs[17:]
+        blocks = blocks_of([ref[...] for ref in x_refs[:4]])
+        blocks = blocks + blocks_of([ref[...] for ref in x_refs[4:]])
+        total = None
+        for item, w_ref in zip(blocks, w_refs):
+            part = mul(item, w_ref[...])
+            total = part if total is None else total + part
         up = total[:, :hidden] + fb[...]
         up_o[...] = up
         act_o[...] = gelu(up).astype(bf16)
@@ -197,7 +201,7 @@
     return pl.pallas_call(
         kernel,
         grid=(rows // block,),
-        in_specs=[rowed(width)] * 4
+        in_specs=[rowed(x.shape[1]) for x in xs]
         + [fixed(w) for w in ws]
         + [fixed(fc1_bias), fixed(qkv_bias)]
         + [rowed(pair)] * 3,
@@ -262,28 +266,44 @@
     )(*gs, *ws, up_pre)
 
 
-def pick(same, first, second):
-    def kernel(same_ref, first_ref, second_ref, own_o, other_o):
+def pick(same, firsts, seconds, axis):
+    sizes = [first.shape[axis] for first in firsts]
+    count = len(firsts)
+    shape = list(firsts[0].shape)
+    shape[axis] = sum(sizes)
+
+    def kernel(same_ref, *refs):
+        own_o, other_o = refs[2 * count :]
+
+        def fill(owns, others):
+            at = 0
+            for own, other, size in zip(owns, others, sizes):
+                spot = (slice(None), slice(at, at + size)) if axis else slice(at, at + size)
+                own_o[spot] = own[...]
+                other_o[spot] = other[...]
+                at += size
+
         @pl.when(same_ref[0] == 1)
         def _():
-            own_o[...] = first_ref[...]
-            other_o[...] = second_ref[...]
+            fill(refs[:count], refs[count : 2 * count])
 
         @pl.when(same_ref[0] != 1)
         def _():
-            own_o[...] = second_ref[...]
-            other_o[...] = first_ref[...]
-
-    whole = pl.BlockSpec(first.shape, lambda i, s: (0, 0))
+            fill(refs[count : 2 * count], refs[:count])
+
+    whole = pl.BlockSpec(tuple(shape), lambda i, s: (0, 0))
     return pl.pallas_call(
         kernel,
         grid_spec=pltpu.PrefetchScalarGridSpec(
-            num_scalar_prefetch=1, grid=(1,), in_specs=[whole] * 2, out_specs=[whole] * 2
-        ),
-        out_shape=[jax.ShapeDtypeStruct(first.shape, first.dtype)] * 2,
-        compiler_params=params(),
-        cost_estimate=cost(0, 8 * first.size),
-    )(same, first, second)
+            num_scalar_prefetch=1,
+            grid=(1,),
+            in_specs=[pl.BlockSpec(x.shape, lambda i, s: (0, 0)) for x in firsts + seconds],
+            out_specs=[whole] * 2,
+        ),
+        out_shape=[jax.ShapeDtypeStruct(tuple(shape), bf16)] * 2,
+        compiler_params=params(),
+        cost_estimate=cost(0, 8 * math.prod(shape)),
+    )(same, *firsts, *seconds)
 
 
 def spread(sides, near_mats, far_mats, transposed, part):
@@ -337,6 +357,11 @@
 def blocks_of(values):
     if len(values) == 2:
         return values
+    if len(values) == 4:
+        return [
+            jnp.concatenate(values[:2], axis=1),
+            jnp.concatenate(values[2:], axis=1),
+        ]
     cut = values[2].shape[1] // 2
     return [
         jnp.concatenate([values[0], values[2][:, :cut]], axis=1),
@@ -344,14 +369,17 @@
     ]
 
 
+def width_of(arrays):
+    return sum(array.shape[1] for array in arrays) // 2
+
+
 def grad_blocks(half, jobs, across):
     rows = jobs[0][0][0].shape[0]
     block = min(1024, rows)
     steps = rows // block
-    sizes = [lefts[0].shape[1] for lefts, _, _ in jobs]
+    sizes = [width_of(lefts) for lefts, _, _ in jobs]
     out_rows = sum(sizes)
-    _, rights, _ = jobs[0]
-    out_cols = rights[0].shape[1] if len(rights) == 2 else rights[2].shape[1]
+    out_cols = width_of(jobs[0][1])
     arrays = [array for lefts, rights, _ in jobs for array in lefts + rights]
     cut = (out_rows, out_cols // 2) if across else (out_rows // 2, out_cols)
 
@@ -360,7 +388,7 @@
         step = pl.program_id(0)
         at = 0
         for size, (lefts, rights, hidden_left) in zip(sizes, jobs):
-            l0, l1 = [ins.pop(0)[...] for _ in lefts]
+            l0, l1 = blocks_of([ins.pop(0)[...] for _ in lefts])
             r0, r1 = blocks_of([ins.pop(0)[...] for _ in rights])
             if hidden_left:
                 pairs = ((l0, r0), (l1, r0), (l0, r1), (l1, r1))
@@ -699,26 +727,33 @@
         jnp.int32
     )
     same = (half == (col_index & 1)).astype(jnp.int32).reshape(1)
-    half = half.reshape(1)
+    hidden = fc1_bias.shape[0]
 
     token_f = tokens.astype(f32)
     ln_local = jnp.stack([jnp.sum(token_f, axis=1), jnp.sum(token_f * token_f, axis=1)])
     ln_sums = ln_local + swap_bits(ln_local, COL, 1)
     ln_far = swap_bits(ln_sums, COL, 2)
-    cut = local_width // 2
-    tail = out_grad[:, cut:]
-    tail_far = swap_bits(after(tail, ln_far), COL, 2)
-    qkv_flat = after(qkv_weight, ln_sums).reshape(local_width, -1)
+    fc1_far = lax.dynamic_slice_in_dim(
+        after(fc1_weight, ln_local), far_block * hidden, hidden, 1
+    )
+    fc1_first = swap_bits(after(fc1_far, ln_far), COL, 2)
+    qkv_flat = after(qkv_weight, fc1_far).reshape(local_width, -1)
+    half = half.reshape(1)
     ln_sums = ln_sums + ln_far
     row_mean = ln_sums[0] / full_width
     variance = ln_sums[1] / full_width - row_mean * row_mean
     inv_std = lax.rsqrt(variance + epsilon)
     centred = (token_f - row_mean[:, None]) * inv_std[:, None]
     normed = (centred * ln_gain + ln_bias).astype(bf16)
-    normed_0 = lax.all_gather(normed, ROW, axis=0, tiled=True)
-    in_own, in_near, in_far = pack_in(packs, fc1_weight, after(qkv_flat, normed))
-    in_first = swap_bits(after(in_far, tail_far), COL, 2)
-    out_own, out_near, out_far = pack_out(packs, fc2_weight, after(out_weight, in_far))
+    cut = local_width // 2
+    normed_0a = lax.all_gather(normed[:, :cut], ROW, axis=0, tiled=True)
+    normed_0b = lax.all_gather(normed[:, cut:], ROW, axis=0, tiled=True)
+    in_own, in_near, qkv_far = pack_in(packs, fc1_weight, after(qkv_flat, normed))
+    qkv_first = swap_bits(after(qkv_far, fc1_first), COL, 2)
+    fc1_second = swap_bits(fc1_first, DP, 1)
+    tail = out_grad[:, cut:]
+    tail_far = swap_bits(after(tail, qkv_first), COL, 2)
+    out_own, out_near, out_far = pack_out(packs, fc2_weight, after(out_weight, in_own))
     cot_0 = lax.all_gather(after(out_grad[:, :cut], normed), ROW, axis=0, tiled=True)
     cot_b = lax.all_gather(
         jnp.concatenate([tail, tail_far], axis=1), ROW, axis=0, tiled=True
@@ -732,46 +767,43 @@
 
     in_1 = swap_bits(after(in_near, normed), COL, 1)
     out_1 = swap_bits(out_near, COL, 1)
-    in_second = swap_bits(in_first, DP, 1)
-    out_first = swap_bits(after(out_far, in_first), COL, 2)
-    in_2, in_pass = pick(after(same, *tables), in_first, in_second)
+    qkv_second = swap_bits(after(qkv_first, fc1_second), DP, 1)
+    normed_2a = swap_bits(after(normed_0a, tail_far), COL, 2)
+    in_2, in_pass = pick(after(same, *tables), [fc1_first, qkv_first], [fc1_second, qkv_second], 1)
     in_3 = swap_bits(in_pass, COL, 1)
-    out_second = swap_bits(after(out_first, in_second), DP, 1)
-    out_2, out_pass = pick(after(same, in_2), out_first, out_second)
-    out_3 = swap_bits(out_pass, COL, 1)
-
-    normed_2 = swap_bits(after(normed_0, out_first), COL, 2)
-    normed_1 = swap_bits(normed_0, COL, 1)
-    normed_3 = swap_bits(normed_2, COL, 1)
-    cot_2 = swap_bits(after(cot_0, normed_2), COL, 2)
+    normed_1 = [swap_bits(normed_0a, COL, 1), swap_bits(normed_0b, COL, 1)]
+    normed_2b = swap_bits(after(normed_0b, normed_2a), COL, 2)
+    out_first = swap_bits(after(out_far, normed_2b), COL, 2)
+    normed_3 = [swap_bits(normed_2a, COL, 1), swap_bits(normed_2b, COL, 1)]
+    normed_all = [normed_0a, normed_0b, normed_2a, normed_2b]
     up_pre, act, q_rot, k_rot, v_low = forward_step(
-        [normed_0, normed_1, normed_2, normed_3],
-        [in_own, in_1, in_2, in_3],
+        normed_all + normed_1 + normed_3,
+        [in_own, in_2, in_1, in_3],
         fc1_bias.reshape(1, -1),
         qkv_bias.reshape(1, -1),
         tables,
     )
+    cot_2 = swap_bits(after(cot_0, out_first, act), COL, 2)
+    out_second = swap_bits(after(out_first, qkv_second), DP, 1)
+    out_2, out_pass = pick(after(same, act), [out_first], [out_second], 0)
+    out_3 = swap_bits(out_pass, COL, 1)
     act_1 = swap_bits(act, COL, 1)
     attn, attn_full, lse = attend(lowest, after(q_rot, act), k_rot, v_low, begin)
     attn_1 = swap_bits(attn, COL, 1)
     cots = [cot_0, cot_2, cot_b]
     cots_1 = [swap_bits(cot_0, COL, 1), swap_bits(cot_2, COL, 1), swap_bits(cot_b, COL, 1)]
+    mix_near, mix_far = spread(
+        [[act, attn], [act_1, attn_1]], [out_own, out_near], [out_2, out_pass], False, 0
+    )
+    mix_recv = swap_bits(after(mix_far, cot_2), COL, 2)
     fc2_keep, fc2_send = grad_blocks(
-        half, [([act, after(act_1, attn)], cots, True)], False
-    )
-    fc2_recv = swap_bits(fc2_send, DP, 1)
+        half, [([act, after(act_1, mix_far)], cots, True)], False
+    )
+    fc2_recv = swap_bits(after(fc2_send, out_second), DP, 1)
     d_up, d_attn, fc1_sums = slope_step(
         cots + cots_1, [out_own, out_2, out_1, out_3], after(up_pre, fc2_send)
     )
     d_up_1 = swap_bits(d_up, COL, 1)
-    mix_near, mix_far = spread(
-        [[act, after(attn, d_up)], [act_1, attn_1]],
-        [out_own, out_near],
-        [out_2, out_pass],
-        False,
-        0,
-    )
-    mix_recv = swap_bits(after(mix_far, cot_2), COL, 2)
 
     def sum_halves(keep, received):
         near, far = add_halves(keep, received)
@@ -780,23 +812,19 @@
             far = (far.astype(f32) + swap_bits(far, DP, bit).astype(f32)).astype(bf16)
         return near, far
 
-    fc1_keep, fc1_send = grad_blocks(
-        half, [([after(normed_0, mix_far), normed_2], [d_up, d_up_1], False)], False
-    )
-    fc2_near, fc2_far = sum_halves(fc2_keep, after(fc2_recv, mix_far))
-    fc2_near_x = swap_bits(fc2_near, DP, 1)
-    fc1_recv = swap_bits(after(fc1_send, fc2_near_x), DP, 1)
+    fc1_keep, fc1_send = grad_blocks(half, [(normed_all, [d_up, d_up_1], False)], False)
+    fc1_recv = swap_bits(after(fc1_send, fc2_recv), DP, 1)
     d_proj, qkv_sums = attend_back(
         lowest, q_rot, k_rot, v_low, begin, after(d_attn, fc1_send), attn_full, lse, tables
     )
     d_proj_1 = swap_bits(d_proj, COL, 1)
+    fc2_near, fc2_far = sum_halves(fc2_keep, after(fc2_recv, d_proj))
     mix_total = (mix_near.astype(f32) + mix_recv.astype(f32)).astype(bf16)
     mixed = lax.psum_scatter(mix_total, ROW, scatter_dimension=0, tiled=True).astype(f32)
     fc2_crossed = swap_bits(after(fc2_far, mix_total), COL, 2)
-    fc1_near, fc1_far = sum_halves(fc1_keep, after(fc1_recv, d_proj))
-    fc1_near_x = swap_bits(after(fc1_near, fc1_recv), DP, 1)
+    fc2_near_x = swap_bits(after(fc2_near, fc1_recv), DP, 1)
     near_a, near_b, far_a, far_b = spread(
-        [[d_up, d_proj], [d_up_1, d_proj_1]],
+        [[d_up, after(d_proj, fc2_far)], [d_up_1, d_proj_1]],
         [in_own, in_near],
         [in_2, in_pass],
         True,
@@ -804,26 +832,28 @@
     )
     recv_a = swap_bits(after(far_a, fc2_crossed), COL, 2)
     recv_b = swap_bits(after(far_b, recv_a), COL, 2)
-    fc2_crossed_x = swap_bits(after(fc2_crossed, fc1_near_x), DP, 1)
+    fc2_crossed_x = swap_bits(after(fc2_crossed, fc2_near_x), DP, 1)
     rest_keep, rest_send = grad_blocks(
         half,
         [
-            ([after(d_proj, far_a), d_proj_1], [normed_0, normed_2], True),
+            ([after(d_proj, far_a), d_proj_1], normed_all, True),
             ([attn, attn_1], cots, True),
         ],
         True,
     )
+    rest_recv = swap_bits(after(rest_send, fc2_crossed_x), DP, 1)
+    fc1_near, fc1_far = sum_halves(fc1_keep, after(fc1_recv, rest_send))
     total_a = (near_a.astype(f32) + recv_a.astype(f32)).astype(bf16)
     d_normed_a = lax.psum_scatter(total_a, ROW, scatter_dimension=0, tiled=True)
-    rest_recv = swap_bits(after(rest_send, fc2_crossed_x), DP, 1)
     (fc2_weight_grad,) = lay_out(places, [fc2_near, fc2_crossed], [fc2_near_x, fc2_crossed_x], 0)
     total_b = (near_b.astype(f32) + recv_b.astype(f32)).astype(bf16)
     d_normed_b = lax.psum_scatter(total_b, ROW, scatter_dimension=0, tiled=True)
+    fc1_near_x = swap_bits(after(fc1_near, rest_recv), DP, 1)
     fc1_crossed = swap_bits(after(fc1_far, total_b), COL, 2)
-    rest_near, rest_far = sum_halves(rest_keep, rest_recv)
-    rest_near_x = swap_bits(after(rest_near, rest_recv), DP, 1)
+    rest_near, rest_far = sum_halves(rest_keep, after(rest_recv, total_b))
+    rest_near_x = swap_bits(after(rest_near, fc1_near_x), DP, 1)
+    rest_crossed = swap_bits(after(rest_far, fc1_crossed), COL, 2)
     fc1_crossed_x = swap_bits(after(fc1_crossed, rest_near_x), DP, 1)
-    rest_crossed = swap_bits(after(rest_far, fc1_crossed), COL, 2)
     rest_crossed_x = swap_bits(after(rest_crossed, fc1_crossed_x), DP, 1)
     d_normed = jnp.concatenate([d_normed_a, d_normed_b], axis=0).astype(f32)
     (fc1_weight_grad,) = lay_out(places, [fc1_near, fc1_crossed], [fc1_near_x, fc1_crossed_x], 1)

time: 509 us -> 482 us (0.947)
  waiting for transfers between devices: 259 us -> 228 us
  starting transfers between devices: 36.7 us -> 46.7 us
    ppermute x43 -> x48, waiting for transfers between devices: 259 us -> 183 us  [swap_bits(): lax.ppermute(value, axis, [(place, place ^ bit) for place in range(count)])]
    all_gather x1 -> x2, waiting for transfers between devices: 0.01 us -> 24.8 us  [the longest x1 24.8 us: step(): normed_0b = lax.all_gather(normed[:, cut:], ROW, axis=0, tiled=True)]
    all_gather x1, waiting for transfers between devices: 0.01 us -> 18.5 us  [step(): lax.all_gather(after(out_grad[:, :cut], normed), ROW, axis=0, tiled=True)]
    ppermute x43 -> x48, starting transfers between devices: 36.5 us -> 46.4 us  [swap_bits(): lax.ppermute(value, axis, [(place, place ^ bit) for place in range(count)])]
    unnamed x83 -> x77, local copies, waits for them, and re-layouts: 14.1 us -> 9.74 us
  transfers between devices with their start and end apart: 49 -> 55, of which waited for: 20 -> 26; matrix products, arithmetic and copies ran while one was open for 6% -> 6% of each run, Pallas kernels for 27% -> 29%
where the time goes in v3:
time: 482 us
  waiting for transfers between devices  228 us (47%)
  Pallas kernels  150 us (31%)
  starting transfers between devices  46.7 us (10%)
  other arithmetic  22 us (5%)
  local copies, waits for them, and re-layouts  20.4 us (4%)
  between operations  14.6 us (3%)
    ppermute x48, waiting for transfers between devices, swap_bits(): lax.ppermute(value, axis, [(place, place ^ bit) for place in range(count)])  183 us
    ppermute x48, starting transfers between devices, swap_bits(): lax.ppermute(value, axis, [(place, place ^ bit) for place in range(count)])  46.4 us
    pallas_call x3, Pallas kernels, grad_blocks(): pl.pallas_call(kernel, grid_spec=pltpu.PrefetchScalarGridSpec(num_scalar_...  33.6 us
    all_gather x1, waiting for transfers between devices, step(): normed_0b = lax.all_gather(normed[:, cut:], ROW, axis=0, tiled=True)  24.8 us
    pallas_call x2, Pallas kernels, spread(): pl.pallas_call(kernel, grid=(rows // block,), in_specs=[rowed(hidden), ro...  23.9 us
    all_gather x1, waiting for transfers between devices, step(): lax.all_gather(after(out_grad[:, :cut], normed), ROW, axis=0, tiled=True)  18.5 us
    pallas_call x1, Pallas kernels, attend_back(): pl.pallas_call(kernel, grid_spec=pltpu.PrefetchScalarGridSpec(num_scalar_...  17.9 us
    pallas_call x1, Pallas kernels, forward_step(): pl.pallas_call(kernel, grid=(rows // block,), in_specs=[rowed(x.shape[1])...  15.7 us
  transfers between devices with their start and end apart: 55, of which 26 were waited for; matrix products, arithmetic and copies ran while one was open for 6% of the time, Pallas kernels for 29%

profile of v3, /device:TPU:0, one launch (start us, length us, event | category | flops | bytes accessed | tf_op | source)
XLA Modules:
  0.0 481.6 jit_solution(8618211189387981602)
XLA Ops:
  35.3 7.2 %collective-permute-done.3.refs_1_ = bf16[512,384]{1,0:T(8,128)(2,1)S(1)} collective-permute-done((bf16[512,384]{1,0:T(8,128)(2,1)}, bf16[512,384]{1,0:T(8,128)(2,1)S(1)}, u32[]{:S(2)}, u32[]{:S(2)}) %collective-permute-start.3) | collective-permute-done | bytes 393248 | tf_op jit(solution)/shard_map/ppermute | solution.py:93
  51.3 24.8 %all-gather.7.cloned.1.call-done.refs_1_.refs_3_ = bf16[2048,256]{1,0:T(8,128)(2,1)} async-done(((bf16[512,256]{1,0:T(8,128)(2,1)}), bf16[2048,256]{1,0:T(8,128)(2,1)}) %all-gather.7.cloned.1.call-update) | async-done | bytes 1048592 | tf_op jit(solution)/shard_map/all_gather | solution.py:750
  79.5 11.2 %collective-permute-done.11.refs_2_ = bf16[512,512]{1,0:T(8,128)(2,1)S(1)} collective-permute-done((bf16[512,512]{1,0:T(8,128)(2,1)}, bf16[512,512]{1,0:T(8,128)(2,1)S(1)}, u32[]{:S(2)}, u32[]{:S(2)}) %collective-permute-start.11) | collective-permute-done | bytes 524320 | tf_op jit(solution)/shard_map/ppermute | solution.py:93
  92.9 7.2 %collective-permute-done.12.refs_3_ = bf16[512,384]{1,0:T(8,128)(2,1)S(1)} collective-permute-done((bf16[512,384]{1,0:T(8,128)(2,1)S(1)}, bf16[512,384]{1,0:T(8,128)(2,1)S(1)}, u32[]{:S(2)}, u32[]{:S(2)}) %collective-permute-start.12) | collective-permute-done | bytes 393248 | tf_op jit(solution)/shard_map/ppermute | solution.py:93
  100.9 5.8 %fusion = (f32[2048,128]{1,0:T(8,128)}, f32[2048,128]{1,0:T(8,128)}, f32[2048,128]{1,0:T(8,128)}) fusion(f32[128]{0:T(128)S(1)} %fusion.22, f32[2048]{0:T(1024)S(1)} %get-tuple-element.232, pred[128]{0:T(512)(128)(4,1)S(1)} %get-tuple-element.237, pred[128]{0:T(512)(128)(4,1)S(1)} %get-tuple-element.238, pred[128]{0:T(512)(128)(4,1)S(1)} %broadcast_compare_fusion.1), kind=kLoop, calls=%fused_computation.12 | loop fusion | flops 1310720 | bytes 3154816 | tf_op jit(solution)/shard_map/jit(_where)/select_n | solution.py:62
  112.6 15.7 %shard_map.205 = (f32[2048,512]{1,0:T(8,128)}, bf16[2048,512]{1,0:T(8,128)(2,1)}, bf16[2048,128]{1,0:T(8,128)(2,1)}, bf16[2048,128]{1,0:T(8,128)(2,1)}, bf16[2048,128]{1,0:T(8,128)(2,1)}) custom-call(bf16[2048,256]{1,0:T(8,128)(2,1)} %all-gather.5.cloned.1.call-done.refs_0_.refs_2_, bf16[2048,256]{1,0:T(8,128)(2,1)} %all-gather.7.cloned.1.call-done.refs_1_.refs_3_, ...), custom_call_target="tpu_custom_call" | custom-call | flops 7516192768 | bytes 18874368 | tf_op jit(solution)/shard_map/pallas_call | solution.py:201
  133.7 18.5 %all-gather.9.cloned.1.call-done.refs_2_.refs_0_.refs_8_ = bf16[2048,256]{1,0:T(8,128)(2,1)} async-done(((bf16[512,256]{1,0:T(8,128)(2,1)}), bf16[2048,256]{1,0:T(8,128)(2,1)}) %all-gather.9.cloned.1.call-update) | async-done | bytes 1048592 | tf_op jit(solution)/shard_map/all_gather | solution.py:757
  156.3 12.0 %shard_map.206 = (bf16[2048,128]{1,0:T(8,128)(2,1)}, f32[2048,128]{1,0:T(8,128)}, f32[2,2048]{1,0:T(2,128)}) custom-call(s32[4]{0:T(128)} %and_select_fusion.lowest_ref, bf16[2048,128]{1,0:T(8,128)(2,1)} %get-tuple-element.113.q_ref, bf16[2048,128]{1,0:T(8,128)(2,1)} %get-tuple-element.114.k_ref, bf16[2048,128]{1,0:T(8,128)(2,1)} %get-tuple-element.115.v_ref, ...), custom_call_target="tpu_custom_call" | custom-call | flops 1073741824 | bytes 3145728 | tf_op jit(solution)/shard_map/pallas_call | solution.py:570
  170.0 6.8 %collective-permute-done.19.refs_3_.refs_1_.refs_9_ = bf16[2048,256]{1,0:T(8,128)(2,1)S(1)} collective-permute-done((bf16[2048,256]{1,0:T(8,128)(2,1)}, bf16[2048,256]{1,0:T(8,128)(2,1)S(1)}, u32[]{:S(2)}, u32[]{:S(2)}) %collective-permute-start.19) | collective-permute-done | bytes 1048608 | tf_op jit(solution)/shard_map/ppermute | solution.py:93
  180.7 10.4 %shard_map.209 = (bf16[2048,512]{1,0:T(8,128)(2,1)}, bf16[2048,512]{1,0:T(8,128)(2,1)}) custom-call(bf16[2048,512]{1,0:T(8,128)(2,1)} %get-tuple-element.111.refs_0_, bf16[2048,128]{1,0:T(8,128)(2,1)} %get-tuple-element.116.refs_1_.refs_6_, bf16[2048,512]{1,0:T(8,128)(2,1)} %collective-permute-done.15.refs_2_.refs_1_, bf16[2048,128]{1,0:T(8,128)(2,1)} %copy-done.35, ...), custom_call_target="tpu_custom_call" | custom-call | flops 5368709120 | bytes 9437184 | tf_op jit(solution)/shard_map/pallas_call | solution.py:343
  191.1 10.4 %shard_map.210 = (bf16[4,256,512]{2,1,0:T(8,128)(2,1)}, bf16[4,256,512]{2,1,0:T(8,128)(2,1)}) custom-call(s32[1]{0:T(128)} %bitcast.15.half_ref, bf16[2048,512]{1,0:T(8,128)(2,1)} %get-tuple-element.111.refs_0_, bf16[2048,512]{1,0:T(8,128)(2,1)} %collective-permute-done.15.refs_2_.refs_1_, ...), custom_call_target="tpu_custom_call" | custom-call | flops 4294967296 | bytes 16777216 | tf_op jit(solution)/shard_map/pallas_call | solution.py:423
  203.7 13.0 %shard_map.211 = (bf16[2048,512]{1,0:T(8,128)(2,1)}, bf16[2048,128]{1,0:T(8,128)(2,1)}, f32[1,512]{1,0:T(1,128)}) custom-call(bf16[2048,256]{1,0:T(8,128)(2,1)} %all-gather.9.cloned.1.call-done.refs_2_.refs_0_.refs_8_, bf16[2048,256]{1,0:T(8,128)(2,1)} %copy-done.31, bf16[2048,512]{1,0:T(8,128)(2,1)} %all-gather.11.cloned.1.call-done.refs_4_.refs_2_.refs_10_, ...), custom_call_target="tpu_custom_call" | custom-call | flops 5368709120 | bytes 14680064 | tf_op jit(solution)/shard_map/pallas_call | solution.py:252
  222.4 10.4 %shard_map.212 = (bf16[4,256,512]{2,1,0:T(8,128)(2,1)}, bf16[4,256,512]{2,1,0:T(8,128)(2,1)}) custom-call(s32[1]{0:T(128)} %bitcast.15.half_ref, bf16[2048,256]{1,0:T(8,128)(2,1)} %all-gather.5.cloned.1.call-done.refs_0_.refs_2_, bf16[2048,256]{1,0:T(8,128)(2,1)} %all-gather.7.cloned.1.call-done.refs_1_.refs_3_, bf16[2048,256]{1,0:T(8,128)(2,1)} %copy-done.29, ...), custom_call_target="tpu_custom_call" | custom-call | flops 4294967296 | bytes 16777216 | tf_op jit(solution)/shard_map/pallas_call | solution.py:423
  232.8 17.9 %shard_map.213 = (bf16[2048,384]{1,0:T(8,128)(2,1)}, f32[1,384]{1,0:T(1,128)}) custom-call(s32[4]{0:T(128)} %and_select_fusion.lowest_ref, bf16[2048,128]{1,0:T(8,128)(2,1)} %get-tuple-element.113.q_ref, bf16[2048,128]{1,0:T(8,128)(2,1)} %get-tuple-element.114.k_ref, bf16[2048,128]{1,0:T(8,128)(2,1)} %get-tuple-element.115.v_ref, ...), custom_call_target="tpu_custom_call" | custom-call | flops 2684354560 | bytes 4194304 | tf_op jit(solution)/shard_map/pallas_call | solution.py:675
  254.6 10.2 %collective-permute-done.20 = bf16[2048,512]{1,0:T(8,128)(2,1)S(1)} collective-permute-done((bf16[2048,512]{1,0:T(8,128)(2,1)S(1)}, bf16[2048,512]{1,0:T(8,128)(2,1)S(1)}, u32[]{:S(2)}, u32[]{:S(2)}) %collective-permute-start.20) | collective-permute-done | bytes 2097184 | tf_op jit(solution)/shard_map/ppermute | solution.py:93
  268.2 13.4 %shard_map.215 = (bf16[1024,512]{1,0:T(8,128)(2,1)}, bf16[1024,512]{1,0:T(8,128)(2,1)}, bf16[1024,512]{1,0:T(8,128)(2,1)}, bf16[1024,512]{1,0:T(8,128)(2,1)}) custom-call(bf16[2048,512]{1,0:T(8,128)(2,1)} %get-tuple-element.135.refs_4_.refs_0_, bf16[2048,384]{1,0:T(8,128)(2,1)} %get-tuple-element.154.refs_1_.refs_0_, bf16[2048,512]{1,0:T(8,128)(2,1)} %copy-done.28, ...), custom_call_target="tpu_custom_call" | custom-call | flops 7516192768 | bytes 11534336 | tf_op jit(solution)/shard_map/pallas_call | solution.py:343
  282.2 24.0 %collective-permute-done.30 = bf16[1024,512]{1,0:T(8,128)(2,1)S(1)} collective-permute-done((bf16[1024,512]{1,0:T(8,128)(2,1)}, bf16[1024,512]{1,0:T(8,128)(2,1)S(1)}, u32[]{:S(2)}, u32[]{:S(2)}) %collective-permute-start.30) | collective-permute-done | bytes 1048608 | tf_op jit(solution)/shard_map/ppermute | solution.py:93
  309.5 23.2 %collective-permute-done.31 = bf16[1024,512]{1,0:T(8,128)(2,1)S(1)} collective-permute-done((bf16[1024,512]{1,0:T(8,128)(2,1)}, bf16[1024,512]{1,0:T(8,128)(2,1)S(1)}, u32[]{:S(2)}, u32[]{:S(2)}) %collective-permute-start.31) | collective-permute-done | bytes 1048608 | tf_op jit(solution)/shard_map/ppermute | solution.py:93
  335.5 22.0 %collective-permute-done.37.received_ref = bf16[4,256,512]{2,1,0:T(8,128)(2,1)S(1)} collective-permute-done((bf16[4,256,512]{2,1,0:T(8,128)(2,1)}, bf16[4,256,512]{2,1,0:T(8,128)(2,1)S(1)}, u32[]{:S(2)}, u32[]{:S(2)}) %collective-permute-start.37) | collective-permute-done | bytes 1048608 | tf_op jit(solution)/shard_map/ppermute | solution.py:93
  358.9 9.9 %collective-permute-done.38.refs_2_ = bf16[2,256,512]{2,1,0:T(8,128)(2,1)S(1)} collective-permute-done((bf16[2,256,512]{2,1,0:T(8,128)(2,1)S(1)}, bf16[2,256,512]{2,1,0:T(8,128)(2,1)S(1)}, u32[]{:S(2)}, u32[]{:S(2)}) %collective-permute-start.38) | collective-permute-done | bytes 524320 | tf_op jit(solution)/shard_map/ppermute | solution.py:93
  371.0 12.8 %shard_map.216 = (bf16[4,512,256]{2,1,0:T(8,128)(2,1)}, bf16[4,512,256]{2,1,0:T(8,128)(2,1)}) custom-call(s32[1]{0:T(128)} %bitcast.15.half_ref, bf16[2048,384]{1,0:T(8,128)(2,1)} %get-tuple-element.154.refs_1_.refs_0_, bf16[2048,384]{1,0:T(8,128)(2,1)} %collective-permute-done.28.refs_3_.refs_1_, ...), custom_call_target="tpu_custom_call" | custom-call | flops 4294967296 | bytes 16777216 | tf_op jit(solution)/shard_map/pallas_call | solution.py:423
  387.6 19.5 %collective-permute-done.40.received_ref = bf16[4,512,256]{2,1,0:T(8,128)(2,1)S(1)} collective-permute-done((bf16[4,512,256]{2,1,0:T(8,128)(2,1)}, bf16[4,512,256]{2,1,0:T(8,128)(2,1)S(1)}, u32[]{:S(2)}, u32[]{:S(2)}) %collective-permute-start.40) | collective-permute-done | bytes 1048608 | tf_op jit(solution)/shard_map/ppermute | solution.py:93
  411.2 9.2 %collective-permute-done.43.refs_2_ = bf16[2,256,512]{2,1,0:T(8,128)(2,1)S(1)} collective-permute-done((bf16[2,256,512]{2,1,0:T(8,128)(2,1)}, bf16[2,256,512]{2,1,0:T(8,128)(2,1)S(1)}, u32[]{:S(2)}, u32[]{:S(2)}) %collective-permute-start.43) | collective-permute-done | bytes 524320 | tf_op jit(solution)/shard_map/ppermute | solution.py:93
  447.3 5.2 %collective-permute-done.47 = f32[1,896]{1,0:T(1,128)S(1)} collective-permute-done((f32[1,896]{1,0:T(1,128)S(1)}, f32[1,896]{1,0:T(1,128)S(1)}, u32[]{:S(2)}, u32[]{:S(2)}) %collective-permute-start.47) | collective-permute-done | bytes 3616 | tf_op jit(solution)/shard_map/ppermute | solution.py:93
  (234 shorter events, 146.3 us)
Async XLA Ops:
  7.2 41.8 %all-gather.5.cloned.1.call-start = ((), (), s32[]{:S(2)}) async-start(), calls=%async_computation.3 | async-start | bytes 1310720 | tf_op jit(solution)/shard_map/all_gather | solution.py:749
  16.7 59.4 %all-gather.7.cloned.1.call-start = ((), (), s32[]{:S(2)}) async-start(), calls=%async_computation.4 | async-start | bytes 1310720 | tf_op jit(solution)/shard_map/all_gather | solution.py:750
  17.5 116.2 %all-gather.11.cloned.1.call-start = ((), (), s32[]{:S(2)}) async-start(), calls=%async_computation.7 | async-start | bytes 2621440 | tf_op jit(solution)/shard_map/all_gather | solution.py:758
  49.0 27.2 %collective-permute-start.5 = (bf16[2048,256]{1,0:T(8,128)(2,1)}, bf16[2048,256]{1,0:T(8,128)(2,1)S(1)}, u32[]{:S(2)}, u32[]{:S(2)}) collective-permute-start(bf16[2048,256]{1,0:T(8,128)(2,1)} %all-gather.5.cloned.1.call-done.refs_0_.refs_2_), channel_id=1, source_target_pairs={{0,2},{1,3},{2,0},{3,1},{4,6},{5,7},{6,4},{7,5},{8,10},{9,11},{10,... | collective-permute-start | bytes 3145736 | tf_op jit(solution)/shard_map/ppermute | solution.py:93
  51.3 100.9 %all-gather.9.cloned.1.call-start = ((), (), s32[]{:S(2)}) async-start(), calls=%async_computation.5 | async-start | bytes 1310720 | tf_op jit(solution)/shard_map/all_gather | solution.py:757
  76.2 24.7 %collective-permute-start.6 = (bf16[2048,256]{1,0:T(8,128)(2,1)}, bf16[2048,256]{1,0:T(8,128)(2,1)}, u32[]{:S(2)}, u32[]{:S(2)}) collective-permute-start(bf16[2048,256]{1,0:T(8,128)(2,1)} %all-gather.7.cloned.1.call-done.refs_1_.refs_3_), channel_id=1, source_target_pairs={{0,2},{1,3},{2,0},{3,1},{4,6},{5,7},{6,4},{7,5},{8,10},{9,11},{10,... | collective-permute-start | bytes 3145736 | tf_op jit(solution)/shard_map/ppermute | solution.py:93
  79.5 30.1 %collective-permute-start.13 = (bf16[512,896]{1,0:T(8,128)(2,1)}, bf16[512,896]{1,0:T(8,128)(2,1)}, u32[]{:S(2)}, u32[]{:S(2)}) collective-permute-start(bf16[512,896]{1,0:T(8,128)(2,1)} %get-tuple-element.109.refs_5_), channel_id=1, source_target_pairs={{0,1},{1,0},{2,3},{3,2},{4,5},{5,4},{6,7},{7,6},{8,9},{9,8},{10,11... | collective-permute-start | bytes 2752520 | tf_op jit(solution)/shard_map/ppermute | solution.py:93
  110.2 311.5 %reduce-scatter.6.cloned.1.call-start = ((), (), s32[]{:S(2)}) async-start(), calls=%async_computation.8 | async-start | bytes 1310720 | tf_op jit(solution)/shard_map/reduce_scatter | solution.py:847
  128.3 51.8 %collective-permute-start.15 = (bf16[2048,512]{1,0:T(8,128)(2,1)}, bf16[2048,512]{1,0:T(8,128)(2,1)}, u32[]{:S(2)}, u32[]{:S(2)}) collective-permute-start(bf16[2048,512]{1,0:T(8,128)(2,1)} %get-tuple-element.111.refs_0_), channel_id=1, source_target_pairs={{0,1},{1,0},{2,3},{3,2},{4,5},{5,4},{6,7},{7,6},{8,9},{9,8},{10,11... | collective-permute-start | bytes 6291464 | tf_op jit(solution)/shard_map/ppermute | solution.py:93
  133.7 67.9 %collective-permute-start.23 = (bf16[2048,512]{1,0:T(8,128)(2,1)}, bf16[2048,512]{1,0:T(8,128)(2,1)}, u32[]{:S(2)}, u32[]{:S(2)}) collective-permute-start(bf16[2048,512]{1,0:T(8,128)(2,1)} %all-gather.11.cloned.1.call-done.refs_4_.refs_2_.refs_10_), channel_id=1, source_target_pairs={{0,1},{1,0},{2,3},{3,2},{4,5},{5,4},{6,7},{7,6},{8,9},{9,8},{10,11... | collective-permute-start | bytes 6291464 | tf_op jit(solution)/shard_map/ppermute | solution.py:93
  152.2 24.6 %collective-permute-start.19 = (bf16[2048,256]{1,0:T(8,128)(2,1)}, bf16[2048,256]{1,0:T(8,128)(2,1)S(1)}, u32[]{:S(2)}, u32[]{:S(2)}) collective-permute-start(bf16[2048,256]{1,0:T(8,128)(2,1)} %all-gather.9.cloned.1.call-done.refs_2_.refs_0_.refs_8_), channel_id=1, source_target_pairs={{0,2},{1,3},{2,0},{3,1},{4,6},{5,7},{6,4},{7,5},{8,10},{9,11},{10,... | collective-permute-start | bytes 3145736 | tf_op jit(solution)/shard_map/ppermute | solution.py:93
  170.0 31.5 %collective-permute-start.21 = (bf16[2048,256]{1,0:T(8,128)(2,1)S(1)}, bf16[2048,256]{1,0:T(8,128)(2,1)S(1)}, u32[]{:S(2)}, u32[]{:S(2)}) collective-permute-start(bf16[2048,256]{1,0:T(8,128)(2,1)S(1)} %copy-done.30), channel_id=1, source_target_pairs={{0,1},{1,0},{2,3},{3,2},{4,5},{5,4},{6,7},{7,6},{8,9},{9,8},{10,11... | collective-permute-start | bytes 3145736 | tf_op jit(solution)/shard_map/ppermute | solution.py:93
  176.8 24.7 %collective-permute-start.22 = (bf16[2048,256]{1,0:T(8,128)(2,1)S(1)}, bf16[2048,256]{1,0:T(8,128)(2,1)S(1)}, u32[]{:S(2)}, u32[]{:S(2)}) collective-permute-start(bf16[2048,256]{1,0:T(8,128)(2,1)S(1)} %collective-permute-done.19.refs_3_.refs_1_.refs_9_), channel_id=1, source_target_pairs={{0,1},{1,0},{2,3},{3,2},{4,5},{5,4},{6,7},{7,6},{8,9},{9,8},{10,11... | collective-permute-start | bytes 3145736 | tf_op jit(solution)/shard_map/ppermute | solution.py:93
  179.9 21.6 %collective-permute-start.24 = (bf16[640,512]{1,0:T(8,128)(2,1)}, bf16[640,512]{1,0:T(8,128)(2,1)S(1)}, u32[]{:S(2)}, u32[]{:S(2)}) collective-permute-start(bf16[640,512]{1,0:T(8,128)(2,1)} %get-tuple-element.119.refs_5_), channel_id=1, source_target_pairs={{0,1},{1,0},{2,3},{3,2},{4,5},{5,4},{6,7},{7,6},{8,9},{9,8},{10,11... | collective-permute-start | bytes 1966088 | tf_op jit(solution)/shard_map/ppermute | solution.py:93
  216.8 47.9 %collective-permute-start.20 = (bf16[2048,512]{1,0:T(8,128)(2,1)S(1)}, bf16[2048,512]{1,0:T(8,128)(2,1)S(1)}, u32[]{:S(2)}, u32[]{:S(2)}) collective-permute-start(bf16[2048,512]{1,0:T(8,128)(2,1)S(1)} %copy-done.27), channel_id=1, source_target_pairs={{0,2},{1,3},{2,0},{3,1},{4,6},{5,7},{6,4},{7,5},{8,10},{9,11},{10,... | collective-permute-start | bytes 6291464 | tf_op jit(solution)/shard_map/ppermute | solution.py:93
  218.3 32.7 %collective-permute-start.27 = (bf16[4,256,512]{2,1,0:T(8,128)(2,1)}, bf16[4,256,512]{2,1,0:T(8,128)(2,1)S(1)}, u32[]{:S(2)}, u32[]{:S(2)}) collective-permute-start(bf16[4,256,512]{2,1,0:T(8,128)(2,1)} %get-tuple-element.143), channel_id=1, source_target_pairs={{0,16},{16,0},{1,17},{17,1},{2,18},{18,2},{3,19},{19,3},{4,20},{20... | collective-permute-start | bytes 3145736 | tf_op jit(solution)/shard_map/ppermute | solution.py:93
  281.6 24.6 %collective-permute-start.30 = (bf16[1024,512]{1,0:T(8,128)(2,1)}, bf16[1024,512]{1,0:T(8,128)(2,1)S(1)}, u32[]{:S(2)}, u32[]{:S(2)}) collective-permute-start(bf16[1024,512]{1,0:T(8,128)(2,1)} %get-tuple-element.150), channel_id=1, source_target_pairs={{0,2},{1,3},{2,0},{3,1},{4,6},{5,7},{6,4},{7,5},{8,10},{9,11},{10,... | collective-permute-start | bytes 3145736 | tf_op jit(solution)/shard_map/ppermute | solution.py:93
  308.8 112.9 %reduce-scatter.8.cloned.1.call-start = ((), (), s32[]{:S(2)}) async-start(), calls=%async_computation.9 | async-start | bytes 1310720 | tf_op jit(solution)/shard_map/reduce_scatter | solution.py:850
  308.9 23.8 %collective-permute-start.31 = (bf16[1024,512]{1,0:T(8,128)(2,1)}, bf16[1024,512]{1,0:T(8,128)(2,1)S(1)}, u32[]{:S(2)}, u32[]{:S(2)}) collective-permute-start(bf16[1024,512]{1,0:T(8,128)(2,1)} %get-tuple-element.153), channel_id=1, source_target_pairs={{0,2},{1,3},{2,0},{3,1},{4,6},{5,7},{6,4},{7,5},{8,10},{9,11},{10,... | collective-permute-start | bytes 3145736 | tf_op jit(solution)/shard_map/ppermute | solution.py:93
  334.0 98.6 %reduce-scatter.4.cloned.1.call-start = ((), (), s32[]{:S(2)}) async-start(), calls=%async_computation.6 | async-start | bytes 2621440 | tf_op jit(solution)/shard_map/reduce_scatter | solution.py:823
  334.0 23.5 %collective-permute-start.37 = (bf16[4,256,512]{2,1,0:T(8,128)(2,1)}, bf16[4,256,512]{2,1,0:T(8,128)(2,1)S(1)}, u32[]{:S(2)}, u32[]{:S(2)}) collective-permute-start(bf16[4,256,512]{2,1,0:T(8,128)(2,1)} %get-tuple-element.158), channel_id=1, source_target_pairs={{0,16},{16,0},{1,17},{17,1},{2,18},{18,2},{3,19},{19,3},{4,20},{20... | collective-permute-start | bytes 3145736 | tf_op jit(solution)/shard_map/ppermute | solution.py:93
  383.8 23.3 %collective-permute-start.40 = (bf16[4,512,256]{2,1,0:T(8,128)(2,1)}, bf16[4,512,256]{2,1,0:T(8,128)(2,1)S(1)}, u32[]{:S(2)}, u32[]{:S(2)}) collective-permute-start(bf16[4,512,256]{2,1,0:T(8,128)(2,1)} %get-tuple-element.161), channel_id=1, source_target_pairs={{0,16},{16,0},{1,17},{17,1},{2,18},{18,2},{3,19},{19,3},{4,20},{20... | collective-permute-start | bytes 3145736 | tf_op jit(solution)/shard_map/ppermute | solution.py:93
  441.4 22.4 %collective-permute-start.46 = (bf16[2,512,256]{2,1,0:T(8,128)(2,1)S(1)}, bf16[2,512,256]{2,1,0:T(8,128)(2,1)S(1)}, u32[]{:S(2)}, u32[]{:S(2)}) collective-permute-start(bf16[2,512,256]{2,1,0:T(8,128)(2,1)S(1)} %collective-permute-done.42.refs_1_), channel_id=1, source_target_pairs={{0,16},{16,0},{1,17},{17,1},{2,18},{18,2},{3,19},{19,3},{4,20},{20... | collective-permute-start | bytes 1572872 | tf_op jit(solution)/shard_map/ppermute | solution.py:93
  452.5 21.7 %collective-permute-start.36 = (f32[3,512]{1,0:T(4,128)S(1)}, f32[3,512]{1,0:T(4,128)S(1)}, u32[]{:S(2)}, u32[]{:S(2)}) collective-permute-start(f32[3,512]{1,0:T(4,128)S(1)} %fusion.30), channel_id=1, source_target_pairs={{0,16},{16,0},{1,17},{17,1},{2,18},{18,2},{3,19},{19,3},{4,20},{20... | collective-permute-start | bytes 18440 | tf_op jit(solution)/shard_map/ppermute | solution.py:93
  (68 other events, 1096.2 us)
Sparse Core Ops, SparseCore 0:
  16.9 29.7 all-gather.4
  48.8 27.3 all-gather.6
  78.3 45.0 all-gather.10
  125.4 26.7 all-gather.8
  309.0 26.2 reduce-scatter.5
  338.0 25.7 reduce-scatter.7
  366.7 42.1 reduce-scatter.3

commit v4 on v3

--- a/solution.py
+++ b/solution.py
@@ -144,9 +144,9 @@
     small = out_weight.shape[0] // 4
 
     def kernel(places_ref, *refs):
-        for place in range(3):
-            refs[6 + place][:tall] = refs[place][...]
-            refs[6 + place][tall:] = refs[3 + place][...]
+        for place in range(4):
+            refs[8 + place][:tall] = refs[place][...]
+            refs[8 + place][tall:] = refs[4 + place][...]
 
     def at(place):
         return lambda step, s: (s[place], 0)
@@ -158,14 +158,14 @@
         grid_spec=pltpu.PrefetchScalarGridSpec(
             num_scalar_prefetch=1,
             grid=(1,),
-            in_specs=[pl.BlockSpec((tall, cols), at(i)) for i in range(3)]
-            + [pl.BlockSpec((small, cols), at(i)) for i in range(3)],
-            out_specs=[whole] * 3,
-        ),
-        out_shape=[shape] * 3,
+            in_specs=[pl.BlockSpec((tall, cols), at(i)) for i in (0, 1, 3, 4)]
+            + [pl.BlockSpec((small, cols), at(i)) for i in (0, 1, 3, 4)],
+            out_specs=[whole] * 4,
+        ),
+        out_shape=[shape] * 4,
         compiler_params=params(),
         cost_estimate=cost(0, 3 * 4 * cols * (tall + small)),
-    )(places, fc2_weight, fc2_weight, fc2_weight, out_weight, out_weight, out_weight)
+    )(places, *[fc2_weight] * 4, *[out_weight] * 4)
 
 
 def forward_step(xs, ws, fc1_bias, qkv_bias, tables):
@@ -314,19 +314,21 @@
     shares = 2 if part else 1
 
     def kernel(*refs):
-        values = [[refs[0][...], refs[1][...]], [refs[2][...], refs[3][...]]]
+        hidden_vals = [refs[0][...], refs[2][...]]
+        pair_vals = jnp.concatenate([refs[1][...], refs[3][...]], axis=1)
         outs = refs[8:]
         for place in range(2):
-            total = None
-            for side in range(2):
-                w = refs[4 + 2 * place + side]
-                if transposed:
-                    add = mul(values[side][0], w[:, :hidden], NT) + mul(
-                        values[side][1], w[:, hidden:], NT
-                    )
-                else:
-                    add = mul(values[side][0], w[:hidden]) + mul(values[side][1], w[hidden:])
-                total = add if total is None else total + add
+            mats = refs[4 + 2 * place : 6 + 2 * place]
+            if transposed:
+                small = jnp.concatenate([w[:, hidden:] for w in mats], axis=1)
+                total = mul(pair_vals, small, NT)
+                for value, w in zip(hidden_vals, mats):
+                    total = total + mul(value, w[:, :hidden], NT)
+            else:
+                small = jnp.concatenate([w[hidden:] for w in mats], axis=0)
+                total = mul(pair_vals, small)
+                for value, w in zip(hidden_vals, mats):
+                    total = total + mul(value, w[:hidden])
             total = total.astype(bf16)
             if part:
                 cut = part // 2
@@ -722,7 +724,9 @@
 
     half = (dp_index & 1).astype(jnp.int32)
     far_block = (1 - (col_index >> 1)) * 2 + half
-    packs = jnp.stack([col_index, col_index ^ 1, far_block]).astype(jnp.int32)
+    packs = jnp.stack(
+        [col_index, col_index ^ 1, far_block, col_index ^ 2, col_index ^ 3]
+    ).astype(jnp.int32)
     places = jnp.stack([col_index, col_index ^ 1, col_index ^ 2, col_index ^ 3, half]).astype(
         jnp.int32
     )
@@ -753,7 +757,7 @@
     fc1_second = swap_bits(fc1_first, DP, 1)
     tail = out_grad[:, cut:]
     tail_far = swap_bits(after(tail, qkv_first), COL, 2)
-    out_own, out_near, out_far = pack_out(packs, fc2_weight, after(out_weight, in_own))
+    out_own, out_near, out_far, out_cross = pack_out(packs, fc2_weight, after(out_weight, in_own))
     cot_0 = lax.all_gather(after(out_grad[:, :cut], normed), ROW, axis=0, tiled=True)
     cot_b = lax.all_gather(
         jnp.concatenate([tail, tail_far], axis=1), ROW, axis=0, tiled=True
@@ -773,7 +777,7 @@
     in_3 = swap_bits(in_pass, COL, 1)
     normed_1 = [swap_bits(normed_0a, COL, 1), swap_bits(normed_0b, COL, 1)]
     normed_2b = swap_bits(after(normed_0b, normed_2a), COL, 2)
-    out_first = swap_bits(after(out_far, normed_2b), COL, 2)
+    out_2 = swap_bits(after(out_far, normed_2b), COL, 2)
     normed_3 = [swap_bits(normed_2a, COL, 1), swap_bits(normed_2b, COL, 1)]
     normed_all = [normed_0a, normed_0b, normed_2a, normed_2b]
     up_pre, act, q_rot, k_rot, v_low = forward_step(
@@ -783,13 +787,12 @@
         qkv_bias.reshape(1, -1),
         tables,
     )
-    cot_2 = swap_bits(after(cot_0, out_first, act), COL, 2)
-    out_second = swap_bits(after(out_first, qkv_second), DP, 1)
-    out_2, out_pass = pick(after(same, act), [out_first], [out_second], 0)
-    out_3 = swap_bits(out_pass, COL, 1)
+    out_pass = swap_bits(after(out_cross, act, out_2), COL, 2)
     act_1 = swap_bits(act, COL, 1)
     attn, attn_full, lse = attend(lowest, after(q_rot, act), k_rot, v_low, begin)
     attn_1 = swap_bits(attn, COL, 1)
+    out_3 = swap_bits(out_pass, COL, 1)
+    cot_2 = swap_bits(after(cot_0, out_pass, attn), COL, 2)
     cots = [cot_0, cot_2, cot_b]
     cots_1 = [swap_bits(cot_0, COL, 1), swap_bits(cot_2, COL, 1), swap_bits(cot_b, COL, 1)]
     mix_near, mix_far = spread(
@@ -799,7 +802,7 @@
     fc2_keep, fc2_send = grad_blocks(
         half, [([act, after(act_1, mix_far)], cots, True)], False
     )
-    fc2_recv = swap_bits(after(fc2_send, out_second), DP, 1)
+    fc2_recv = swap_bits(after(fc2_send, qkv_second), DP, 1)
     d_up, d_attn, fc1_sums = slope_step(
         cots + cots_1, [out_own, out_2, out_1, out_3], after(up_pre, fc2_send)
     )
@@ -812,17 +815,15 @@
             far = (far.astype(f32) + swap_bits(far, DP, bit).astype(f32)).astype(bf16)
         return near, far
 
-    fc1_keep, fc1_send = grad_blocks(half, [(normed_all, [d_up, d_up_1], False)], False)
-    fc1_recv = swap_bits(after(fc1_send, fc2_recv), DP, 1)
     d_proj, qkv_sums = attend_back(
-        lowest, q_rot, k_rot, v_low, begin, after(d_attn, fc1_send), attn_full, lse, tables
+        lowest, q_rot, k_rot, v_low, begin, d_attn, attn_full, lse, tables
     )
     d_proj_1 = swap_bits(d_proj, COL, 1)
     fc2_near, fc2_far = sum_halves(fc2_keep, after(fc2_recv, d_proj))
     mix_total = (mix_near.astype(f32) + mix_recv.astype(f32)).astype(bf16)
     mixed = lax.psum_scatter(mix_total, ROW, scatter_dimension=0, tiled=True).astype(f32)
     fc2_crossed = swap_bits(after(fc2_far, mix_total), COL, 2)
-    fc2_near_x = swap_bits(after(fc2_near, fc1_recv), DP, 1)
+    fc2_near_x = swap_bits(fc2_near, DP, 1)
     near_a, near_b, far_a, far_b = spread(
         [[d_up, after(d_proj, fc2_far)], [d_up_1, d_proj_1]],
         [in_own, in_near],
@@ -831,21 +832,27 @@
         local_rows,
     )
     recv_a = swap_bits(after(far_a, fc2_crossed), COL, 2)
-    recv_b = swap_bits(after(far_b, recv_a), COL, 2)
     fc2_crossed_x = swap_bits(after(fc2_crossed, fc2_near_x), DP, 1)
+    fc1_keep, fc1_send = grad_blocks(
+        half, [(normed_all, [after(d_up, far_a), d_up_1], False)], False
+    )
+    fc1_recv = swap_bits(after(fc1_send, fc2_crossed_x), DP, 1)
     rest_keep, rest_send = grad_blocks(
         half,
         [
-            ([after(d_proj, far_a), d_proj_1], normed_all, True),
+            ([after(d_proj, fc1_send), d_proj_1], normed_all, True),
             ([attn, attn_1], cots, True),
         ],
         True,
     )
-    rest_recv = swap_bits(after(rest_send, fc2_crossed_x), DP, 1)
-    fc1_near, fc1_far = sum_halves(fc1_keep, after(fc1_recv, rest_send))
+    recv_b = swap_bits(after(far_b, recv_a), COL, 2)
     total_a = (near_a.astype(f32) + recv_a.astype(f32)).astype(bf16)
     d_normed_a = lax.psum_scatter(total_a, ROW, scatter_dimension=0, tiled=True)
-    (fc2_weight_grad,) = lay_out(places, [fc2_near, fc2_crossed], [fc2_near_x, fc2_crossed_x], 0)
+    (fc2_weight_grad,) = lay_out(
+        places, [fc2_near, after(fc2_crossed, rest_send)], [fc2_near_x, fc2_crossed_x], 0
+    )
+    fc1_near, fc1_far = sum_halves(fc1_keep, after(fc1_recv, rest_send))
+    rest_recv = swap_bits(after(rest_send, fc1_recv), DP, 1)
     total_b = (near_b.astype(f32) + recv_b.astype(f32)).astype(bf16)
     d_normed_b = lax.psum_scatter(total_b, ROW, scatter_dimension=0, tiled=True)
     fc1_near_x = swap_bits(after(fc1_near, rest_recv), DP, 1)
@@ -853,13 +860,13 @@
     rest_near, rest_far = sum_halves(rest_keep, after(rest_recv, total_b))
     rest_near_x = swap_bits(after(rest_near, fc1_near_x), DP, 1)
     rest_crossed = swap_bits(after(rest_far, fc1_crossed), COL, 2)
-    fc1_crossed_x = swap_bits(after(fc1_crossed, rest_near_x), DP, 1)
-    rest_crossed_x = swap_bits(after(rest_crossed, fc1_crossed_x), DP, 1)
+    rest_crossed_x = swap_bits(after(rest_crossed, rest_near_x), DP, 1)
+    fc1_crossed_x = swap_bits(after(fc1_crossed, rest_crossed_x), DP, 1)
     d_normed = jnp.concatenate([d_normed_a, d_normed_b], axis=0).astype(f32)
-    (fc1_weight_grad,) = lay_out(places, [fc1_near, fc1_crossed], [fc1_near_x, fc1_crossed_x], 1)
     qkv_weight_grad, out_weight_grad = lay_out(
         places, [rest_near, rest_crossed], [rest_near_x, rest_crossed_x], 2
     )
+    (fc1_weight_grad,) = lay_out(places, [fc1_near, fc1_crossed], [fc1_near_x, fc1_crossed_x], 1)
 
     out = (token_f + mixed + out_bias).astype(bf16)
     d_hat = d_normed * ln_gain

time: 482 us -> 447 us (0.927)
  waiting for transfers between devices: 228 us -> 203 us
  starting transfers between devices: 46.7 us -> 41.6 us
    all_gather x1, waiting for transfers between devices: 18.5 us -> 0.01 us  [step(): lax.all_gather(after(out_grad[:, :cut], normed), ROW, axis=0, tiled=True)]
    ppermute x48, waiting for transfers between devices: 183 us -> 175 us  [swap_bits(): lax.ppermute(value, axis, [(place, place ^ bit) for place in range(count)])]
    ppermute x48, starting transfers between devices: 46.4 us -> 41.3 us  [swap_bits(): lax.ppermute(value, axis, [(place, place ^ bit) for place in range(count)])]
    unnamed x77 -> x71, local copies, waits for them, and re-layouts: 9.74 us -> 9 us
  transfers between devices with their start and end apart: 55 -> 55, of which waited for: 26 -> 24; matrix products, arithmetic and copies ran while one was open for 6% -> 7% of each run, Pallas kernels for 29% -> 32%
where the time goes in v4:
time: 447 us
  waiting for transfers between devices  203 us (45%)
  Pallas kernels  146 us (33%)
  starting transfers between devices  41.6 us (9%)
  other arithmetic  21.4 us (5%)
  local copies, waits for them, and re-layouts  20.3 us (5%)
  between operations  14.6 us (3%)
    ppermute x48, waiting for transfers between devices, swap_bits(): lax.ppermute(value, axis, [(place, place ^ bit) for place in range(count)])  175 us
    ppermute x48, starting transfers between devices, swap_bits(): lax.ppermute(value, axis, [(place, place ^ bit) for place in range(count)])  41.3 us
    pallas_call x3, Pallas kernels, grad_blocks(): pl.pallas_call(kernel, grid_spec=pltpu.PrefetchScalarGridSpec(num_scalar_...  33.5 us
    all_gather x1, waiting for transfers between devices, step(): normed_0b = lax.all_gather(normed[:, cut:], ROW, axis=0, tiled=True)  26.5 us
    pallas_call x2, Pallas kernels, spread(): pl.pallas_call(kernel, grid=(rows // block,), in_specs=[rowed(hidden), ro...  21.8 us
    pallas_call x1, Pallas kernels, attend_back(): pl.pallas_call(kernel, grid_spec=pltpu.PrefetchScalarGridSpec(num_scalar_...  18.1 us
    pallas_call x1, Pallas kernels, forward_step(): pl.pallas_call(kernel, grid=(rows // block,), in_specs=[rowed(x.shape[1])...  15.6 us
    pallas_call x3, Pallas kernels, lay_out(): pl.pallas_call(kernel, grid_spec=pltpu.PrefetchScalarGridSpec(num_scalar_...  13.2 us
  transfers between devices with their start and end apart: 55, of which 24 were waited for; matrix products, arithmetic and copies ran while one was open for 7% of the time, Pallas kernels for 32%

profile of v4, /device:TPU:0, one launch (start us, length us, event | category | flops | bytes accessed | tf_op | source)
XLA Modules:
  0.0 446.8 jit_solution(2145909790815685172)
XLA Ops:
  34.6 7.2 %collective-permute-done.3.refs_1_ = bf16[512,384]{1,0:T(8,128)(2,1)S(1)} collective-permute-done((bf16[512,384]{1,0:T(8,128)(2,1)}, bf16[512,384]{1,0:T(8,128)(2,1)S(1)}, u32[]{:S(2)}, u32[]{:S(2)}) %collective-permute-start.3) | collective-permute-done | bytes 393248 | tf_op jit(solution)/shard_map/ppermute | solution.py:93
  43.2 4.9 %collective-permute-done.4 = bf16[512,256]{1,0:T(8,128)(2,1)S(1)} collective-permute-done((bf16[512,256]{1,0:T(8,128)(2,1)S(1)}, bf16[512,256]{1,0:T(8,128)(2,1)S(1)}, u32[]{:S(2)}, u32[]{:S(2)}) %collective-permute-start.4) | collective-permute-done | bytes 262176 | tf_op jit(solution)/shard_map/ppermute | solution.py:93
  49.7 26.5 %all-gather.7.cloned.1.call-done.refs_1_.refs_3_ = bf16[2048,256]{1,0:T(8,128)(2,1)} async-done(((bf16[512,256]{1,0:T(8,128)(2,1)}), bf16[2048,256]{1,0:T(8,128)(2,1)}) %all-gather.7.cloned.1.call-update) | async-done | bytes 1048592 | tf_op jit(solution)/shard_map/all_gather | solution.py:754
  79.6 11.5 %collective-permute-done.11.refs_2_ = bf16[512,512]{1,0:T(8,128)(2,1)S(1)} collective-permute-done((bf16[512,512]{1,0:T(8,128)(2,1)}, bf16[512,512]{1,0:T(8,128)(2,1)S(1)}, u32[]{:S(2)}, u32[]{:S(2)}) %collective-permute-start.11) | collective-permute-done | bytes 524320 | tf_op jit(solution)/shard_map/ppermute | solution.py:93
  94.1 6.4 %collective-permute-done.12.refs_3_ = bf16[512,384]{1,0:T(8,128)(2,1)S(1)} collective-permute-done((bf16[512,384]{1,0:T(8,128)(2,1)S(1)}, bf16[512,384]{1,0:T(8,128)(2,1)S(1)}, u32[]{:S(2)}, u32[]{:S(2)}) %collective-permute-start.12) | collective-permute-done | bytes 393248 | tf_op jit(solution)/shard_map/ppermute | solution.py:93
  100.9 5.8 %fusion = (f32[2048,128]{1,0:T(8,128)}, f32[2048,128]{1,0:T(8,128)}, f32[2048,128]{1,0:T(8,128)}) fusion(f32[128]{0:T(128)S(1)} %fusion.22, f32[2048]{0:T(1024)S(1)} %get-tuple-element.228, pred[128]{0:T(512)(128)(4,1)S(1)} %get-tuple-element.233, pred[128]{0:T(512)(128)(4,1)S(1)} %get-tuple-element.234, pred[128]{0:T(512)(128)(4,1)S(1)} %broadcast_compare_fusion.1), kind=kLoop, calls=%fused_computation.12 | loop fusion | flops 1310720 | bytes 3154816 | tf_op jit(solution)/shard_map/jit(_where)/select_n | solution.py:62
  115.8 15.6 %shard_map.205 = (f32[2048,512]{1,0:T(8,128)}, bf16[2048,512]{1,0:T(8,128)(2,1)}, bf16[2048,128]{1,0:T(8,128)(2,1)}, bf16[2048,128]{1,0:T(8,128)(2,1)}, bf16[2048,128]{1,0:T(8,128)(2,1)}) custom-call(bf16[2048,256]{1,0:T(8,128)(2,1)} %all-gather.5.cloned.1.call-done.refs_0_.refs_2_, bf16[2048,256]{1,0:T(8,128)(2,1)} %all-gather.7.cloned.1.call-done.refs_1_.refs_3_, ...), custom_call_target="tpu_custom_call" | custom-call | flops 7516192768 | bytes 18874368 | tf_op jit(solution)/shard_map/pallas_call | solution.py:201
  133.9 12.0 %shard_map.206 = (bf16[2048,128]{1,0:T(8,128)(2,1)}, f32[2048,128]{1,0:T(8,128)}, f32[2,2048]{1,0:T(2,128)}) custom-call(s32[4]{0:T(128)} %and_select_fusion.lowest_ref, bf16[2048,128]{1,0:T(8,128)(2,1)} %get-tuple-element.111.q_ref, bf16[2048,128]{1,0:T(8,128)(2,1)} %get-tuple-element.112.k_ref, bf16[2048,128]{1,0:T(8,128)(2,1)} %get-tuple-element.113.v_ref, ...), custom_call_target="tpu_custom_call" | custom-call | flops 1073741824 | bytes 3145728 | tf_op jit(solution)/shard_map/pallas_call | solution.py:572
  157.5 17.4 %collective-permute-done.19.refs_3_.refs_1_.refs_9_ = bf16[2048,256]{1,0:T(8,128)(2,1)S(1)} collective-permute-done((bf16[2048,256]{1,0:T(8,128)(2,1)}, bf16[2048,256]{1,0:T(8,128)(2,1)S(1)}, u32[]{:S(2)}, u32[]{:S(2)}) %collective-permute-start.19) | collective-permute-done | bytes 1048608 | tf_op jit(solution)/shard_map/ppermute | solution.py:93
  175.3 9.4 %shard_map.208 = (bf16[2048,512]{1,0:T(8,128)(2,1)}, bf16[2048,512]{1,0:T(8,128)(2,1)}) custom-call(bf16[2048,512]{1,0:T(8,128)(2,1)} %get-tuple-element.109.refs_0_, bf16[2048,128]{1,0:T(8,128)(2,1)} %get-tuple-element.114.refs_1_.refs_6_, bf16[2048,512]{1,0:T(8,128)(2,1)} %collective-permute-done.15.refs_2_.refs_1_, bf16[2048,128]{1,0:T(8,128)(2,1)} %copy-done.32, ...), custom_call_target="tpu_custom_call" | custom-call | flops 5368709120 | bytes 9437184 | tf_op jit(solution)/shard_map/pallas_call | solution.py:345
  185.5 10.3 %shard_map.209 = (bf16[4,256,512]{2,1,0:T(8,128)(2,1)}, bf16[4,256,512]{2,1,0:T(8,128)(2,1)}) custom-call(s32[1]{0:T(128)} %bitcast.17.half_ref, bf16[2048,512]{1,0:T(8,128)(2,1)} %get-tuple-element.109.refs_0_, bf16[2048,512]{1,0:T(8,128)(2,1)} %collective-permute-done.15.refs_2_.refs_1_, ...), custom_call_target="tpu_custom_call" | custom-call | flops 4294967296 | bytes 16777216 | tf_op jit(solution)/shard_map/pallas_call | solution.py:425
  198.4 12.9 %shard_map.210 = (bf16[2048,512]{1,0:T(8,128)(2,1)}, bf16[2048,128]{1,0:T(8,128)(2,1)}, f32[1,512]{1,0:T(1,128)}) custom-call(bf16[2048,256]{1,0:T(8,128)(2,1)} %all-gather.9.cloned.1.call-done.refs_2_.refs_0_.refs_8_, bf16[2048,256]{1,0:T(8,128)(2,1)} %copy-done.26, bf16[2048,512]{1,0:T(8,128)(2,1)} %all-gather.11.cloned.1.call-done.refs_4_.refs_2_.refs_10_, ...), custom_call_target="tpu_custom_call" | custom-call | flops 5368709120 | bytes 14680064 | tf_op jit(solution)/shard_map/pallas_call | solution.py:252
  213.0 18.1 %shard_map.211 = (bf16[2048,384]{1,0:T(8,128)(2,1)}, f32[1,384]{1,0:T(1,128)}) custom-call(s32[4]{0:T(128)} %and_select_fusion.lowest_ref, bf16[2048,128]{1,0:T(8,128)(2,1)} %get-tuple-element.111.q_ref, bf16[2048,128]{1,0:T(8,128)(2,1)} %get-tuple-element.112.k_ref, bf16[2048,128]{1,0:T(8,128)(2,1)} %get-tuple-element.113.v_ref, ...), custom_call_target="tpu_custom_call" | custom-call | flops 2684354560 | bytes 4194304 | tf_op jit(solution)/shard_map/pallas_call | solution.py:677
  231.3 5.9 %collective-permute-done.26.received_ref = bf16[4,256,512]{2,1,0:T(8,128)(2,1)S(1)} collective-permute-done((bf16[4,256,512]{2,1,0:T(8,128)(2,1)}, bf16[4,256,512]{2,1,0:T(8,128)(2,1)S(1)}, u32[]{:S(2)}, u32[]{:S(2)}) %collective-permute-start.26) | collective-permute-done | bytes 1048608 | tf_op jit(solution)/shard_map/ppermute | solution.py:93
  245.3 12.4 %shard_map.213 = (bf16[1024,512]{1,0:T(8,128)(2,1)}, bf16[1024,512]{1,0:T(8,128)(2,1)}, bf16[1024,512]{1,0:T(8,128)(2,1)}, bf16[1024,512]{1,0:T(8,128)(2,1)}) custom-call(bf16[2048,512]{1,0:T(8,128)(2,1)} %get-tuple-element.148.refs_0_.refs_4_, bf16[2048,384]{1,0:T(8,128)(2,1)} %get-tuple-element.150.refs_1_.refs_0_, ...), custom_call_target="tpu_custom_call" | custom-call | flops 7516192768 | bytes 11534336 | tf_op jit(solution)/shard_map/pallas_call | solution.py:345
  258.4 23.9 %collective-permute-done.30 = bf16[1024,512]{1,0:T(8,128)(2,1)S(1)} collective-permute-done((bf16[1024,512]{1,0:T(8,128)(2,1)}, bf16[1024,512]{1,0:T(8,128)(2,1)S(1)}, u32[]{:S(2)}, u32[]{:S(2)}) %collective-permute-start.30) | collective-permute-done | bytes 1048608 | tf_op jit(solution)/shard_map/ppermute | solution.py:93
  285.7 23.1 %collective-permute-done.31 = bf16[1024,512]{1,0:T(8,128)(2,1)S(1)} collective-permute-done((bf16[1024,512]{1,0:T(8,128)(2,1)}, bf16[1024,512]{1,0:T(8,128)(2,1)S(1)}, u32[]{:S(2)}, u32[]{:S(2)}) %collective-permute-start.31) | collective-permute-done | bytes 1048608 | tf_op jit(solution)/shard_map/ppermute | solution.py:93
  311.7 10.6 %collective-permute-done.37.refs_2_ = bf16[2,256,512]{2,1,0:T(8,128)(2,1)S(1)} collective-permute-done((bf16[2,256,512]{2,1,0:T(8,128)(2,1)S(1)}, bf16[2,256,512]{2,1,0:T(8,128)(2,1)S(1)}, u32[]{:S(2)}, u32[]{:S(2)}) %collective-permute-start.37) | collective-permute-done | bytes 524320 | tf_op jit(solution)/shard_map/ppermute | solution.py:93
  323.8 10.5 %shard_map.214 = (bf16[4,256,512]{2,1,0:T(8,128)(2,1)}, bf16[4,256,512]{2,1,0:T(8,128)(2,1)}) custom-call(s32[1]{0:T(128)} %bitcast.17.half_ref, bf16[2048,256]{1,0:T(8,128)(2,1)} %all-gather.5.cloned.1.call-done.refs_0_.refs_2_, bf16[2048,256]{1,0:T(8,128)(2,1)} %all-gather.7.cloned.1.call-done.refs_1_.refs_3_, bf16[2048,256]{1,0:T(8,128)(2,1)} %copy-done.25, ...), custom_call_target="tpu_custom_call" | custom-call | flops 4294967296 | bytes 16777216 | tf_op jit(solution)/shard_map/pallas_call | solution.py:425
  335.2 12.7 %shard_map.215 = (bf16[4,512,256]{2,1,0:T(8,128)(2,1)}, bf16[4,512,256]{2,1,0:T(8,128)(2,1)}) custom-call(s32[1]{0:T(128)} %bitcast.17.half_ref, bf16[2048,384]{1,0:T(8,128)(2,1)} %get-tuple-element.150.refs_1_.refs_0_, bf16[2048,384]{1,0:T(8,128)(2,1)} %copy-done.24, bf16[2048,256]{1,0:T(8,128)(2,1)} %all-gather.5.cloned.1.call-done.refs_0_.refs_2_, ...), custom_call_target="tpu_custom_call" | custom-call | flops 4294967296 | bytes 16777216 | tf_op jit(solution)/shard_map/pallas_call | solution.py:425
  347.9 9.5 %collective-permute-done.39.received_ref = bf16[4,256,512]{2,1,0:T(8,128)(2,1)S(1)} collective-permute-done((bf16[4,256,512]{2,1,0:T(8,128)(2,1)}, bf16[4,256,512]{2,1,0:T(8,128)(2,1)S(1)}, u32[]{:S(2)}, u32[]{:S(2)}) %collective-permute-start.39) | collective-permute-done | bytes 1048608 | tf_op jit(solution)/shard_map/ppermute | solution.py:93
  361.7 18.9 %collective-permute-done.40.received_ref = bf16[4,512,256]{2,1,0:T(8,128)(2,1)S(1)} collective-permute-done((bf16[4,512,256]{2,1,0:T(8,128)(2,1)}, bf16[4,512,256]{2,1,0:T(8,128)(2,1)S(1)}, u32[]{:S(2)}, u32[]{:S(2)}) %collective-permute-start.40) | collective-permute-done | bytes 1048608 | tf_op jit(solution)/shard_map/ppermute | solution.py:93
  384.9 8.5 %collective-permute-done.43.refs_2_ = bf16[2,256,512]{2,1,0:T(8,128)(2,1)} collective-permute-done((bf16[2,256,512]{2,1,0:T(8,128)(2,1)}, bf16[2,256,512]{2,1,0:T(8,128)(2,1)}, u32[]{:S(2)}, u32[]{:S(2)}) %collective-permute-start.43) | collective-permute-done | bytes 524320 | tf_op jit(solution)/shard_map/ppermute | solution.py:93
  397.8 7.5 %collective-permute-done.44.refs_2_ = bf16[2,512,256]{2,1,0:T(8,128)(2,1)S(1)} collective-permute-done((bf16[2,512,256]{2,1,0:T(8,128)(2,1)}, bf16[2,512,256]{2,1,0:T(8,128)(2,1)S(1)}, u32[]{:S(2)}, u32[]{:S(2)}) %collective-permute-start.44) | collective-permute-done | bytes 524320 | tf_op jit(solution)/shard_map/ppermute | solution.py:93
  (227 shorter events, 130.9 us)
Async XLA Ops:
  7.2 41.0 %all-gather.5.cloned.1.call-start = ((), (), s32[]{:S(2)}) async-start(), calls=%async_computation.3 | async-start | bytes 1310720 | tf_op jit(solution)/shard_map/all_gather | solution.py:753
  16.7 59.4 %all-gather.7.cloned.1.call-start = ((), (), s32[]{:S(2)}) async-start(), calls=%async_computation.4 | async-start | bytes 1310720 | tf_op jit(solution)/shard_map/all_gather | solution.py:754
  20.7 125.1 %all-gather.9.cloned.1.call-start = ((), (), s32[]{:S(2)}) async-start(), calls=%async_computation.5 | async-start | bytes 1310720 | tf_op jit(solution)/shard_map/all_gather | solution.py:761
  48.2 28.0 %collective-permute-start.5 = (bf16[2048,256]{1,0:T(8,128)(2,1)}, bf16[2048,256]{1,0:T(8,128)(2,1)S(1)}, u32[]{:S(2)}, u32[]{:S(2)}) collective-permute-start(bf16[2048,256]{1,0:T(8,128)(2,1)} %all-gather.5.cloned.1.call-done.refs_0_.refs_2_), channel_id=1, source_target_pairs={{0,2},{1,3},{2,0},{3,1},{4,6},{5,7},{6,4},{7,5},{8,10},{9,11},{10,... | collective-permute-start | bytes 3145736 | tf_op jit(solution)/shard_map/ppermute | solution.py:93
  49.6 102.6 %all-gather.11.cloned.1.call-start = ((), (), s32[]{:S(2)}) async-start(), calls=%async_computation.7 | async-start | bytes 2621440 | tf_op jit(solution)/shard_map/all_gather | solution.py:762
  76.2 24.7 %collective-permute-start.6 = (bf16[2048,256]{1,0:T(8,128)(2,1)}, bf16[2048,256]{1,0:T(8,128)(2,1)}, u32[]{:S(2)}, u32[]{:S(2)}) collective-permute-start(bf16[2048,256]{1,0:T(8,128)(2,1)} %all-gather.7.cloned.1.call-done.refs_1_.refs_3_), channel_id=1, source_target_pairs={{0,2},{1,3},{2,0},{3,1},{4,6},{5,7},{6,4},{7,5},{8,10},{9,11},{10,... | collective-permute-start | bytes 3145736 | tf_op jit(solution)/shard_map/ppermute | solution.py:93
  79.5 30.2 %collective-permute-start.13 = (bf16[512,896]{1,0:T(8,128)(2,1)}, bf16[512,896]{1,0:T(8,128)(2,1)}, u32[]{:S(2)}, u32[]{:S(2)}) collective-permute-start(bf16[512,896]{1,0:T(8,128)(2,1)} %get-tuple-element.107.refs_5_), channel_id=1, source_target_pairs={{0,1},{1,0},{2,3},{3,2},{4,5},{5,4},{6,7},{7,6},{8,9},{9,8},{10,11... | collective-permute-start | bytes 2752520 | tf_op jit(solution)/shard_map/ppermute | solution.py:93
  93.4 300.7 %reduce-scatter.6.cloned.1.call-start = ((), (), s32[]{:S(2)}) async-start(), calls=%async_computation.8 | async-start | bytes 1310720 | tf_op jit(solution)/shard_map/reduce_scatter | solution.py:850
  93.5 22.2 %collective-permute-start.7 = (bf16[2048,256]{1,0:T(8,128)(2,1)}, bf16[2048,256]{1,0:T(8,128)(2,1)}, u32[]{:S(2)}, u32[]{:S(2)}) collective-permute-start(bf16[2048,256]{1,0:T(8,128)(2,1)} %all-gather.5.cloned.1.call-done.refs_0_.refs_2_), channel_id=1, source_target_pairs={{0,1},{1,0},{2,3},{3,2},{4,5},{5,4},{6,7},{7,6},{8,9},{9,8},{10,11... | collective-permute-start | bytes 3145736 | tf_op jit(solution)/shard_map/ppermute | solution.py:93
  131.4 43.4 %collective-permute-start.15 = (bf16[2048,512]{1,0:T(8,128)(2,1)}, bf16[2048,512]{1,0:T(8,128)(2,1)}, u32[]{:S(2)}, u32[]{:S(2)}) collective-permute-start(bf16[2048,512]{1,0:T(8,128)(2,1)} %get-tuple-element.109.refs_0_), channel_id=1, source_target_pairs={{0,1},{1,0},{2,3},{3,2},{4,5},{5,4},{6,7},{7,6},{8,9},{9,8},{10,11... | collective-permute-start | bytes 6291464 | tf_op jit(solution)/shard_map/ppermute | solution.py:93
  149.8 25.0 %collective-permute-start.19 = (bf16[2048,256]{1,0:T(8,128)(2,1)}, bf16[2048,256]{1,0:T(8,128)(2,1)S(1)}, u32[]{:S(2)}, u32[]{:S(2)}) collective-permute-start(bf16[2048,256]{1,0:T(8,128)(2,1)} %all-gather.9.cloned.1.call-done.refs_2_.refs_0_.refs_8_), channel_id=1, source_target_pairs={{0,2},{1,3},{2,0},{3,1},{4,6},{5,7},{6,4},{7,5},{8,10},{9,11},{10,... | collective-permute-start | bytes 3145736 | tf_op jit(solution)/shard_map/ppermute | solution.py:93
  152.2 43.6 %collective-permute-start.23 = (bf16[2048,512]{1,0:T(8,128)(2,1)}, bf16[2048,512]{1,0:T(8,128)(2,1)S(1)}, u32[]{:S(2)}, u32[]{:S(2)}) collective-permute-start(bf16[2048,512]{1,0:T(8,128)(2,1)} %all-gather.11.cloned.1.call-done.refs_4_.refs_2_.refs_10_), channel_id=1, source_target_pairs={{0,1},{1,0},{2,3},{3,2},{4,5},{5,4},{6,7},{7,6},{8,9},{9,8},{10,11... | collective-permute-start | bytes 6291464 | tf_op jit(solution)/shard_map/ppermute | solution.py:93
  152.7 32.1 %collective-permute-start.24 = (bf16[640,512]{1,0:T(8,128)(2,1)}, bf16[640,512]{1,0:T(8,128)(2,1)}, u32[]{:S(2)}, u32[]{:S(2)}) collective-permute-start(bf16[640,512]{1,0:T(8,128)(2,1)} %get-tuple-element.117.refs_5_), channel_id=1, source_target_pairs={{0,1},{1,0},{2,3},{3,2},{4,5},{5,4},{6,7},{7,6},{8,9},{9,8},{10,11... | collective-permute-start | bytes 1966088 | tf_op jit(solution)/shard_map/ppermute | solution.py:93
  157.3 38.5 %collective-permute-start.21 = (bf16[2048,256]{1,0:T(8,128)(2,1)}, bf16[2048,256]{1,0:T(8,128)(2,1)S(1)}, u32[]{:S(2)}, u32[]{:S(2)}) collective-permute-start(bf16[2048,256]{1,0:T(8,128)(2,1)} %all-gather.9.cloned.1.call-done.refs_2_.refs_0_.refs_8_), channel_id=1, source_target_pairs={{0,1},{1,0},{2,3},{3,2},{4,5},{5,4},{6,7},{7,6},{8,9},{9,8},{10,11... | collective-permute-start | bytes 3145736 | tf_op jit(solution)/shard_map/ppermute | solution.py:93
  184.8 56.1 %collective-permute-start.20 = (bf16[2048,512]{1,0:T(8,128)(2,1)}, bf16[2048,512]{1,0:T(8,128)(2,1)S(1)}, u32[]{:S(2)}, u32[]{:S(2)}) collective-permute-start(bf16[2048,512]{1,0:T(8,128)(2,1)} %get-tuple-element.126), channel_id=1, source_target_pairs={{0,2},{1,3},{2,0},{3,1},{4,6},{5,7},{6,4},{7,5},{8,10},{9,11},{10,... | collective-permute-start | bytes 6291464 | tf_op jit(solution)/shard_map/ppermute | solution.py:93
  211.4 32.8 %collective-permute-start.27 = (bf16[2048,512]{1,0:T(8,128)(2,1)}, bf16[2048,512]{1,0:T(8,128)(2,1)}, u32[]{:S(2)}, u32[]{:S(2)}) collective-permute-start(bf16[2048,512]{1,0:T(8,128)(2,1)} %get-tuple-element.148.refs_0_.refs_4_), channel_id=1, source_target_pairs={{0,1},{1,0},{2,3},{3,2},{4,5},{5,4},{6,7},{7,6},{8,9},{9,8},{10,11... | collective-permute-start | bytes 6291464 | tf_op jit(solution)/shard_map/ppermute | solution.py:93
  211.5 25.8 %collective-permute-start.26 = (bf16[4,256,512]{2,1,0:T(8,128)(2,1)}, bf16[4,256,512]{2,1,0:T(8,128)(2,1)S(1)}, u32[]{:S(2)}, u32[]{:S(2)}) collective-permute-start(bf16[4,256,512]{2,1,0:T(8,128)(2,1)} %get-tuple-element.137), channel_id=1, source_target_pairs={{0,16},{16,0},{1,17},{17,1},{2,18},{18,2},{3,19},{19,3},{4,20},{20... | collective-permute-start | bytes 3145736 | tf_op jit(solution)/shard_map/ppermute | solution.py:93
  257.7 24.6 %collective-permute-start.30 = (bf16[1024,512]{1,0:T(8,128)(2,1)}, bf16[1024,512]{1,0:T(8,128)(2,1)S(1)}, u32[]{:S(2)}, u32[]{:S(2)}) collective-permute-start(bf16[1024,512]{1,0:T(8,128)(2,1)} %get-tuple-element.144), channel_id=1, source_target_pairs={{0,2},{1,3},{2,0},{3,1},{4,6},{5,7},{6,4},{7,5},{8,10},{9,11},{10,... | collective-permute-start | bytes 3145736 | tf_op jit(solution)/shard_map/ppermute | solution.py:93
  285.0 109.1 %reduce-scatter.8.cloned.1.call-start = ((), (), s32[]{:S(2)}) async-start(), calls=%async_computation.9 | async-start | bytes 1310720 | tf_op jit(solution)/shard_map/reduce_scatter | solution.py:857
  285.0 23.8 %collective-permute-start.31 = (bf16[1024,512]{1,0:T(8,128)(2,1)}, bf16[1024,512]{1,0:T(8,128)(2,1)S(1)}, u32[]{:S(2)}, u32[]{:S(2)}) collective-permute-start(bf16[1024,512]{1,0:T(8,128)(2,1)} %get-tuple-element.147), channel_id=1, source_target_pairs={{0,2},{1,3},{2,0},{3,1},{4,6},{5,7},{6,4},{7,5},{8,10},{9,11},{10,... | collective-permute-start | bytes 3145736 | tf_op jit(solution)/shard_map/ppermute | solution.py:93
  310.1 95.3 %reduce-scatter.4.cloned.1.call-start = ((), (), s32[]{:S(2)}) async-start(), calls=%async_computation.6 | async-start | bytes 2621440 | tf_op jit(solution)/shard_map/reduce_scatter | solution.py:824
  334.3 23.1 %collective-permute-start.39 = (bf16[4,256,512]{2,1,0:T(8,128)(2,1)}, bf16[4,256,512]{2,1,0:T(8,128)(2,1)S(1)}, u32[]{:S(2)}, u32[]{:S(2)}) collective-permute-start(bf16[4,256,512]{2,1,0:T(8,128)(2,1)} %get-tuple-element.155), channel_id=1, source_target_pairs={{0,16},{16,0},{1,17},{17,1},{2,18},{18,2},{3,19},{19,3},{4,20},{20... | collective-permute-start | bytes 3145736 | tf_op jit(solution)/shard_map/ppermute | solution.py:93
  357.4 23.2 %collective-permute-start.40 = (bf16[4,512,256]{2,1,0:T(8,128)(2,1)}, bf16[4,512,256]{2,1,0:T(8,128)(2,1)S(1)}, u32[]{:S(2)}, u32[]{:S(2)}) collective-permute-start(bf16[4,512,256]{2,1,0:T(8,128)(2,1)} %get-tuple-element.156), channel_id=1, source_target_pairs={{0,16},{16,0},{1,17},{17,1},{2,18},{18,2},{3,19},{19,3},{4,20},{20... | collective-permute-start | bytes 3145736 | tf_op jit(solution)/shard_map/ppermute | solution.py:93
  361.1 23.2 %collective-permute-start.41 = (bf16[2,256,512]{2,1,0:T(8,128)(2,1)}, bf16[2,256,512]{2,1,0:T(8,128)(2,1)}, u32[]{:S(2)}, u32[]{:S(2)}) collective-permute-start(bf16[2,256,512]{2,1,0:T(8,128)(2,1)} %get-tuple-element.163), channel_id=1, source_target_pairs={{0,2},{1,3},{2,0},{3,1},{4,6},{5,7},{6,4},{7,5},{8,10},{9,11},{10,... | collective-permute-start | bytes 1572872 | tf_op jit(solution)/shard_map/ppermute | solution.py:93
  (65 other events, 913.1 us)
Sparse Core Ops, SparseCore 0:
  16.9 29.7 all-gather.4
  48.8 27.3 all-gather.6
  77.7 27.3 all-gather.8
  107.1 45.0 all-gather.10
  285.1 26.5 reduce-scatter.5
  314.4 25.7 reduce-scatter.7
  343.1 42.1 reduce-scatter.3

commit v5 on v4

--- a/solution.py
+++ b/solution.py
@@ -32,7 +32,7 @@
 
 
 def params():
-    return pltpu.CompilerParams(vmem_limit_bytes=56 * 1024 * 1024)
+    return pltpu.CompilerParams(vmem_limit_bytes=67000000)
 
 
 def cost(flops, bytes_accessed, transcendentals=0):
@@ -144,9 +144,9 @@
     small = out_weight.shape[0] // 4
 
     def kernel(places_ref, *refs):
-        for place in range(4):
-            refs[8 + place][:tall] = refs[place][...]
-            refs[8 + place][tall:] = refs[4 + place][...]
+        for place in range(3):
+            refs[6 + place][:tall] = refs[place][...]
+            refs[6 + place][tall:] = refs[3 + place][...]
 
     def at(place):
         return lambda step, s: (s[place], 0)
@@ -158,14 +158,14 @@
         grid_spec=pltpu.PrefetchScalarGridSpec(
             num_scalar_prefetch=1,
             grid=(1,),
-            in_specs=[pl.BlockSpec((tall, cols), at(i)) for i in (0, 1, 3, 4)]
-            + [pl.BlockSpec((small, cols), at(i)) for i in (0, 1, 3, 4)],
-            out_specs=[whole] * 4,
-        ),
-        out_shape=[shape] * 4,
+            in_specs=[pl.BlockSpec((tall, cols), at(i)) for i in range(3)]
+            + [pl.BlockSpec((small, cols), at(i)) for i in range(3)],
+            out_specs=[whole] * 3,
+        ),
+        out_shape=[shape] * 3,
         compiler_params=params(),
         cost_estimate=cost(0, 3 * 4 * cols * (tall + small)),
-    )(places, *[fc2_weight] * 4, *[out_weight] * 4)
+    )(places, fc2_weight, fc2_weight, fc2_weight, out_weight, out_weight, out_weight)
 
 
 def forward_step(xs, ws, fc1_bias, qkv_bias, tables):
@@ -218,29 +218,40 @@
     )(*xs, *ws, fc1_bias, qkv_bias, *tables)
 
 
-def slope_step(gs, ws, up_pre):
+def slope_step(gs, ws, up_pre, same):
     rows = gs[0].shape[0]
     hidden = up_pre.shape[1]
     pair = ws[0].shape[0] - hidden
     block = min(512, rows)
 
     def kernel(*refs):
-        g_refs, w_refs, up = refs[:6], refs[6:10], refs[10]
-        dup_o, dattn_o, bias_o = refs[11:]
+        g_refs, w_refs, up, flag = refs[:6], refs[6:12], refs[12], refs[13]
+        dup_o, dattn_o, bias_o, second, fourth = refs[14:]
+
+        @pl.when(pl.program_id(0) == 0)
+        def _():
+            bias_o[...] = jnp.zeros_like(bias_o)
+
+            @pl.when(flag[0] == 1)
+            def _():
+                second[...] = w_refs[1][...]
+                fourth[...] = w_refs[3][...]
+
+            @pl.when(flag[0] != 1)
+            def _():
+                second[...] = w_refs[4][...]
+                fourth[...] = w_refs[5][...]
+
         cots = blocks_of([ref[...] for ref in g_refs[:3]])
         cots = cots + blocks_of([ref[...] for ref in g_refs[3:]])
         total = None
-        for cot, w_ref in zip(cots, w_refs):
+        for cot, w_ref in zip(cots, (w_refs[0], second, w_refs[2], fourth)):
             part = mul(cot, w_ref[...], NT)
             total = part if total is None else total + part
         d_up = (total[:, :hidden] * gelu_slope(up[...])).astype(bf16)
         dup_o[...] = d_up
         dattn_o[...] = total[:, hidden:].astype(bf16)
 
-        @pl.when(pl.program_id(0) == 0)
-        def _():
-            bias_o[...] = jnp.zeros_like(bias_o)
-
         bias_o[...] += jnp.sum(d_up.astype(f32), axis=0, keepdims=True)
 
     def rowed(cols):
@@ -252,18 +263,20 @@
     return pl.pallas_call(
         kernel,
         grid=(rows // block,),
-        in_specs=[rowed(g.shape[1]) for g in gs] + [fixed(w.shape) for w in ws] + [rowed(hidden)],
+        in_specs=[rowed(g.shape[1]) for g in gs] + [fixed(w.shape) for w in ws] + [rowed(hidden)]
+        + [pl.BlockSpec(memory_space=pltpu.SMEM)],
         out_specs=[rowed(hidden), rowed(pair), fixed((1, hidden))],
         out_shape=[
             jax.ShapeDtypeStruct((rows, hidden), bf16),
             jax.ShapeDtypeStruct((rows, pair), bf16),
             jax.ShapeDtypeStruct((1, hidden), f32),
         ],
+        scratch_shapes=[pltpu.VMEM(ws[0].shape, bf16)] * 2,
         compiler_params=params(),
         cost_estimate=cost(
             8 * rows * ws[0].shape[1] * (hidden + pair), 8 * rows * ws[0].shape[1] + 6 * rows * hidden
         ),
-    )(*gs, *ws, up_pre)
+    )(*gs, *ws, up_pre, same)
 
 
 def pick(same, firsts, seconds, axis):
@@ -306,19 +319,37 @@
     )(same, *firsts, *seconds)
 
 
-def spread(sides, near_mats, far_mats, transposed, part):
+def spread(sides, near_mats, far_mats, transposed, part, same=None):
     rows, hidden = sides[0][0].shape
     pair = sides[0][1].shape[1]
     width = near_mats[0].shape[0] if transposed else near_mats[0].shape[1]
     block = min(1024, rows)
     shares = 2 if part else 1
 
+    count = 2 * shares
+    flags = [] if same is None else [same]
+
     def kernel(*refs):
+        far = refs[6:8]
+        if flags:
+            far, flag = refs[9 + count :], refs[8]
+
+            @pl.when(pl.program_id(0) == 0)
+            def _():
+                @pl.when(flag[0] == 1)
+                def _():
+                    far[0][...] = refs[6][...]
+                    far[1][...] = refs[7][...]
+
+                @pl.when(flag[0] != 1)
+                def _():
+                    far[0][...] = refs[7][...]
+                    far[1][...] = refs[6][...]
+
         hidden_vals = [refs[0][...], refs[2][...]]
         pair_vals = jnp.concatenate([refs[1][...], refs[3][...]], axis=1)
-        outs = refs[8:]
-        for place in range(2):
-            mats = refs[4 + 2 * place : 6 + 2 * place]
+        outs = refs[8 + len(flags) : 8 + len(flags) + count]
+        for mats, place in ((refs[4:6], 0), (far, 1)):
             if transposed:
                 small = jnp.concatenate([w[:, hidden:] for w in mats], axis=1)
                 total = mul(pair_vals, small, NT)
@@ -346,14 +377,16 @@
         kernel,
         grid=(rows // block,),
         in_specs=[rowed(hidden), rowed(pair)] * 2
-        + [pl.BlockSpec(w.shape, lambda i: (0, 0)) for w in near_mats + far_mats],
+        + [pl.BlockSpec(w.shape, lambda i: (0, 0)) for w in near_mats + far_mats]
+        + [pl.BlockSpec(memory_space=pltpu.SMEM) for _ in flags],
         out_specs=[pl.BlockSpec((block // shares, width), lambda i: (i, 0))] * (2 * shares),
+        scratch_shapes=[pltpu.VMEM(w.shape, bf16) for w in far_mats] if flags else [],
         out_shape=[jax.ShapeDtypeStruct((rows // shares, width), bf16)] * (2 * shares),
         compiler_params=params(),
         cost_estimate=cost(
             8 * rows * width * (hidden + pair), 4 * rows * (hidden + pair + width)
         ),
-    )(*sides[0], *sides[1], *near_mats, *far_mats)
+    )(*sides[0], *sides[1], *near_mats, *far_mats, *flags)
 
 
 def blocks_of(values):
@@ -377,7 +410,7 @@
 
 def grad_blocks(half, jobs, across):
     rows = jobs[0][0][0].shape[0]
-    block = min(1024, rows)
+    block = min(2048, rows)
     steps = rows // block
     sizes = [width_of(lefts) for lefts, _, _ in jobs]
     out_rows = sum(sizes)
@@ -724,9 +757,7 @@
 
     half = (dp_index & 1).astype(jnp.int32)
     far_block = (1 - (col_index >> 1)) * 2 + half
-    packs = jnp.stack(
-        [col_index, col_index ^ 1, far_block, col_index ^ 2, col_index ^ 3]
-    ).astype(jnp.int32)
+    packs = jnp.stack([col_index, col_index ^ 1, far_block]).astype(jnp.int32)
     places = jnp.stack([col_index, col_index ^ 1, col_index ^ 2, col_index ^ 3, half]).astype(
         jnp.int32
     )
@@ -757,7 +788,7 @@
     fc1_second = swap_bits(fc1_first, DP, 1)
     tail = out_grad[:, cut:]
     tail_far = swap_bits(after(tail, qkv_first), COL, 2)
-    out_own, out_near, out_far, out_cross = pack_out(packs, fc2_weight, after(out_weight, in_own))
+    out_own, out_near, out_far = pack_out(packs, fc2_weight, after(out_weight, in_own))
     cot_0 = lax.all_gather(after(out_grad[:, :cut], normed), ROW, axis=0, tiled=True)
     cot_b = lax.all_gather(
         jnp.concatenate([tail, tail_far], axis=1), ROW, axis=0, tiled=True
@@ -777,7 +808,7 @@
     in_3 = swap_bits(in_pass, COL, 1)
     normed_1 = [swap_bits(normed_0a, COL, 1), swap_bits(normed_0b, COL, 1)]
     normed_2b = swap_bits(after(normed_0b, normed_2a), COL, 2)
-    out_2 = swap_bits(after(out_far, normed_2b), COL, 2)
+    out_first = swap_bits(after(out_far, normed_2b), COL, 2)
     normed_3 = [swap_bits(normed_2a, COL, 1), swap_bits(normed_2b, COL, 1)]
     normed_all = [normed_0a, normed_0b, normed_2a, normed_2b]
     up_pre, act, q_rot, k_rot, v_low = forward_step(
@@ -787,16 +818,17 @@
         qkv_bias.reshape(1, -1),
         tables,
     )
-    out_pass = swap_bits(after(out_cross, act, out_2), COL, 2)
+    out_second = swap_bits(after(out_first, act, qkv_second), DP, 1)
+    cot_2 = swap_bits(after(cot_0, out_first, act), COL, 2)
     act_1 = swap_bits(act, COL, 1)
     attn, attn_full, lse = attend(lowest, after(q_rot, act), k_rot, v_low, begin)
     attn_1 = swap_bits(attn, COL, 1)
-    out_3 = swap_bits(out_pass, COL, 1)
-    cot_2 = swap_bits(after(cot_0, out_pass, attn), COL, 2)
+    out_third = swap_bits(after(out_first, act), COL, 1)
+    out_fourth = swap_bits(out_second, COL, 1)
     cots = [cot_0, cot_2, cot_b]
     cots_1 = [swap_bits(cot_0, COL, 1), swap_bits(cot_2, COL, 1), swap_bits(cot_b, COL, 1)]
     mix_near, mix_far = spread(
-        [[act, attn], [act_1, attn_1]], [out_own, out_near], [out_2, out_pass], False, 0
+        [[act, attn], [act_1, attn_1]], [out_own, out_near], [out_first, out_second], False, 0, same
     )
     mix_recv = swap_bits(after(mix_far, cot_2), COL, 2)
     fc2_keep, fc2_send = grad_blocks(
@@ -804,7 +836,10 @@
     )
     fc2_recv = swap_bits(after(fc2_send, qkv_second), DP, 1)
     d_up, d_attn, fc1_sums = slope_step(
-        cots + cots_1, [out_own, out_2, out_1, out_3], after(up_pre, fc2_send)
+        cots + cots_1,
+        [out_own, out_first, out_1, out_third, out_second, out_fourth],
+        after(up_pre, fc2_send),
+        same,
     )
     d_up_1 = swap_bits(d_up, COL, 1)
 
@@ -832,6 +867,7 @@
         local_rows,
     )
     recv_a = swap_bits(after(far_a, fc2_crossed), COL, 2)
+    recv_b = swap_bits(after(far_b, fc2_crossed), COL, 2)
     fc2_crossed_x = swap_bits(after(fc2_crossed, fc2_near_x), DP, 1)
     fc1_keep, fc1_send = grad_blocks(
         half, [(normed_all, [after(d_up, far_a), d_up_1], False)], False
@@ -845,7 +881,6 @@
         ],
         True,
     )
-    recv_b = swap_bits(after(far_b, recv_a), COL, 2)
     total_a = (near_a.astype(f32) + recv_a.astype(f32)).astype(bf16)
     d_normed_a = lax.psum_scatter(total_a, ROW, scatter_dimension=0, tiled=True)
     (fc2_weight_grad,) = lay_out(

time: 447 us -> 458 us (1.025)
  waiting for transfers between devices: 203 us -> 211 us
  starting transfers between devices: 41.6 us -> 47 us
    all_gather x1, waiting for transfers between devices: 0.01 us -> 16.9 us  [step(): lax.all_gather(after(out_grad[:, :cut], normed), ROW, axis=0, tiled=True)]
    ppermute x48 -> x49, waiting for transfers between devices: 175 us -> 169 us  [swap_bits(): lax.ppermute(value, axis, [(place, place ^ bit) for place in range(count)])]
    ppermute x48 -> x49, starting transfers between devices: 41.3 us -> 46.5 us  [swap_bits(): lax.ppermute(value, axis, [(place, place ^ bit) for place in range(count)])]
  transfers between devices with their start and end apart: 55 -> 56, of which waited for: 24 -> 27; matrix products, arithmetic and copies ran while one was open for 7% -> 7% of each run, Pallas kernels for 32% -> 30%
where the time goes in v5:
time: 458 us; the launch traced here: 457 us
  waiting for transfers between devices  211 us (46%)
  Pallas kernels  142 us (31%)
  starting transfers between devices  47 us (10%)
  other arithmetic  24.6 us (5%)
  local copies, waits for them, and re-layouts  18.2 us (4%)
  between operations  14.5 us (3%)
    ppermute x49, waiting for transfers between devices, swap_bits(): lax.ppermute(value, axis, [(place, place ^ bit) for place in range(count)])  169 us
    ppermute x49, starting transfers between devices, swap_bits(): lax.ppermute(value, axis, [(place, place ^ bit) for place in range(count)])  46.5 us
    pallas_call x3, Pallas kernels, grad_blocks(): pl.pallas_call(kernel, grid_spec=pltpu.PrefetchScalarGridSpec(num_scalar_...  29.7 us
    all_gather x1, waiting for transfers between devices, step(): normed_0b = lax.all_gather(normed[:, cut:], ROW, axis=0, tiled=True)  24.8 us
    pallas_call x2, Pallas kernels, spread(): pl.pallas_call(kernel, grid=(rows // block,), in_specs=[rowed(hidden), ro...  21.8 us
    pallas_call x1, Pallas kernels, attend_back(): pl.pallas_call(kernel, grid_spec=pltpu.PrefetchScalarGridSpec(num_scalar_...  18.1 us
    all_gather x1, waiting for transfers between devices, step(): lax.all_gather(after(out_grad[:, :cut], normed), ROW, axis=0, tiled=True)  16.9 us
    pallas_call x1, Pallas kernels, forward_step(): pl.pallas_call(kernel, grid=(rows // block,), in_specs=[rowed(x.shape[1])...  15.7 us
  transfers between devices with their start and end apart: 56, of which 27 were waited for; matrix products, arithmetic and copies ran while one was open for 7% of the time, Pallas kernels for 30%

profile of v5, /device:TPU:0, one launch (start us, length us, event | category | flops | bytes accessed | tf_op | source)
XLA Modules:
  0.0 457.2 jit_solution(17273028648593745899)
XLA Ops:
  36.4 6.1 %collective-permute-done.3.refs_1_ = bf16[512,384]{1,0:T(8,128)(2,1)S(1)} collective-permute-done((bf16[512,384]{1,0:T(8,128)(2,1)}, bf16[512,384]{1,0:T(8,128)(2,1)S(1)}, u32[]{:S(2)}, u32[]{:S(2)}) %collective-permute-start.3) | collective-permute-done | bytes 393248 | tf_op jit(solution)/shard_map/ppermute | solution.py:93
  51.4 24.8 %all-gather.7.cloned.1.call-done.refs_1_.refs_3_ = bf16[2048,256]{1,0:T(8,128)(2,1)} async-done(((bf16[512,256]{1,0:T(8,128)(2,1)}), bf16[2048,256]{1,0:T(8,128)(2,1)}) %all-gather.7.cloned.1.call-update) | async-done | bytes 1048592 | tf_op jit(solution)/shard_map/all_gather | solution.py:785
  79.5 11.3 %collective-permute-done.11.refs_2_ = bf16[512,512]{1,0:T(8,128)(2,1)} collective-permute-done((bf16[512,512]{1,0:T(8,128)(2,1)}, bf16[512,512]{1,0:T(8,128)(2,1)}, u32[]{:S(2)}, u32[]{:S(2)}) %collective-permute-start.11) | collective-permute-done | bytes 524320 | tf_op jit(solution)/shard_map/ppermute | solution.py:93
  93.0 7.1 %collective-permute-done.12.refs_3_ = bf16[512,384]{1,0:T(8,128)(2,1)S(1)} collective-permute-done((bf16[512,384]{1,0:T(8,128)(2,1)S(1)}, bf16[512,384]{1,0:T(8,128)(2,1)S(1)}, u32[]{:S(2)}, u32[]{:S(2)}) %collective-permute-start.12) | collective-permute-done | bytes 393248 | tf_op jit(solution)/shard_map/ppermute | solution.py:93
  101.4 5.8 %fusion = (f32[2048,128]{1,0:T(8,128)}, f32[2048,128]{1,0:T(8,128)}, f32[2048,128]{1,0:T(8,128)}) fusion(f32[128]{0:T(128)S(1)} %fusion.22, f32[2048]{0:T(1024)S(1)} %get-tuple-element.228, pred[128]{0:T(512)(128)(4,1)S(1)} %get-tuple-element.233, pred[128]{0:T(512)(128)(4,1)S(1)} %get-tuple-element.234, pred[128]{0:T(512)(128)(4,1)S(1)} %broadcast_compare_fusion.1), kind=kLoop, calls=%fused_computation.12 | loop fusion | flops 1310720 | bytes 3154816 | tf_op jit(solution)/shard_map/jit(_where)/select_n | solution.py:62
  112.8 15.7 %shard_map.205 = (f32[2048,512]{1,0:T(8,128)}, bf16[2048,512]{1,0:T(8,128)(2,1)}, bf16[2048,128]{1,0:T(8,128)(2,1)}, bf16[2048,128]{1,0:T(8,128)(2,1)}, bf16[2048,128]{1,0:T(8,128)(2,1)}) custom-call(bf16[2048,256]{1,0:T(8,128)(2,1)} %all-gather.5.cloned.1.call-done.refs_0_.refs_2_, bf16[2048,256]{1,0:T(8,128)(2,1)} %all-gather.7.cloned.1.call-done.refs_1_.refs_3_, ...), custom_call_target="tpu_custom_call" | custom-call | flops 7516192768 | bytes 18874368 | tf_op jit(solution)/shard_map/pallas_call | solution.py:201
  134.7 16.9 %all-gather.9.cloned.1.call-done.refs_2_.refs_0_.refs_8_ = bf16[2048,256]{1,0:T(8,128)(2,1)} async-done(((bf16[512,256]{1,0:T(8,128)(2,1)}), bf16[2048,256]{1,0:T(8,128)(2,1)}) %all-gather.9.cloned.1.call-update) | async-done | bytes 1048592 | tf_op jit(solution)/shard_map/all_gather | solution.py:792
  153.6 12.0 %shard_map.206 = (bf16[2048,128]{1,0:T(8,128)(2,1)}, f32[2048,128]{1,0:T(8,128)}, f32[2,2048]{1,0:T(2,128)}) custom-call(s32[4]{0:T(128)} %and_select_fusion.lowest_ref, bf16[2048,128]{1,0:T(8,128)(2,1)} %get-tuple-element.111.q_ref, bf16[2048,128]{1,0:T(8,128)(2,1)} %get-tuple-element.112.k_ref, bf16[2048,128]{1,0:T(8,128)(2,1)} %get-tuple-element.113.v_ref, ...), custom_call_target="tpu_custom_call" | custom-call | flops 1073741824 | bytes 3145728 | tf_op jit(solution)/shard_map/pallas_call | solution.py:605
  168.0 8.4 %collective-permute-done.19.refs_3_.refs_1_.refs_9_ = bf16[2048,256]{1,0:T(8,128)(2,1)} collective-permute-done((bf16[2048,256]{1,0:T(8,128)(2,1)}, bf16[2048,256]{1,0:T(8,128)(2,1)}, u32[]{:S(2)}, u32[]{:S(2)}) %collective-permute-start.19) | collective-permute-done | bytes 1048608 | tf_op jit(solution)/shard_map/ppermute | solution.py:93
  176.4 6.7 %collective-permute-done.18.refs_7_.refs_10_ = bf16[640,512]{1,0:T(8,128)(2,1)} collective-permute-done((bf16[640,512]{1,0:T(8,128)(2,1)}, bf16[640,512]{1,0:T(8,128)(2,1)}, u32[]{:S(2)}, u32[]{:S(2)}) %collective-permute-start.18) | collective-permute-done | bytes 655392 | tf_op jit(solution)/shard_map/ppermute | solution.py:93
  183.6 9.4 %shard_map.208 = (bf16[2048,512]{1,0:T(8,128)(2,1)}, bf16[2048,512]{1,0:T(8,128)(2,1)}) custom-call(bf16[2048,512]{1,0:T(8,128)(2,1)} %get-tuple-element.109.refs_0_, bf16[2048,128]{1,0:T(8,128)(2,1)} %get-tuple-element.114.refs_1_.refs_6_, bf16[2048,512]{1,0:T(8,128)(2,1)} %collective-permute-done.15.refs_2_.refs_1_, ...), custom_call_target="tpu_custom_call" | custom-call | flops 5368709120 | bytes 9437184 | tf_op jit(solution)/shard_map/pallas_call | solution.py:376
  193.6 9.4 %shard_map.209 = (bf16[4,256,512]{2,1,0:T(8,128)(2,1)}, bf16[4,256,512]{2,1,0:T(8,128)(2,1)}) custom-call(s32[1]{0:T(128)} %bitcast.15.half_ref, bf16[2048,512]{1,0:T(8,128)(2,1)} %get-tuple-element.109.refs_0_, bf16[2048,512]{1,0:T(8,128)(2,1)} %collective-permute-done.15.refs_2_.refs_1_, ...), custom_call_target="tpu_custom_call" | custom-call | flops 4294967296 | bytes 16777216 | tf_op jit(solution)/shard_map/pallas_call | solution.py:458
  203.1 13.5 %shard_map.210 = (bf16[2048,512]{1,0:T(8,128)(2,1)}, bf16[2048,128]{1,0:T(8,128)(2,1)}, f32[1,512]{1,0:T(1,128)}) custom-call(bf16[2048,256]{1,0:T(8,128)(2,1)} %all-gather.9.cloned.1.call-done.refs_2_.refs_0_.refs_8_, bf16[2048,256]{1,0:T(8,128)(2,1)} %collective-permute-done.19.refs_3_.refs_1_.refs_9_, ...), custom_call_target="tpu_custom_call" | custom-call | flops 5368709120 | bytes 14680064 | tf_op jit(solution)/shard_map/pallas_call | solution.py:263
  218.2 18.1 %shard_map.211 = (bf16[2048,384]{1,0:T(8,128)(2,1)}, f32[1,384]{1,0:T(1,128)}) custom-call(s32[4]{0:T(128)} %and_select_fusion.lowest_ref, bf16[2048,128]{1,0:T(8,128)(2,1)} %get-tuple-element.111.q_ref, bf16[2048,128]{1,0:T(8,128)(2,1)} %get-tuple-element.112.k_ref, bf16[2048,128]{1,0:T(8,128)(2,1)} %get-tuple-element.113.v_ref, ...), custom_call_target="tpu_custom_call" | custom-call | flops 2684354560 | bytes 4194304 | tf_op jit(solution)/shard_map/pallas_call | solution.py:710
  236.4 6.1 %collective-permute-done.27.received_ref = bf16[4,256,512]{2,1,0:T(8,128)(2,1)} collective-permute-done((bf16[4,256,512]{2,1,0:T(8,128)(2,1)}, bf16[4,256,512]{2,1,0:T(8,128)(2,1)}, u32[]{:S(2)}, u32[]{:S(2)}) %collective-permute-start.27) | collective-permute-done | bytes 1048608 | tf_op jit(solution)/shard_map/ppermute | solution.py:93
  250.7 12.4 %shard_map.213 = (bf16[1024,512]{1,0:T(8,128)(2,1)}, bf16[1024,512]{1,0:T(8,128)(2,1)}, bf16[1024,512]{1,0:T(8,128)(2,1)}, bf16[1024,512]{1,0:T(8,128)(2,1)}) custom-call(bf16[2048,512]{1,0:T(8,128)(2,1)} %get-tuple-element.148.refs_0_.refs_4_, bf16[2048,384]{1,0:T(8,128)(2,1)} %get-tuple-element.150.refs_1_.refs_0_, ...), custom_call_target="tpu_custom_call" | custom-call | flops 7516192768 | bytes 11534336 | tf_op jit(solution)/shard_map/pallas_call | solution.py:376
  264.5 23.3 %collective-permute-done.31 = bf16[1024,512]{1,0:T(8,128)(2,1)S(1)} collective-permute-done((bf16[1024,512]{1,0:T(8,128)(2,1)}, bf16[1024,512]{1,0:T(8,128)(2,1)S(1)}, u32[]{:S(2)}, u32[]{:S(2)}) %collective-permute-start.31) | collective-permute-done | bytes 1048608 | tf_op jit(solution)/shard_map/ppermute | solution.py:93
  291.3 22.8 %collective-permute-done.32 = bf16[1024,512]{1,0:T(8,128)(2,1)S(1)} collective-permute-done((bf16[1024,512]{1,0:T(8,128)(2,1)S(1)}, bf16[1024,512]{1,0:T(8,128)(2,1)S(1)}, u32[]{:S(2)}, u32[]{:S(2)}) %collective-permute-start.32) | collective-permute-done | bytes 1048608 | tf_op jit(solution)/shard_map/ppermute | solution.py:93
  317.0 10.0 %collective-permute-done.38.refs_2_ = bf16[2,256,512]{2,1,0:T(8,128)(2,1)S(1)} collective-permute-done((bf16[2,256,512]{2,1,0:T(8,128)(2,1)S(1)}, bf16[2,256,512]{2,1,0:T(8,128)(2,1)S(1)}, u32[]{:S(2)}, u32[]{:S(2)}) %collective-permute-start.38) | collective-permute-done | bytes 524320 | tf_op jit(solution)/shard_map/ppermute | solution.py:93
  329.4 9.5 %shard_map.214 = (bf16[4,256,512]{2,1,0:T(8,128)(2,1)}, bf16[4,256,512]{2,1,0:T(8,128)(2,1)}) custom-call(s32[1]{0:T(128)} %bitcast.15.half_ref, bf16[2048,256]{1,0:T(8,128)(2,1)} %all-gather.5.cloned.1.call-done.refs_0_.refs_2_, bf16[2048,256]{1,0:T(8,128)(2,1)} %all-gather.7.cloned.1.call-done.refs_1_.refs_3_, ...), custom_call_target="tpu_custom_call" | custom-call | flops 4294967296 | bytes 16777216 | tf_op jit(solution)/shard_map/pallas_call | solution.py:458
  341.4 10.7 %shard_map.215 = (bf16[4,512,256]{2,1,0:T(8,128)(2,1)}, bf16[4,512,256]{2,1,0:T(8,128)(2,1)}) custom-call(s32[1]{0:T(128)} %bitcast.15.half_ref, bf16[2048,384]{1,0:T(8,128)(2,1)} %get-tuple-element.150.refs_1_.refs_0_, bf16[2048,384]{1,0:T(8,128)(2,1)} %collective-permute-done.29.refs_3_.refs_1_, ...), custom_call_target="tpu_custom_call" | custom-call | flops 4294967296 | bytes 16777216 | tf_op jit(solution)/shard_map/pallas_call | solution.py:458
  352.2 10.6 %collective-permute-done.40.received_ref = bf16[4,256,512]{2,1,0:T(8,128)(2,1)} collective-permute-done((bf16[4,256,512]{2,1,0:T(8,128)(2,1)}, bf16[4,256,512]{2,1,0:T(8,128)(2,1)}, u32[]{:S(2)}, u32[]{:S(2)}) %collective-permute-start.40) | collective-permute-done | bytes 1048608 | tf_op jit(solution)/shard_map/ppermute | solution.py:93
  367.4 18.7 %collective-permute-done.41.received_ref = bf16[4,512,256]{2,1,0:T(8,128)(2,1)} collective-permute-done((bf16[4,512,256]{2,1,0:T(8,128)(2,1)}, bf16[4,512,256]{2,1,0:T(8,128)(2,1)}, u32[]{:S(2)}, u32[]{:S(2)}) %collective-permute-start.41) | collective-permute-done | bytes 1048608 | tf_op jit(solution)/shard_map/ppermute | solution.py:93
  398.8 8.5 %collective-permute-done.34 = f32[2,512]{1,0:T(2,128)S(1)} collective-permute-done((f32[2,512]{1,0:T(2,128)S(1)}, f32[2,512]{1,0:T(2,128)S(1)}, u32[]{:S(2)}, u32[]{:S(2)}) %collective-permute-start.34) | collective-permute-done | bytes 4128 | tf_op jit(solution)/shard_map/ppermute | solution.py:93
  (189 shorter events, 145.0 us)
Async XLA Ops:
  7.2 41.8 %all-gather.5.cloned.1.call-start = ((), (), s32[]{:S(2)}) async-start(), calls=%async_computation.3 | async-start | bytes 1310720 | tf_op jit(solution)/shard_map/all_gather | solution.py:784
  16.7 59.4 %all-gather.7.cloned.1.call-start = ((), (), s32[]{:S(2)}) async-start(), calls=%async_computation.4 | async-start | bytes 1310720 | tf_op jit(solution)/shard_map/all_gather | solution.py:785
  17.5 116.7 %all-gather.11.cloned.1.call-start = ((), (), s32[]{:S(2)}) async-start(), calls=%async_computation.7 | async-start | bytes 2621440 | tf_op jit(solution)/shard_map/all_gather | solution.py:793
  49.0 27.2 %collective-permute-start.5 = (bf16[2048,256]{1,0:T(8,128)(2,1)}, bf16[2048,256]{1,0:T(8,128)(2,1)}, u32[]{:S(2)}, u32[]{:S(2)}) collective-permute-start(bf16[2048,256]{1,0:T(8,128)(2,1)} %all-gather.5.cloned.1.call-done.refs_0_.refs_2_), channel_id=1, source_target_pairs={{0,2},{1,3},{2,0},{3,1},{4,6},{5,7},{6,4},{7,5},{8,10},{9,11},{10,... | collective-permute-start | bytes 3145736 | tf_op jit(solution)/shard_map/ppermute | solution.py:93
  51.3 100.3 %all-gather.9.cloned.1.call-start = ((), (), s32[]{:S(2)}) async-start(), calls=%async_computation.5 | async-start | bytes 1310720 | tf_op jit(solution)/shard_map/all_gather | solution.py:792
  76.2 24.7 %collective-permute-start.6 = (bf16[2048,256]{1,0:T(8,128)(2,1)}, bf16[2048,256]{1,0:T(8,128)(2,1)}, u32[]{:S(2)}, u32[]{:S(2)}) collective-permute-start(bf16[2048,256]{1,0:T(8,128)(2,1)} %all-gather.7.cloned.1.call-done.refs_1_.refs_3_), channel_id=1, source_target_pairs={{0,2},{1,3},{2,0},{3,1},{4,6},{5,7},{6,4},{7,5},{8,10},{9,11},{10,... | collective-permute-start | bytes 3145736 | tf_op jit(solution)/shard_map/ppermute | solution.py:93
  79.5 30.5 %collective-permute-start.13 = (bf16[512,896]{1,0:T(8,128)(2,1)}, bf16[512,896]{1,0:T(8,128)(2,1)}, u32[]{:S(2)}, u32[]{:S(2)}) collective-permute-start(bf16[512,896]{1,0:T(8,128)(2,1)} %get-tuple-element.107.refs_5_), channel_id=1, source_target_pairs={{0,1},{1,0},{2,3},{3,2},{4,5},{5,4},{6,7},{7,6},{8,9},{9,8},{10,11... | collective-permute-start | bytes 2752520 | tf_op jit(solution)/shard_map/ppermute | solution.py:93
  110.0 278.0 %reduce-scatter.6.cloned.1.call-start = ((), (), s32[]{:S(2)}) async-start(), calls=%async_computation.8 | async-start | bytes 1310720 | tf_op jit(solution)/shard_map/reduce_scatter | solution.py:885
  128.5 54.6 %collective-permute-start.15 = (bf16[2048,512]{1,0:T(8,128)(2,1)}, bf16[2048,512]{1,0:T(8,128)(2,1)}, u32[]{:S(2)}, u32[]{:S(2)}) collective-permute-start(bf16[2048,512]{1,0:T(8,128)(2,1)} %get-tuple-element.109.refs_0_), channel_id=1, source_target_pairs={{0,1},{1,0},{2,3},{3,2},{4,5},{5,4},{6,7},{7,6},{8,9},{9,8},{10,11... | collective-permute-start | bytes 6291464 | tf_op jit(solution)/shard_map/ppermute | solution.py:93
  134.2 31.4 %collective-permute-start.24 = (bf16[640,512]{1,0:T(8,128)(2,1)}, bf16[640,512]{1,0:T(8,128)(2,1)}, u32[]{:S(2)}, u32[]{:S(2)}) collective-permute-start(bf16[640,512]{1,0:T(8,128)(2,1)} %get-tuple-element.117.refs_5_), channel_id=1, source_target_pairs={{0,1},{1,0},{2,3},{3,2},{4,5},{5,4},{6,7},{7,6},{8,9},{9,8},{10,11... | collective-permute-start | bytes 1966088 | tf_op jit(solution)/shard_map/ppermute | solution.py:93
  134.2 68.9 %collective-permute-start.23 = (bf16[2048,512]{1,0:T(8,128)(2,1)}, bf16[2048,512]{1,0:T(8,128)(2,1)}, u32[]{:S(2)}, u32[]{:S(2)}) collective-permute-start(bf16[2048,512]{1,0:T(8,128)(2,1)} %all-gather.11.cloned.1.call-done.refs_4_.refs_2_.refs_10_), channel_id=1, source_target_pairs={{0,1},{1,0},{2,3},{3,2},{4,5},{5,4},{6,7},{7,6},{8,9},{9,8},{10,11... | collective-permute-start | bytes 6291464 | tf_op jit(solution)/shard_map/ppermute | solution.py:93
  151.6 24.7 %collective-permute-start.19 = (bf16[2048,256]{1,0:T(8,128)(2,1)}, bf16[2048,256]{1,0:T(8,128)(2,1)}, u32[]{:S(2)}, u32[]{:S(2)}) collective-permute-start(bf16[2048,256]{1,0:T(8,128)(2,1)} %all-gather.9.cloned.1.call-done.refs_2_.refs_0_.refs_8_), channel_id=1, source_target_pairs={{0,2},{1,3},{2,0},{3,1},{4,6},{5,7},{6,4},{7,5},{8,10},{9,11},{10,... | collective-permute-start | bytes 3145736 | tf_op jit(solution)/shard_map/ppermute | solution.py:93
  167.8 25.2 %collective-permute-start.21 = (bf16[2048,256]{1,0:T(8,128)(2,1)}, bf16[2048,256]{1,0:T(8,128)(2,1)}, u32[]{:S(2)}, u32[]{:S(2)}) collective-permute-start(bf16[2048,256]{1,0:T(8,128)(2,1)} %all-gather.9.cloned.1.call-done.refs_2_.refs_0_.refs_8_), channel_id=1, source_target_pairs={{0,1},{1,0},{2,3},{3,2},{4,5},{5,4},{6,7},{7,6},{8,9},{9,8},{10,11... | collective-permute-start | bytes 3145736 | tf_op jit(solution)/shard_map/ppermute | solution.py:93
  176.4 26.7 %collective-permute-start.22 = (bf16[2048,256]{1,0:T(8,128)(2,1)}, bf16[2048,256]{1,0:T(8,128)(2,1)}, u32[]{:S(2)}, u32[]{:S(2)}) collective-permute-start(bf16[2048,256]{1,0:T(8,128)(2,1)} %collective-permute-done.19.refs_3_.refs_1_.refs_9_), channel_id=1, source_target_pairs={{0,1},{1,0},{2,3},{3,2},{4,5},{5,4},{6,7},{7,6},{8,9},{9,8},{10,11... | collective-permute-start | bytes 3145736 | tf_op jit(solution)/shard_map/ppermute | solution.py:93
  193.0 52.1 %collective-permute-start.20 = (bf16[2048,512]{1,0:T(8,128)(2,1)}, bf16[2048,512]{1,0:T(8,128)(2,1)}, u32[]{:S(2)}, u32[]{:S(2)}) collective-permute-start(bf16[2048,512]{1,0:T(8,128)(2,1)} %get-tuple-element.125), channel_id=1, source_target_pairs={{0,2},{1,3},{2,0},{3,1},{4,6},{5,7},{6,4},{7,5},{8,10},{9,11},{10,... | collective-permute-start | bytes 6291464 | tf_op jit(solution)/shard_map/ppermute | solution.py:93
  216.6 34.2 %collective-permute-start.28 = (bf16[2048,512]{1,0:T(8,128)(2,1)}, bf16[2048,512]{1,0:T(8,128)(2,1)}, u32[]{:S(2)}, u32[]{:S(2)}) collective-permute-start(bf16[2048,512]{1,0:T(8,128)(2,1)} %get-tuple-element.148.refs_0_.refs_4_), channel_id=1, source_target_pairs={{0,1},{1,0},{2,3},{3,2},{4,5},{5,4},{6,7},{7,6},{8,9},{9,8},{10,11... | collective-permute-start | bytes 6291464 | tf_op jit(solution)/shard_map/ppermute | solution.py:93
  216.6 25.9 %collective-permute-start.27 = (bf16[4,256,512]{2,1,0:T(8,128)(2,1)}, bf16[4,256,512]{2,1,0:T(8,128)(2,1)}, u32[]{:S(2)}, u32[]{:S(2)}) collective-permute-start(bf16[4,256,512]{2,1,0:T(8,128)(2,1)} %get-tuple-element.137), channel_id=1, source_target_pairs={{0,16},{16,0},{1,17},{17,1},{2,18},{18,2},{3,19},{19,3},{4,20},{20... | collective-permute-start | bytes 3145736 | tf_op jit(solution)/shard_map/ppermute | solution.py:93
  263.1 24.6 %collective-permute-start.31 = (bf16[1024,512]{1,0:T(8,128)(2,1)}, bf16[1024,512]{1,0:T(8,128)(2,1)S(1)}, u32[]{:S(2)}, u32[]{:S(2)}) collective-permute-start(bf16[1024,512]{1,0:T(8,128)(2,1)} %get-tuple-element.144), channel_id=1, source_target_pairs={{0,2},{1,3},{2,0},{3,1},{4,6},{5,7},{6,4},{7,5},{8,10},{9,11},{10,... | collective-permute-start | bytes 3145736 | tf_op jit(solution)/shard_map/ppermute | solution.py:93
  290.5 97.6 %reduce-scatter.8.cloned.1.call-start = ((), (), s32[]{:S(2)}) async-start(), calls=%async_computation.9 | async-start | bytes 1310720 | tf_op jit(solution)/shard_map/reduce_scatter | solution.py:892
  290.5 23.6 %collective-permute-start.32 = (bf16[1024,512]{1,0:T(8,128)(2,1)S(1)}, bf16[1024,512]{1,0:T(8,128)(2,1)S(1)}, u32[]{:S(2)}, u32[]{:S(2)}) collective-permute-start(bf16[1024,512]{1,0:T(8,128)(2,1)S(1)} %copy-done.13), channel_id=1, source_target_pairs={{0,2},{1,3},{2,0},{3,1},{4,6},{5,7},{6,4},{7,5},{8,10},{9,11},{10,... | collective-permute-start | bytes 3145736 | tf_op jit(solution)/shard_map/ppermute | solution.py:93
  315.4 93.4 %reduce-scatter.4.cloned.1.call-start = ((), (), s32[]{:S(2)}) async-start(), calls=%async_computation.6 | async-start | bytes 2621440 | tf_op jit(solution)/shard_map/reduce_scatter | solution.py:859
  362.8 23.3 %collective-permute-start.41 = (bf16[4,512,256]{2,1,0:T(8,128)(2,1)}, bf16[4,512,256]{2,1,0:T(8,128)(2,1)}, u32[]{:S(2)}, u32[]{:S(2)}) collective-permute-start(bf16[4,512,256]{2,1,0:T(8,128)(2,1)} %get-tuple-element.156), channel_id=1, source_target_pairs={{0,16},{16,0},{1,17},{17,1},{2,18},{18,2},{3,19},{19,3},{4,20},{20... | collective-permute-start | bytes 3145736 | tf_op jit(solution)/shard_map/ppermute | solution.py:93
  367.4 25.2 %collective-permute-start.42 = (bf16[2,256,512]{2,1,0:T(8,128)(2,1)}, bf16[2,256,512]{2,1,0:T(8,128)(2,1)}, u32[]{:S(2)}, u32[]{:S(2)}) collective-permute-start(bf16[2,256,512]{2,1,0:T(8,128)(2,1)} %get-tuple-element.163), channel_id=1, source_target_pairs={{0,2},{1,3},{2,0},{3,1},{4,6},{5,7},{6,4},{7,5},{8,10},{9,11},{10,... | collective-permute-start | bytes 1572872 | tf_op jit(solution)/shard_map/ppermute | solution.py:93
  422.6 23.4 %collective-permute-start.48 = (bf16[2,256,512]{2,1,0:T(8,128)(2,1)}, bf16[2,256,512]{2,1,0:T(8,128)(2,1)}, u32[]{:S(2)}, u32[]{:S(2)}) collective-permute-start(bf16[2,256,512]{2,1,0:T(8,128)(2,1)} %collective-permute-done.42.refs_1_), channel_id=1, source_target_pairs={{0,16},{16,0},{1,17},{17,1},{2,18},{18,2},{3,19},{19,3},{4,20},{20... | collective-permute-start | bytes 1572872 | tf_op jit(solution)/shard_map/ppermute | solution.py:93
  (46 other events, 660.3 us)
Sparse Core Ops, SparseCore 0:
  16.9 29.7 all-gather.4
  48.8 27.3 all-gather.6
  78.3 45.0 all-gather.10
  124.8 26.7 all-gather.8
  290.6 25.8 reduce-scatter.5
  319.2 25.7 reduce-scatter.7
  347.9 42.1 reduce-scatter.3

commit v6 on v5

--- a/solution.py
+++ b/solution.py
@@ -324,9 +324,8 @@
     pair = sides[0][1].shape[1]
     width = near_mats[0].shape[0] if transposed else near_mats[0].shape[1]
     block = min(1024, rows)
-    shares = 2 if part else 1
-
-    count = 2 * shares
+
+    count = 3
     flags = [] if same is None else [same]
 
     def kernel(*refs):
@@ -361,14 +360,13 @@
                 for value, w in zip(hidden_vals, mats):
                     total = total + mul(value, w[:hidden])
             total = total.astype(bf16)
-            if part:
-                cut = part // 2
-                for piece in range(block // part):
-                    spot = slice(piece * cut, (piece + 1) * cut)
-                    outs[2 * place][spot] = total[piece * part : piece * part + cut]
-                    outs[2 * place + 1][spot] = total[piece * part + cut : (piece + 1) * part]
-            else:
-                outs[place][...] = total
+            cut = part // 2
+            for piece in range(block // part):
+                spot = slice(piece * cut, (piece + 1) * cut)
+                outs[place][spot] = total[piece * part : piece * part + cut]
+                outs[2][spot, place * width : (place + 1) * width] = total[
+                    piece * part + cut : (piece + 1) * part
+                ]
 
     def rowed(cols):
         return pl.BlockSpec((block, cols), lambda i: (i, 0))
@@ -379,9 +377,17 @@
         in_specs=[rowed(hidden), rowed(pair)] * 2
         + [pl.BlockSpec(w.shape, lambda i: (0, 0)) for w in near_mats + far_mats]
         + [pl.BlockSpec(memory_space=pltpu.SMEM) for _ in flags],
-        out_specs=[pl.BlockSpec((block // shares, width), lambda i: (i, 0))] * (2 * shares),
+        out_specs=[
+            pl.BlockSpec((block // 2, width), lambda i: (i, 0)),
+            pl.BlockSpec((block // 2, width), lambda i: (i, 0)),
+            pl.BlockSpec((block // 2, 2 * width), lambda i: (i, 0)),
+        ],
         scratch_shapes=[pltpu.VMEM(w.shape, bf16) for w in far_mats] if flags else [],
-        out_shape=[jax.ShapeDtypeStruct((rows // shares, width), bf16)] * (2 * shares),
+        out_shape=[
+            jax.ShapeDtypeStruct((rows // 2, width), bf16),
+            jax.ShapeDtypeStruct((rows // 2, width), bf16),
+            jax.ShapeDtypeStruct((rows // 2, 2 * width), bf16),
+        ],
         compiler_params=params(),
         cost_estimate=cost(
             8 * rows * width * (hidden + pair), 4 * rows * (hidden + pair + width)
@@ -808,7 +814,7 @@
     in_3 = swap_bits(in_pass, COL, 1)
     normed_1 = [swap_bits(normed_0a, COL, 1), swap_bits(normed_0b, COL, 1)]
     normed_2b = swap_bits(after(normed_0b, normed_2a), COL, 2)
-    out_first = swap_bits(after(out_far, normed_2b), COL, 2)
+    out_first = swap_bits(after(out_far, normed_2a), COL, 2)
     normed_3 = [swap_bits(normed_2a, COL, 1), swap_bits(normed_2b, COL, 1)]
     normed_all = [normed_0a, normed_0b, normed_2a, normed_2b]
     up_pre, act, q_rot, k_rot, v_low = forward_step(
@@ -827,9 +833,15 @@
     out_fourth = swap_bits(out_second, COL, 1)
     cots = [cot_0, cot_2, cot_b]
     cots_1 = [swap_bits(cot_0, COL, 1), swap_bits(cot_2, COL, 1), swap_bits(cot_b, COL, 1)]
-    mix_near, mix_far = spread(
-        [[act, attn], [act_1, attn_1]], [out_own, out_near], [out_first, out_second], False, 0, same
-    )
+    mix_near, mix_far, mix_both = spread(
+        [[act, attn], [act_1, attn_1]],
+        [out_own, out_near],
+        [out_first, out_second],
+        False,
+        local_rows,
+        same,
+    )
+    mix_b = lax.psum_scatter(mix_both, ROW, scatter_dimension=0, tiled=True)
     mix_recv = swap_bits(after(mix_far, cot_2), COL, 2)
     fc2_keep, fc2_send = grad_blocks(
         half, [([act, after(act_1, mix_far)], cots, True)], False
@@ -855,11 +867,9 @@
     )
     d_proj_1 = swap_bits(d_proj, COL, 1)
     fc2_near, fc2_far = sum_halves(fc2_keep, after(fc2_recv, d_proj))
-    mix_total = (mix_near.astype(f32) + mix_recv.astype(f32)).astype(bf16)
-    mixed = lax.psum_scatter(mix_total, ROW, scatter_dimension=0, tiled=True).astype(f32)
-    fc2_crossed = swap_bits(after(fc2_far, mix_total), COL, 2)
+    fc2_crossed = swap_bits(after(fc2_far, mix_recv), COL, 2)
     fc2_near_x = swap_bits(fc2_near, DP, 1)
-    near_a, near_b, far_a, far_b = spread(
+    near_a, far_a, both_b = spread(
         [[d_up, after(d_proj, fc2_far)], [d_up_1, d_proj_1]],
         [in_own, in_near],
         [in_2, in_pass],
@@ -867,7 +877,7 @@
         local_rows,
     )
     recv_a = swap_bits(after(far_a, fc2_crossed), COL, 2)
-    recv_b = swap_bits(after(far_b, fc2_crossed), COL, 2)
+    part_b = lax.psum_scatter(both_b, ROW, scatter_dimension=0, tiled=True)
     fc2_crossed_x = swap_bits(after(fc2_crossed, fc2_near_x), DP, 1)
     fc1_keep, fc1_send = grad_blocks(
         half, [(normed_all, [after(d_up, far_a), d_up_1], False)], False
@@ -883,21 +893,26 @@
     )
     total_a = (near_a.astype(f32) + recv_a.astype(f32)).astype(bf16)
     d_normed_a = lax.psum_scatter(total_a, ROW, scatter_dimension=0, tiled=True)
+    mix_total = (after(mix_near, total_a).astype(f32) + mix_recv.astype(f32)).astype(bf16)
+    mix_a = lax.psum_scatter(mix_total, ROW, scatter_dimension=0, tiled=True)
     (fc2_weight_grad,) = lay_out(
         places, [fc2_near, after(fc2_crossed, rest_send)], [fc2_near_x, fc2_crossed_x], 0
     )
     fc1_near, fc1_far = sum_halves(fc1_keep, after(fc1_recv, rest_send))
     rest_recv = swap_bits(after(rest_send, fc1_recv), DP, 1)
-    total_b = (near_b.astype(f32) + recv_b.astype(f32)).astype(bf16)
-    d_normed_b = lax.psum_scatter(total_b, ROW, scatter_dimension=0, tiled=True)
+    mix_recv_b = swap_bits(after(mix_b[:, local_width:], recv_a), COL, 2)
+    mixed_b = mix_b[:, :local_width].astype(f32) + mix_recv_b.astype(f32)
+    mixed = jnp.concatenate([mix_a.astype(f32), mixed_b], axis=0)
     fc1_near_x = swap_bits(after(fc1_near, rest_recv), DP, 1)
-    fc1_crossed = swap_bits(after(fc1_far, total_b), COL, 2)
-    rest_near, rest_far = sum_halves(rest_keep, after(rest_recv, total_b))
+    fc1_crossed = swap_bits(after(fc1_far, mix_recv_b), COL, 2)
+    part_recv = swap_bits(after(part_b[:, local_width:], fc1_crossed), COL, 2)
+    rest_near, rest_far = sum_halves(rest_keep, rest_recv)
     rest_near_x = swap_bits(after(rest_near, fc1_near_x), DP, 1)
-    rest_crossed = swap_bits(after(rest_far, fc1_crossed), COL, 2)
+    rest_crossed = swap_bits(after(rest_far, part_recv), COL, 2)
     rest_crossed_x = swap_bits(after(rest_crossed, rest_near_x), DP, 1)
     fc1_crossed_x = swap_bits(after(fc1_crossed, rest_crossed_x), DP, 1)
-    d_normed = jnp.concatenate([d_normed_a, d_normed_b], axis=0).astype(f32)
+    d_normed_b = part_b[:, :local_width].astype(f32) + part_recv.astype(f32)
+    d_normed = jnp.concatenate([d_normed_a.astype(f32), d_normed_b], axis=0)
     qkv_weight_grad, out_weight_grad = lay_out(
         places, [rest_near, rest_crossed], [rest_near_x, rest_crossed_x], 2
     )
@@ -911,16 +926,15 @@
     tokens_grad = out_grad.astype(f32) + inv_std[:, None] * (
         d_hat - back_sums[0][:, None] / full_width - centred * (back_sums[1][:, None] / full_width)
     )
-    vector_sums = total_over(
-        jnp.stack(
-            [
-                jnp.sum(d_normed * centred, axis=0),
-                jnp.sum(d_normed, axis=0),
-                jnp.sum(out_grad.astype(f32), axis=0),
-            ]
-        ),
-        (ROW, DP),
-    )
+    vectors = jnp.stack(
+        [
+            jnp.sum(d_normed * centred, axis=0),
+            jnp.sum(d_normed, axis=0),
+            jnp.sum(out_grad.astype(f32), axis=0),
+        ]
+    )
+    vectors = total_over(vectors, (DP,))
+    vector_sums = total_over(vectors, (ROW,))
     bias_sums = total_over(jnp.concatenate([qkv_sums, fc1_sums], axis=1), (DP,))[0]
     return (
         out,

time: 458 us -> 466 us (1.017)
  waiting for transfers between devices: 211 us -> 216 us
    ppermute x49 -> x50, waiting for transfers between devices: 169 us -> 189 us  [swap_bits(): lax.ppermute(value, axis, [(place, place ^ bit) for place in range(count)])]
    all_gather x1, waiting for transfers between devices: 16.9 us -> 0.01 us  [step(): lax.all_gather(after(out_grad[:, :cut], normed), ROW, axis=0, tiled=True)]
    ppermute x49 -> x50, starting transfers between devices: 46.5 us -> 49.9 us  [swap_bits(): lax.ppermute(value, axis, [(place, place ^ bit) for place in range(count)])]
  transfers between devices with their start and end apart: 56 -> 58, of which waited for: 27 -> 30; matrix products, arithmetic and copies ran while one was open for 7% -> 8% of each run, Pallas kernels for 30% -> 30%
where the time goes in v6:
time: 466 us; the launch traced here: 465 us
  waiting for transfers between devices  216 us (46%)
  Pallas kernels  142 us (30%)
  starting transfers between devices  50.7 us (11%)
  other arithmetic  22.3 us (5%)
  local copies, waits for them, and re-layouts  19.3 us (4%)
  between operations  14.6 us (3%)
    ppermute x50, waiting for transfers between devices, swap_bits(): lax.ppermute(value, axis, [(place, place ^ bit) for place in range(count)])  189 us
    ppermute x50, starting transfers between devices, swap_bits(): lax.ppermute(value, axis, [(place, place ^ bit) for place in range(count)])  49.9 us
    pallas_call x3, Pallas kernels, grad_blocks(): pl.pallas_call(kernel, grid_spec=pltpu.PrefetchScalarGridSpec(num_scalar_...  29.6 us
    all_gather x1, waiting for transfers between devices, step(): normed_0b = lax.all_gather(normed[:, cut:], ROW, axis=0, tiled=True)  26.5 us
    pallas_call x2, Pallas kernels, spread(): pl.pallas_call(kernel, grid=(rows // block,), in_specs=[rowed(hidden), ro...  22.1 us
    pallas_call x1, Pallas kernels, attend_back(): pl.pallas_call(kernel, grid_spec=pltpu.PrefetchScalarGridSpec(num_scalar_...  18 us
    pallas_call x1, Pallas kernels, forward_step(): pl.pallas_call(kernel, grid=(rows // block,), in_specs=[rowed(x.shape[1])...  16.1 us
    pallas_call x1, Pallas kernels, slope_step(): pl.pallas_call(kernel, grid=(rows // block,), in_specs=[rowed(g.shape[1])...  13.5 us
  transfers between devices with their start and end apart: 58, of which 30 were waited for; matrix products, arithmetic and copies ran while one was open for 8% of the time, Pallas kernels for 30%

profile of v6, /device:TPU:0, one launch (start us, length us, event | category | flops | bytes accessed | tf_op | source)
XLA Modules:
  0.0 465.4 jit_solution(7886863044943091448)
XLA Ops:
  35.6 6.2 %collective-permute-done.3.refs_1_ = bf16[512,384]{1,0:T(8,128)(2,1)S(1)} collective-permute-done((bf16[512,384]{1,0:T(8,128)(2,1)}, bf16[512,384]{1,0:T(8,128)(2,1)S(1)}, u32[]{:S(2)}, u32[]{:S(2)}) %collective-permute-start.3) | collective-permute-done | bytes 393248 | tf_op jit(solution)/shard_map/ppermute | solution.py:93
  43.2 4.9 %collective-permute-done.4 = bf16[512,256]{1,0:T(8,128)(2,1)S(1)} collective-permute-done((bf16[512,256]{1,0:T(8,128)(2,1)S(1)}, bf16[512,256]{1,0:T(8,128)(2,1)S(1)}, u32[]{:S(2)}, u32[]{:S(2)}) %collective-permute-start.4) | collective-permute-done | bytes 262176 | tf_op jit(solution)/shard_map/ppermute | solution.py:93
  49.7 26.5 %all-gather.7.cloned.1.call-done.refs_1_.refs_3_ = bf16[2048,256]{1,0:T(8,128)(2,1)} async-done(((bf16[512,256]{1,0:T(8,128)(2,1)}), bf16[2048,256]{1,0:T(8,128)(2,1)}) %all-gather.7.cloned.1.call-update) | async-done | bytes 1048592 | tf_op jit(solution)/shard_map/all_gather | solution.py:791
  79.6 11.6 %collective-permute-done.11.refs_2_ = bf16[512,512]{1,0:T(8,128)(2,1)} collective-permute-done((bf16[512,512]{1,0:T(8,128)(2,1)}, bf16[512,512]{1,0:T(8,128)(2,1)}, u32[]{:S(2)}, u32[]{:S(2)}) %collective-permute-start.11) | collective-permute-done | bytes 524320 | tf_op jit(solution)/shard_map/ppermute | solution.py:93
  94.1 6.3 %collective-permute-done.12.refs_3_ = bf16[512,384]{1,0:T(8,128)(2,1)S(1)} collective-permute-done((bf16[512,384]{1,0:T(8,128)(2,1)S(1)}, bf16[512,384]{1,0:T(8,128)(2,1)S(1)}, u32[]{:S(2)}, u32[]{:S(2)}) %collective-permute-start.12) | collective-permute-done | bytes 393248 | tf_op jit(solution)/shard_map/ppermute | solution.py:93
  100.9 5.8 %fusion = (f32[2048,128]{1,0:T(8,128)}, f32[2048,128]{1,0:T(8,128)}, f32[2048,128]{1,0:T(8,128)}) fusion(f32[128]{0:T(128)S(1)} %fusion.21, f32[2048]{0:T(1024)S(1)} %get-tuple-element.231, pred[128]{0:T(512)(128)(4,1)S(1)} %get-tuple-element.236, pred[128]{0:T(512)(128)(4,1)S(1)} %get-tuple-element.237, pred[128]{0:T(512)(128)(4,1)S(1)} %broadcast_compare_fusion.1), kind=kLoop, calls=%fused_computation.8 | loop fusion | flops 1310720 | bytes 3154816 | tf_op jit(solution)/shard_map/jit(_where)/select_n | solution.py:62
  112.6 16.1 %shard_map.205 = (f32[2048,512]{1,0:T(8,128)}, bf16[2048,512]{1,0:T(8,128)(2,1)}, bf16[2048,128]{1,0:T(8,128)(2,1)}, bf16[2048,128]{1,0:T(8,128)(2,1)}, bf16[2048,128]{1,0:T(8,128)(2,1)}) custom-call(bf16[2048,256]{1,0:T(8,128)(2,1)} %all-gather.5.cloned.1.call-done.refs_0_.refs_2_, bf16[2048,256]{1,0:T(8,128)(2,1)} %all-gather.7.cloned.1.call-done.refs_1_.refs_3_, ...), custom_call_target="tpu_custom_call" | custom-call | flops 7516192768 | bytes 18874368 | tf_op jit(solution)/shard_map/pallas_call | solution.py:201
  134.0 15.6 %collective-permute-done.17.refs_6_.refs_7_ = bf16[640,512]{1,0:T(8,128)(2,1)} collective-permute-done((bf16[640,512]{1,0:T(8,128)(2,1)}, bf16[640,512]{1,0:T(8,128)(2,1)}, u32[]{:S(2)}, u32[]{:S(2)}) %collective-permute-start.17) | collective-permute-done | bytes 655392 | tf_op jit(solution)/shard_map/ppermute | solution.py:93
  154.2 12.0 %shard_map.206 = (bf16[2048,128]{1,0:T(8,128)(2,1)}, f32[2048,128]{1,0:T(8,128)}, f32[2,2048]{1,0:T(2,128)}) custom-call(s32[4]{0:T(128)} %and_select_fusion.lowest_ref, bf16[2048,128]{1,0:T(8,128)(2,1)} %get-tuple-element.112.q_ref, bf16[2048,128]{1,0:T(8,128)(2,1)} %get-tuple-element.113.k_ref, bf16[2048,128]{1,0:T(8,128)(2,1)} %get-tuple-element.114.v_ref, ...), custom_call_target="tpu_custom_call" | custom-call | flops 1073741824 | bytes 3145728 | tf_op jit(solution)/shard_map/pallas_call | solution.py:611
  174.3 9.6 %shard_map.208 = (bf16[1024,512]{1,0:T(8,128)(2,1)}, bf16[1024,512]{1,0:T(8,128)(2,1)}, bf16[1024,1024]{1,0:T(8,128)(2,1)}) custom-call(bf16[2048,512]{1,0:T(8,128)(2,1)} %get-tuple-element.110.refs_0_, bf16[2048,128]{1,0:T(8,128)(2,1)} %get-tuple-element.115.refs_1_.refs_6_, bf16[2048,512]{1,0:T(8,128)(2,1)} %collective-permute-done.15.refs_2_.refs_1_, ...), custom_call_target="tpu_custom_call" | custom-call | flops 5368709120 | bytes 9437184 | tf_op jit(solution)/shard_map/pallas_call | solution.py:374
  184.8 9.4 %shard_map.209 = (bf16[4,256,512]{2,1,0:T(8,128)(2,1)}, bf16[4,256,512]{2,1,0:T(8,128)(2,1)}) custom-call(s32[1]{0:T(128)} %bitcast.15.half_ref, bf16[2048,512]{1,0:T(8,128)(2,1)} %get-tuple-element.110.refs_0_, bf16[2048,512]{1,0:T(8,128)(2,1)} %collective-permute-done.15.refs_2_.refs_1_, ...), custom_call_target="tpu_custom_call" | custom-call | flops 4294967296 | bytes 16777216 | tf_op jit(solution)/shard_map/pallas_call | solution.py:464
  194.3 13.5 %shard_map.210 = (bf16[2048,512]{1,0:T(8,128)(2,1)}, bf16[2048,128]{1,0:T(8,128)(2,1)}, f32[1,512]{1,0:T(1,128)}) custom-call(bf16[2048,256]{1,0:T(8,128)(2,1)} %all-gather.9.cloned.1.call-done.refs_2_.refs_0_.refs_8_, bf16[2048,256]{1,0:T(8,128)(2,1)} %collective-permute-done.19.refs_3_.refs_1_.refs_9_, ...), custom_call_target="tpu_custom_call" | custom-call | flops 5368709120 | bytes 14680064 | tf_op jit(solution)/shard_map/pallas_call | solution.py:263
  208.3 18.0 %shard_map.211 = (bf16[2048,384]{1,0:T(8,128)(2,1)}, f32[1,384]{1,0:T(1,128)}) custom-call(s32[4]{0:T(128)} %and_select_fusion.lowest_ref, bf16[2048,128]{1,0:T(8,128)(2,1)} %get-tuple-element.112.q_ref, bf16[2048,128]{1,0:T(8,128)(2,1)} %get-tuple-element.113.k_ref, bf16[2048,128]{1,0:T(8,128)(2,1)} %get-tuple-element.114.v_ref, ...), custom_call_target="tpu_custom_call" | custom-call | flops 2684354560 | bytes 4194304 | tf_op jit(solution)/shard_map/pallas_call | solution.py:716
  227.8 24.3 %collective-permute-done.26.received_ref = bf16[4,256,512]{2,1,0:T(8,128)(2,1)} collective-permute-done((bf16[4,256,512]{2,1,0:T(8,128)(2,1)}, bf16[4,256,512]{2,1,0:T(8,128)(2,1)}, u32[]{:S(2)}, u32[]{:S(2)}) %collective-permute-start.26) | collective-permute-done | bytes 1048608 | tf_op jit(solution)/shard_map/ppermute | solution.py:93
  254.8 12.4 %shard_map.213 = (bf16[1024,512]{1,0:T(8,128)(2,1)}, bf16[1024,512]{1,0:T(8,128)(2,1)}, bf16[1024,1024]{1,0:T(8,128)(2,1)}) custom-call(bf16[2048,512]{1,0:T(8,128)(2,1)} %get-tuple-element.150.refs_0_.refs_4_, bf16[2048,384]{1,0:T(8,128)(2,1)} %get-tuple-element.156.refs_1_.refs_0_, bf16[2048,512]{1,0:T(8,128)(2,1)} %collective-permute-done.27.refs_2_.refs_5_, ...), custom_call_target="tpu_custom_call" | custom-call | flops 7516192768 | bytes 11534336 | tf_op jit(solution)/shard_map/pallas_call | solution.py:374
  268.9 23.5 %collective-permute-done.29 = bf16[1024,512]{1,0:T(8,128)(2,1)} collective-permute-done((bf16[1024,512]{1,0:T(8,128)(2,1)}, bf16[1024,512]{1,0:T(8,128)(2,1)}, u32[]{:S(2)}, u32[]{:S(2)}) %collective-permute-start.29) | collective-permute-done | bytes 1048608 | tf_op jit(solution)/shard_map/ppermute | solution.py:93
  293.8 11.2 %collective-permute-done.30.refs_1_ = bf16[2,256,512]{2,1,0:T(8,128)(2,1)} collective-permute-done((bf16[2,256,512]{2,1,0:T(8,128)(2,1)S(1)}, bf16[2,256,512]{2,1,0:T(8,128)(2,1)}, u32[]{:S(2)}, u32[]{:S(2)}) %collective-permute-start.30) | collective-permute-done | bytes 524320 | tf_op jit(solution)/shard_map/ppermute | solution.py:93
  308.0 20.2 %collective-permute-done.31 = bf16[1024,512]{1,0:T(8,128)(2,1)S(1)} collective-permute-done((bf16[1024,512]{1,0:T(8,128)(2,1)}, bf16[1024,512]{1,0:T(8,128)(2,1)S(1)}, u32[]{:S(2)}, u32[]{:S(2)}) %collective-permute-start.31) | collective-permute-done | bytes 1048608 | tf_op jit(solution)/shard_map/ppermute | solution.py:93
  332.0 9.4 %shard_map.214 = (bf16[4,256,512]{2,1,0:T(8,128)(2,1)}, bf16[4,256,512]{2,1,0:T(8,128)(2,1)}) custom-call(s32[1]{0:T(128)} %bitcast.15.half_ref, bf16[2048,256]{1,0:T(8,128)(2,1)} %all-gather.5.cloned.1.call-done.refs_0_.refs_2_, bf16[2048,256]{1,0:T(8,128)(2,1)} %all-gather.7.cloned.1.call-done.refs_1_.refs_3_, ...), custom_call_target="tpu_custom_call" | custom-call | flops 4294967296 | bytes 16777216 | tf_op jit(solution)/shard_map/pallas_call | solution.py:464
  344.1 10.7 %shard_map.215 = (bf16[4,512,256]{2,1,0:T(8,128)(2,1)}, bf16[4,512,256]{2,1,0:T(8,128)(2,1)}) custom-call(s32[1]{0:T(128)} %bitcast.15.half_ref, bf16[2048,384]{1,0:T(8,128)(2,1)} %get-tuple-element.156.refs_1_.refs_0_, bf16[2048,384]{1,0:T(8,128)(2,1)} %collective-permute-done.28.refs_3_.refs_1_, ...), custom_call_target="tpu_custom_call" | custom-call | flops 4294967296 | bytes 16777216 | tf_op jit(solution)/shard_map/pallas_call | solution.py:464
  354.8 10.8 %collective-permute-done.35.received_ref = bf16[4,256,512]{2,1,0:T(8,128)(2,1)} collective-permute-done((bf16[4,256,512]{2,1,0:T(8,128)(2,1)}, bf16[4,256,512]{2,1,0:T(8,128)(2,1)}, u32[]{:S(2)}, u32[]{:S(2)}) %collective-permute-start.35) | collective-permute-done | bytes 1048608 | tf_op jit(solution)/shard_map/ppermute | solution.py:93
  381.7 9.1 %collective-permute-done.36.refs_1_ = bf16[2,256,512]{2,1,0:T(8,128)(2,1)} collective-permute-done((bf16[2,256,512]{2,1,0:T(8,128)(2,1)}, bf16[2,256,512]{2,1,0:T(8,128)(2,1)}, u32[]{:S(2)}, u32[]{:S(2)}) %collective-permute-start.36) | collective-permute-done | bytes 524320 | tf_op jit(solution)/shard_map/ppermute | solution.py:93
  407.4 7.5 %collective-permute-done.46.refs_2_ = bf16[2,512,256]{2,1,0:T(8,128)(2,1)} collective-permute-done((bf16[2,512,256]{2,1,0:T(8,128)(2,1)S(1)}, bf16[2,512,256]{2,1,0:T(8,128)(2,1)}, u32[]{:S(2)}, u32[]{:S(2)}) %collective-permute-start.46) | collective-permute-done | bytes 524320 | tf_op jit(solution)/shard_map/ppermute | solution.py:93
  419.6 10.8 %collective-permute-done.40 = f32[3,512]{1,0:T(4,128)S(1)} collective-permute-done((f32[3,512]{1,0:T(4,128)S(1)}, f32[3,512]{1,0:T(4,128)S(1)}, u32[]{:S(2)}, u32[]{:S(2)}) %collective-permute-start.40) | collective-permute-done | bytes 6176 | tf_op jit(solution)/shard_map/ppermute | solution.py:93
  (207 shorter events, 145.6 us)
Async XLA Ops:
  7.2 41.0 %all-gather.5.cloned.1.call-start = ((), (), s32[]{:S(2)}) async-start(), calls=%async_computation.4 | async-start | bytes 1310720 | tf_op jit(solution)/shard_map/all_gather | solution.py:790
  16.7 59.4 %all-gather.7.cloned.1.call-start = ((), (), s32[]{:S(2)}) async-start(), calls=%async_computation.5 | async-start | bytes 1310720 | tf_op jit(solution)/shard_map/all_gather | solution.py:791
  20.7 113.3 %all-gather.9.cloned.1.call-start = ((), (), s32[]{:S(2)}) async-start(), calls=%async_computation.6 | async-start | bytes 1310720 | tf_op jit(solution)/shard_map/all_gather | solution.py:798
  48.2 28.0 %collective-permute-start.5 = (bf16[2048,256]{1,0:T(8,128)(2,1)}, bf16[2048,256]{1,0:T(8,128)(2,1)}, u32[]{:S(2)}, u32[]{:S(2)}) collective-permute-start(bf16[2048,256]{1,0:T(8,128)(2,1)} %all-gather.5.cloned.1.call-done.refs_0_.refs_2_), channel_id=1, source_target_pairs={{0,2},{1,3},{2,0},{3,1},{4,6},{5,7},{6,4},{7,5},{8,10},{9,11},{10,... | collective-permute-start | bytes 3145736 | tf_op jit(solution)/shard_map/ppermute | solution.py:93
  49.6 102.6 %all-gather.11.cloned.1.call-start = ((), (), s32[]{:S(2)}) async-start(), calls=%async_computation.7 | async-start | bytes 2621440 | tf_op jit(solution)/shard_map/all_gather | solution.py:799
  76.2 24.7 %collective-permute-start.6 = (bf16[2048,256]{1,0:T(8,128)(2,1)}, bf16[2048,256]{1,0:T(8,128)(2,1)}, u32[]{:S(2)}, u32[]{:S(2)}) collective-permute-start(bf16[2048,256]{1,0:T(8,128)(2,1)} %all-gather.7.cloned.1.call-done.refs_1_.refs_3_), channel_id=1, source_target_pairs={{0,2},{1,3},{2,0},{3,1},{4,6},{5,7},{6,4},{7,5},{8,10},{9,11},{10,... | collective-permute-start | bytes 3145736 | tf_op jit(solution)/shard_map/ppermute | solution.py:93
  79.5 30.1 %collective-permute-start.13 = (bf16[512,896]{1,0:T(8,128)(2,1)}, bf16[512,896]{1,0:T(8,128)(2,1)}, u32[]{:S(2)}, u32[]{:S(2)}) collective-permute-start(bf16[512,896]{1,0:T(8,128)(2,1)} %get-tuple-element.108.refs_5_), channel_id=1, source_target_pairs={{0,1},{1,0},{2,3},{3,2},{4,5},{5,4},{6,7},{7,6},{8,9},{9,8},{10,11... | collective-permute-start | bytes 2752520 | tf_op jit(solution)/shard_map/ppermute | solution.py:93
  93.5 273.9 %reduce-scatter.7.cloned.1.call-start = ((), (), s32[]{:S(2)}) async-start(), calls=%async_computation.9 | async-start | bytes 2621440 | tf_op jit(solution)/shard_map/reduce_scatter | solution.py:844
  128.6 45.7 %collective-permute-start.15 = (bf16[2048,512]{1,0:T(8,128)(2,1)}, bf16[2048,512]{1,0:T(8,128)(2,1)}, u32[]{:S(2)}, u32[]{:S(2)}) collective-permute-start(bf16[2048,512]{1,0:T(8,128)(2,1)} %get-tuple-element.110.refs_0_), channel_id=1, source_target_pairs={{0,1},{1,0},{2,3},{3,2},{4,5},{5,4},{6,7},{7,6},{8,9},{9,8},{10,11... | collective-permute-start | bytes 6291464 | tf_op jit(solution)/shard_map/ppermute | solution.py:93
  149.6 24.7 %collective-permute-start.19 = (bf16[2048,256]{1,0:T(8,128)(2,1)}, bf16[2048,256]{1,0:T(8,128)(2,1)}, u32[]{:S(2)}, u32[]{:S(2)}) collective-permute-start(bf16[2048,256]{1,0:T(8,128)(2,1)} %all-gather.9.cloned.1.call-done.refs_2_.refs_0_.refs_8_), channel_id=1, source_target_pairs={{0,2},{1,3},{2,0},{3,1},{4,6},{5,7},{6,4},{7,5},{8,10},{9,11},{10,... | collective-permute-start | bytes 3145736 | tf_op jit(solution)/shard_map/ppermute | solution.py:93
  152.2 42.1 %collective-permute-start.22 = (bf16[2048,512]{1,0:T(8,128)(2,1)}, bf16[2048,512]{1,0:T(8,128)(2,1)}, u32[]{:S(2)}, u32[]{:S(2)}) collective-permute-start(bf16[2048,512]{1,0:T(8,128)(2,1)} %all-gather.11.cloned.1.call-done.refs_4_.refs_2_.refs_10_), channel_id=1, source_target_pairs={{0,1},{1,0},{2,3},{3,2},{4,5},{5,4},{6,7},{7,6},{8,9},{9,8},{10,11... | collective-permute-start | bytes 6291464 | tf_op jit(solution)/shard_map/ppermute | solution.py:93
  169.7 24.6 %collective-permute-start.20 = (bf16[2048,256]{1,0:T(8,128)(2,1)}, bf16[2048,256]{1,0:T(8,128)(2,1)}, u32[]{:S(2)}, u32[]{:S(2)}) collective-permute-start(bf16[2048,256]{1,0:T(8,128)(2,1)} %all-gather.9.cloned.1.call-done.refs_2_.refs_0_.refs_8_), channel_id=1, source_target_pairs={{0,1},{1,0},{2,3},{3,2},{4,5},{5,4},{6,7},{7,6},{8,9},{9,8},{10,11... | collective-permute-start | bytes 3145736 | tf_op jit(solution)/shard_map/ppermute | solution.py:93
  174.3 20.0 %collective-permute-start.21 = (bf16[2048,256]{1,0:T(8,128)(2,1)}, bf16[2048,256]{1,0:T(8,128)(2,1)}, u32[]{:S(2)}, u32[]{:S(2)}) collective-permute-start(bf16[2048,256]{1,0:T(8,128)(2,1)} %collective-permute-done.19.refs_3_.refs_1_.refs_9_), channel_id=1, source_target_pairs={{0,1},{1,0},{2,3},{3,2},{4,5},{5,4},{6,7},{7,6},{8,9},{9,8},{10,11... | collective-permute-start | bytes 3145736 | tf_op jit(solution)/shard_map/ppermute | solution.py:93
  183.9 196.1 %reduce-scatter.11.cloned.1.call-start = ((), (), s32[]{:S(2)}) async-start(), calls=%async_computation.11 | async-start | bytes 2621440 | tf_op jit(solution)/shard_map/reduce_scatter | solution.py:880
  207.8 47.0 %collective-permute-start.27 = (bf16[2048,512]{1,0:T(8,128)(2,1)}, bf16[2048,512]{1,0:T(8,128)(2,1)}, u32[]{:S(2)}, u32[]{:S(2)}) collective-permute-start(bf16[2048,512]{1,0:T(8,128)(2,1)} %get-tuple-element.150.refs_0_.refs_4_), channel_id=1, source_target_pairs={{0,1},{1,0},{2,3},{3,2},{4,5},{5,4},{6,7},{7,6},{8,9},{9,8},{10,11... | collective-permute-start | bytes 6291464 | tf_op jit(solution)/shard_map/ppermute | solution.py:93
  226.2 28.5 %collective-permute-start.28 = (bf16[2048,384]{1,0:T(8,128)(2,1)}, bf16[2048,384]{1,0:T(8,128)(2,1)}, u32[]{:S(2)}, u32[]{:S(2)}) collective-permute-start(bf16[2048,384]{1,0:T(8,128)(2,1)} %get-tuple-element.156.refs_1_.refs_0_), channel_id=1, source_target_pairs={{0,1},{1,0},{2,3},{3,2},{4,5},{5,4},{6,7},{7,6},{8,9},{9,8},{10,11... | collective-permute-start | bytes 4718600 | tf_op jit(solution)/shard_map/ppermute | solution.py:93
  226.3 25.8 %collective-permute-start.26 = (bf16[4,256,512]{2,1,0:T(8,128)(2,1)}, bf16[4,256,512]{2,1,0:T(8,128)(2,1)}, u32[]{:S(2)}, u32[]{:S(2)}) collective-permute-start(bf16[4,256,512]{2,1,0:T(8,128)(2,1)} %get-tuple-element.137), channel_id=1, source_target_pairs={{0,16},{16,0},{1,17},{17,1},{2,18},{18,2},{3,19},{19,3},{4,20},{20... | collective-permute-start | bytes 3145736 | tf_op jit(solution)/shard_map/ppermute | solution.py:93
  267.3 127.9 %reduce-scatter.9.cloned.1.call-start = ((), (), s32[]{:S(2)}) async-start(), calls=%async_computation.10 | async-start | bytes 1310720 | tf_op jit(solution)/shard_map/reduce_scatter | solution.py:895
  267.3 25.0 %collective-permute-start.29 = (bf16[1024,512]{1,0:T(8,128)(2,1)}, bf16[1024,512]{1,0:T(8,128)(2,1)}, u32[]{:S(2)}, u32[]{:S(2)}) collective-permute-start(bf16[1024,512]{1,0:T(8,128)(2,1)} %get-tuple-element.143), channel_id=1, source_target_pairs={{0,2},{1,3},{2,0},{3,1},{4,6},{5,7},{6,4},{7,5},{8,10},{9,11},{10,... | collective-permute-start | bytes 3145736 | tf_op jit(solution)/shard_map/ppermute | solution.py:93
  305.0 23.1 %collective-permute-start.31 = (bf16[1024,512]{1,0:T(8,128)(2,1)}, bf16[1024,512]{1,0:T(8,128)(2,1)S(1)}, u32[]{:S(2)}, u32[]{:S(2)}) collective-permute-start(bf16[1024,512]{1,0:T(8,128)(2,1)} %get-tuple-element.145), channel_id=1, source_target_pairs={{0,2},{1,3},{2,0},{3,1},{4,6},{5,7},{6,4},{7,5},{8,10},{9,11},{10,... | collective-permute-start | bytes 3145736 | tf_op jit(solution)/shard_map/ppermute | solution.py:93
  306.5 23.2 %collective-permute-start.33 = (bf16[2,256,512]{2,1,0:T(8,128)(2,1)S(1)}, bf16[2,256,512]{2,1,0:T(8,128)(2,1)S(1)}, u32[]{:S(2)}, u32[]{:S(2)}) collective-permute-start(bf16[2,256,512]{2,1,0:T(8,128)(2,1)S(1)} %copy-done.5), channel_id=1, source_target_pairs={{0,16},{16,0},{1,17},{17,1},{2,18},{18,2},{3,19},{19,3},{4,20},{20... | collective-permute-start | bytes 1572872 | tf_op jit(solution)/shard_map/ppermute | solution.py:93
  329.4 73.4 %reduce-scatter.5.cloned.1.call-start = ((), (), s32[]{:S(2)}) async-start(), calls=%async_computation.8 | async-start | bytes 1310720 | tf_op jit(solution)/shard_map/reduce_scatter | solution.py:897
  342.3 23.3 %collective-permute-start.35 = (bf16[4,256,512]{2,1,0:T(8,128)(2,1)}, bf16[4,256,512]{2,1,0:T(8,128)(2,1)}, u32[]{:S(2)}, u32[]{:S(2)}) collective-permute-start(bf16[4,256,512]{2,1,0:T(8,128)(2,1)} %get-tuple-element.155), channel_id=1, source_target_pairs={{0,16},{16,0},{1,17},{17,1},{2,18},{18,2},{3,19},{19,3},{4,20},{20... | collective-permute-start | bytes 3145736 | tf_op jit(solution)/shard_map/ppermute | solution.py:93
  365.6 26.6 %collective-permute-start.43 = (bf16[4,512,256]{2,1,0:T(8,128)(2,1)}, bf16[4,512,256]{2,1,0:T(8,128)(2,1)}, u32[]{:S(2)}, u32[]{:S(2)}) collective-permute-start(bf16[4,512,256]{2,1,0:T(8,128)(2,1)} %get-tuple-element.163), channel_id=1, source_target_pairs={{0,16},{16,0},{1,17},{17,1},{2,18},{18,2},{3,19},{19,3},{4,20},{20... | collective-permute-start | bytes 3145736 | tf_op jit(solution)/shard_map/ppermute | solution.py:93
  (51 other events, 712.6 us)
Sparse Core Ops, SparseCore 0:
  16.9 29.7 all-gather.4
  48.8 27.3 all-gather.6
  77.7 27.3 all-gather.8
  107.1 45.0 all-gather.10
  184.1 43.5 reduce-scatter.6
  267.4 43.4 reduce-scatter.10
  329.6 27.1 reduce-scatter.8
  373.5 25.7 reduce-scatter.4

commit v7 on v6

--- a/solution.py
+++ b/solution.py
@@ -364,7 +364,7 @@
             for piece in range(block // part):
                 spot = slice(piece * cut, (piece + 1) * cut)
                 outs[place][spot] = total[piece * part : piece * part + cut]
-                outs[2][spot, place * width : (place + 1) * width] = total[
+                outs[2][piece * part + place * cut : piece * part + (place + 1) * cut] = total[
                     piece * part + cut : (piece + 1) * part
                 ]
 
@@ -380,13 +380,13 @@
         out_specs=[
             pl.BlockSpec((block // 2, width), lambda i: (i, 0)),
             pl.BlockSpec((block // 2, width), lambda i: (i, 0)),
-            pl.BlockSpec((block // 2, 2 * width), lambda i: (i, 0)),
+            pl.BlockSpec((block, width), lambda i: (i, 0)),
         ],
         scratch_shapes=[pltpu.VMEM(w.shape, bf16) for w in far_mats] if flags else [],
         out_shape=[
             jax.ShapeDtypeStruct((rows // 2, width), bf16),
             jax.ShapeDtypeStruct((rows // 2, width), bf16),
-            jax.ShapeDtypeStruct((rows // 2, 2 * width), bf16),
+            jax.ShapeDtypeStruct((rows, width), bf16),
         ],
         compiler_params=params(),
         cost_estimate=cost(
@@ -543,6 +543,79 @@
         compiler_params=params(),
         cost_estimate=cost(0, 24 * mine[0].size),
     )(places, *mine, *theirs)
+
+
+def column(row):
+    return jnp.broadcast_to(row, (8, row.shape[1])).T[:, :1]
+
+
+def norm_terms(tokens_ref, stats_ref, gain_ref, first_ref, both_ref, far_ref):
+    cut = first_ref.shape[0]
+    x_hat = (tokens_ref[...].astype(f32) - column(stats_ref[0:1])) * column(stats_ref[1:2])
+    d_normed = jnp.concatenate(
+        [
+            first_ref[...].astype(f32),
+            both_ref[:cut].astype(f32) + far_ref[...].astype(f32),
+        ],
+        axis=0,
+    )
+    return x_hat, d_normed, d_normed * gain_ref[...]
+
+
+def norm_sums(tokens, stats, gain, first, both, far, cot_sum):
+    def kernel(*refs):
+        x_hat, d_normed, d_hat = norm_terms(*refs[:6])
+        cot_ref, rows_o, vectors_o = refs[6:]
+        rows_o[0:1] = jnp.sum(d_hat.T, axis=0, keepdims=True)
+        rows_o[1:2] = jnp.sum((d_hat * x_hat).T, axis=0, keepdims=True)
+        vectors_o[0:1] = jnp.sum(d_normed * x_hat, axis=0, keepdims=True)
+        vectors_o[1:2] = jnp.sum(d_normed, axis=0, keepdims=True)
+        vectors_o[2:3] = cot_ref[...]
+
+    rows, width = tokens.shape
+    return pl.pallas_call(
+        kernel,
+        out_shape=[
+            jax.ShapeDtypeStruct((2, rows), f32),
+            jax.ShapeDtypeStruct((3, width), f32),
+        ],
+        compiler_params=params(),
+        cost_estimate=cost(12 * tokens.size, 5 * tokens.size),
+    )(tokens, stats, gain, first, both, far, cot_sum)
+
+
+def norm_back(tokens, stats, gain, first, both, far, sums, out_grad, full_width):
+    def kernel(*refs):
+        x_hat, _, d_hat = norm_terms(*refs[:6])
+        stats_ref, sums_ref, cot_ref, out_ref = refs[1], refs[6], refs[7], refs[8]
+        inv_std = column(stats_ref[1:2])
+        mean = column(sums_ref[0:1]) / full_width
+        slope = column(sums_ref[1:2]) / full_width
+        out_ref[...] = cot_ref[...].astype(f32) + inv_std * (d_hat - mean - x_hat * slope)
+
+    return pl.pallas_call(
+        kernel,
+        out_shape=jax.ShapeDtypeStruct(tokens.shape, f32),
+        compiler_params=params(),
+        cost_estimate=cost(12 * tokens.size, 11 * tokens.size),
+    )(tokens, stats, gain, first, both, far, sums, out_grad)
+
+
+def output_sum(tokens, first, both, far, bias):
+    cut = first.shape[0]
+
+    def kernel(tokens_ref, first_ref, both_ref, far_ref, bias_ref, out_ref):
+        base = tokens_ref[...].astype(f32) + bias_ref[...]
+        out_ref[:cut] = (base[:cut] + first_ref[...].astype(f32)).astype(bf16)
+        mixed = both_ref[:cut].astype(f32) + far_ref[...].astype(f32)
+        out_ref[cut:] = (base[cut:] + mixed).astype(bf16)
+
+    return pl.pallas_call(
+        kernel,
+        out_shape=jax.ShapeDtypeStruct(tokens.shape, bf16),
+        compiler_params=params(),
+        cost_estimate=cost(4 * tokens.size, 7 * tokens.size),
+    )(tokens, first, both, far, bias)
 
 
 def attend(lowest, q_rot, k_rot, v_low, begin):
@@ -862,15 +935,17 @@
             far = (far.astype(f32) + swap_bits(far, DP, bit).astype(f32)).astype(bf16)
         return near, far
 
+    fc1_keep, fc1_send = grad_blocks(half, [(normed_all, [d_up, d_up_1], False)], False)
+    fc2_near, fc2_far = sum_halves(fc2_keep, after(fc2_recv, fc1_send))
+    fc1_recv = swap_bits(after(fc1_send, fc2_recv), DP, 1)
+    fc2_crossed = swap_bits(after(fc2_far, mix_recv), COL, 2)
     d_proj, qkv_sums = attend_back(
-        lowest, q_rot, k_rot, v_low, begin, d_attn, attn_full, lse, tables
+        lowest, q_rot, k_rot, v_low, begin, after(d_attn, fc2_near), attn_full, lse, tables
     )
     d_proj_1 = swap_bits(d_proj, COL, 1)
-    fc2_near, fc2_far = sum_halves(fc2_keep, after(fc2_recv, d_proj))
-    fc2_crossed = swap_bits(after(fc2_far, mix_recv), COL, 2)
-    fc2_near_x = swap_bits(fc2_near, DP, 1)
+    fc2_near_x = swap_bits(after(fc2_near, fc1_recv), DP, 1)
     near_a, far_a, both_b = spread(
-        [[d_up, after(d_proj, fc2_far)], [d_up_1, d_proj_1]],
+        [[d_up, d_proj], [d_up_1, d_proj_1]],
         [in_own, in_near],
         [in_2, in_pass],
         True,
@@ -879,62 +954,49 @@
     recv_a = swap_bits(after(far_a, fc2_crossed), COL, 2)
     part_b = lax.psum_scatter(both_b, ROW, scatter_dimension=0, tiled=True)
     fc2_crossed_x = swap_bits(after(fc2_crossed, fc2_near_x), DP, 1)
-    fc1_keep, fc1_send = grad_blocks(
-        half, [(normed_all, [after(d_up, far_a), d_up_1], False)], False
-    )
-    fc1_recv = swap_bits(after(fc1_send, fc2_crossed_x), DP, 1)
     rest_keep, rest_send = grad_blocks(
         half,
         [
-            ([after(d_proj, fc1_send), d_proj_1], normed_all, True),
+            ([after(d_proj, far_a), d_proj_1], normed_all, True),
             ([attn, attn_1], cots, True),
         ],
         True,
     )
+    rest_recv = swap_bits(after(rest_send, fc2_crossed_x), DP, 1)
+    fc1_near, fc1_far = sum_halves(fc1_keep, after(fc1_recv, rest_send))
     total_a = (near_a.astype(f32) + recv_a.astype(f32)).astype(bf16)
     d_normed_a = lax.psum_scatter(total_a, ROW, scatter_dimension=0, tiled=True)
     mix_total = (after(mix_near, total_a).astype(f32) + mix_recv.astype(f32)).astype(bf16)
     mix_a = lax.psum_scatter(mix_total, ROW, scatter_dimension=0, tiled=True)
+    fc1_crossed = swap_bits(after(fc1_far, recv_a), COL, 2)
+    cut = local_rows // 2
+    mix_recv_b = swap_bits(after(mix_b[cut:], fc1_crossed), COL, 2)
+    part_recv = swap_bits(after(part_b[cut:], mix_recv_b), COL, 2)
     (fc2_weight_grad,) = lay_out(
         places, [fc2_near, after(fc2_crossed, rest_send)], [fc2_near_x, fc2_crossed_x], 0
     )
     fc1_near, fc1_far = sum_halves(fc1_keep, after(fc1_recv, rest_send))
     rest_recv = swap_bits(after(rest_send, fc1_recv), DP, 1)
-    mix_recv_b = swap_bits(after(mix_b[:, local_width:], recv_a), COL, 2)
-    mixed_b = mix_b[:, :local_width].astype(f32) + mix_recv_b.astype(f32)
-    mixed = jnp.concatenate([mix_a.astype(f32), mixed_b], axis=0)
-    fc1_near_x = swap_bits(after(fc1_near, rest_recv), DP, 1)
-    fc1_crossed = swap_bits(after(fc1_far, mix_recv_b), COL, 2)
-    part_recv = swap_bits(after(part_b[:, local_width:], fc1_crossed), COL, 2)
     rest_near, rest_far = sum_halves(rest_keep, rest_recv)
-    rest_near_x = swap_bits(after(rest_near, fc1_near_x), DP, 1)
+    rest_near_x = swap_bits(after(rest_near, rest_recv), DP, 1)
     rest_crossed = swap_bits(after(rest_far, part_recv), COL, 2)
     rest_crossed_x = swap_bits(after(rest_crossed, rest_near_x), DP, 1)
-    fc1_crossed_x = swap_bits(after(fc1_crossed, rest_crossed_x), DP, 1)
-    d_normed_b = part_b[:, :local_width].astype(f32) + part_recv.astype(f32)
-    d_normed = jnp.concatenate([d_normed_a.astype(f32), d_normed_b], axis=0)
+    fc1_near_x = swap_bits(after(fc1_near, rest_crossed_x), DP, 1)
+    fc1_crossed_x = swap_bits(after(fc1_crossed, fc1_near_x), DP, 1)
     qkv_weight_grad, out_weight_grad = lay_out(
         places, [rest_near, rest_crossed], [rest_near_x, rest_crossed_x], 2
     )
     (fc1_weight_grad,) = lay_out(places, [fc1_near, fc1_crossed], [fc1_near_x, fc1_crossed_x], 1)
 
-    out = (token_f + mixed + out_bias).astype(bf16)
-    d_hat = d_normed * ln_gain
-    back_sums = total_over(
-        jnp.stack([jnp.sum(d_hat, axis=1), jnp.sum(d_hat * centred, axis=1)]), (COL,)
-    )
-    tokens_grad = out_grad.astype(f32) + inv_std[:, None] * (
-        d_hat - back_sums[0][:, None] / full_width - centred * (back_sums[1][:, None] / full_width)
-    )
-    vectors = jnp.stack(
-        [
-            jnp.sum(d_normed * centred, axis=0),
-            jnp.sum(d_normed, axis=0),
-            jnp.sum(out_grad.astype(f32), axis=0),
-        ]
-    )
+    stats = jnp.stack([row_mean, inv_std])
+    cot_sum = jnp.sum(out_grad.astype(f32), axis=0, keepdims=True)
+    terms = (tokens, stats, ln_gain.reshape(1, -1), d_normed_a, part_b, part_recv)
+    row_sums, vectors = norm_sums(*terms, cot_sum)
     vectors = total_over(vectors, (DP,))
+    row_sums = total_over(row_sums, (COL,))
     vector_sums = total_over(vectors, (ROW,))
+    tokens_grad = norm_back(*terms, row_sums, out_grad, full_width)
+    out = output_sum(tokens, mix_a, mix_b, mix_recv_b, out_bias.reshape(1, -1))
     bias_sums = total_over(jnp.concatenate([qkv_sums, fc1_sums], axis=1), (DP,))[0]
     return (
         out,

time: 466 us -> 489 us (1.049)
  waiting for transfers between devices: 216 us -> 238 us
  Pallas kernels: 142 us -> 151 us
  starting transfers between devices: 50.7 us -> 44 us
    all_gather x1, waiting for transfers between devices: 0.01 us -> 16.4 us  [step(): lax.all_gather(after(out_grad[:, :cut], normed), ROW, axis=0, tiled=True)]
    pallas_call x0 -> x3, Pallas kernels: none -> 8.89 us  [the longest x1 3.44 us: norm_back(): pl.pallas_call(kernel, out_shape=jax.ShapeDtypeStruct(tokens.shape, f32),...]
    ppermute x50, starting transfers between devices: 49.9 us -> 43 us  [swap_bits(): lax.ppermute(value, axis, [(place, place ^ bit) for place in range(count)])]
    ppermute x50, waiting for transfers between devices: 189 us -> 196 us  [swap_bits(): lax.ppermute(value, axis, [(place, place ^ bit) for place in range(count)])]
  transfers between devices with their start and end apart: 58 -> 58, of which waited for: 30 -> 29; matrix products, arithmetic and copies ran while one was open for 8% -> 7% of each run, Pallas kernels for 30% -> 27%
where the time goes in v7:
time: 489 us; the launch traced here: 488 us
  waiting for transfers between devices  238 us (49%)
  Pallas kernels  151 us (31%)
  starting transfers between devices  44 us (9%)
  local copies, waits for them, and re-layouts  21.1 us (4%)
  other arithmetic  19.9 us (4%)
  between operations  14.4 us (3%)
    ppermute x50, waiting for transfers between devices, swap_bits(): lax.ppermute(value, axis, [(place, place ^ bit) for place in range(count)])  196 us
    ppermute x50, starting transfers between devices, swap_bits(): lax.ppermute(value, axis, [(place, place ^ bit) for place in range(count)])  43 us
    pallas_call x3, Pallas kernels, grad_blocks(): pl.pallas_call(kernel, grid_spec=pltpu.PrefetchScalarGridSpec(num_scalar_...  29.8 us
    all_gather x1, waiting for transfers between devices, step(): normed_0b = lax.all_gather(normed[:, cut:], ROW, axis=0, tiled=True)  25.6 us
    pallas_call x2, Pallas kernels, spread(): pl.pallas_call(kernel, grid=(rows // block,), in_specs=[rowed(hidden), ro...  22 us
    pallas_call x1, Pallas kernels, attend_back(): pl.pallas_call(kernel, grid_spec=pltpu.PrefetchScalarGridSpec(num_scalar_...  17.9 us
    all_gather x1, waiting for transfers between devices, step(): lax.all_gather(after(out_grad[:, :cut], normed), ROW, axis=0, tiled=True)  16.4 us
    pallas_call x1, Pallas kernels, forward_step(): pl.pallas_call(kernel, grid=(rows // block,), in_specs=[rowed(x.shape[1])...  15.6 us
  transfers between devices with their start and end apart: 58, of which 29 were waited for; matrix products, arithmetic and copies ran while one was open for 7% of the time, Pallas kernels for 27%

profile of v7, /device:TPU:0, one launch (start us, length us, event | category | flops | bytes accessed | tf_op | source)
XLA Modules:
  0.0 488.4 jit_solution(8890094289881370422)
XLA Ops:
  50.5 25.6 %all-gather.7.cloned.1.call-done.refs_1_.refs_3_ = bf16[2048,256]{1,0:T(8,128)(2,1)} async-done(((bf16[512,256]{1,0:T(8,128)(2,1)}), bf16[2048,256]{1,0:T(8,128)(2,1)}) %all-gather.7.cloned.1.call-update) | async-done | bytes 1048592 | tf_op jit(solution)/shard_map/all_gather | solution.py:864
  79.5 11.3 %collective-permute-done.11.refs_2_ = bf16[512,512]{1,0:T(8,128)(2,1)} collective-permute-done((bf16[512,512]{1,0:T(8,128)(2,1)}, bf16[512,512]{1,0:T(8,128)(2,1)}, u32[]{:S(2)}, u32[]{:S(2)}) %collective-permute-start.11) | collective-permute-done | bytes 524320 | tf_op jit(solution)/shard_map/ppermute | solution.py:93
  93.0 7.1 %collective-permute-done.12.refs_3_ = bf16[512,384]{1,0:T(8,128)(2,1)S(1)} collective-permute-done((bf16[512,384]{1,0:T(8,128)(2,1)S(1)}, bf16[512,384]{1,0:T(8,128)(2,1)S(1)}, u32[]{:S(2)}, u32[]{:S(2)}) %collective-permute-start.12) | collective-permute-done | bytes 393248 | tf_op jit(solution)/shard_map/ppermute | solution.py:93
  112.9 15.6 %shard_map.205 = (f32[2048,512]{1,0:T(8,128)}, bf16[2048,512]{1,0:T(8,128)(2,1)}, bf16[2048,128]{1,0:T(8,128)(2,1)}, bf16[2048,128]{1,0:T(8,128)(2,1)}, bf16[2048,128]{1,0:T(8,128)(2,1)}) custom-call(bf16[2048,256]{1,0:T(8,128)(2,1)} %all-gather.5.cloned.1.call-done.refs_0_.refs_2_, bf16[2048,256]{1,0:T(8,128)(2,1)} %all-gather.7.cloned.1.call-done.refs_1_.refs_3_, ...), custom_call_target="tpu_custom_call" | custom-call | flops 7516192768 | bytes 18874368 | tf_op jit(solution)/shard_map/pallas_call | solution.py:201
  134.7 16.4 %all-gather.9.cloned.1.call-done.refs_2_.refs_0_.refs_8_ = bf16[2048,256]{1,0:T(8,128)(2,1)} async-done(((bf16[512,256]{1,0:T(8,128)(2,1)}), bf16[2048,256]{1,0:T(8,128)(2,1)}) %all-gather.9.cloned.1.call-update) | async-done | bytes 1048592 | tf_op jit(solution)/shard_map/all_gather | solution.py:871
  153.1 12.0 %shard_map.206 = (bf16[2048,128]{1,0:T(8,128)(2,1)}, f32[2048,128]{1,0:T(8,128)}, f32[2,2048]{1,0:T(2,128)}) custom-call(s32[4]{0:T(128)} %and_select_fusion.lowest_ref, bf16[2048,128]{1,0:T(8,128)(2,1)} %get-tuple-element.114.q_ref, bf16[2048,128]{1,0:T(8,128)(2,1)} %get-tuple-element.115.k_ref, bf16[2048,128]{1,0:T(8,128)(2,1)} %get-tuple-element.116.v_ref, ...), custom_call_target="tpu_custom_call" | custom-call | flops 1073741824 | bytes 3145728 | tf_op jit(solution)/shard_map/pallas_call | solution.py:684
  167.6 8.2 %collective-permute-done.19.refs_3_.refs_1_.refs_9_ = bf16[2048,256]{1,0:T(8,128)(2,1)} collective-permute-done((bf16[2048,256]{1,0:T(8,128)(2,1)}, bf16[2048,256]{1,0:T(8,128)(2,1)}, u32[]{:S(2)}, u32[]{:S(2)}) %collective-permute-start.19) | collective-permute-done | bytes 1048608 | tf_op jit(solution)/shard_map/ppermute | solution.py:93
  183.2 9.6 %shard_map.208 = (bf16[1024,512]{1,0:T(8,128)(2,1)}, bf16[1024,512]{1,0:T(8,128)(2,1)}, bf16[2048,512]{1,0:T(8,128)(2,1)}) custom-call(bf16[2048,512]{1,0:T(8,128)(2,1)} %get-tuple-element.112.refs_0_, bf16[2048,128]{1,0:T(8,128)(2,1)} %get-tuple-element.117.refs_1_.refs_6_, bf16[2048,512]{1,0:T(8,128)(2,1)} %collective-permute-done.15.refs_2_.refs_1_, ...), custom_call_target="tpu_custom_call" | custom-call | flops 5368709120 | bytes 9437184 | tf_op jit(solution)/shard_map/pallas_call | solution.py:374
  192.8 9.5 %shard_map.209 = (bf16[4,256,512]{2,1,0:T(8,128)(2,1)}, bf16[4,256,512]{2,1,0:T(8,128)(2,1)}) custom-call(s32[1]{0:T(128)} %bitcast.15.half_ref, bf16[2048,512]{1,0:T(8,128)(2,1)} %get-tuple-element.112.refs_0_, bf16[2048,512]{1,0:T(8,128)(2,1)} %collective-permute-done.15.refs_2_.refs_1_, ...), custom_call_target="tpu_custom_call" | custom-call | flops 4294967296 | bytes 16777216 | tf_op jit(solution)/shard_map/pallas_call | solution.py:464
  202.3 13.5 %shard_map.210 = (bf16[2048,512]{1,0:T(8,128)(2,1)}, bf16[2048,128]{1,0:T(8,128)(2,1)}, f32[1,512]{1,0:T(1,128)}) custom-call(bf16[2048,256]{1,0:T(8,128)(2,1)} %all-gather.9.cloned.1.call-done.refs_2_.refs_0_.refs_8_, bf16[2048,256]{1,0:T(8,128)(2,1)} %collective-permute-done.19.refs_3_.refs_1_.refs_9_, ...), custom_call_target="tpu_custom_call" | custom-call | flops 5368709120 | bytes 14680064 | tf_op jit(solution)/shard_map/pallas_call | solution.py:263
  220.3 9.5 %shard_map.211 = (bf16[4,256,512]{2,1,0:T(8,128)(2,1)}, bf16[4,256,512]{2,1,0:T(8,128)(2,1)}) custom-call(s32[1]{0:T(128)} %bitcast.15.half_ref, bf16[2048,256]{1,0:T(8,128)(2,1)} %all-gather.5.cloned.1.call-done.refs_0_.refs_2_, bf16[2048,256]{1,0:T(8,128)(2,1)} %all-gather.7.cloned.1.call-done.refs_1_.refs_3_, ...), custom_call_target="tpu_custom_call" | custom-call | flops 4294967296 | bytes 16777216 | tf_op jit(solution)/shard_map/pallas_call | solution.py:464
  229.8 12.2 %collective-permute-done.26.received_ref = bf16[4,256,512]{2,1,0:T(8,128)(2,1)} collective-permute-done((bf16[4,256,512]{2,1,0:T(8,128)(2,1)}, bf16[4,256,512]{2,1,0:T(8,128)(2,1)}, u32[]{:S(2)}, u32[]{:S(2)}) %collective-permute-start.26) | collective-permute-done | bytes 1048608 | tf_op jit(solution)/shard_map/ppermute | solution.py:93
  244.7 17.9 %shard_map.213 = (bf16[2048,384]{1,0:T(8,128)(2,1)}, f32[1,384]{1,0:T(1,128)}) custom-call(s32[4]{0:T(128)} %and_select_fusion.lowest_ref, bf16[2048,128]{1,0:T(8,128)(2,1)} %get-tuple-element.114.q_ref, bf16[2048,128]{1,0:T(8,128)(2,1)} %get-tuple-element.115.k_ref, bf16[2048,128]{1,0:T(8,128)(2,1)} %get-tuple-element.116.v_ref, ...), custom_call_target="tpu_custom_call" | custom-call | flops 2684354560 | bytes 4194304 | tf_op jit(solution)/shard_map/pallas_call | solution.py:789
  266.4 12.4 %shard_map.214 = (bf16[1024,512]{1,0:T(8,128)(2,1)}, bf16[1024,512]{1,0:T(8,128)(2,1)}, bf16[2048,512]{1,0:T(8,128)(2,1)}) custom-call(bf16[2048,512]{1,0:T(8,128)(2,1)} %get-tuple-element.133.refs_4_.refs_0_, bf16[2048,384]{1,0:T(8,128)(2,1)} %get-tuple-element.154.refs_1_.refs_0_, bf16[2048,512]{1,0:T(8,128)(2,1)} %collective-permute-done.27.refs_5_.refs_2_, ...), custom_call_target="tpu_custom_call" | custom-call | flops 7516192768 | bytes 11534336 | tf_op jit(solution)/shard_map/pallas_call | solution.py:374
  280.6 24.7 %collective-permute-done.29 = bf16[1024,512]{1,0:T(8,128)(2,1)} collective-permute-done((bf16[1024,512]{1,0:T(8,128)(2,1)S(1)}, bf16[1024,512]{1,0:T(8,128)(2,1)}, u32[]{:S(2)}, u32[]{:S(2)}) %collective-permute-start.29) | collective-permute-done | bytes 1048608 | tf_op jit(solution)/shard_map/ppermute | solution.py:93
  305.9 12.7 %collective-permute-done.30.refs_1_ = bf16[2,256,512]{2,1,0:T(8,128)(2,1)S(1)} collective-permute-done((bf16[2,256,512]{2,1,0:T(8,128)(2,1)}, bf16[2,256,512]{2,1,0:T(8,128)(2,1)S(1)}, u32[]{:S(2)}, u32[]{:S(2)}) %collective-permute-start.30) | collective-permute-done | bytes 524320 | tf_op jit(solution)/shard_map/ppermute | solution.py:93
  320.7 21.8 %collective-permute-done.31 = bf16[1024,512]{1,0:T(8,128)(2,1)S(1)} collective-permute-done((bf16[1024,512]{1,0:T(8,128)(2,1)}, bf16[1024,512]{1,0:T(8,128)(2,1)S(1)}, u32[]{:S(2)}, u32[]{:S(2)}) %collective-permute-start.31) | collective-permute-done | bytes 1048608 | tf_op jit(solution)/shard_map/ppermute | solution.py:93
  344.0 10.8 %shard_map.215 = (bf16[4,512,256]{2,1,0:T(8,128)(2,1)}, bf16[4,512,256]{2,1,0:T(8,128)(2,1)}) custom-call(s32[1]{0:T(128)} %bitcast.15.half_ref, bf16[2048,384]{1,0:T(8,128)(2,1)} %get-tuple-element.154.refs_1_.refs_0_, bf16[2048,384]{1,0:T(8,128)(2,1)} %collective-permute-done.28.refs_3_.refs_1_, ...), custom_call_target="tpu_custom_call" | custom-call | flops 4294967296 | bytes 16777216 | tf_op jit(solution)/shard_map/pallas_call | solution.py:464
  360.4 9.3 %collective-permute-done.33.refs_1_ = bf16[2,256,512]{2,1,0:T(8,128)(2,1)S(1)} collective-permute-done((bf16[2,256,512]{2,1,0:T(8,128)(2,1)}, bf16[2,256,512]{2,1,0:T(8,128)(2,1)S(1)}, u32[]{:S(2)}, u32[]{:S(2)}) %collective-permute-start.33) | collective-permute-done | bytes 524320 | tf_op jit(solution)/shard_map/ppermute | solution.py:93
  386.4 7.8 %collective-permute-done.43.refs_2_ = bf16[2,512,256]{2,1,0:T(8,128)(2,1)} collective-permute-done((bf16[2,512,256]{2,1,0:T(8,128)(2,1)}, bf16[2,512,256]{2,1,0:T(8,128)(2,1)}, u32[]{:S(2)}, u32[]{:S(2)}) %collective-permute-start.43) | collective-permute-done | bytes 524320 | tf_op jit(solution)/shard_map/ppermute | solution.py:93
  398.1 12.8 %collective-permute-done.44.refs_3_ = bf16[2,512,256]{2,1,0:T(8,128)(2,1)S(1)} collective-permute-done((bf16[2,512,256]{2,1,0:T(8,128)(2,1)S(1)}, bf16[2,512,256]{2,1,0:T(8,128)(2,1)S(1)}, u32[]{:S(2)}, u32[]{:S(2)}) %collective-permute-start.44) | collective-permute-done | bytes 524320 | tf_op jit(solution)/shard_map/ppermute | solution.py:93
  414.3 8.0 %collective-permute-done.48.refs_2_ = bf16[2,256,512]{2,1,0:T(8,128)(2,1)} collective-permute-done((bf16[2,256,512]{2,1,0:T(8,128)(2,1)}, bf16[2,256,512]{2,1,0:T(8,128)(2,1)}, u32[]{:S(2)}, u32[]{:S(2)}) %collective-permute-start.48) | collective-permute-done | bytes 524320 | tf_op jit(solution)/shard_map/ppermute | solution.py:93
  428.0 11.9 %collective-permute-done.38 = f32[3,512]{1,0:T(4,128)S(1)} collective-permute-done((f32[3,512]{1,0:T(4,128)}, f32[3,512]{1,0:T(4,128)S(1)}, u32[]{:S(2)}, u32[]{:S(2)}) %collective-permute-start.38) | collective-permute-done | bytes 6176 | tf_op jit(solution)/shard_map/ppermute | solution.py:93
  445.5 6.9 %collective-permute-done.45 = f32[1,896]{1,0:T(1,128)S(1)} collective-permute-done((f32[1,896]{1,0:T(1,128)S(1)}, f32[1,896]{1,0:T(1,128)S(1)}, u32[]{:S(2)}, u32[]{:S(2)}) %collective-permute-start.45) | collective-permute-done | bytes 3616 | tf_op jit(solution)/shard_map/ppermute | solution.py:93
  (195 shorter events, 166.4 us)
Async XLA Ops:
  7.2 41.0 %all-gather.5.cloned.1.call-start = ((), (), s32[]{:S(2)}) async-start(), calls=%async_computation.4 | async-start | bytes 1310720 | tf_op jit(solution)/shard_map/all_gather | solution.py:863
  16.7 59.4 %all-gather.7.cloned.1.call-start = ((), (), s32[]{:S(2)}) async-start(), calls=%async_computation.5 | async-start | bytes 1310720 | tf_op jit(solution)/shard_map/all_gather | solution.py:864
  20.7 113.5 %all-gather.11.cloned.1.call-start = ((), (), s32[]{:S(2)}) async-start(), calls=%async_computation.7 | async-start | bytes 2621440 | tf_op jit(solution)/shard_map/all_gather | solution.py:872
  48.2 28.0 %collective-permute-start.5 = (bf16[2048,256]{1,0:T(8,128)(2,1)}, bf16[2048,256]{1,0:T(8,128)(2,1)}, u32[]{:S(2)}, u32[]{:S(2)}) collective-permute-start(bf16[2048,256]{1,0:T(8,128)(2,1)} %all-gather.5.cloned.1.call-done.refs_0_.refs_2_), channel_id=1, source_target_pairs={{0,2},{1,3},{2,0},{3,1},{4,6},{5,7},{6,4},{7,5},{8,10},{9,11},{10,... | collective-permute-start | bytes 3145736 | tf_op jit(solution)/shard_map/ppermute | solution.py:93
  50.5 100.6 %all-gather.9.cloned.1.call-start = ((), (), s32[]{:S(2)}) async-start(), calls=%async_computation.6 | async-start | bytes 1310720 | tf_op jit(solution)/shard_map/all_gather | solution.py:871
  76.2 24.7 %collective-permute-start.6 = (bf16[2048,256]{1,0:T(8,128)(2,1)}, bf16[2048,256]{1,0:T(8,128)(2,1)}, u32[]{:S(2)}, u32[]{:S(2)}) collective-permute-start(bf16[2048,256]{1,0:T(8,128)(2,1)} %all-gather.7.cloned.1.call-done.refs_1_.refs_3_), channel_id=1, source_target_pairs={{0,2},{1,3},{2,0},{3,1},{4,6},{5,7},{6,4},{7,5},{8,10},{9,11},{10,... | collective-permute-start | bytes 3145736 | tf_op jit(solution)/shard_map/ppermute | solution.py:93
  79.5 30.6 %collective-permute-start.13 = (bf16[512,896]{1,0:T(8,128)(2,1)}, bf16[512,896]{1,0:T(8,128)(2,1)}, u32[]{:S(2)}, u32[]{:S(2)}) collective-permute-start(bf16[512,896]{1,0:T(8,128)(2,1)} %get-tuple-element.110.refs_5_), channel_id=1, source_target_pairs={{0,1},{1,0},{2,3},{3,2},{4,5},{5,4},{6,7},{7,6},{8,9},{9,8},{10,11... | collective-permute-start | bytes 2752520 | tf_op jit(solution)/shard_map/ppermute | solution.py:93
  110.1 249.3 %reduce-scatter.7.cloned.1.call-start = ((), (), s32[]{:S(2)}) async-start(), calls=%async_computation.9 | async-start | bytes 2621440 | tf_op jit(solution)/shard_map/reduce_scatter | solution.py:917
  128.5 54.1 %collective-permute-start.15 = (bf16[2048,512]{1,0:T(8,128)(2,1)}, bf16[2048,512]{1,0:T(8,128)(2,1)}, u32[]{:S(2)}, u32[]{:S(2)}) collective-permute-start(bf16[2048,512]{1,0:T(8,128)(2,1)} %get-tuple-element.112.refs_0_), channel_id=1, source_target_pairs={{0,1},{1,0},{2,3},{3,2},{4,5},{5,4},{6,7},{7,6},{8,9},{9,8},{10,11... | collective-permute-start | bytes 6291464 | tf_op jit(solution)/shard_map/ppermute | solution.py:93
  133.7 31.5 %collective-permute-start.23 = (bf16[640,512]{1,0:T(8,128)(2,1)}, bf16[640,512]{1,0:T(8,128)(2,1)}, u32[]{:S(2)}, u32[]{:S(2)}) collective-permute-start(bf16[640,512]{1,0:T(8,128)(2,1)} %get-tuple-element.120.refs_5_), channel_id=1, source_target_pairs={{0,1},{1,0},{2,3},{3,2},{4,5},{5,4},{6,7},{7,6},{8,9},{9,8},{10,11... | collective-permute-start | bytes 1966088 | tf_op jit(solution)/shard_map/ppermute | solution.py:93
  134.2 68.1 %collective-permute-start.22 = (bf16[2048,512]{1,0:T(8,128)(2,1)}, bf16[2048,512]{1,0:T(8,128)(2,1)}, u32[]{:S(2)}, u32[]{:S(2)}) collective-permute-start(bf16[2048,512]{1,0:T(8,128)(2,1)} %all-gather.11.cloned.1.call-done.refs_4_.refs_2_.refs_10_), channel_id=1, source_target_pairs={{0,1},{1,0},{2,3},{3,2},{4,5},{5,4},{6,7},{7,6},{8,9},{9,8},{10,11... | collective-permute-start | bytes 6291464 | tf_op jit(solution)/shard_map/ppermute | solution.py:93
  151.1 24.7 %collective-permute-start.19 = (bf16[2048,256]{1,0:T(8,128)(2,1)}, bf16[2048,256]{1,0:T(8,128)(2,1)}, u32[]{:S(2)}, u32[]{:S(2)}) collective-permute-start(bf16[2048,256]{1,0:T(8,128)(2,1)} %all-gather.9.cloned.1.call-done.refs_2_.refs_0_.refs_8_), channel_id=1, source_target_pairs={{0,2},{1,3},{2,0},{3,1},{4,6},{5,7},{6,4},{7,5},{8,10},{9,11},{10,... | collective-permute-start | bytes 3145736 | tf_op jit(solution)/shard_map/ppermute | solution.py:93
  167.4 34.8 %collective-permute-start.20 = (bf16[2048,256]{1,0:T(8,128)(2,1)}, bf16[2048,256]{1,0:T(8,128)(2,1)}, u32[]{:S(2)}, u32[]{:S(2)}) collective-permute-start(bf16[2048,256]{1,0:T(8,128)(2,1)} %all-gather.9.cloned.1.call-done.refs_2_.refs_0_.refs_8_), channel_id=1, source_target_pairs={{0,1},{1,0},{2,3},{3,2},{4,5},{5,4},{6,7},{7,6},{8,9},{9,8},{10,11... | collective-permute-start | bytes 3145736 | tf_op jit(solution)/shard_map/ppermute | solution.py:93
  175.8 26.5 %collective-permute-start.21 = (bf16[2048,256]{1,0:T(8,128)(2,1)}, bf16[2048,256]{1,0:T(8,128)(2,1)}, u32[]{:S(2)}, u32[]{:S(2)}) collective-permute-start(bf16[2048,256]{1,0:T(8,128)(2,1)} %collective-permute-done.19.refs_3_.refs_1_.refs_9_), channel_id=1, source_target_pairs={{0,1},{1,0},{2,3},{3,2},{4,5},{5,4},{6,7},{7,6},{8,9},{9,8},{10,11... | collective-permute-start | bytes 3145736 | tf_op jit(solution)/shard_map/ppermute | solution.py:93
  215.9 154.3 %reduce-scatter.11.cloned.1.call-start = ((), (), s32[]{:S(2)}) async-start(), calls=%async_computation.11 | async-start | bytes 2621440 | tf_op jit(solution)/shard_map/reduce_scatter | solution.py:955
  216.1 25.9 %collective-permute-start.26 = (bf16[4,256,512]{2,1,0:T(8,128)(2,1)}, bf16[4,256,512]{2,1,0:T(8,128)(2,1)}, u32[]{:S(2)}, u32[]{:S(2)}) collective-permute-start(bf16[4,256,512]{2,1,0:T(8,128)(2,1)} %get-tuple-element.136), channel_id=1, source_target_pairs={{0,16},{16,0},{1,17},{17,1},{2,18},{18,2},{3,19},{19,3},{4,20},{20... | collective-permute-start | bytes 3145736 | tf_op jit(solution)/shard_map/ppermute | solution.py:93
  278.8 144.9 %reduce-scatter.9.cloned.1.call-start = ((), (), s32[]{:S(2)}) async-start(), calls=%async_computation.10 | async-start | bytes 1310720 | tf_op jit(solution)/shard_map/reduce_scatter | solution.py:968
  280.0 25.3 %collective-permute-start.29 = (bf16[1024,512]{1,0:T(8,128)(2,1)S(1)}, bf16[1024,512]{1,0:T(8,128)(2,1)}, u32[]{:S(2)}, u32[]{:S(2)}) collective-permute-start(bf16[1024,512]{1,0:T(8,128)(2,1)S(1)} %copy-done.12), channel_id=1, source_target_pairs={{0,2},{1,3},{2,0},{3,1},{4,6},{5,7},{6,4},{7,5},{8,10},{9,11},{10,... | collective-permute-start | bytes 3145736 | tf_op jit(solution)/shard_map/ppermute | solution.py:93
  319.2 35.6 %collective-permute-start.32 = (bf16[4,256,512]{2,1,0:T(8,128)(2,1)}, bf16[4,256,512]{2,1,0:T(8,128)(2,1)}, u32[]{:S(2)}, u32[]{:S(2)}) collective-permute-start(bf16[4,256,512]{2,1,0:T(8,128)(2,1)} %get-tuple-element.153), channel_id=1, source_target_pairs={{0,16},{16,0},{1,17},{17,1},{2,18},{18,2},{3,19},{19,3},{4,20},{20... | collective-permute-start | bytes 3145736 | tf_op jit(solution)/shard_map/ppermute | solution.py:93
  343.7 116.8 %reduce-scatter.5.cloned.1.call-start = ((), (), s32[]{:S(2)}) async-start(), calls=%async_computation.8 | async-start | bytes 1310720 | tf_op jit(solution)/shard_map/reduce_scatter | solution.py:970
  397.0 25.3 %collective-permute-start.48 = (bf16[2,256,512]{2,1,0:T(8,128)(2,1)}, bf16[2,256,512]{2,1,0:T(8,128)(2,1)}, u32[]{:S(2)}, u32[]{:S(2)}) collective-permute-start(bf16[2,256,512]{2,1,0:T(8,128)(2,1)} %get-tuple-element.179.refs_0_), channel_id=1, source_target_pairs={{0,16},{16,0},{1,17},{17,1},{2,18},{18,2},{3,19},{19,3},{4,20},{20... | collective-permute-start | bytes 1572872 | tf_op jit(solution)/shard_map/ppermute | solution.py:93
  411.7 31.2 %collective-permute-start.46 = (bf16[2,256,512]{2,1,0:T(8,128)(2,1)}, bf16[2,256,512]{2,1,0:T(8,128)(2,1)}, u32[]{:S(2)}, u32[]{:S(2)}) collective-permute-start(bf16[2,256,512]{2,1,0:T(8,128)(2,1)} %get-tuple-element.176.refs_0_), channel_id=1, source_target_pairs={{0,16},{16,0},{1,17},{17,1},{2,18},{18,2},{3,19},{19,3},{4,20},{20... | collective-permute-start | bytes 1572872 | tf_op jit(solution)/shard_map/ppermute | solution.py:93
  422.2 34.0 %collective-permute-start.49 = (bf16[2,256,512]{2,1,0:T(8,128)(2,1)}, bf16[2,256,512]{2,1,0:T(8,128)(2,1)}, u32[]{:S(2)}, u32[]{:S(2)}) collective-permute-start(bf16[2,256,512]{2,1,0:T(8,128)(2,1)} %copy-done.2), channel_id=1, source_target_pairs={{0,16},{16,0},{1,17},{17,1},{2,18},{18,2},{3,19},{19,3},{4,20},{20... | collective-permute-start | bytes 1572872 | tf_op jit(solution)/shard_map/ppermute | solution.py:93
  442.9 34.3 %collective-permute-start.47 = (bf16[2,256,512]{2,1,0:T(8,128)(2,1)}, bf16[2,256,512]{2,1,0:T(8,128)(2,1)}, u32[]{:S(2)}, u32[]{:S(2)}) collective-permute-start(bf16[2,256,512]{2,1,0:T(8,128)(2,1)} %copy-done.3), channel_id=1, source_target_pairs={{0,16},{16,0},{1,17},{17,1},{2,18},{18,2},{3,19},{19,3},{4,20},{20... | collective-permute-start | bytes 1572872 | tf_op jit(solution)/shard_map/ppermute | solution.py:93
  (48 other events, 763.9 us)
Sparse Core Ops, SparseCore 0:
  16.9 29.7 all-gather.4
  48.8 27.3 all-gather.6
  77.7 45.0 all-gather.10
  124.2 26.7 all-gather.8
  216.0 42.2 reduce-scatter.6
  278.9 42.1 reduce-scatter.10
  343.9 25.7 reduce-scatter.8
  380.4 26.6 reduce-scatter.4

commit v8 on v7

--- a/solution.py
+++ b/solution.py
@@ -935,17 +935,21 @@
             far = (far.astype(f32) + swap_bits(far, DP, bit).astype(f32)).astype(bf16)
         return near, far
 
-    fc1_keep, fc1_send = grad_blocks(half, [(normed_all, [d_up, d_up_1], False)], False)
-    fc2_near, fc2_far = sum_halves(fc2_keep, after(fc2_recv, fc1_send))
+    mix_total = (after(mix_near, d_up).astype(f32) + mix_recv.astype(f32)).astype(bf16)
+    mix_a = lax.psum_scatter(mix_total, ROW, scatter_dimension=0, tiled=True)
+    fc1_keep, fc1_send = grad_blocks(
+        half, [(normed_all, [after(d_up, mix_total), d_up_1], False)], False
+    )
     fc1_recv = swap_bits(after(fc1_send, fc2_recv), DP, 1)
+    d_proj, qkv_sums = attend_back(
+        lowest, q_rot, k_rot, v_low, begin, after(d_attn, fc1_send), attn_full, lse, tables
+    )
+    d_proj_1 = swap_bits(d_proj, COL, 1)
+    fc2_near, fc2_far = sum_halves(fc2_keep, after(fc2_recv, d_proj))
     fc2_crossed = swap_bits(after(fc2_far, mix_recv), COL, 2)
-    d_proj, qkv_sums = attend_back(
-        lowest, q_rot, k_rot, v_low, begin, after(d_attn, fc2_near), attn_full, lse, tables
-    )
-    d_proj_1 = swap_bits(d_proj, COL, 1)
     fc2_near_x = swap_bits(after(fc2_near, fc1_recv), DP, 1)
     near_a, far_a, both_b = spread(
-        [[d_up, d_proj], [d_up_1, d_proj_1]],
+        [[d_up, after(d_proj, fc2_near)], [d_up_1, d_proj_1]],
         [in_own, in_near],
         [in_2, in_pass],
         True,
@@ -966,19 +970,15 @@
     fc1_near, fc1_far = sum_halves(fc1_keep, after(fc1_recv, rest_send))
     total_a = (near_a.astype(f32) + recv_a.astype(f32)).astype(bf16)
     d_normed_a = lax.psum_scatter(total_a, ROW, scatter_dimension=0, tiled=True)
-    mix_total = (after(mix_near, total_a).astype(f32) + mix_recv.astype(f32)).astype(bf16)
-    mix_a = lax.psum_scatter(mix_total, ROW, scatter_dimension=0, tiled=True)
     fc1_crossed = swap_bits(after(fc1_far, recv_a), COL, 2)
+    rest_near, rest_far = sum_halves(rest_keep, rest_recv)
+    rest_near_x = swap_bits(after(rest_near, rest_recv), DP, 1)
     cut = local_rows // 2
     mix_recv_b = swap_bits(after(mix_b[cut:], fc1_crossed), COL, 2)
     part_recv = swap_bits(after(part_b[cut:], mix_recv_b), COL, 2)
     (fc2_weight_grad,) = lay_out(
-        places, [fc2_near, after(fc2_crossed, rest_send)], [fc2_near_x, fc2_crossed_x], 0
-    )
-    fc1_near, fc1_far = sum_halves(fc1_keep, after(fc1_recv, rest_send))
-    rest_recv = swap_bits(after(rest_send, fc1_recv), DP, 1)
-    rest_near, rest_far = sum_halves(rest_keep, rest_recv)
-    rest_near_x = swap_bits(after(rest_near, rest_recv), DP, 1)
+        places, [fc2_near, after(fc2_crossed, rest_near)], [fc2_near_x, fc2_crossed_x], 0
+    )
     rest_crossed = swap_bits(after(rest_far, part_recv), COL, 2)
     rest_crossed_x = swap_bits(after(rest_crossed, rest_near_x), DP, 1)
     fc1_near_x = swap_bits(after(fc1_near, rest_crossed_x), DP, 1)

time: 489 us -> 494 us (1.010)
  waiting for transfers between devices: 238 us -> 245 us
    ppermute x50, waiting for transfers between devices: 196 us -> 203 us  [swap_bits(): lax.ppermute(value, axis, [(place, place ^ bit) for place in range(count)])]
  transfers between devices with their start and end apart: 58 -> 58, of which waited for: 29 -> 28; matrix products, arithmetic and copies ran while one was open for 7% -> 7% of each run, Pallas kernels for 27% -> 27%
where the time goes in v8:
time: 494 us; the launch traced here: 493 us
  waiting for transfers between devices  245 us (50%)
  Pallas kernels  151 us (31%)
  starting transfers between devices  43 us (9%)
  local copies, waits for them, and re-layouts  20.8 us (4%)
  other arithmetic  18.4 us (4%)
  between operations  14.5 us (3%)
    ppermute x50, waiting for transfers between devices, swap_bits(): lax.ppermute(value, axis, [(place, place ^ bit) for place in range(count)])  203 us
    ppermute x50, starting transfers between devices, swap_bits(): lax.ppermute(value, axis, [(place, place ^ bit) for place in range(count)])  42 us
    pallas_call x3, Pallas kernels, grad_blocks(): pl.pallas_call(kernel, grid_spec=pltpu.PrefetchScalarGridSpec(num_scalar_...  29.6 us
    all_gather x1, waiting for transfers between devices, step(): normed_0b = lax.all_gather(normed[:, cut:], ROW, axis=0, tiled=True)  25.6 us
    pallas_call x2, Pallas kernels, spread(): pl.pallas_call(kernel, grid=(rows // block,), in_specs=[rowed(hidden), ro...  22.1 us
    pallas_call x1, Pallas kernels, attend_back(): pl.pallas_call(kernel, grid_spec=pltpu.PrefetchScalarGridSpec(num_scalar_...  17.9 us
    all_gather x1, waiting for transfers between devices, step(): lax.all_gather(after(out_grad[:, :cut], normed), ROW, axis=0, tiled=True)  16.4 us
    pallas_call x1, Pallas kernels, forward_step(): pl.pallas_call(kernel, grid=(rows // block,), in_specs=[rowed(x.shape[1])...  15.6 us
  transfers between devices with their start and end apart: 58, of which 28 were waited for; matrix products, arithmetic and copies ran while one was open for 7% of the time, Pallas kernels for 27%

profile of v8, /device:TPU:0, one launch (start us, length us, event | category | flops | bytes accessed | tf_op | source)
XLA Modules:
  0.0 492.7 jit_solution(18357089875239869314)
XLA Ops:
  50.5 25.6 %all-gather.7.cloned.1.call-done.refs_1_.refs_3_ = bf16[2048,256]{1,0:T(8,128)(2,1)} async-done(((bf16[512,256]{1,0:T(8,128)(2,1)}), bf16[2048,256]{1,0:T(8,128)(2,1)}) %all-gather.7.cloned.1.call-update) | async-done | bytes 1048592 | tf_op jit(solution)/shard_map/all_gather | solution.py:864
  79.5 11.3 %collective-permute-done.11.refs_2_ = bf16[512,512]{1,0:T(8,128)(2,1)} collective-permute-done((bf16[512,512]{1,0:T(8,128)(2,1)}, bf16[512,512]{1,0:T(8,128)(2,1)}, u32[]{:S(2)}, u32[]{:S(2)}) %collective-permute-start.11) | collective-permute-done | bytes 524320 | tf_op jit(solution)/shard_map/ppermute | solution.py:93
  93.0 7.1 %collective-permute-done.12.refs_3_ = bf16[512,384]{1,0:T(8,128)(2,1)S(1)} collective-permute-done((bf16[512,384]{1,0:T(8,128)(2,1)S(1)}, bf16[512,384]{1,0:T(8,128)(2,1)S(1)}, u32[]{:S(2)}, u32[]{:S(2)}) %collective-permute-start.12) | collective-permute-done | bytes 393248 | tf_op jit(solution)/shard_map/ppermute | solution.py:93
  112.9 15.6 %shard_map.205 = (f32[2048,512]{1,0:T(8,128)}, bf16[2048,512]{1,0:T(8,128)(2,1)}, bf16[2048,128]{1,0:T(8,128)(2,1)}, bf16[2048,128]{1,0:T(8,128)(2,1)}, bf16[2048,128]{1,0:T(8,128)(2,1)}) custom-call(bf16[2048,256]{1,0:T(8,128)(2,1)} %all-gather.5.cloned.1.call-done.refs_0_.refs_2_, bf16[2048,256]{1,0:T(8,128)(2,1)} %all-gather.7.cloned.1.call-done.refs_1_.refs_3_, ...), custom_call_target="tpu_custom_call" | custom-call | flops 7516192768 | bytes 18874368 | tf_op jit(solution)/shard_map/pallas_call | solution.py:201
  134.7 16.4 %all-gather.9.cloned.1.call-done.refs_2_.refs_0_.refs_8_ = bf16[2048,256]{1,0:T(8,128)(2,1)} async-done(((bf16[512,256]{1,0:T(8,128)(2,1)}), bf16[2048,256]{1,0:T(8,128)(2,1)}) %all-gather.9.cloned.1.call-update) | async-done | bytes 1048592 | tf_op jit(solution)/shard_map/all_gather | solution.py:871
  153.1 12.0 %shard_map.206 = (bf16[2048,128]{1,0:T(8,128)(2,1)}, f32[2048,128]{1,0:T(8,128)}, f32[2,2048]{1,0:T(2,128)}) custom-call(s32[4]{0:T(128)} %and_select_fusion.lowest_ref, bf16[2048,128]{1,0:T(8,128)(2,1)} %get-tuple-element.116.q_ref, bf16[2048,128]{1,0:T(8,128)(2,1)} %get-tuple-element.117.k_ref, bf16[2048,128]{1,0:T(8,128)(2,1)} %get-tuple-element.118.v_ref, ...), custom_call_target="tpu_custom_call" | custom-call | flops 1073741824 | bytes 3145728 | tf_op jit(solution)/shard_map/pallas_call | solution.py:684
  167.5 8.3 %collective-permute-done.19.refs_3_.refs_1_.refs_9_ = bf16[2048,256]{1,0:T(8,128)(2,1)} collective-permute-done((bf16[2048,256]{1,0:T(8,128)(2,1)}, bf16[2048,256]{1,0:T(8,128)(2,1)}, u32[]{:S(2)}, u32[]{:S(2)}) %collective-permute-start.19) | collective-permute-done | bytes 1048608 | tf_op jit(solution)/shard_map/ppermute | solution.py:93
  175.8 6.8 %collective-permute-done.18.refs_7_.refs_10_ = bf16[640,512]{1,0:T(8,128)(2,1)} collective-permute-done((bf16[640,512]{1,0:T(8,128)(2,1)}, bf16[640,512]{1,0:T(8,128)(2,1)}, u32[]{:S(2)}, u32[]{:S(2)}) %collective-permute-start.18) | collective-permute-done | bytes 655392 | tf_op jit(solution)/shard_map/ppermute | solution.py:93
  183.1 9.6 %shard_map.208 = (bf16[1024,512]{1,0:T(8,128)(2,1)}, bf16[1024,512]{1,0:T(8,128)(2,1)}, bf16[2048,512]{1,0:T(8,128)(2,1)}) custom-call(bf16[2048,512]{1,0:T(8,128)(2,1)} %get-tuple-element.114.refs_0_, bf16[2048,128]{1,0:T(8,128)(2,1)} %get-tuple-element.119.refs_1_.refs_6_, bf16[2048,512]{1,0:T(8,128)(2,1)} %collective-permute-done.15.refs_2_.refs_1_, ...), custom_call_target="tpu_custom_call" | custom-call | flops 5368709120 | bytes 9437184 | tf_op jit(solution)/shard_map/pallas_call | solution.py:374
  192.7 9.4 %shard_map.209 = (bf16[4,256,512]{2,1,0:T(8,128)(2,1)}, bf16[4,256,512]{2,1,0:T(8,128)(2,1)}) custom-call(s32[1]{0:T(128)} %bitcast.15.half_ref, bf16[2048,512]{1,0:T(8,128)(2,1)} %get-tuple-element.114.refs_0_, bf16[2048,512]{1,0:T(8,128)(2,1)} %collective-permute-done.15.refs_2_.refs_1_, ...), custom_call_target="tpu_custom_call" | custom-call | flops 4294967296 | bytes 16777216 | tf_op jit(solution)/shard_map/pallas_call | solution.py:464
  202.2 13.5 %shard_map.210 = (bf16[2048,512]{1,0:T(8,128)(2,1)}, bf16[2048,128]{1,0:T(8,128)(2,1)}, f32[1,512]{1,0:T(1,128)}) custom-call(bf16[2048,256]{1,0:T(8,128)(2,1)} %all-gather.9.cloned.1.call-done.refs_2_.refs_0_.refs_8_, bf16[2048,256]{1,0:T(8,128)(2,1)} %collective-permute-done.19.refs_3_.refs_1_.refs_9_, ...), custom_call_target="tpu_custom_call" | custom-call | flops 5368709120 | bytes 14680064 | tf_op jit(solution)/shard_map/pallas_call | solution.py:263
  216.6 24.9 %collective-permute-done.26 = bf16[1024,512]{1,0:T(8,128)(2,1)S(1)} collective-permute-done((bf16[1024,512]{1,0:T(8,128)(2,1)}, bf16[1024,512]{1,0:T(8,128)(2,1)S(1)}, u32[]{:S(2)}, u32[]{:S(2)}) %collective-permute-start.26) | collective-permute-done | bytes 1048608 | tf_op jit(solution)/shard_map/ppermute | solution.py:93
  242.8 9.5 %shard_map.211 = (bf16[4,256,512]{2,1,0:T(8,128)(2,1)}, bf16[4,256,512]{2,1,0:T(8,128)(2,1)}) custom-call(s32[1]{0:T(128)} %bitcast.15.half_ref, bf16[2048,256]{1,0:T(8,128)(2,1)} %all-gather.5.cloned.1.call-done.refs_0_.refs_2_, bf16[2048,256]{1,0:T(8,128)(2,1)} %all-gather.7.cloned.1.call-done.refs_1_.refs_3_, ...), custom_call_target="tpu_custom_call" | custom-call | flops 4294967296 | bytes 16777216 | tf_op jit(solution)/shard_map/pallas_call | solution.py:464
  252.3 17.9 %shard_map.212 = (bf16[2048,384]{1,0:T(8,128)(2,1)}, f32[1,384]{1,0:T(1,128)}) custom-call(s32[4]{0:T(128)} %and_select_fusion.lowest_ref, bf16[2048,128]{1,0:T(8,128)(2,1)} %get-tuple-element.116.q_ref, bf16[2048,128]{1,0:T(8,128)(2,1)} %get-tuple-element.117.k_ref, bf16[2048,128]{1,0:T(8,128)(2,1)} %get-tuple-element.118.v_ref, ...), custom_call_target="tpu_custom_call" | custom-call | flops 2684354560 | bytes 4194304 | tf_op jit(solution)/shard_map/pallas_call | solution.py:789
  271.7 24.4 %collective-permute-done.28.received_ref = bf16[4,256,512]{2,1,0:T(8,128)(2,1)} collective-permute-done((bf16[4,256,512]{2,1,0:T(8,128)(2,1)}, bf16[4,256,512]{2,1,0:T(8,128)(2,1)}, u32[]{:S(2)}, u32[]{:S(2)}) %collective-permute-start.28) | collective-permute-done | bytes 1048608 | tf_op jit(solution)/shard_map/ppermute | solution.py:93
  298.7 12.4 %shard_map.214 = (bf16[1024,512]{1,0:T(8,128)(2,1)}, bf16[1024,512]{1,0:T(8,128)(2,1)}, bf16[2048,512]{1,0:T(8,128)(2,1)}) custom-call(bf16[2048,512]{1,0:T(8,128)(2,1)} %get-tuple-element.139.refs_4_.refs_0_, bf16[2048,384]{1,0:T(8,128)(2,1)} %get-tuple-element.154.refs_1_.refs_0_, bf16[2048,512]{1,0:T(8,128)(2,1)} %collective-permute-done.27.refs_5_.refs_2_, ...), custom_call_target="tpu_custom_call" | custom-call | flops 7516192768 | bytes 11534336 | tf_op jit(solution)/shard_map/pallas_call | solution.py:374
  311.9 13.2 %collective-permute-done.31.refs_1_ = bf16[2,256,512]{2,1,0:T(8,128)(2,1)} collective-permute-done((bf16[2,256,512]{2,1,0:T(8,128)(2,1)}, bf16[2,256,512]{2,1,0:T(8,128)(2,1)}, u32[]{:S(2)}, u32[]{:S(2)}) %collective-permute-start.31) | collective-permute-done | bytes 524320 | tf_op jit(solution)/shard_map/ppermute | solution.py:93
  327.1 22.0 %collective-permute-done.32 = bf16[1024,512]{1,0:T(8,128)(2,1)S(1)} collective-permute-done((bf16[1024,512]{1,0:T(8,128)(2,1)}, bf16[1024,512]{1,0:T(8,128)(2,1)S(1)}, u32[]{:S(2)}, u32[]{:S(2)}) %collective-permute-start.32) | collective-permute-done | bytes 1048608 | tf_op jit(solution)/shard_map/ppermute | solution.py:93
  352.2 10.3 %collective-permute-done.41.refs_2_ = bf16[2,256,512]{2,1,0:T(8,128)(2,1)S(1)} collective-permute-done((bf16[2,256,512]{2,1,0:T(8,128)(2,1)S(1)}, bf16[2,256,512]{2,1,0:T(8,128)(2,1)S(1)}, u32[]{:S(2)}, u32[]{:S(2)}) %collective-permute-start.41) | collective-permute-done | bytes 524320 | tf_op jit(solution)/shard_map/ppermute | solution.py:93
  364.8 10.7 %shard_map.215 = (bf16[4,512,256]{2,1,0:T(8,128)(2,1)}, bf16[4,512,256]{2,1,0:T(8,128)(2,1)}) custom-call(s32[1]{0:T(128)} %bitcast.15.half_ref, bf16[2048,384]{1,0:T(8,128)(2,1)} %get-tuple-element.154.refs_1_.refs_0_, bf16[2048,384]{1,0:T(8,128)(2,1)} %collective-permute-done.30.refs_3_.refs_1_, ...), custom_call_target="tpu_custom_call" | custom-call | flops 4294967296 | bytes 16777216 | tf_op jit(solution)/shard_map/pallas_call | solution.py:464
  380.2 10.8 %collective-permute-done.33.refs_1_ = bf16[2,256,512]{2,1,0:T(8,128)(2,1)} collective-permute-done((bf16[2,256,512]{2,1,0:T(8,128)(2,1)}, bf16[2,256,512]{2,1,0:T(8,128)(2,1)}, u32[]{:S(2)}, u32[]{:S(2)}) %collective-permute-start.33) | collective-permute-done | bytes 524320 | tf_op jit(solution)/shard_map/ppermute | solution.py:93
  393.2 6.3 %collective-permute-done.34.far_ref = bf16[256,512]{1,0:T(8,128)(2,1)} collective-permute-done((bf16[256,512]{1,0:T(8,128)(2,1)S(1)}, bf16[256,512]{1,0:T(8,128)(2,1)}, u32[]{:S(2)}, u32[]{:S(2)}) %collective-permute-start.34) | collective-permute-done | bytes 262176 | tf_op jit(solution)/shard_map/ppermute | solution.py:93
  420.9 11.2 %collective-permute-done.46.refs_3_ = bf16[2,512,256]{2,1,0:T(8,128)(2,1)S(1)} collective-permute-done((bf16[2,512,256]{2,1,0:T(8,128)(2,1)S(1)}, bf16[2,512,256]{2,1,0:T(8,128)(2,1)S(1)}, u32[]{:S(2)}, u32[]{:S(2)}) %collective-permute-start.46) | collective-permute-done | bytes 524320 | tf_op jit(solution)/shard_map/ppermute | solution.py:93
  449.1 8.2 %collective-permute-done.47 = f32[1,896]{1,0:T(1,128)S(1)} collective-permute-done((f32[1,896]{1,0:T(1,128)S(1)}, f32[1,896]{1,0:T(1,128)S(1)}, u32[]{:S(2)}, u32[]{:S(2)}) %collective-permute-start.47) | collective-permute-done | bytes 3616 | tf_op jit(solution)/shard_map/ppermute | solution.py:93
  (195 shorter events, 161.0 us)
Async XLA Ops:
  7.2 41.0 %all-gather.5.cloned.1.call-start = ((), (), s32[]{:S(2)}) async-start(), calls=%async_computation.4 | async-start | bytes 1310720 | tf_op jit(solution)/shard_map/all_gather | solution.py:863
  16.7 59.4 %all-gather.7.cloned.1.call-start = ((), (), s32[]{:S(2)}) async-start(), calls=%async_computation.5 | async-start | bytes 1310720 | tf_op jit(solution)/shard_map/all_gather | solution.py:864
  20.7 113.5 %all-gather.11.cloned.1.call-start = ((), (), s32[]{:S(2)}) async-start(), calls=%async_computation.7 | async-start | bytes 2621440 | tf_op jit(solution)/shard_map/all_gather | solution.py:872
  48.2 28.0 %collective-permute-start.5 = (bf16[2048,256]{1,0:T(8,128)(2,1)}, bf16[2048,256]{1,0:T(8,128)(2,1)}, u32[]{:S(2)}, u32[]{:S(2)}) collective-permute-start(bf16[2048,256]{1,0:T(8,128)(2,1)} %all-gather.5.cloned.1.call-done.refs_0_.refs_2_), channel_id=1, source_target_pairs={{0,2},{1,3},{2,0},{3,1},{4,6},{5,7},{6,4},{7,5},{8,10},{9,11},{10,... | collective-permute-start | bytes 3145736 | tf_op jit(solution)/shard_map/ppermute | solution.py:93
  50.5 100.6 %all-gather.9.cloned.1.call-start = ((), (), s32[]{:S(2)}) async-start(), calls=%async_computation.6 | async-start | bytes 1310720 | tf_op jit(solution)/shard_map/all_gather | solution.py:871
  76.2 24.7 %collective-permute-start.6 = (bf16[2048,256]{1,0:T(8,128)(2,1)}, bf16[2048,256]{1,0:T(8,128)(2,1)}, u32[]{:S(2)}, u32[]{:S(2)}) collective-permute-start(bf16[2048,256]{1,0:T(8,128)(2,1)} %all-gather.7.cloned.1.call-done.refs_1_.refs_3_), channel_id=1, source_target_pairs={{0,2},{1,3},{2,0},{3,1},{4,6},{5,7},{6,4},{7,5},{8,10},{9,11},{10,... | collective-permute-start | bytes 3145736 | tf_op jit(solution)/shard_map/ppermute | solution.py:93
  79.5 30.6 %collective-permute-start.13 = (bf16[512,896]{1,0:T(8,128)(2,1)}, bf16[512,896]{1,0:T(8,128)(2,1)}, u32[]{:S(2)}, u32[]{:S(2)}) collective-permute-start(bf16[512,896]{1,0:T(8,128)(2,1)} %get-tuple-element.112.refs_5_), channel_id=1, source_target_pairs={{0,1},{1,0},{2,3},{3,2},{4,5},{5,4},{6,7},{7,6},{8,9},{9,8},{10,11... | collective-permute-start | bytes 2752520 | tf_op jit(solution)/shard_map/ppermute | solution.py:93
  110.1 269.1 %reduce-scatter.7.cloned.1.call-start = ((), (), s32[]{:S(2)}) async-start(), calls=%async_computation.9 | async-start | bytes 2621440 | tf_op jit(solution)/shard_map/reduce_scatter | solution.py:917
  128.5 54.1 %collective-permute-start.15 = (bf16[2048,512]{1,0:T(8,128)(2,1)}, bf16[2048,512]{1,0:T(8,128)(2,1)}, u32[]{:S(2)}, u32[]{:S(2)}) collective-permute-start(bf16[2048,512]{1,0:T(8,128)(2,1)} %get-tuple-element.114.refs_0_), channel_id=1, source_target_pairs={{0,1},{1,0},{2,3},{3,2},{4,5},{5,4},{6,7},{7,6},{8,9},{9,8},{10,11... | collective-permute-start | bytes 6291464 | tf_op jit(solution)/shard_map/ppermute | solution.py:93
  133.7 31.5 %collective-permute-start.23 = (bf16[640,512]{1,0:T(8,128)(2,1)}, bf16[640,512]{1,0:T(8,128)(2,1)}, u32[]{:S(2)}, u32[]{:S(2)}) collective-permute-start(bf16[640,512]{1,0:T(8,128)(2,1)} %get-tuple-element.122.refs_5_), channel_id=1, source_target_pairs={{0,1},{1,0},{2,3},{3,2},{4,5},{5,4},{6,7},{7,6},{8,9},{9,8},{10,11... | collective-permute-start | bytes 1966088 | tf_op jit(solution)/shard_map/ppermute | solution.py:93
  134.2 68.0 %collective-permute-start.22 = (bf16[2048,512]{1,0:T(8,128)(2,1)}, bf16[2048,512]{1,0:T(8,128)(2,1)}, u32[]{:S(2)}, u32[]{:S(2)}) collective-permute-start(bf16[2048,512]{1,0:T(8,128)(2,1)} %all-gather.11.cloned.1.call-done.refs_4_.refs_2_.refs_10_), channel_id=1, source_target_pairs={{0,1},{1,0},{2,3},{3,2},{4,5},{5,4},{6,7},{7,6},{8,9},{9,8},{10,11... | collective-permute-start | bytes 6291464 | tf_op jit(solution)/shard_map/ppermute | solution.py:93
  151.1 24.7 %collective-permute-start.19 = (bf16[2048,256]{1,0:T(8,128)(2,1)}, bf16[2048,256]{1,0:T(8,128)(2,1)}, u32[]{:S(2)}, u32[]{:S(2)}) collective-permute-start(bf16[2048,256]{1,0:T(8,128)(2,1)} %all-gather.9.cloned.1.call-done.refs_2_.refs_0_.refs_8_), channel_id=1, source_target_pairs={{0,2},{1,3},{2,0},{3,1},{4,6},{5,7},{6,4},{7,5},{8,10},{9,11},{10,... | collective-permute-start | bytes 3145736 | tf_op jit(solution)/shard_map/ppermute | solution.py:93
  167.4 34.7 %collective-permute-start.20 = (bf16[2048,256]{1,0:T(8,128)(2,1)}, bf16[2048,256]{1,0:T(8,128)(2,1)}, u32[]{:S(2)}, u32[]{:S(2)}) collective-permute-start(bf16[2048,256]{1,0:T(8,128)(2,1)} %all-gather.9.cloned.1.call-done.refs_2_.refs_0_.refs_8_), channel_id=1, source_target_pairs={{0,1},{1,0},{2,3},{3,2},{4,5},{5,4},{6,7},{7,6},{8,9},{9,8},{10,11... | collective-permute-start | bytes 3145736 | tf_op jit(solution)/shard_map/ppermute | solution.py:93
  175.8 26.4 %collective-permute-start.21 = (bf16[2048,256]{1,0:T(8,128)(2,1)}, bf16[2048,256]{1,0:T(8,128)(2,1)}, u32[]{:S(2)}, u32[]{:S(2)}) collective-permute-start(bf16[2048,256]{1,0:T(8,128)(2,1)} %collective-permute-done.19.refs_3_.refs_1_.refs_9_), channel_id=1, source_target_pairs={{0,1},{1,0},{2,3},{3,2},{4,5},{5,4},{6,7},{7,6},{8,9},{9,8},{10,11... | collective-permute-start | bytes 3145736 | tf_op jit(solution)/shard_map/ppermute | solution.py:93
  215.6 27.1 %collective-permute-start.27 = (bf16[2048,512]{1,0:T(8,128)(2,1)}, bf16[2048,512]{1,0:T(8,128)(2,1)}, u32[]{:S(2)}, u32[]{:S(2)}) collective-permute-start(bf16[2048,512]{1,0:T(8,128)(2,1)} %get-tuple-element.139.refs_4_.refs_0_), channel_id=1, source_target_pairs={{0,1},{1,0},{2,3},{3,2},{4,5},{5,4},{6,7},{7,6},{8,9},{9,8},{10,11... | collective-permute-start | bytes 6291464 | tf_op jit(solution)/shard_map/ppermute | solution.py:93
  215.7 25.8 %collective-permute-start.26 = (bf16[1024,512]{1,0:T(8,128)(2,1)}, bf16[1024,512]{1,0:T(8,128)(2,1)S(1)}, u32[]{:S(2)}, u32[]{:S(2)}) collective-permute-start(bf16[1024,512]{1,0:T(8,128)(2,1)} %get-tuple-element.137), channel_id=1, source_target_pairs={{0,2},{1,3},{2,0},{3,1},{4,6},{5,7},{6,4},{7,5},{8,10},{9,11},{10,... | collective-permute-start | bytes 3145736 | tf_op jit(solution)/shard_map/ppermute | solution.py:93
  216.4 175.1 %reduce-scatter.11.cloned.1.call-start = ((), (), s32[]{:S(2)}) async-start(), calls=%async_computation.11 | async-start | bytes 2621440 | tf_op jit(solution)/shard_map/reduce_scatter | solution.py:959
  270.2 28.5 %collective-permute-start.30 = (bf16[2048,384]{1,0:T(8,128)(2,1)}, bf16[2048,384]{1,0:T(8,128)(2,1)}, u32[]{:S(2)}, u32[]{:S(2)}) collective-permute-start(bf16[2048,384]{1,0:T(8,128)(2,1)} %get-tuple-element.154.refs_1_.refs_0_), channel_id=1, source_target_pairs={{0,1},{1,0},{2,3},{3,2},{4,5},{5,4},{6,7},{7,6},{8,9},{9,8},{10,11... | collective-permute-start | bytes 4718600 | tf_op jit(solution)/shard_map/ppermute | solution.py:93
  270.2 25.9 %collective-permute-start.28 = (bf16[4,256,512]{2,1,0:T(8,128)(2,1)}, bf16[4,256,512]{2,1,0:T(8,128)(2,1)}, u32[]{:S(2)}, u32[]{:S(2)}) collective-permute-start(bf16[4,256,512]{2,1,0:T(8,128)(2,1)} %get-tuple-element.142), channel_id=1, source_target_pairs={{0,16},{16,0},{1,17},{17,1},{2,18},{18,2},{3,19},{19,3},{4,20},{20... | collective-permute-start | bytes 3145736 | tf_op jit(solution)/shard_map/ppermute | solution.py:93
  311.2 126.2 %reduce-scatter.9.cloned.1.call-start = ((), (), s32[]{:S(2)}) async-start(), calls=%async_computation.10 | async-start | bytes 1310720 | tf_op jit(solution)/shard_map/reduce_scatter | solution.py:972
  325.0 24.0 %collective-permute-start.32 = (bf16[1024,512]{1,0:T(8,128)(2,1)}, bf16[1024,512]{1,0:T(8,128)(2,1)S(1)}, u32[]{:S(2)}, u32[]{:S(2)}) collective-permute-start(bf16[1024,512]{1,0:T(8,128)(2,1)} %get-tuple-element.160), channel_id=1, source_target_pairs={{0,2},{1,3},{2,0},{3,1},{4,6},{5,7},{6,4},{7,5},{8,10},{9,11},{10,... | collective-permute-start | bytes 3145736 | tf_op jit(solution)/shard_map/ppermute | solution.py:93
  325.6 25.1 %collective-permute-start.29 = (bf16[4,256,512]{2,1,0:T(8,128)(2,1)S(1)}, bf16[4,256,512]{2,1,0:T(8,128)(2,1)}, u32[]{:S(2)}, u32[]{:S(2)}) collective-permute-start(bf16[4,256,512]{2,1,0:T(8,128)(2,1)S(1)} %copy-done.12), channel_id=1, source_target_pairs={{0,16},{16,0},{1,17},{17,1},{2,18},{18,2},{3,19},{19,3},{4,20},{20... | collective-permute-start | bytes 3145736 | tf_op jit(solution)/shard_map/ppermute | solution.py:93
  350.3 114.5 %reduce-scatter.5.cloned.1.call-start = ((), (), s32[]{:S(2)}) async-start(), calls=%async_computation.8 | async-start | bytes 1310720 | tf_op jit(solution)/shard_map/reduce_scatter | solution.py:939
  446.5 35.1 %collective-permute-start.49 = (bf16[2,256,512]{2,1,0:T(8,128)(2,1)}, bf16[2,256,512]{2,1,0:T(8,128)(2,1)}, u32[]{:S(2)}, u32[]{:S(2)}) collective-permute-start(bf16[2,256,512]{2,1,0:T(8,128)(2,1)} %collective-permute-done.33.refs_1_), channel_id=1, source_target_pairs={{0,16},{16,0},{1,17},{17,1},{2,18},{18,2},{3,19},{19,3},{4,20},{20... | collective-permute-start | bytes 1572872 | tf_op jit(solution)/shard_map/ppermute | solution.py:93
  (48 other events, 710.0 us)
Sparse Core Ops, SparseCore 0:
  16.9 29.7 all-gather.4
  48.8 27.3 all-gather.6
  77.7 45.0 all-gather.10
  124.2 26.7 all-gather.8
  216.5 42.9 reduce-scatter.6
  311.3 42.0 reduce-scatter.10
  356.3 26.4 reduce-scatter.8
  400.2 26.7 reduce-scatter.4

commit v9 on v8

--- a/solution.py
+++ b/solution.py
@@ -898,7 +898,7 @@
         tables,
     )
     out_second = swap_bits(after(out_first, act, qkv_second), DP, 1)
-    cot_2 = swap_bits(after(cot_0, out_first, act), COL, 2)
+    cot_2 = swap_bits(cot_0, COL, 2)
     act_1 = swap_bits(act, COL, 1)
     attn, attn_full, lse = attend(lowest, after(q_rot, act), k_rot, v_low, begin)
     attn_1 = swap_bits(attn, COL, 1)
@@ -947,7 +947,7 @@
     d_proj_1 = swap_bits(d_proj, COL, 1)
     fc2_near, fc2_far = sum_halves(fc2_keep, after(fc2_recv, d_proj))
     fc2_crossed = swap_bits(after(fc2_far, mix_recv), COL, 2)
-    fc2_near_x = swap_bits(after(fc2_near, fc1_recv), DP, 1)
+    fc2_near_x = swap_bits(fc2_near, DP, 1)
     near_a, far_a, both_b = spread(
         [[d_up, after(d_proj, fc2_near)], [d_up_1, d_proj_1]],
         [in_own, in_near],
@@ -955,9 +955,9 @@
         True,
         local_rows,
     )
-    recv_a = swap_bits(after(far_a, fc2_crossed), COL, 2)
+    recv_a = swap_bits(far_a, COL, 2)
     part_b = lax.psum_scatter(both_b, ROW, scatter_dimension=0, tiled=True)
-    fc2_crossed_x = swap_bits(after(fc2_crossed, fc2_near_x), DP, 1)
+    fc2_crossed_x = swap_bits(fc2_crossed, DP, 1)
     rest_keep, rest_send = grad_blocks(
         half,
         [
@@ -966,23 +966,23 @@
         ],
         True,
     )
-    rest_recv = swap_bits(after(rest_send, fc2_crossed_x), DP, 1)
+    rest_recv = swap_bits(rest_send, DP, 1)
     fc1_near, fc1_far = sum_halves(fc1_keep, after(fc1_recv, rest_send))
     total_a = (near_a.astype(f32) + recv_a.astype(f32)).astype(bf16)
     d_normed_a = lax.psum_scatter(total_a, ROW, scatter_dimension=0, tiled=True)
-    fc1_crossed = swap_bits(after(fc1_far, recv_a), COL, 2)
+    fc1_crossed = swap_bits(fc1_far, COL, 2)
     rest_near, rest_far = sum_halves(rest_keep, rest_recv)
-    rest_near_x = swap_bits(after(rest_near, rest_recv), DP, 1)
+    rest_near_x = swap_bits(rest_near, DP, 1)
     cut = local_rows // 2
-    mix_recv_b = swap_bits(after(mix_b[cut:], fc1_crossed), COL, 2)
-    part_recv = swap_bits(after(part_b[cut:], mix_recv_b), COL, 2)
+    mix_recv_b = swap_bits(mix_b[cut:], COL, 2)
+    part_recv = swap_bits(part_b[cut:], COL, 2)
     (fc2_weight_grad,) = lay_out(
         places, [fc2_near, after(fc2_crossed, rest_near)], [fc2_near_x, fc2_crossed_x], 0
     )
-    rest_crossed = swap_bits(after(rest_far, part_recv), COL, 2)
-    rest_crossed_x = swap_bits(after(rest_crossed, rest_near_x), DP, 1)
-    fc1_near_x = swap_bits(after(fc1_near, rest_crossed_x), DP, 1)
-    fc1_crossed_x = swap_bits(after(fc1_crossed, fc1_near_x), DP, 1)
+    rest_crossed = swap_bits(rest_far, COL, 2)
+    rest_crossed_x = swap_bits(rest_crossed, DP, 1)
+    fc1_near_x = swap_bits(fc1_near, DP, 1)
+    fc1_crossed_x = swap_bits(fc1_crossed, DP, 1)
     qkv_weight_grad, out_weight_grad = lay_out(
         places, [rest_near, rest_crossed], [rest_near_x, rest_crossed_x], 2
     )

time: 494 us -> 504 us (1.020)
  waiting for transfers between devices: 245 us -> 253 us
    all_gather x1, waiting for transfers between devices: 16.4 us -> 0.01 us  [step(): lax.all_gather(after(out_grad[:, :cut], normed), ROW, axis=0, tiled=True)]
    all_gather x1, waiting for transfers between devices: 0.01 us -> 16.3 us  [step(): lax.all_gather(jnp.concatenate([tail, tail_far], axis=1), ROW, axis=0, ti...]
    ppermute x50, waiting for transfers between devices: 203 us -> 209 us  [swap_bits(): lax.ppermute(value, axis, [(place, place ^ bit) for place in range(count)])]
  transfers between devices with their start and end apart: 58 -> 58, of which waited for: 28 -> 23; matrix products, arithmetic and copies ran while one was open for 7% -> 6% of each run, Pallas kernels for 27% -> 19%
where the time goes in v9:
time: 504 us; the launch traced here: 503 us
  waiting for transfers between devices  253 us (50%)
  Pallas kernels  151 us (30%)
  starting transfers between devices  47.2 us (9%)
  other arithmetic  19.7 us (4%)
  local copies, waits for them, and re-layouts  18.1 us (4%)
  between operations  14.4 us (3%)
    ppermute x50, waiting for transfers between devices, swap_bits(): lax.ppermute(value, axis, [(place, place ^ bit) for place in range(count)])  209 us
    ppermute x50, starting transfers between devices, swap_bits(): lax.ppermute(value, axis, [(place, place ^ bit) for place in range(count)])  46.6 us
    pallas_call x3, Pallas kernels, grad_blocks(): pl.pallas_call(kernel, grid_spec=pltpu.PrefetchScalarGridSpec(num_scalar_...  29.4 us
    all_gather x1, waiting for transfers between devices, step(): normed_0b = lax.all_gather(normed[:, cut:], ROW, axis=0, tiled=True)  25.7 us
    pallas_call x2, Pallas kernels, spread(): pl.pallas_call(kernel, grid=(rows // block,), in_specs=[rowed(hidden), ro...  22 us
    pallas_call x1, Pallas kernels, attend_back(): pl.pallas_call(kernel, grid_spec=pltpu.PrefetchScalarGridSpec(num_scalar_...  17.9 us
    all_gather x1, waiting for transfers between devices, step(): lax.all_gather(jnp.concatenate([tail, tail_far], axis=1), ROW, axis=0, ti...  16.3 us
    pallas_call x1, Pallas kernels, forward_step(): pl.pallas_call(kernel, grid=(rows // block,), in_specs=[rowed(x.shape[1])...  15.9 us
  transfers between devices with their start and end apart: 58, of which 23 were waited for; matrix products, arithmetic and copies ran while one was open for 6% of the time, Pallas kernels for 19%

profile of v9, /device:TPU:0, one launch (start us, length us, event | category | flops | bytes accessed | tf_op | source)
XLA Modules:
  0.0 503.2 jit_solution(2351035035549120788)
XLA Ops:
  36.4 6.1 %collective-permute-done.3.refs_1_ = bf16[512,384]{1,0:T(8,128)(2,1)S(1)} collective-permute-done((bf16[512,384]{1,0:T(8,128)(2,1)}, bf16[512,384]{1,0:T(8,128)(2,1)S(1)}, u32[]{:S(2)}, u32[]{:S(2)}) %collective-permute-start.3) | collective-permute-done | bytes 393248 | tf_op jit(solution)/shard_map/ppermute | solution.py:93
  50.5 25.7 %all-gather.7.cloned.1.call-done.refs_1_.refs_3_ = bf16[2048,256]{1,0:T(8,128)(2,1)} async-done(((bf16[512,256]{1,0:T(8,128)(2,1)}), bf16[2048,256]{1,0:T(8,128)(2,1)}) %all-gather.7.cloned.1.call-update) | async-done | bytes 1048592 | tf_op jit(solution)/shard_map/all_gather | solution.py:864
  79.6 11.6 %collective-permute-done.11.refs_2_ = bf16[512,512]{1,0:T(8,128)(2,1)} collective-permute-done((bf16[512,512]{1,0:T(8,128)(2,1)}, bf16[512,512]{1,0:T(8,128)(2,1)}, u32[]{:S(2)}, u32[]{:S(2)}) %collective-permute-start.11) | collective-permute-done | bytes 524320 | tf_op jit(solution)/shard_map/ppermute | solution.py:93
  94.2 6.3 %collective-permute-done.12.refs_3_ = bf16[512,384]{1,0:T(8,128)(2,1)S(1)} collective-permute-done((bf16[512,384]{1,0:T(8,128)(2,1)S(1)}, bf16[512,384]{1,0:T(8,128)(2,1)S(1)}, u32[]{:S(2)}, u32[]{:S(2)}) %collective-permute-start.12) | collective-permute-done | bytes 393248 | tf_op jit(solution)/shard_map/ppermute | solution.py:93
  100.9 5.7 %fusion = (f32[2048,128]{1,0:T(8,128)}, f32[2048,128]{1,0:T(8,128)}, f32[2048,128]{1,0:T(8,128)}) fusion(f32[128]{0:T(128)S(1)} %fusion.12, f32[2048]{0:T(1024)S(1)} %get-tuple-element.205, pred[128]{0:T(512)(128)(4,1)S(1)} %get-tuple-element.209, pred[128]{0:T(512)(128)(4,1)S(1)} %get-tuple-element.210, pred[128]{0:T(512)(128)(4,1)S(1)} %broadcast_compare_fusion.1), kind=kLoop, calls=%fused_computation.7 | loop fusion | flops 1310720 | bytes 3154816 | tf_op jit(solution)/shard_map/jit(_where)/select_n | solution.py:62
  112.7 15.9 %shard_map.205 = (f32[2048,512]{1,0:T(8,128)}, bf16[2048,512]{1,0:T(8,128)(2,1)}, bf16[2048,128]{1,0:T(8,128)(2,1)}, bf16[2048,128]{1,0:T(8,128)(2,1)}, bf16[2048,128]{1,0:T(8,128)(2,1)}) custom-call(bf16[2048,256]{1,0:T(8,128)(2,1)} %all-gather.5.cloned.1.call-done.refs_0_.refs_2_, bf16[2048,256]{1,0:T(8,128)(2,1)} %all-gather.7.cloned.1.call-done.refs_1_.refs_3_, ...), custom_call_target="tpu_custom_call" | custom-call | flops 7516192768 | bytes 18874368 | tf_op jit(solution)/shard_map/pallas_call | solution.py:201
  135.3 16.3 %all-gather.11.cloned.1.call-done.refs_4_.refs_2_.refs_10_ = bf16[2048,512]{1,0:T(8,128)(2,1)} async-done(((bf16[512,512]{1,0:T(8,128)(2,1)}), bf16[2048,512]{1,0:T(8,128)(2,1)}) %all-gather.11.cloned.1.call-update) | async-done | bytes 2097168 | tf_op jit(solution)/shard_map/all_gather | solution.py:872
  152.2 12.0 %shard_map.206 = (bf16[2048,128]{1,0:T(8,128)(2,1)}, f32[2048,128]{1,0:T(8,128)}, f32[2,2048]{1,0:T(2,128)}) custom-call(s32[4]{0:T(128)} %and_select_fusion.lowest_ref, bf16[2048,128]{1,0:T(8,128)(2,1)} %get-tuple-element.103.q_ref, bf16[2048,128]{1,0:T(8,128)(2,1)} %get-tuple-element.104.k_ref, bf16[2048,128]{1,0:T(8,128)(2,1)} %get-tuple-element.105.v_ref, ...), custom_call_target="tpu_custom_call" | custom-call | flops 1073741824 | bytes 3145728 | tf_op jit(solution)/shard_map/pallas_call | solution.py:684
  166.3 6.2 %collective-permute-done.19.refs_3_.refs_1_.refs_9_ = bf16[2048,256]{1,0:T(8,128)(2,1)} collective-permute-done((bf16[2048,256]{1,0:T(8,128)(2,1)}, bf16[2048,256]{1,0:T(8,128)(2,1)}, u32[]{:S(2)}, u32[]{:S(2)}) %collective-permute-start.19) | collective-permute-done | bytes 1048608 | tf_op jit(solution)/shard_map/ppermute | solution.py:93
  173.0 8.8 %collective-permute-done.18.refs_7_.refs_10_ = bf16[640,512]{1,0:T(8,128)(2,1)} collective-permute-done((bf16[640,512]{1,0:T(8,128)(2,1)}, bf16[640,512]{1,0:T(8,128)(2,1)}, u32[]{:S(2)}, u32[]{:S(2)}) %collective-permute-start.18) | collective-permute-done | bytes 655392 | tf_op jit(solution)/shard_map/ppermute | solution.py:93
  182.4 9.6 %shard_map.208 = (bf16[1024,512]{1,0:T(8,128)(2,1)}, bf16[1024,512]{1,0:T(8,128)(2,1)}, bf16[2048,512]{1,0:T(8,128)(2,1)}) custom-call(bf16[2048,512]{1,0:T(8,128)(2,1)} %get-tuple-element.101.refs_0_, bf16[2048,128]{1,0:T(8,128)(2,1)} %get-tuple-element.106.refs_1_.refs_6_, bf16[2048,512]{1,0:T(8,128)(2,1)} %collective-permute-done.15.refs_2_.refs_1_, ...), custom_call_target="tpu_custom_call" | custom-call | flops 5368709120 | bytes 9437184 | tf_op jit(solution)/shard_map/pallas_call | solution.py:374
  192.0 9.4 %shard_map.209 = (bf16[4,256,512]{2,1,0:T(8,128)(2,1)}, bf16[4,256,512]{2,1,0:T(8,128)(2,1)}) custom-call(s32[1]{0:T(128)} %bitcast.15.half_ref, bf16[2048,512]{1,0:T(8,128)(2,1)} %get-tuple-element.101.refs_0_, bf16[2048,512]{1,0:T(8,128)(2,1)} %collective-permute-done.15.refs_2_.refs_1_, ...), custom_call_target="tpu_custom_call" | custom-call | flops 4294967296 | bytes 16777216 | tf_op jit(solution)/shard_map/pallas_call | solution.py:464
  201.5 13.4 %shard_map.210 = (bf16[2048,512]{1,0:T(8,128)(2,1)}, bf16[2048,128]{1,0:T(8,128)(2,1)}, f32[1,512]{1,0:T(1,128)}) custom-call(bf16[2048,256]{1,0:T(8,128)(2,1)} %all-gather.9.cloned.1.call-done.refs_2_.refs_0_.refs_8_, bf16[2048,256]{1,0:T(8,128)(2,1)} %collective-permute-done.19.refs_3_.refs_1_.refs_9_, ...), custom_call_target="tpu_custom_call" | custom-call | flops 5368709120 | bytes 14680064 | tf_op jit(solution)/shard_map/pallas_call | solution.py:263
  216.5 24.2 %collective-permute-done.26 = bf16[1024,512]{1,0:T(8,128)(2,1)S(1)} collective-permute-done((bf16[1024,512]{1,0:T(8,128)(2,1)}, bf16[1024,512]{1,0:T(8,128)(2,1)S(1)}, u32[]{:S(2)}, u32[]{:S(2)}) %collective-permute-start.26) | collective-permute-done | bytes 1048608 | tf_op jit(solution)/shard_map/ppermute | solution.py:93
  243.3 9.4 %shard_map.212 = (bf16[4,256,512]{2,1,0:T(8,128)(2,1)}, bf16[4,256,512]{2,1,0:T(8,128)(2,1)}) custom-call(s32[1]{0:T(128)} %bitcast.15.half_ref, bf16[2048,256]{1,0:T(8,128)(2,1)} %all-gather.5.cloned.1.call-done.refs_0_.refs_2_, bf16[2048,256]{1,0:T(8,128)(2,1)} %all-gather.7.cloned.1.call-done.refs_1_.refs_3_, ...), custom_call_target="tpu_custom_call" | custom-call | flops 4294967296 | bytes 16777216 | tf_op jit(solution)/shard_map/pallas_call | solution.py:464
  252.7 17.9 %shard_map.213 = (bf16[2048,384]{1,0:T(8,128)(2,1)}, f32[1,384]{1,0:T(1,128)}) custom-call(s32[4]{0:T(128)} %and_select_fusion.lowest_ref, bf16[2048,128]{1,0:T(8,128)(2,1)} %get-tuple-element.103.q_ref, bf16[2048,128]{1,0:T(8,128)(2,1)} %get-tuple-element.104.k_ref, bf16[2048,128]{1,0:T(8,128)(2,1)} %get-tuple-element.105.v_ref, ...), custom_call_target="tpu_custom_call" | custom-call | flops 2684354560 | bytes 4194304 | tf_op jit(solution)/shard_map/pallas_call | solution.py:789
  272.1 24.3 %collective-permute-done.29.received_ref = bf16[4,256,512]{2,1,0:T(8,128)(2,1)} collective-permute-done((bf16[4,256,512]{2,1,0:T(8,128)(2,1)}, bf16[4,256,512]{2,1,0:T(8,128)(2,1)}, u32[]{:S(2)}, u32[]{:S(2)}) %collective-permute-start.29) | collective-permute-done | bytes 1048608 | tf_op jit(solution)/shard_map/ppermute | solution.py:93
  299.1 12.4 %shard_map.215 = (bf16[1024,512]{1,0:T(8,128)(2,1)}, bf16[1024,512]{1,0:T(8,128)(2,1)}, bf16[2048,512]{1,0:T(8,128)(2,1)}) custom-call(bf16[2048,512]{1,0:T(8,128)(2,1)} %get-tuple-element.126.refs_4_.refs_0_, bf16[2048,384]{1,0:T(8,128)(2,1)} %get-tuple-element.142.refs_1_.refs_0_, bf16[2048,512]{1,0:T(8,128)(2,1)} %collective-permute-done.28.refs_5_.refs_2_, ...), custom_call_target="tpu_custom_call" | custom-call | flops 7516192768 | bytes 11534336 | tf_op jit(solution)/shard_map/pallas_call | solution.py:374
  314.3 23.2 %collective-permute-done.31 = bf16[1024,512]{1,0:T(8,128)(2,1)S(1)} collective-permute-done((bf16[1024,512]{1,0:T(8,128)(2,1)S(1)}, bf16[1024,512]{1,0:T(8,128)(2,1)S(1)}, u32[]{:S(2)}, u32[]{:S(2)}) %collective-permute-start.31) | collective-permute-done | bytes 1048608 | tf_op jit(solution)/shard_map/ppermute | solution.py:93
  341.3 10.6 %shard_map.218 = (bf16[4,512,256]{2,1,0:T(8,128)(2,1)}, bf16[4,512,256]{2,1,0:T(8,128)(2,1)}) custom-call(s32[1]{0:T(128)} %bitcast.15.half_ref, bf16[2048,384]{1,0:T(8,128)(2,1)} %get-tuple-element.142.refs_1_.refs_0_, bf16[2048,384]{1,0:T(8,128)(2,1)} %collective-permute-done.30.refs_3_.refs_1_, ...), custom_call_target="tpu_custom_call" | custom-call | flops 4294967296 | bytes 16777216 | tf_op jit(solution)/shard_map/pallas_call | solution.py:464
  355.6 10.6 %collective-permute-done.43.received_ref = bf16[4,256,512]{2,1,0:T(8,128)(2,1)} collective-permute-done((bf16[4,256,512]{2,1,0:T(8,128)(2,1)}, bf16[4,256,512]{2,1,0:T(8,128)(2,1)}, u32[]{:S(2)}, u32[]{:S(2)}) %collective-permute-start.43) | collective-permute-done | bytes 1048608 | tf_op jit(solution)/shard_map/ppermute | solution.py:93
  370.3 18.3 %collective-permute-done.38.received_ref = bf16[4,512,256]{2,1,0:T(8,128)(2,1)} collective-permute-done((bf16[4,512,256]{2,1,0:T(8,128)(2,1)}, bf16[4,512,256]{2,1,0:T(8,128)(2,1)}, u32[]{:S(2)}, u32[]{:S(2)}) %collective-permute-start.38) | collective-permute-done | bytes 1048608 | tf_op jit(solution)/shard_map/ppermute | solution.py:93
  395.9 13.2 %collective-permute-done.42 = f32[1,896]{1,0:T(1,128)S(1)} collective-permute-done((f32[1,896]{1,0:T(1,128)S(1)}, f32[1,896]{1,0:T(1,128)S(1)}, u32[]{:S(2)}, u32[]{:S(2)}) %collective-permute-start.42) | collective-permute-done | bytes 3616 | tf_op jit(solution)/shard_map/ppermute | solution.py:93
  421.5 34.7 %collective-permute-done.35 = f32[3,512]{1,0:T(4,128)S(1)} collective-permute-done((f32[3,512]{1,0:T(4,128)}, f32[3,512]{1,0:T(4,128)S(1)}, u32[]{:S(2)}, u32[]{:S(2)}) %collective-permute-start.35) | collective-permute-done | bytes 6176 | tf_op jit(solution)/shard_map/ppermute | solution.py:93
  (183 shorter events, 142.7 us)
Async XLA Ops:
  7.2 41.8 %all-gather.5.cloned.1.call-start = ((), (), s32[]{:S(2)}) async-start(), calls=%async_computation.4 | async-start | bytes 1310720 | tf_op jit(solution)/shard_map/all_gather | solution.py:863
  16.7 59.4 %all-gather.7.cloned.1.call-start = ((), (), s32[]{:S(2)}) async-start(), calls=%async_computation.5 | async-start | bytes 1310720 | tf_op jit(solution)/shard_map/all_gather | solution.py:864
  17.5 117.4 %all-gather.9.cloned.1.call-start = ((), (), s32[]{:S(2)}) async-start(), calls=%async_computation.6 | async-start | bytes 1310720 | tf_op jit(solution)/shard_map/all_gather | solution.py:871
  50.5 101.2 %all-gather.11.cloned.1.call-start = ((), (), s32[]{:S(2)}) async-start(), calls=%async_computation.7 | async-start | bytes 2621440 | tf_op jit(solution)/shard_map/all_gather | solution.py:872
  79.5 30.2 %collective-permute-start.13 = (bf16[512,896]{1,0:T(8,128)(2,1)}, bf16[512,896]{1,0:T(8,128)(2,1)}, u32[]{:S(2)}, u32[]{:S(2)}) collective-permute-start(bf16[512,896]{1,0:T(8,128)(2,1)} %get-tuple-element.99.refs_5_), channel_id=1, source_target_pairs={{0,1},{1,0},{2,3},{3,2},{4,5},{5,4},{6,7},{7,6},{8,9},{9,8},{10,11... | collective-permute-start | bytes 2752520 | tf_op jit(solution)/shard_map/ppermute | solution.py:93
  93.5 301.4 %reduce-scatter.11.cloned.1.call-start = ((), (), s32[]{:S(2)}) async-start(), calls=%async_computation.11 | async-start | bytes 2621440 | tf_op jit(solution)/shard_map/reduce_scatter | solution.py:959
  128.6 53.3 %collective-permute-start.15 = (bf16[2048,512]{1,0:T(8,128)(2,1)}, bf16[2048,512]{1,0:T(8,128)(2,1)}, u32[]{:S(2)}, u32[]{:S(2)}) collective-permute-start(bf16[2048,512]{1,0:T(8,128)(2,1)} %get-tuple-element.101.refs_0_), channel_id=1, source_target_pairs={{0,1},{1,0},{2,3},{3,2},{4,5},{5,4},{6,7},{7,6},{8,9},{9,8},{10,11... | collective-permute-start | bytes 6291464 | tf_op jit(solution)/shard_map/ppermute | solution.py:93
  132.6 32.2 %collective-permute-start.23 = (bf16[640,512]{1,0:T(8,128)(2,1)}, bf16[640,512]{1,0:T(8,128)(2,1)}, u32[]{:S(2)}, u32[]{:S(2)}) collective-permute-start(bf16[640,512]{1,0:T(8,128)(2,1)} %get-tuple-element.109.refs_5_), channel_id=1, source_target_pairs={{0,1},{1,0},{2,3},{3,2},{4,5},{5,4},{6,7},{7,6},{8,9},{9,8},{10,11... | collective-permute-start | bytes 1966088 | tf_op jit(solution)/shard_map/ppermute | solution.py:93
  132.7 31.5 %collective-permute-start.17 = (bf16[640,512]{1,0:T(8,128)(2,1)}, bf16[640,512]{1,0:T(8,128)(2,1)}, u32[]{:S(2)}, u32[]{:S(2)}) collective-permute-start(bf16[640,512]{1,0:T(8,128)(2,1)} %get-tuple-element.111), channel_id=1, source_target_pairs={{0,2},{1,3},{2,0},{3,1},{4,6},{5,7},{6,4},{7,5},{8,10},{9,11},{10,... | collective-permute-start | bytes 1966088 | tf_op jit(solution)/shard_map/ppermute | solution.py:93
  134.9 37.7 %collective-permute-start.19 = (bf16[2048,256]{1,0:T(8,128)(2,1)}, bf16[2048,256]{1,0:T(8,128)(2,1)}, u32[]{:S(2)}, u32[]{:S(2)}) collective-permute-start(bf16[2048,256]{1,0:T(8,128)(2,1)} %all-gather.9.cloned.1.call-done.refs_2_.refs_0_.refs_8_), channel_id=1, source_target_pairs={{0,2},{1,3},{2,0},{3,1},{4,6},{5,7},{6,4},{7,5},{8,10},{9,11},{10,... | collective-permute-start | bytes 3145736 | tf_op jit(solution)/shard_map/ppermute | solution.py:93
  151.6 49.8 %collective-permute-start.22 = (bf16[2048,512]{1,0:T(8,128)(2,1)}, bf16[2048,512]{1,0:T(8,128)(2,1)}, u32[]{:S(2)}, u32[]{:S(2)}) collective-permute-start(bf16[2048,512]{1,0:T(8,128)(2,1)} %all-gather.11.cloned.1.call-done.refs_4_.refs_2_.refs_10_), channel_id=1, source_target_pairs={{0,1},{1,0},{2,3},{3,2},{4,5},{5,4},{6,7},{7,6},{8,9},{9,8},{10,11... | collective-permute-start | bytes 6291464 | tf_op jit(solution)/shard_map/ppermute | solution.py:93
  172.5 28.9 %collective-permute-start.20 = (bf16[2048,256]{1,0:T(8,128)(2,1)}, bf16[2048,256]{1,0:T(8,128)(2,1)}, u32[]{:S(2)}, u32[]{:S(2)}) collective-permute-start(bf16[2048,256]{1,0:T(8,128)(2,1)} %all-gather.9.cloned.1.call-done.refs_2_.refs_0_.refs_8_), channel_id=1, source_target_pairs={{0,1},{1,0},{2,3},{3,2},{4,5},{5,4},{6,7},{7,6},{8,9},{9,8},{10,11... | collective-permute-start | bytes 3145736 | tf_op jit(solution)/shard_map/ppermute | solution.py:93
  311.6 106.0 %reduce-scatter.9.cloned.1.call-start = ((), (), s32[]{:S(2)}) async-start(), calls=%async_computation.10 | async-start | bytes 1310720 | tf_op jit(solution)/shard_map/reduce_scatter | solution.py:972
  338.7 119.0 %reduce-scatter.7.cloned.1.call-start = ((), (), s32[]{:S(2)}) async-start(), calls=%async_computation.9 | async-start | bytes 2621440 | tf_op jit(solution)/shard_map/reduce_scatter | solution.py:917
  339.5 131.5 %reduce-scatter.5.cloned.1.call-start = ((), (), s32[]{:S(2)}) async-start(), calls=%async_computation.8 | async-start | bytes 1310720 | tf_op jit(solution)/shard_map/reduce_scatter | solution.py:939
  352.0 36.7 %collective-permute-start.38 = (bf16[4,512,256]{2,1,0:T(8,128)(2,1)}, bf16[4,512,256]{2,1,0:T(8,128)(2,1)}, u32[]{:S(2)}, u32[]{:S(2)}) collective-permute-start(bf16[4,512,256]{2,1,0:T(8,128)(2,1)} %get-tuple-element.144), channel_id=1, source_target_pairs={{0,16},{16,0},{1,17},{17,1},{2,18},{18,2},{3,19},{19,3},{4,20},{20... | collective-permute-start | bytes 3145736 | tf_op jit(solution)/shard_map/ppermute | solution.py:93
  352.5 40.3 %collective-permute-start.47 = (bf16[2,256,512]{2,1,0:T(8,128)(2,1)}, bf16[2,256,512]{2,1,0:T(8,128)(2,1)}, u32[]{:S(2)}, u32[]{:S(2)}) collective-permute-start(bf16[2,256,512]{2,1,0:T(8,128)(2,1)} %get-tuple-element.157), channel_id=1, source_target_pairs={{0,2},{1,3},{2,0},{3,1},{4,6},{5,7},{6,4},{7,5},{8,10},{9,11},{10,... | collective-permute-start | bytes 1572872 | tf_op jit(solution)/shard_map/ppermute | solution.py:93
  354.1 56.4 %collective-permute-start.48 = (bf16[2,256,512]{2,1,0:T(8,128)(2,1)}, bf16[2,256,512]{2,1,0:T(8,128)(2,1)}, u32[]{:S(2)}, u32[]{:S(2)}) collective-permute-start(bf16[2,256,512]{2,1,0:T(8,128)(2,1)} %get-tuple-element.135.refs_0_), channel_id=1, source_target_pairs={{0,16},{16,0},{1,17},{17,1},{2,18},{18,2},{3,19},{19,3},{4,20},{20... | collective-permute-start | bytes 1572872 | tf_op jit(solution)/shard_map/ppermute | solution.py:93
  368.9 44.9 %collective-permute-start.44 = (bf16[2,256,512]{2,1,0:T(8,128)(2,1)}, bf16[2,256,512]{2,1,0:T(8,128)(2,1)}, u32[]{:S(2)}, u32[]{:S(2)}) collective-permute-start(bf16[2,256,512]{2,1,0:T(8,128)(2,1)} %get-tuple-element.155), channel_id=1, source_target_pairs={{0,2},{1,3},{2,0},{3,1},{4,6},{5,7},{6,4},{7,5},{8,10},{9,11},{10,... | collective-permute-start | bytes 1572872 | tf_op jit(solution)/shard_map/ppermute | solution.py:93
  410.5 52.5 %collective-permute-start.45 = (bf16[2,256,512]{2,1,0:T(8,128)(2,1)}, bf16[2,256,512]{2,1,0:T(8,128)(2,1)}, u32[]{:S(2)}, u32[]{:S(2)}) collective-permute-start(bf16[2,256,512]{2,1,0:T(8,128)(2,1)} %get-tuple-element.154.refs_0_), channel_id=1, source_target_pairs={{0,16},{16,0},{1,17},{17,1},{2,18},{18,2},{3,19},{19,3},{4,20},{20... | collective-permute-start | bytes 1572872 | tf_op jit(solution)/shard_map/ppermute | solution.py:93
  413.7 63.9 %collective-permute-start.46 = (bf16[2,256,512]{2,1,0:T(8,128)(2,1)}, bf16[2,256,512]{2,1,0:T(8,128)(2,1)}, u32[]{:S(2)}, u32[]{:S(2)}) collective-permute-start(bf16[2,256,512]{2,1,0:T(8,128)(2,1)} %collective-permute-done.44.refs_1_), channel_id=1, source_target_pairs={{0,16},{16,0},{1,17},{17,1},{2,18},{18,2},{3,19},{19,3},{4,20},{20... | collective-permute-start | bytes 1572872 | tf_op jit(solution)/shard_map/ppermute | solution.py:93
  414.3 67.7 %collective-permute-start.40 = (bf16[2,512,256]{2,1,0:T(8,128)(2,1)}, bf16[2,512,256]{2,1,0:T(8,128)(2,1)}, u32[]{:S(2)}, u32[]{:S(2)}) collective-permute-start(bf16[2,512,256]{2,1,0:T(8,128)(2,1)} %get-tuple-element.145.refs_0_), channel_id=1, source_target_pairs={{0,16},{16,0},{1,17},{17,1},{2,18},{18,2},{3,19},{19,3},{4,20},{20... | collective-permute-start | bytes 1572872 | tf_op jit(solution)/shard_map/ppermute | solution.py:93
  415.8 66.3 %collective-permute-start.41 = (bf16[2,512,256]{2,1,0:T(8,128)(2,1)}, bf16[2,512,256]{2,1,0:T(8,128)(2,1)}, u32[]{:S(2)}, u32[]{:S(2)}) collective-permute-start(bf16[2,512,256]{2,1,0:T(8,128)(2,1)} %collective-permute-done.39.refs_1_), channel_id=1, source_target_pairs={{0,16},{16,0},{1,17},{17,1},{2,18},{18,2},{3,19},{19,3},{4,20},{20... | collective-permute-start | bytes 1572872 | tf_op jit(solution)/shard_map/ppermute | solution.py:93
  420.7 35.5 %collective-permute-start.35 = (f32[3,512]{1,0:T(4,128)}, f32[3,512]{1,0:T(4,128)S(1)}, u32[]{:S(2)}, u32[]{:S(2)}) collective-permute-start(f32[3,512]{1,0:T(4,128)} %get-tuple-element.141), channel_id=1, source_target_pairs={{0,16},{16,0},{1,17},{17,1},{2,18},{18,2},{3,19},{19,3},{4,20},{20... | collective-permute-start | bytes 18440 | tf_op jit(solution)/shard_map/ppermute | solution.py:93
  (42 other events, 788.9 us)
Sparse Core Ops, SparseCore 0:
  16.9 29.7 all-gather.4
  48.8 27.3 all-gather.6
  77.7 27.3 all-gather.8
  106.6 45.0 all-gather.10
  311.7 42.4 reduce-scatter.10
  356.9 26.4 reduce-scatter.8
  386.3 42.0 reduce-scatter.6
  430.7 26.4 reduce-scatter.4

commit v10 on v9

--- a/solution.py
+++ b/solution.py
@@ -510,8 +510,13 @@
                 elif kind == 1:
                     outs[0][:, pl.ds(pl.multiple_of(spot * cols, 128), cols)] = value
                 else:
-                    outs[0][:, pl.ds(pl.multiple_of(spot * hidden, 128), hidden)] = value[:hidden].T
+                    outs[2][spot] = value[:hidden].T
                     outs[1][spot] = value[hidden:]
+            if kind == 2:
+                lanes = hidden // 3
+                for part in range(3):
+                    spot = slice(part * lanes, (part + 1) * lanes)
+                    outs[0][:, part] = jnp.stack([outs[2][i, :, spot] for i in range(4)], axis=1)
 
         @pl.when(half == places_ref[4])
         def _():
@@ -528,16 +533,20 @@
         shapes = [(2 * cut, 4 * cols)]
         out_specs = [pl.BlockSpec((cut, 4 * cols), lambda h, s: (h, 0))]
     else:
-        shapes = [(2 * cols, 4 * hidden), (4, cut - hidden, 2 * cols)]
+        shapes = [(2 * cols, 3, 4, hidden // 3), (4, cut - hidden, 2 * cols)]
         out_specs = [
-            pl.BlockSpec((cols, 4 * hidden), lambda h, s: (h, 0)),
+            pl.BlockSpec((cols, 3, 4, hidden // 3), lambda h, s: (h, 0, 0, 0)),
             pl.BlockSpec((4, cut - hidden, cols), lambda h, s: (0, 0, h)),
         ]
     part = pl.BlockSpec((2, cut, cols), lambda h, s: (0, 0, 0))
     return pl.pallas_call(
         kernel,
         grid_spec=pltpu.PrefetchScalarGridSpec(
-            num_scalar_prefetch=1, grid=(2,), in_specs=[part] * 4, out_specs=out_specs
+            num_scalar_prefetch=1,
+            grid=(2,),
+            in_specs=[part] * 4,
+            out_specs=out_specs,
+            scratch_shapes=[pltpu.VMEM((4, cols, hidden), f32)] if kind == 2 else [],
         ),
         out_shape=[jax.ShapeDtypeStruct(shape, f32) for shape in shapes],
         compiler_params=params(),
@@ -967,14 +976,15 @@
         True,
     )
     rest_recv = swap_bits(rest_send, DP, 1)
-    fc1_near, fc1_far = sum_halves(fc1_keep, after(fc1_recv, rest_send))
+    cut = local_rows // 2
+    mix_recv_b = swap_bits(mix_b[cut:], COL, 2)
+    out = output_sum(tokens, mix_a, mix_b, mix_recv_b, out_bias.reshape(1, -1))
+    fc1_near, fc1_far = sum_halves(after(fc1_keep, out), after(fc1_recv, rest_send))
     total_a = (near_a.astype(f32) + recv_a.astype(f32)).astype(bf16)
     d_normed_a = lax.psum_scatter(total_a, ROW, scatter_dimension=0, tiled=True)
     fc1_crossed = swap_bits(fc1_far, COL, 2)
     rest_near, rest_far = sum_halves(rest_keep, rest_recv)
     rest_near_x = swap_bits(rest_near, DP, 1)
-    cut = local_rows // 2
-    mix_recv_b = swap_bits(mix_b[cut:], COL, 2)
     part_recv = swap_bits(part_b[cut:], COL, 2)
     (fc2_weight_grad,) = lay_out(
         places, [fc2_near, after(fc2_crossed, rest_near)], [fc2_near_x, fc2_crossed_x], 0
@@ -992,18 +1002,17 @@
     cot_sum = jnp.sum(out_grad.astype(f32), axis=0, keepdims=True)
     terms = (tokens, stats, ln_gain.reshape(1, -1), d_normed_a, part_b, part_recv)
     row_sums, vectors = norm_sums(*terms, cot_sum)
-    vectors = total_over(vectors, (DP,))
     row_sums = total_over(row_sums, (COL,))
-    vector_sums = total_over(vectors, (ROW,))
+    vectors = total_over(vectors, (ROW,))
+    vector_sums = total_over(vectors, (DP,))
     tokens_grad = norm_back(*terms, row_sums, out_grad, full_width)
-    out = output_sum(tokens, mix_a, mix_b, mix_recv_b, out_bias.reshape(1, -1))
     bias_sums = total_over(jnp.concatenate([qkv_sums, fc1_sums], axis=1), (DP,))[0]
     return (
         out,
         tokens_grad,
         vector_sums[0],
         vector_sums[1],
-        qkv_weight_grad.reshape(qkv_weight.shape),
+        jnp.transpose(qkv_weight_grad, (0, 2, 1, 3)),
         bias_sums[: 3 * pair_dim].reshape(qkv_bias.shape),
         out_weight_grad.reshape(out_weight.shape),
         fc1_weight_grad,

time: 504 us -> 497 us (0.986)
  waiting for transfers between devices: 253 us -> 245 us
  local copies, waits for them, and re-layouts: 18.1 us -> 12.8 us
    ppermute x50, waiting for transfers between devices: 209 us -> 168 us  [swap_bits(): lax.ppermute(value, axis, [(place, place ^ bit) for place in range(count)])]
    reduce_scatter x1, waiting for transfers between devices: 0.01 us -> 16.8 us  [step(): d_normed_a = lax.psum_scatter(total_a, ROW, scatter_dimension=0, tiled=True)]
    reduce_scatter x1, waiting for transfers between devices: 0.01 us -> 16.4 us  [step(): mix_a = lax.psum_scatter(mix_total, ROW, scatter_dimension=0, tiled=True)]
  transfers between devices with their start and end apart: 58 -> 58, of which waited for: 23 -> 27; matrix products, arithmetic and copies ran while one was open for 6% -> 5% of each run, Pallas kernels for 19% -> 29%
where the time goes in v10:
time: 497 us; the launch traced here: 492 us
  waiting for transfers between devices  245 us (49%)
  Pallas kernels  155 us (31%)
  starting transfers between devices  46.4 us (9%)
  other arithmetic  18.4 us (4%)
  between operations  14.6 us (3%)
  local copies, waits for them, and re-layouts  12.8 us (3%)
    ppermute x50, waiting for transfers between devices, swap_bits(): lax.ppermute(value, axis, [(place, place ^ bit) for place in range(count)])  168 us
    ppermute x50, starting transfers between devices, swap_bits(): lax.ppermute(value, axis, [(place, place ^ bit) for place in range(count)])  45.3 us
    pallas_call x3, Pallas kernels, grad_blocks(): pl.pallas_call(kernel, grid_spec=pltpu.PrefetchScalarGridSpec(num_scalar_...  29.6 us
    all_gather x1, waiting for transfers between devices, step(): normed_0b = lax.all_gather(normed[:, cut:], ROW, axis=0, tiled=True)  25.7 us
    pallas_call x2, Pallas kernels, spread(): pl.pallas_call(kernel, grid=(rows // block,), in_specs=[rowed(hidden), ro...  22 us
    pallas_call x1, Pallas kernels, attend_back(): pl.pallas_call(kernel, grid_spec=pltpu.PrefetchScalarGridSpec(num_scalar_...  17.9 us
    pallas_call x3, Pallas kernels, lay_out(): pl.pallas_call(kernel, grid_spec=pltpu.PrefetchScalarGridSpec(num_scalar_...  17 us
    reduce_scatter x1, waiting for transfers between devices, step(): d_normed_a = lax.psum_scatter(total_a, ROW, scatter_dimension=0, tiled=True)  16.8 us
  transfers between devices with their start and end apart: 58, of which 27 were waited for; matrix products, arithmetic and copies ran while one was open for 5% of the time, Pallas kernels for 29%

profile of v10, /device:TPU:0, one launch (start us, length us, event | category | flops | bytes accessed | tf_op | source)
XLA Modules:
  0.0 492.2 jit_solution(18047108424840188138)
XLA Ops:
  50.5 25.7 %all-gather.7.cloned.1.call-done.refs_1_.refs_3_ = bf16[2048,256]{1,0:T(8,128)(2,1)} async-done(((bf16[512,256]{1,0:T(8,128)(2,1)}), bf16[2048,256]{1,0:T(8,128)(2,1)}) %all-gather.7.cloned.1.call-update) | async-done | bytes 1048592 | tf_op jit(solution)/shard_map/all_gather | solution.py:873
  79.6 11.6 %collective-permute-done.11.refs_2_ = bf16[512,512]{1,0:T(8,128)(2,1)} collective-permute-done((bf16[512,512]{1,0:T(8,128)(2,1)}, bf16[512,512]{1,0:T(8,128)(2,1)}, u32[]{:S(2)}, u32[]{:S(2)}) %collective-permute-start.11) | collective-permute-done | bytes 524320 | tf_op jit(solution)/shard_map/ppermute | solution.py:93
  94.2 6.3 %collective-permute-done.12.refs_3_ = bf16[512,384]{1,0:T(8,128)(2,1)S(1)} collective-permute-done((bf16[512,384]{1,0:T(8,128)(2,1)S(1)}, bf16[512,384]{1,0:T(8,128)(2,1)S(1)}, u32[]{:S(2)}, u32[]{:S(2)}) %collective-permute-start.12) | collective-permute-done | bytes 393248 | tf_op jit(solution)/shard_map/ppermute | solution.py:93
  112.8 15.9 %shard_map.205 = (f32[2048,512]{1,0:T(8,128)}, bf16[2048,512]{1,0:T(8,128)(2,1)}, bf16[2048,128]{1,0:T(8,128)(2,1)}, bf16[2048,128]{1,0:T(8,128)(2,1)}, bf16[2048,128]{1,0:T(8,128)(2,1)}) custom-call(bf16[2048,256]{1,0:T(8,128)(2,1)} %all-gather.5.cloned.1.call-done.refs_0_.refs_2_, bf16[2048,256]{1,0:T(8,128)(2,1)} %all-gather.7.cloned.1.call-done.refs_1_.refs_3_, ...), custom_call_target="tpu_custom_call" | custom-call | flops 7516192768 | bytes 18874368 | tf_op jit(solution)/shard_map/pallas_call | solution.py:201
  135.4 16.3 %all-gather.11.cloned.1.call-done.refs_4_.refs_2_.refs_10_ = bf16[2048,512]{1,0:T(8,128)(2,1)} async-done(((bf16[512,512]{1,0:T(8,128)(2,1)}), bf16[2048,512]{1,0:T(8,128)(2,1)}) %all-gather.11.cloned.1.call-update) | async-done | bytes 2097168 | tf_op jit(solution)/shard_map/all_gather | solution.py:881
  152.2 12.0 %shard_map.206 = (bf16[2048,128]{1,0:T(8,128)(2,1)}, f32[2048,128]{1,0:T(8,128)}, f32[2,2048]{1,0:T(2,128)}) custom-call(s32[4]{0:T(128)} %and_select_fusion.lowest_ref, bf16[2048,128]{1,0:T(8,128)(2,1)} %get-tuple-element.104.q_ref, bf16[2048,128]{1,0:T(8,128)(2,1)} %get-tuple-element.105.k_ref, bf16[2048,128]{1,0:T(8,128)(2,1)} %get-tuple-element.106.v_ref, ...), custom_call_target="tpu_custom_call" | custom-call | flops 1073741824 | bytes 3145728 | tf_op jit(solution)/shard_map/pallas_call | solution.py:693
  166.3 6.3 %collective-permute-done.19.refs_3_.refs_1_.refs_9_ = bf16[2048,256]{1,0:T(8,128)(2,1)} collective-permute-done((bf16[2048,256]{1,0:T(8,128)(2,1)}, bf16[2048,256]{1,0:T(8,128)(2,1)}, u32[]{:S(2)}, u32[]{:S(2)}) %collective-permute-start.19) | collective-permute-done | bytes 1048608 | tf_op jit(solution)/shard_map/ppermute | solution.py:93
  173.2 8.7 %collective-permute-done.18.refs_7_.refs_10_ = bf16[640,512]{1,0:T(8,128)(2,1)} collective-permute-done((bf16[640,512]{1,0:T(8,128)(2,1)}, bf16[640,512]{1,0:T(8,128)(2,1)}, u32[]{:S(2)}, u32[]{:S(2)}) %collective-permute-start.18) | collective-permute-done | bytes 655392 | tf_op jit(solution)/shard_map/ppermute | solution.py:93
  182.4 9.6 %shard_map.208 = (bf16[1024,512]{1,0:T(8,128)(2,1)}, bf16[1024,512]{1,0:T(8,128)(2,1)}, bf16[2048,512]{1,0:T(8,128)(2,1)}) custom-call(bf16[2048,512]{1,0:T(8,128)(2,1)} %get-tuple-element.102.refs_0_, bf16[2048,128]{1,0:T(8,128)(2,1)} %get-tuple-element.107.refs_1_.refs_6_, bf16[2048,512]{1,0:T(8,128)(2,1)} %collective-permute-done.15.refs_2_.refs_1_, ...), custom_call_target="tpu_custom_call" | custom-call | flops 5368709120 | bytes 9437184 | tf_op jit(solution)/shard_map/pallas_call | solution.py:374
  192.0 9.4 %shard_map.209 = (bf16[4,256,512]{2,1,0:T(8,128)(2,1)}, bf16[4,256,512]{2,1,0:T(8,128)(2,1)}) custom-call(s32[1]{0:T(128)} %bitcast.15.half_ref, bf16[2048,512]{1,0:T(8,128)(2,1)} %get-tuple-element.102.refs_0_, bf16[2048,512]{1,0:T(8,128)(2,1)} %collective-permute-done.15.refs_2_.refs_1_, ...), custom_call_target="tpu_custom_call" | custom-call | flops 4294967296 | bytes 16777216 | tf_op jit(solution)/shard_map/pallas_call | solution.py:464
  201.5 13.5 %shard_map.210 = (bf16[2048,512]{1,0:T(8,128)(2,1)}, bf16[2048,128]{1,0:T(8,128)(2,1)}, f32[1,512]{1,0:T(1,128)}) custom-call(bf16[2048,256]{1,0:T(8,128)(2,1)} %all-gather.9.cloned.1.call-done.refs_2_.refs_0_.refs_8_, bf16[2048,256]{1,0:T(8,128)(2,1)} %collective-permute-done.19.refs_3_.refs_1_.refs_9_, ...), custom_call_target="tpu_custom_call" | custom-call | flops 5368709120 | bytes 14680064 | tf_op jit(solution)/shard_map/pallas_call | solution.py:263
  217.2 23.6 %collective-permute-done.26 = bf16[1024,512]{1,0:T(8,128)(2,1)S(1)} collective-permute-done((bf16[1024,512]{1,0:T(8,128)(2,1)}, bf16[1024,512]{1,0:T(8,128)(2,1)S(1)}, u32[]{:S(2)}, u32[]{:S(2)}) %collective-permute-start.26) | collective-permute-done | bytes 1048608 | tf_op jit(solution)/shard_map/ppermute | solution.py:93
  242.1 9.5 %shard_map.212 = (bf16[4,256,512]{2,1,0:T(8,128)(2,1)}, bf16[4,256,512]{2,1,0:T(8,128)(2,1)}) custom-call(s32[1]{0:T(128)} %bitcast.15.half_ref, bf16[2048,256]{1,0:T(8,128)(2,1)} %all-gather.5.cloned.1.call-done.refs_0_.refs_2_, bf16[2048,256]{1,0:T(8,128)(2,1)} %all-gather.7.cloned.1.call-done.refs_1_.refs_3_, ...), custom_call_target="tpu_custom_call" | custom-call | flops 4294967296 | bytes 16777216 | tf_op jit(solution)/shard_map/pallas_call | solution.py:464
  251.6 17.9 %shard_map.213 = (bf16[2048,384]{1,0:T(8,128)(2,1)}, f32[1,384]{1,0:T(1,128)}) custom-call(s32[4]{0:T(128)} %and_select_fusion.lowest_ref, bf16[2048,128]{1,0:T(8,128)(2,1)} %get-tuple-element.104.q_ref, bf16[2048,128]{1,0:T(8,128)(2,1)} %get-tuple-element.105.k_ref, bf16[2048,128]{1,0:T(8,128)(2,1)} %get-tuple-element.106.v_ref, ...), custom_call_target="tpu_custom_call" | custom-call | flops 2684354560 | bytes 4194304 | tf_op jit(solution)/shard_map/pallas_call | solution.py:798
  271.0 24.4 %collective-permute-done.29.received_ref = bf16[4,256,512]{2,1,0:T(8,128)(2,1)} collective-permute-done((bf16[4,256,512]{2,1,0:T(8,128)(2,1)}, bf16[4,256,512]{2,1,0:T(8,128)(2,1)}, u32[]{:S(2)}, u32[]{:S(2)}) %collective-permute-start.29) | collective-permute-done | bytes 1048608 | tf_op jit(solution)/shard_map/ppermute | solution.py:93
  298.1 12.4 %shard_map.215 = (bf16[1024,512]{1,0:T(8,128)(2,1)}, bf16[1024,512]{1,0:T(8,128)(2,1)}, bf16[2048,512]{1,0:T(8,128)(2,1)}) custom-call(bf16[2048,512]{1,0:T(8,128)(2,1)} %get-tuple-element.127.refs_4_.refs_0_, bf16[2048,384]{1,0:T(8,128)(2,1)} %get-tuple-element.143.refs_1_.refs_0_, bf16[2048,512]{1,0:T(8,128)(2,1)} %collective-permute-done.28.refs_5_.refs_2_, ...), custom_call_target="tpu_custom_call" | custom-call | flops 7516192768 | bytes 11534336 | tf_op jit(solution)/shard_map/pallas_call | solution.py:374
  313.2 23.2 %collective-permute-done.31 = bf16[1024,512]{1,0:T(8,128)(2,1)S(1)} collective-permute-done((bf16[1024,512]{1,0:T(8,128)(2,1)S(1)}, bf16[1024,512]{1,0:T(8,128)(2,1)S(1)}, u32[]{:S(2)}, u32[]{:S(2)}) %collective-permute-start.31) | collective-permute-done | bytes 1048608 | tf_op jit(solution)/shard_map/ppermute | solution.py:93
  339.2 10.6 %shard_map.218 = (bf16[4,512,256]{2,1,0:T(8,128)(2,1)}, bf16[4,512,256]{2,1,0:T(8,128)(2,1)}) custom-call(s32[1]{0:T(128)} %bitcast.15.half_ref, bf16[2048,384]{1,0:T(8,128)(2,1)} %get-tuple-element.143.refs_1_.refs_0_, bf16[2048,384]{1,0:T(8,128)(2,1)} %collective-permute-done.30.refs_3_.refs_1_, ...), custom_call_target="tpu_custom_call" | custom-call | flops 4294967296 | bytes 16777216 | tf_op jit(solution)/shard_map/pallas_call | solution.py:464
  365.6 16.4 %reduce-scatter.5.cloned.1.call-done.first_ref = bf16[256,512]{1,0:T(8,128)(2,1)} async-done(((bf16[1024,512]{1,0:T(8,128)(2,1)}), bf16[256,512]{1,0:T(8,128)(2,1)}) %reduce-scatter.5.cloned.1.call-update) | async-done | bytes 262160 | tf_op jit(solution)/shard_map/reduce_scatter | solution.py:948
  393.8 16.8 %reduce-scatter.9.cloned.1.call-done.refs_3_ = bf16[256,512]{1,0:T(8,128)(2,1)} async-done(((bf16[1024,512]{1,0:T(8,128)(2,1)}), bf16[256,512]{1,0:T(8,128)(2,1)}) %reduce-scatter.9.cloned.1.call-update) | async-done | bytes 262160 | tf_op jit(solution)/shard_map/reduce_scatter | solution.py:984
  430.4 9.8 %collective-permute-done.45.refs_2_ = bf16[2,256,512]{2,1,0:T(8,128)(2,1)} collective-permute-done((bf16[2,256,512]{2,1,0:T(8,128)(2,1)}, bf16[2,256,512]{2,1,0:T(8,128)(2,1)}, u32[]{:S(2)}, u32[]{:S(2)}) %collective-permute-start.45) | collective-permute-done | bytes 524320 | tf_op jit(solution)/shard_map/ppermute | solution.py:93
  455.7 6.9 %collective-permute-done.40.refs_2_ = bf16[2,512,256]{2,1,0:T(8,128)(2,1)} collective-permute-done((bf16[2,512,256]{2,1,0:T(8,128)(2,1)}, bf16[2,512,256]{2,1,0:T(8,128)(2,1)}, u32[]{:S(2)}, u32[]{:S(2)}) %collective-permute-start.40) | collective-permute-done | bytes 524320 | tf_op jit(solution)/shard_map/ppermute | solution.py:93
  462.6 9.8 %collective-permute-done.41.refs_3_ = bf16[2,512,256]{2,1,0:T(8,128)(2,1)} collective-permute-done((bf16[2,512,256]{2,1,0:T(8,128)(2,1)}, bf16[2,512,256]{2,1,0:T(8,128)(2,1)}, u32[]{:S(2)}, u32[]{:S(2)}) %collective-permute-start.41) | collective-permute-done | bytes 524320 | tf_op jit(solution)/shard_map/ppermute | solution.py:93
  472.4 8.1 %shard_map.220 = (f32[512,3,4,128]{3,2,1,0:T(4,128)}, f32[4,128,512]{2,1,0:T(8,128)}) custom-call(s32[5]{0:T(128)} %stack.48.places_ref, bf16[2,512,256]{2,1,0:T(8,128)(2,1)} %get-tuple-element.146.refs_0_, bf16[2,512,256]{2,1,0:T(8,128)(2,1)} %collective-permute-done.39.refs_1_, bf16[2,512,256]{2,1,0:T(8,128)(2,1)} %collective-permute-done.40.refs_2_, ...), custom_call_target="tpu_custom_call" | custom-call | bytes 6291456 | tf_op jit(solution)/shard_map/pallas_call | solution.py:542
  (183 shorter events, 152.9 us)
Async XLA Ops:
  7.2 41.8 %all-gather.5.cloned.1.call-start = ((), (), s32[]{:S(2)}) async-start(), calls=%async_computation.4 | async-start | bytes 1310720 | tf_op jit(solution)/shard_map/all_gather | solution.py:872
  16.7 59.4 %all-gather.7.cloned.1.call-start = ((), (), s32[]{:S(2)}) async-start(), calls=%async_computation.5 | async-start | bytes 1310720 | tf_op jit(solution)/shard_map/all_gather | solution.py:873
  17.5 117.4 %all-gather.9.cloned.1.call-start = ((), (), s32[]{:S(2)}) async-start(), calls=%async_computation.6 | async-start | bytes 1310720 | tf_op jit(solution)/shard_map/all_gather | solution.py:880
  50.5 101.2 %all-gather.11.cloned.1.call-start = ((), (), s32[]{:S(2)}) async-start(), calls=%async_computation.7 | async-start | bytes 2621440 | tf_op jit(solution)/shard_map/all_gather | solution.py:881
  93.5 257.0 %reduce-scatter.7.cloned.1.call-start = ((), (), s32[]{:S(2)}) async-start(), calls=%async_computation.9 | async-start | bytes 2621440 | tf_op jit(solution)/shard_map/reduce_scatter | solution.py:926
  128.7 53.2 %collective-permute-start.15 = (bf16[2048,512]{1,0:T(8,128)(2,1)}, bf16[2048,512]{1,0:T(8,128)(2,1)}, u32[]{:S(2)}, u32[]{:S(2)}) collective-permute-start(bf16[2048,512]{1,0:T(8,128)(2,1)} %get-tuple-element.102.refs_0_), channel_id=1, source_target_pairs={{0,1},{1,0},{2,3},{3,2},{4,5},{5,4},{6,7},{7,6},{8,9},{9,8},{10,11... | collective-permute-start | bytes 6291464 | tf_op jit(solution)/shard_map/ppermute | solution.py:93
  132.7 32.2 %collective-permute-start.23 = (bf16[640,512]{1,0:T(8,128)(2,1)}, bf16[640,512]{1,0:T(8,128)(2,1)}, u32[]{:S(2)}, u32[]{:S(2)}) collective-permute-start(bf16[640,512]{1,0:T(8,128)(2,1)} %get-tuple-element.110.refs_5_), channel_id=1, source_target_pairs={{0,1},{1,0},{2,3},{3,2},{4,5},{5,4},{6,7},{7,6},{8,9},{9,8},{10,11... | collective-permute-start | bytes 1966088 | tf_op jit(solution)/shard_map/ppermute | solution.py:93
  132.8 31.4 %collective-permute-start.17 = (bf16[640,512]{1,0:T(8,128)(2,1)}, bf16[640,512]{1,0:T(8,128)(2,1)}, u32[]{:S(2)}, u32[]{:S(2)}) collective-permute-start(bf16[640,512]{1,0:T(8,128)(2,1)} %get-tuple-element.112), channel_id=1, source_target_pairs={{0,2},{1,3},{2,0},{3,1},{4,6},{5,7},{6,4},{7,5},{8,10},{9,11},{10,... | collective-permute-start | bytes 1966088 | tf_op jit(solution)/shard_map/ppermute | solution.py:93
  134.9 37.7 %collective-permute-start.19 = (bf16[2048,256]{1,0:T(8,128)(2,1)}, bf16[2048,256]{1,0:T(8,128)(2,1)}, u32[]{:S(2)}, u32[]{:S(2)}) collective-permute-start(bf16[2048,256]{1,0:T(8,128)(2,1)} %all-gather.9.cloned.1.call-done.refs_2_.refs_0_.refs_8_), channel_id=1, source_target_pairs={{0,2},{1,3},{2,0},{3,1},{4,6},{5,7},{6,4},{7,5},{8,10},{9,11},{10,... | collective-permute-start | bytes 3145736 | tf_op jit(solution)/shard_map/ppermute | solution.py:93
  151.6 49.8 %collective-permute-start.22 = (bf16[2048,512]{1,0:T(8,128)(2,1)}, bf16[2048,512]{1,0:T(8,128)(2,1)}, u32[]{:S(2)}, u32[]{:S(2)}) collective-permute-start(bf16[2048,512]{1,0:T(8,128)(2,1)} %all-gather.11.cloned.1.call-done.refs_4_.refs_2_.refs_10_), channel_id=1, source_target_pairs={{0,1},{1,0},{2,3},{3,2},{4,5},{5,4},{6,7},{7,6},{8,9},{9,8},{10,11... | collective-permute-start | bytes 6291464 | tf_op jit(solution)/shard_map/ppermute | solution.py:93
  216.6 136.9 %reduce-scatter.11.cloned.1.call-start = ((), (), s32[]{:S(2)}) async-start(), calls=%async_computation.11 | async-start | bytes 2621440 | tf_op jit(solution)/shard_map/reduce_scatter | solution.py:968
  310.6 71.4 %reduce-scatter.5.cloned.1.call-start = ((), (), s32[]{:S(2)}) async-start(), calls=%async_computation.8 | async-start | bytes 1310720 | tf_op jit(solution)/shard_map/reduce_scatter | solution.py:948
  311.3 99.3 %reduce-scatter.9.cloned.1.call-start = ((), (), s32[]{:S(2)}) async-start(), calls=%async_computation.10 | async-start | bytes 1310720 | tf_op jit(solution)/shard_map/reduce_scatter | solution.py:984
  349.9 38.6 %collective-permute-start.38 = (bf16[4,512,256]{2,1,0:T(8,128)(2,1)}, bf16[4,512,256]{2,1,0:T(8,128)(2,1)}, u32[]{:S(2)}, u32[]{:S(2)}) collective-permute-start(bf16[4,512,256]{2,1,0:T(8,128)(2,1)} %get-tuple-element.145), channel_id=1, source_target_pairs={{0,16},{16,0},{1,17},{17,1},{2,18},{18,2},{3,19},{19,3},{4,20},{20... | collective-permute-start | bytes 3145736 | tf_op jit(solution)/shard_map/ppermute | solution.py:93
  351.5 30.5 %collective-permute-start.27 = (bf16[256,512]{1,0:T(8,128)(2,1)S(1)}, bf16[256,512]{1,0:T(8,128)(2,1)}, u32[]{:S(2)}, u32[]{:S(2)}) collective-permute-start(bf16[256,512]{1,0:T(8,128)(2,1)S(1)} %slice.65), channel_id=1, source_target_pairs={{0,2},{1,3},{2,0},{3,1},{4,6},{5,7},{6,4},{7,5},{8,10},{9,11},{10,... | collective-permute-start | bytes 786440 | tf_op jit(solution)/shard_map/ppermute | solution.py:93
  353.0 60.7 %collective-permute-start.47 = (bf16[2,256,512]{2,1,0:T(8,128)(2,1)}, bf16[2,256,512]{2,1,0:T(8,128)(2,1)}, u32[]{:S(2)}, u32[]{:S(2)}) collective-permute-start(bf16[2,256,512]{2,1,0:T(8,128)(2,1)} %get-tuple-element.159), channel_id=1, source_target_pairs={{0,2},{1,3},{2,0},{3,1},{4,6},{5,7},{6,4},{7,5},{8,10},{9,11},{10,... | collective-permute-start | bytes 1572872 | tf_op jit(solution)/shard_map/ppermute | solution.py:93
  355.2 36.4 %collective-permute-start.32 = (bf16[256,512]{1,0:T(8,128)(2,1)}, bf16[256,512]{1,0:T(8,128)(2,1)}, u32[]{:S(2)}, u32[]{:S(2)}) collective-permute-start(bf16[256,512]{1,0:T(8,128)(2,1)} %slice.66), channel_id=1, source_target_pairs={{0,2},{1,3},{2,0},{3,1},{4,6},{5,7},{6,4},{7,5},{8,10},{9,11},{10,... | collective-permute-start | bytes 786440 | tf_op jit(solution)/shard_map/ppermute | solution.py:93
  364.1 55.7 %collective-permute-start.48 = (bf16[2,256,512]{2,1,0:T(8,128)(2,1)}, bf16[2,256,512]{2,1,0:T(8,128)(2,1)}, u32[]{:S(2)}, u32[]{:S(2)}) collective-permute-start(bf16[2,256,512]{2,1,0:T(8,128)(2,1)} %get-tuple-element.136.refs_0_), channel_id=1, source_target_pairs={{0,16},{16,0},{1,17},{17,1},{2,18},{18,2},{3,19},{19,3},{4,20},{20... | collective-permute-start | bytes 1572872 | tf_op jit(solution)/shard_map/ppermute | solution.py:93
  387.0 33.7 %collective-permute-start.44 = (bf16[2,256,512]{2,1,0:T(8,128)(2,1)}, bf16[2,256,512]{2,1,0:T(8,128)(2,1)}, u32[]{:S(2)}, u32[]{:S(2)}) collective-permute-start(bf16[2,256,512]{2,1,0:T(8,128)(2,1)} %get-tuple-element.157), channel_id=1, source_target_pairs={{0,2},{1,3},{2,0},{3,1},{4,6},{5,7},{6,4},{7,5},{8,10},{9,11},{10,... | collective-permute-start | bytes 1572872 | tf_op jit(solution)/shard_map/ppermute | solution.py:93
  420.7 30.7 %collective-permute-start.46 = (bf16[2,256,512]{2,1,0:T(8,128)(2,1)}, bf16[2,256,512]{2,1,0:T(8,128)(2,1)}, u32[]{:S(2)}, u32[]{:S(2)}) collective-permute-start(bf16[2,256,512]{2,1,0:T(8,128)(2,1)} %collective-permute-done.44.refs_1_), channel_id=1, source_target_pairs={{0,16},{16,0},{1,17},{17,1},{2,18},{18,2},{3,19},{19,3},{4,20},{20... | collective-permute-start | bytes 1572872 | tf_op jit(solution)/shard_map/ppermute | solution.py:93
  422.1 40.5 %collective-permute-start.40 = (bf16[2,512,256]{2,1,0:T(8,128)(2,1)}, bf16[2,512,256]{2,1,0:T(8,128)(2,1)}, u32[]{:S(2)}, u32[]{:S(2)}) collective-permute-start(bf16[2,512,256]{2,1,0:T(8,128)(2,1)} %get-tuple-element.146.refs_0_), channel_id=1, source_target_pairs={{0,16},{16,0},{1,17},{17,1},{2,18},{18,2},{3,19},{19,3},{4,20},{20... | collective-permute-start | bytes 1572872 | tf_op jit(solution)/shard_map/ppermute | solution.py:93
  424.3 48.1 %collective-permute-start.41 = (bf16[2,512,256]{2,1,0:T(8,128)(2,1)}, bf16[2,512,256]{2,1,0:T(8,128)(2,1)}, u32[]{:S(2)}, u32[]{:S(2)}) collective-permute-start(bf16[2,512,256]{2,1,0:T(8,128)(2,1)} %collective-permute-done.39.refs_1_), channel_id=1, source_target_pairs={{0,16},{16,0},{1,17},{17,1},{2,18},{18,2},{3,19},{19,3},{4,20},{20... | collective-permute-start | bytes 1572872 | tf_op jit(solution)/shard_map/ppermute | solution.py:93
  428.9 51.6 %collective-permute-start.34 = (f32[2,512]{1,0:T(2,128)S(1)}, f32[2,512]{1,0:T(2,128)S(1)}, u32[]{:S(2)}, u32[]{:S(2)}) collective-permute-start(f32[2,512]{1,0:T(2,128)S(1)} %add.106), channel_id=1, source_target_pairs={{0,2},{1,3},{2,0},{3,1},{4,6},{5,7},{6,4},{7,5},{8,10},{9,11},{10,... | collective-permute-start | bytes 12296 | tf_op jit(solution)/shard_map/ppermute | solution.py:93
  440.1 44.4 %collective-permute-start.37 = (f32[3,512]{1,0:T(4,128)S(1)}, f32[3,512]{1,0:T(4,128)S(1)}, u32[]{:S(2)}, u32[]{:S(2)}) collective-permute-start(f32[3,512]{1,0:T(4,128)S(1)} %add.109), channel_id=1, source_target_pairs={{0,16},{16,0},{1,17},{17,1},{2,18},{18,2},{3,19},{19,3},{4,20},{20... | collective-permute-start | bytes 18440 | tf_op jit(solution)/shard_map/ppermute | solution.py:93
  (43 other events, 790.4 us)
Sparse Core Ops, SparseCore 0:
  16.9 29.7 all-gather.4
  48.8 27.3 all-gather.6
  77.7 27.3 all-gather.8
  106.6 45.0 all-gather.10
  216.7 41.5 reduce-scatter.6
  310.7 42.4 reduce-scatter.10
  355.4 26.4 reduce-scatter.4
  384.8 25.7 reduce-scatter.8

commit v11 on v9

--- a/solution.py
+++ b/solution.py
@@ -898,7 +898,7 @@
         tables,
     )
     out_second = swap_bits(after(out_first, act, qkv_second), DP, 1)
-    cot_2 = swap_bits(cot_0, COL, 2)
+    cot_2 = swap_bits(after(cot_0, act), COL, 2)
     act_1 = swap_bits(act, COL, 1)
     attn, attn_full, lse = attend(lowest, after(q_rot, act), k_rot, v_low, begin)
     attn_1 = swap_bits(attn, COL, 1)
@@ -967,14 +967,15 @@
         True,
     )
     rest_recv = swap_bits(rest_send, DP, 1)
+    cut = local_rows // 2
+    mix_recv_b = swap_bits(mix_b[cut:], COL, 2)
+    out = output_sum(tokens, mix_a, mix_b, mix_recv_b, out_bias.reshape(1, -1))
     fc1_near, fc1_far = sum_halves(fc1_keep, after(fc1_recv, rest_send))
     total_a = (near_a.astype(f32) + recv_a.astype(f32)).astype(bf16)
     d_normed_a = lax.psum_scatter(total_a, ROW, scatter_dimension=0, tiled=True)
     fc1_crossed = swap_bits(fc1_far, COL, 2)
     rest_near, rest_far = sum_halves(rest_keep, rest_recv)
     rest_near_x = swap_bits(rest_near, DP, 1)
-    cut = local_rows // 2
-    mix_recv_b = swap_bits(mix_b[cut:], COL, 2)
     part_recv = swap_bits(part_b[cut:], COL, 2)
     (fc2_weight_grad,) = lay_out(
         places, [fc2_near, after(fc2_crossed, rest_near)], [fc2_near_x, fc2_crossed_x], 0
@@ -992,11 +993,10 @@
     cot_sum = jnp.sum(out_grad.astype(f32), axis=0, keepdims=True)
     terms = (tokens, stats, ln_gain.reshape(1, -1), d_normed_a, part_b, part_recv)
     row_sums, vectors = norm_sums(*terms, cot_sum)
-    vectors = total_over(vectors, (DP,))
     row_sums = total_over(row_sums, (COL,))
-    vector_sums = total_over(vectors, (ROW,))
+    vectors = total_over(vectors, (ROW,))
+    vector_sums = total_over(vectors, (DP,))
     tokens_grad = norm_back(*terms, row_sums, out_grad, full_width)
-    out = output_sum(tokens, mix_a, mix_b, mix_recv_b, out_bias.reshape(1, -1))
     bias_sums = total_over(jnp.concatenate([qkv_sums, fc1_sums], axis=1), (DP,))[0]
     return (
         out,

time: 504 us -> 491 us (0.974)
  waiting for transfers between devices: 253 us -> 242 us
    ppermute x50, waiting for transfers between devices: 209 us -> 182 us  [swap_bits(): lax.ppermute(value, axis, [(place, place ^ bit) for place in range(count)])]
    reduce_scatter x1, waiting for transfers between devices: 0.01 us -> 16.8 us  [step(): mix_a = lax.psum_scatter(mix_total, ROW, scatter_dimension=0, tiled=True)]
    all_gather x1, waiting for transfers between devices: 0.01 us -> 16.6 us  [step(): lax.all_gather(after(out_grad[:, :cut], normed), ROW, axis=0, tiled=True)]
    all_gather x1, waiting for transfers between devices: 16.3 us -> 0.01 us  [step(): lax.all_gather(jnp.concatenate([tail, tail_far], axis=1), ROW, axis=0, ti...]
  transfers between devices with their start and end apart: 58 -> 58, of which waited for: 23 -> 27; matrix products, arithmetic and copies ran while one was open for 6% -> 7% of each run, Pallas kernels for 19% -> 20%
where the time goes in v11:
time: 491 us; the launch traced here: 490 us
  waiting for transfers between devices  242 us (49%)
  Pallas kernels  151 us (31%)
  starting transfers between devices  44.2 us (9%)
  other arithmetic  19.7 us (4%)
  local copies, waits for them, and re-layouts  18.9 us (4%)
  between operations  14.4 us (3%)
    ppermute x50, waiting for transfers between devices, swap_bits(): lax.ppermute(value, axis, [(place, place ^ bit) for place in range(count)])  182 us
    ppermute x50, starting transfers between devices, swap_bits(): lax.ppermute(value, axis, [(place, place ^ bit) for place in range(count)])  43.5 us
    pallas_call x3, Pallas kernels, grad_blocks(): pl.pallas_call(kernel, grid_spec=pltpu.PrefetchScalarGridSpec(num_scalar_...  29.5 us
    all_gather x1, waiting for transfers between devices, step(): normed_0b = lax.all_gather(normed[:, cut:], ROW, axis=0, tiled=True)  25.6 us
    pallas_call x2, Pallas kernels, spread(): pl.pallas_call(kernel, grid=(rows // block,), in_specs=[rowed(hidden), ro...  22 us
    pallas_call x1, Pallas kernels, attend_back(): pl.pallas_call(kernel, grid_spec=pltpu.PrefetchScalarGridSpec(num_scalar_...  17.9 us
    reduce_scatter x1, waiting for transfers between devices, step(): mix_a = lax.psum_scatter(mix_total, ROW, scatter_dimension=0, tiled=True)  16.8 us
    all_gather x1, waiting for transfers between devices, step(): lax.all_gather(after(out_grad[:, :cut], normed), ROW, axis=0, tiled=True)  16.6 us
  transfers between devices with their start and end apart: 58, of which 27 were waited for; matrix products, arithmetic and copies ran while one was open for 7% of the time, Pallas kernels for 20%

profile of v11, /device:TPU:0, one launch (start us, length us, event | category | flops | bytes accessed | tf_op | source)
XLA Modules:
  0.0 490.1 jit_solution(12567672550012276399)
XLA Ops:
  35.6 6.2 %collective-permute-done.3.refs_1_ = bf16[512,384]{1,0:T(8,128)(2,1)S(1)} collective-permute-done((bf16[512,384]{1,0:T(8,128)(2,1)}, bf16[512,384]{1,0:T(8,128)(2,1)S(1)}, u32[]{:S(2)}, u32[]{:S(2)}) %collective-permute-start.3) | collective-permute-done | bytes 393248 | tf_op jit(solution)/shard_map/ppermute | solution.py:93
  50.5 25.6 %all-gather.7.cloned.1.call-done.refs_1_.refs_3_ = bf16[2048,256]{1,0:T(8,128)(2,1)} async-done(((bf16[512,256]{1,0:T(8,128)(2,1)}), bf16[2048,256]{1,0:T(8,128)(2,1)}) %all-gather.7.cloned.1.call-update) | async-done | bytes 1048592 | tf_op jit(solution)/shard_map/all_gather | solution.py:864
  79.5 11.3 %collective-permute-done.11.refs_2_ = bf16[512,512]{1,0:T(8,128)(2,1)} collective-permute-done((bf16[512,512]{1,0:T(8,128)(2,1)}, bf16[512,512]{1,0:T(8,128)(2,1)}, u32[]{:S(2)}, u32[]{:S(2)}) %collective-permute-start.11) | collective-permute-done | bytes 524320 | tf_op jit(solution)/shard_map/ppermute | solution.py:93
  93.0 7.1 %collective-permute-done.12.refs_3_ = bf16[512,384]{1,0:T(8,128)(2,1)S(1)} collective-permute-done((bf16[512,384]{1,0:T(8,128)(2,1)S(1)}, bf16[512,384]{1,0:T(8,128)(2,1)S(1)}, u32[]{:S(2)}, u32[]{:S(2)}) %collective-permute-start.12) | collective-permute-done | bytes 393248 | tf_op jit(solution)/shard_map/ppermute | solution.py:93
  101.4 5.7 %fusion = (f32[2048,128]{1,0:T(8,128)}, f32[2048,128]{1,0:T(8,128)}, f32[2048,128]{1,0:T(8,128)}) fusion(f32[128]{0:T(128)S(1)} %fusion.12, f32[2048]{0:T(1024)S(1)} %get-tuple-element.207, pred[128]{0:T(512)(128)(4,1)S(1)} %get-tuple-element.211, pred[128]{0:T(512)(128)(4,1)S(1)} %get-tuple-element.212, pred[128]{0:T(512)(128)(4,1)S(1)} %broadcast_compare_fusion.1), kind=kLoop, calls=%fused_computation.7 | loop fusion | flops 1310720 | bytes 3154816 | tf_op jit(solution)/shard_map/jit(_where)/select_n | solution.py:62
  112.9 15.6 %shard_map.205 = (f32[2048,512]{1,0:T(8,128)}, bf16[2048,512]{1,0:T(8,128)(2,1)}, bf16[2048,128]{1,0:T(8,128)(2,1)}, bf16[2048,128]{1,0:T(8,128)(2,1)}, bf16[2048,128]{1,0:T(8,128)(2,1)}) custom-call(bf16[2048,256]{1,0:T(8,128)(2,1)} %all-gather.5.cloned.1.call-done.refs_0_.refs_2_, bf16[2048,256]{1,0:T(8,128)(2,1)} %all-gather.7.cloned.1.call-done.refs_1_.refs_3_, ...), custom_call_target="tpu_custom_call" | custom-call | flops 7516192768 | bytes 18874368 | tf_op jit(solution)/shard_map/pallas_call | solution.py:201
  134.5 16.6 %all-gather.9.cloned.1.call-done.refs_2_.refs_0_.refs_8_ = bf16[2048,256]{1,0:T(8,128)(2,1)} async-done(((bf16[512,256]{1,0:T(8,128)(2,1)}), bf16[2048,256]{1,0:T(8,128)(2,1)}) %all-gather.9.cloned.1.call-update) | async-done | bytes 1048592 | tf_op jit(solution)/shard_map/all_gather | solution.py:871
  153.1 12.0 %shard_map.206 = (bf16[2048,128]{1,0:T(8,128)(2,1)}, f32[2048,128]{1,0:T(8,128)}, f32[2,2048]{1,0:T(2,128)}) custom-call(s32[4]{0:T(128)} %and_select_fusion.lowest_ref, bf16[2048,128]{1,0:T(8,128)(2,1)} %get-tuple-element.104.q_ref, bf16[2048,128]{1,0:T(8,128)(2,1)} %get-tuple-element.105.k_ref, bf16[2048,128]{1,0:T(8,128)(2,1)} %get-tuple-element.106.v_ref, ...), custom_call_target="tpu_custom_call" | custom-call | flops 1073741824 | bytes 3145728 | tf_op jit(solution)/shard_map/pallas_call | solution.py:684
  167.6 8.2 %collective-permute-done.19.refs_3_.refs_1_.refs_9_ = bf16[2048,256]{1,0:T(8,128)(2,1)} collective-permute-done((bf16[2048,256]{1,0:T(8,128)(2,1)}, bf16[2048,256]{1,0:T(8,128)(2,1)}, u32[]{:S(2)}, u32[]{:S(2)}) %collective-permute-start.19) | collective-permute-done | bytes 1048608 | tf_op jit(solution)/shard_map/ppermute | solution.py:93
  175.8 6.9 %collective-permute-done.18.refs_7_.refs_10_ = bf16[640,512]{1,0:T(8,128)(2,1)} collective-permute-done((bf16[640,512]{1,0:T(8,128)(2,1)}, bf16[640,512]{1,0:T(8,128)(2,1)}, u32[]{:S(2)}, u32[]{:S(2)}) %collective-permute-start.18) | collective-permute-done | bytes 655392 | tf_op jit(solution)/shard_map/ppermute | solution.py:93
  183.2 9.6 %shard_map.208 = (bf16[1024,512]{1,0:T(8,128)(2,1)}, bf16[1024,512]{1,0:T(8,128)(2,1)}, bf16[2048,512]{1,0:T(8,128)(2,1)}) custom-call(bf16[2048,512]{1,0:T(8,128)(2,1)} %get-tuple-element.102.refs_0_, bf16[2048,128]{1,0:T(8,128)(2,1)} %get-tuple-element.107.refs_1_.refs_6_, bf16[2048,512]{1,0:T(8,128)(2,1)} %collective-permute-done.15.refs_2_.refs_1_, ...), custom_call_target="tpu_custom_call" | custom-call | flops 5368709120 | bytes 9437184 | tf_op jit(solution)/shard_map/pallas_call | solution.py:374
  192.8 9.4 %shard_map.209 = (bf16[4,256,512]{2,1,0:T(8,128)(2,1)}, bf16[4,256,512]{2,1,0:T(8,128)(2,1)}) custom-call(s32[1]{0:T(128)} %bitcast.15.half_ref, bf16[2048,512]{1,0:T(8,128)(2,1)} %get-tuple-element.102.refs_0_, bf16[2048,512]{1,0:T(8,128)(2,1)} %collective-permute-done.15.refs_2_.refs_1_, ...), custom_call_target="tpu_custom_call" | custom-call | flops 4294967296 | bytes 16777216 | tf_op jit(solution)/shard_map/pallas_call | solution.py:464
  202.3 13.4 %shard_map.210 = (bf16[2048,512]{1,0:T(8,128)(2,1)}, bf16[2048,128]{1,0:T(8,128)(2,1)}, f32[1,512]{1,0:T(1,128)}) custom-call(bf16[2048,256]{1,0:T(8,128)(2,1)} %all-gather.9.cloned.1.call-done.refs_2_.refs_0_.refs_8_, bf16[2048,256]{1,0:T(8,128)(2,1)} %collective-permute-done.19.refs_3_.refs_1_.refs_9_, ...), custom_call_target="tpu_custom_call" | custom-call | flops 5368709120 | bytes 14680064 | tf_op jit(solution)/shard_map/pallas_call | solution.py:263
  216.4 25.2 %collective-permute-done.26 = bf16[1024,512]{1,0:T(8,128)(2,1)S(1)} collective-permute-done((bf16[1024,512]{1,0:T(8,128)(2,1)}, bf16[1024,512]{1,0:T(8,128)(2,1)S(1)}, u32[]{:S(2)}, u32[]{:S(2)}) %collective-permute-start.26) | collective-permute-done | bytes 1048608 | tf_op jit(solution)/shard_map/ppermute | solution.py:93
  244.1 9.4 %shard_map.212 = (bf16[4,256,512]{2,1,0:T(8,128)(2,1)}, bf16[4,256,512]{2,1,0:T(8,128)(2,1)}) custom-call(s32[1]{0:T(128)} %bitcast.15.half_ref, bf16[2048,256]{1,0:T(8,128)(2,1)} %all-gather.5.cloned.1.call-done.refs_0_.refs_2_, bf16[2048,256]{1,0:T(8,128)(2,1)} %all-gather.7.cloned.1.call-done.refs_1_.refs_3_, ...), custom_call_target="tpu_custom_call" | custom-call | flops 4294967296 | bytes 16777216 | tf_op jit(solution)/shard_map/pallas_call | solution.py:464
  253.5 17.9 %shard_map.213 = (bf16[2048,384]{1,0:T(8,128)(2,1)}, f32[1,384]{1,0:T(1,128)}) custom-call(s32[4]{0:T(128)} %and_select_fusion.lowest_ref, bf16[2048,128]{1,0:T(8,128)(2,1)} %get-tuple-element.104.q_ref, bf16[2048,128]{1,0:T(8,128)(2,1)} %get-tuple-element.105.k_ref, bf16[2048,128]{1,0:T(8,128)(2,1)} %get-tuple-element.106.v_ref, ...), custom_call_target="tpu_custom_call" | custom-call | flops 2684354560 | bytes 4194304 | tf_op jit(solution)/shard_map/pallas_call | solution.py:789
  272.9 24.4 %collective-permute-done.29.received_ref = bf16[4,256,512]{2,1,0:T(8,128)(2,1)} collective-permute-done((bf16[4,256,512]{2,1,0:T(8,128)(2,1)}, bf16[4,256,512]{2,1,0:T(8,128)(2,1)}, u32[]{:S(2)}, u32[]{:S(2)}) %collective-permute-start.29) | collective-permute-done | bytes 1048608 | tf_op jit(solution)/shard_map/ppermute | solution.py:93
  299.9 12.4 %shard_map.215 = (bf16[1024,512]{1,0:T(8,128)(2,1)}, bf16[1024,512]{1,0:T(8,128)(2,1)}, bf16[2048,512]{1,0:T(8,128)(2,1)}) custom-call(bf16[2048,512]{1,0:T(8,128)(2,1)} %get-tuple-element.128.refs_4_.refs_0_, bf16[2048,384]{1,0:T(8,128)(2,1)} %get-tuple-element.144.refs_1_.refs_0_, bf16[2048,512]{1,0:T(8,128)(2,1)} %collective-permute-done.28.refs_5_.refs_2_, ...), custom_call_target="tpu_custom_call" | custom-call | flops 7516192768 | bytes 11534336 | tf_op jit(solution)/shard_map/pallas_call | solution.py:374
  314.2 24.1 %collective-permute-done.31 = bf16[1024,512]{1,0:T(8,128)(2,1)S(1)} collective-permute-done((bf16[1024,512]{1,0:T(8,128)(2,1)S(1)}, bf16[1024,512]{1,0:T(8,128)(2,1)S(1)}, u32[]{:S(2)}, u32[]{:S(2)}) %collective-permute-start.31) | collective-permute-done | bytes 1048608 | tf_op jit(solution)/shard_map/ppermute | solution.py:93
  342.1 10.7 %shard_map.218 = (bf16[4,512,256]{2,1,0:T(8,128)(2,1)}, bf16[4,512,256]{2,1,0:T(8,128)(2,1)}) custom-call(s32[1]{0:T(128)} %bitcast.15.half_ref, bf16[2048,384]{1,0:T(8,128)(2,1)} %get-tuple-element.144.refs_1_.refs_0_, bf16[2048,384]{1,0:T(8,128)(2,1)} %collective-permute-done.30.refs_3_.refs_1_, ...), custom_call_target="tpu_custom_call" | custom-call | flops 4294967296 | bytes 16777216 | tf_op jit(solution)/shard_map/pallas_call | solution.py:464
  355.4 11.6 %collective-permute-done.43.received_ref = bf16[4,256,512]{2,1,0:T(8,128)(2,1)} collective-permute-done((bf16[4,256,512]{2,1,0:T(8,128)(2,1)}, bf16[4,256,512]{2,1,0:T(8,128)(2,1)}, u32[]{:S(2)}, u32[]{:S(2)}) %collective-permute-start.43) | collective-permute-done | bytes 1048608 | tf_op jit(solution)/shard_map/ppermute | solution.py:93
  370.2 19.3 %collective-permute-done.38.received_ref = bf16[4,512,256]{2,1,0:T(8,128)(2,1)} collective-permute-done((bf16[4,512,256]{2,1,0:T(8,128)(2,1)}, bf16[4,512,256]{2,1,0:T(8,128)(2,1)}, u32[]{:S(2)}, u32[]{:S(2)}) %collective-permute-start.38) | collective-permute-done | bytes 1048608 | tf_op jit(solution)/shard_map/ppermute | solution.py:93
  395.8 14.1 %collective-permute-done.42 = f32[1,896]{1,0:T(1,128)S(1)} collective-permute-done((f32[1,896]{1,0:T(1,128)S(1)}, f32[1,896]{1,0:T(1,128)S(1)}, u32[]{:S(2)}, u32[]{:S(2)}) %collective-permute-start.42) | collective-permute-done | bytes 3616 | tf_op jit(solution)/shard_map/ppermute | solution.py:93
  441.1 16.8 %reduce-scatter.5.cloned.1.call-done.first_ref = bf16[256,512]{1,0:T(8,128)(2,1)} async-done(((bf16[1024,512]{1,0:T(8,128)(2,1)}), bf16[256,512]{1,0:T(8,128)(2,1)}) %reduce-scatter.5.cloned.1.call-update) | async-done | bytes 262160 | tf_op jit(solution)/shard_map/reduce_scatter | solution.py:939
  (183 shorter events, 142.3 us)
Async XLA Ops:
  7.2 41.0 %all-gather.5.cloned.1.call-start = ((), (), s32[]{:S(2)}) async-start(), calls=%async_computation.4 | async-start | bytes 1310720 | tf_op jit(solution)/shard_map/all_gather | solution.py:863
  16.7 59.4 %all-gather.7.cloned.1.call-start = ((), (), s32[]{:S(2)}) async-start(), calls=%async_computation.5 | async-start | bytes 1310720 | tf_op jit(solution)/shard_map/all_gather | solution.py:864
  20.7 113.7 %all-gather.11.cloned.1.call-start = ((), (), s32[]{:S(2)}) async-start(), calls=%async_computation.7 | async-start | bytes 2621440 | tf_op jit(solution)/shard_map/all_gather | solution.py:872
  50.5 100.6 %all-gather.9.cloned.1.call-start = ((), (), s32[]{:S(2)}) async-start(), calls=%async_computation.6 | async-start | bytes 1310720 | tf_op jit(solution)/shard_map/all_gather | solution.py:871
  79.5 30.6 %collective-permute-start.13 = (bf16[512,896]{1,0:T(8,128)(2,1)}, bf16[512,896]{1,0:T(8,128)(2,1)}, u32[]{:S(2)}, u32[]{:S(2)}) collective-permute-start(bf16[512,896]{1,0:T(8,128)(2,1)} %get-tuple-element.100.refs_5_), channel_id=1, source_target_pairs={{0,1},{1,0},{2,3},{3,2},{4,5},{5,4},{6,7},{7,6},{8,9},{9,8},{10,11... | collective-permute-start | bytes 2752520 | tf_op jit(solution)/shard_map/ppermute | solution.py:93
  110.1 284.7 %reduce-scatter.11.cloned.1.call-start = ((), (), s32[]{:S(2)}) async-start(), calls=%async_computation.11 | async-start | bytes 2621440 | tf_op jit(solution)/shard_map/reduce_scatter | solution.py:959
  128.5 54.2 %collective-permute-start.15 = (bf16[2048,512]{1,0:T(8,128)(2,1)}, bf16[2048,512]{1,0:T(8,128)(2,1)}, u32[]{:S(2)}, u32[]{:S(2)}) collective-permute-start(bf16[2048,512]{1,0:T(8,128)(2,1)} %get-tuple-element.102.refs_0_), channel_id=1, source_target_pairs={{0,1},{1,0},{2,3},{3,2},{4,5},{5,4},{6,7},{7,6},{8,9},{9,8},{10,11... | collective-permute-start | bytes 6291464 | tf_op jit(solution)/shard_map/ppermute | solution.py:93
  132.3 32.9 %collective-permute-start.23 = (bf16[640,512]{1,0:T(8,128)(2,1)}, bf16[640,512]{1,0:T(8,128)(2,1)}, u32[]{:S(2)}, u32[]{:S(2)}) collective-permute-start(bf16[640,512]{1,0:T(8,128)(2,1)} %get-tuple-element.110.refs_5_), channel_id=1, source_target_pairs={{0,1},{1,0},{2,3},{3,2},{4,5},{5,4},{6,7},{7,6},{8,9},{9,8},{10,11... | collective-permute-start | bytes 1966088 | tf_op jit(solution)/shard_map/ppermute | solution.py:93
  132.7 32.5 %collective-permute-start.17 = (bf16[640,512]{1,0:T(8,128)(2,1)}, bf16[640,512]{1,0:T(8,128)(2,1)}, u32[]{:S(2)}, u32[]{:S(2)}) collective-permute-start(bf16[640,512]{1,0:T(8,128)(2,1)} %get-tuple-element.112), channel_id=1, source_target_pairs={{0,2},{1,3},{2,0},{3,1},{4,6},{5,7},{6,4},{7,5},{8,10},{9,11},{10,... | collective-permute-start | bytes 1966088 | tf_op jit(solution)/shard_map/ppermute | solution.py:93
  134.4 67.9 %collective-permute-start.22 = (bf16[2048,512]{1,0:T(8,128)(2,1)}, bf16[2048,512]{1,0:T(8,128)(2,1)}, u32[]{:S(2)}, u32[]{:S(2)}) collective-permute-start(bf16[2048,512]{1,0:T(8,128)(2,1)} %all-gather.11.cloned.1.call-done.refs_4_.refs_2_.refs_10_), channel_id=1, source_target_pairs={{0,1},{1,0},{2,3},{3,2},{4,5},{5,4},{6,7},{7,6},{8,9},{9,8},{10,11... | collective-permute-start | bytes 6291464 | tf_op jit(solution)/shard_map/ppermute | solution.py:93
  167.5 34.8 %collective-permute-start.20 = (bf16[2048,256]{1,0:T(8,128)(2,1)}, bf16[2048,256]{1,0:T(8,128)(2,1)}, u32[]{:S(2)}, u32[]{:S(2)}) collective-permute-start(bf16[2048,256]{1,0:T(8,128)(2,1)} %all-gather.9.cloned.1.call-done.refs_2_.refs_0_.refs_8_), channel_id=1, source_target_pairs={{0,1},{1,0},{2,3},{3,2},{4,5},{5,4},{6,7},{7,6},{8,9},{9,8},{10,11... | collective-permute-start | bytes 3145736 | tf_op jit(solution)/shard_map/ppermute | solution.py:93
  312.4 106.0 %reduce-scatter.9.cloned.1.call-start = ((), (), s32[]{:S(2)}) async-start(), calls=%async_computation.10 | async-start | bytes 1310720 | tf_op jit(solution)/shard_map/reduce_scatter | solution.py:975
  339.5 89.6 %reduce-scatter.7.cloned.1.call-start = ((), (), s32[]{:S(2)}) async-start(), calls=%async_computation.9 | async-start | bytes 2621440 | tf_op jit(solution)/shard_map/reduce_scatter | solution.py:917
  340.3 117.6 %reduce-scatter.5.cloned.1.call-start = ((), (), s32[]{:S(2)}) async-start(), calls=%async_computation.8 | async-start | bytes 1310720 | tf_op jit(solution)/shard_map/reduce_scatter | solution.py:939
  352.8 36.7 %collective-permute-start.38 = (bf16[4,512,256]{2,1,0:T(8,128)(2,1)}, bf16[4,512,256]{2,1,0:T(8,128)(2,1)}, u32[]{:S(2)}, u32[]{:S(2)}) collective-permute-start(bf16[4,512,256]{2,1,0:T(8,128)(2,1)} %get-tuple-element.146), channel_id=1, source_target_pairs={{0,16},{16,0},{1,17},{17,1},{2,18},{18,2},{3,19},{19,3},{4,20},{20... | collective-permute-start | bytes 3145736 | tf_op jit(solution)/shard_map/ppermute | solution.py:93
  353.4 39.3 %collective-permute-start.47 = (bf16[2,256,512]{2,1,0:T(8,128)(2,1)}, bf16[2,256,512]{2,1,0:T(8,128)(2,1)}, u32[]{:S(2)}, u32[]{:S(2)}) collective-permute-start(bf16[2,256,512]{2,1,0:T(8,128)(2,1)} %get-tuple-element.159), channel_id=1, source_target_pairs={{0,2},{1,3},{2,0},{3,1},{4,6},{5,7},{6,4},{7,5},{8,10},{9,11},{10,... | collective-permute-start | bytes 1572872 | tf_op jit(solution)/shard_map/ppermute | solution.py:93
  354.0 56.4 %collective-permute-start.48 = (bf16[2,256,512]{2,1,0:T(8,128)(2,1)}, bf16[2,256,512]{2,1,0:T(8,128)(2,1)}, u32[]{:S(2)}, u32[]{:S(2)}) collective-permute-start(bf16[2,256,512]{2,1,0:T(8,128)(2,1)} %get-tuple-element.137.refs_0_), channel_id=1, source_target_pairs={{0,16},{16,0},{1,17},{17,1},{2,18},{18,2},{3,19},{19,3},{4,20},{20... | collective-permute-start | bytes 1572872 | tf_op jit(solution)/shard_map/ppermute | solution.py:93
  369.7 43.9 %collective-permute-start.44 = (bf16[2,256,512]{2,1,0:T(8,128)(2,1)}, bf16[2,256,512]{2,1,0:T(8,128)(2,1)}, u32[]{:S(2)}, u32[]{:S(2)}) collective-permute-start(bf16[2,256,512]{2,1,0:T(8,128)(2,1)} %get-tuple-element.157), channel_id=1, source_target_pairs={{0,2},{1,3},{2,0},{3,1},{4,6},{5,7},{6,4},{7,5},{8,10},{9,11},{10,... | collective-permute-start | bytes 1572872 | tf_op jit(solution)/shard_map/ppermute | solution.py:93
  392.7 28.8 %collective-permute-start.49 = (bf16[2,256,512]{2,1,0:T(8,128)(2,1)}, bf16[2,256,512]{2,1,0:T(8,128)(2,1)}, u32[]{:S(2)}, u32[]{:S(2)}) collective-permute-start(bf16[2,256,512]{2,1,0:T(8,128)(2,1)} %collective-permute-done.47.refs_1_), channel_id=1, source_target_pairs={{0,16},{16,0},{1,17},{17,1},{2,18},{18,2},{3,19},{19,3},{4,20},{20... | collective-permute-start | bytes 1572872 | tf_op jit(solution)/shard_map/ppermute | solution.py:93
  413.6 51.0 %collective-permute-start.46 = (bf16[2,256,512]{2,1,0:T(8,128)(2,1)}, bf16[2,256,512]{2,1,0:T(8,128)(2,1)}, u32[]{:S(2)}, u32[]{:S(2)}) collective-permute-start(bf16[2,256,512]{2,1,0:T(8,128)(2,1)} %collective-permute-done.44.refs_1_), channel_id=1, source_target_pairs={{0,16},{16,0},{1,17},{17,1},{2,18},{18,2},{3,19},{19,3},{4,20},{20... | collective-permute-start | bytes 1572872 | tf_op jit(solution)/shard_map/ppermute | solution.py:93
  414.2 54.8 %collective-permute-start.40 = (bf16[2,512,256]{2,1,0:T(8,128)(2,1)}, bf16[2,512,256]{2,1,0:T(8,128)(2,1)}, u32[]{:S(2)}, u32[]{:S(2)}) collective-permute-start(bf16[2,512,256]{2,1,0:T(8,128)(2,1)} %get-tuple-element.147.refs_0_), channel_id=1, source_target_pairs={{0,16},{16,0},{1,17},{17,1},{2,18},{18,2},{3,19},{19,3},{4,20},{20... | collective-permute-start | bytes 1572872 | tf_op jit(solution)/shard_map/ppermute | solution.py:93
  416.3 52.7 %collective-permute-start.41 = (bf16[2,512,256]{2,1,0:T(8,128)(2,1)}, bf16[2,512,256]{2,1,0:T(8,128)(2,1)}, u32[]{:S(2)}, u32[]{:S(2)}) collective-permute-start(bf16[2,512,256]{2,1,0:T(8,128)(2,1)} %collective-permute-done.39.refs_1_), channel_id=1, source_target_pairs={{0,16},{16,0},{1,17},{17,1},{2,18},{18,2},{3,19},{19,3},{4,20},{20... | collective-permute-start | bytes 1572872 | tf_op jit(solution)/shard_map/ppermute | solution.py:93
  433.9 44.8 %collective-permute-start.34 = (f32[2,512]{1,0:T(2,128)S(1)}, f32[2,512]{1,0:T(2,128)S(1)}, u32[]{:S(2)}, u32[]{:S(2)}) collective-permute-start(f32[2,512]{1,0:T(2,128)S(1)} %add.106), channel_id=1, source_target_pairs={{0,2},{1,3},{2,0},{3,1},{4,6},{5,7},{6,4},{7,5},{8,10},{9,11},{10,... | collective-permute-start | bytes 12296 | tf_op jit(solution)/shard_map/ppermute | solution.py:93
  438.8 43.9 %collective-permute-start.37 = (f32[3,512]{1,0:T(4,128)S(1)}, f32[3,512]{1,0:T(4,128)S(1)}, u32[]{:S(2)}, u32[]{:S(2)}) collective-permute-start(f32[3,512]{1,0:T(4,128)S(1)} %add.109), channel_id=1, source_target_pairs={{0,16},{16,0},{1,17},{17,1},{2,18},{18,2},{3,19},{19,3},{4,20},{20... | collective-permute-start | bytes 18440 | tf_op jit(solution)/shard_map/ppermute | solution.py:93
  (42 other events, 744.8 us)
Sparse Core Ops, SparseCore 0:
  16.9 29.7 all-gather.4
  48.8 27.3 all-gather.6
  77.7 45.0 all-gather.10
  124.2 26.7 all-gather.8
  312.5 42.0 reduce-scatter.10
  357.4 26.4 reduce-scatter.8
  386.8 42.2 reduce-scatter.6
  431.4 26.4 reduce-scatter.4

commit v12 on v11

--- a/solution.py
+++ b/solution.py
@@ -31,8 +31,8 @@
 ROW, COL, DP = "row", "col", "dp"
 
 
-def params():
-    return pltpu.CompilerParams(vmem_limit_bytes=67000000)
+def params(limit=67000000):
+    return pltpu.CompilerParams(vmem_limit_bytes=limit)
 
 
 def cost(flops, bytes_accessed, transcendentals=0):
@@ -211,7 +211,7 @@
             jax.ShapeDtypeStruct((rows, hidden), bf16),
         ]
         + [jax.ShapeDtypeStruct((rows, pair), bf16)] * 3,
-        compiler_params=params(),
+        compiler_params=params(40 << 20),
         cost_estimate=cost(
             8 * rows * width * (hidden + 3 * pair), 8 * rows * width + 10 * rows * hidden
         ),
@@ -994,7 +994,8 @@
     terms = (tokens, stats, ln_gain.reshape(1, -1), d_normed_a, part_b, part_recv)
     row_sums, vectors = norm_sums(*terms, cot_sum)
     row_sums = total_over(row_sums, (COL,))
-    vectors = total_over(vectors, (ROW,))
+    for bit in all_bits(ROW):
+        vectors = vectors + swap_bits(vectors, ROW, bit)
     vector_sums = total_over(vectors, (DP,))
     tokens_grad = norm_back(*terms, row_sums, out_grad, full_width)
     bias_sums = total_over(jnp.concatenate([qkv_sums, fc1_sums], axis=1), (DP,))[0]

time: 491 us -> 491 us (level)
  local copies, waits for them, and re-layouts: 18.9 us -> 25.3 us
  waiting for transfers between devices: 242 us -> 237 us
    unnamed x19 -> x39, local copies, waits for them, and re-layouts: 5.24 us -> 11.7 us
    all_gather x1, waiting for transfers between devices: 16.6 us -> 11.3 us  [step(): lax.all_gather(after(out_grad[:, :cut], normed), ROW, axis=0, tiled=True)]
where the time goes in v12:
time: 491 us; the launch traced here: 490 us
  waiting for transfers between devices  237 us (48%)
  Pallas kernels  149 us (30%)
  starting transfers between devices  44.4 us (9%)
  local copies, waits for them, and re-layouts  25.3 us (5%)
  other arithmetic  19.6 us (4%)
  between operations  14.5 us (3%)
    ppermute x50, waiting for transfers between devices, swap_bits(): lax.ppermute(value, axis, [(place, place ^ bit) for place in range(count)])  182 us
    ppermute x50, starting transfers between devices, swap_bits(): lax.ppermute(value, axis, [(place, place ^ bit) for place in range(count)])  43.6 us
    pallas_call x3, Pallas kernels, grad_blocks(): pl.pallas_call(kernel, grid_spec=pltpu.PrefetchScalarGridSpec(num_scalar_...  29.5 us
    all_gather x1, waiting for transfers between devices, step(): normed_0b = lax.all_gather(normed[:, cut:], ROW, axis=0, tiled=True)  25.7 us
    pallas_call x2, Pallas kernels, spread(): pl.pallas_call(kernel, grid=(rows // block,), in_specs=[rowed(hidden), ro...  22 us
    pallas_call x1, Pallas kernels, attend_back(): pl.pallas_call(kernel, grid_spec=pltpu.PrefetchScalarGridSpec(num_scalar_...  17.9 us
    reduce_scatter x1, waiting for transfers between devices, step(): mix_a = lax.psum_scatter(mix_total, ROW, scatter_dimension=0, tiled=True)  16.8 us
    pallas_call x1, Pallas kernels, forward_step(): pl.pallas_call(kernel, grid=(rows // block,), in_specs=[rowed(x.shape[1])...  14.1 us
  transfers between devices with their start and end apart: 58, of which 27 were waited for; matrix products, arithmetic and copies ran while one was open for 7% of the time, Pallas kernels for 20%

profile of v12, /device:TPU:0, one launch (start us, length us, event | category | flops | bytes accessed | tf_op | source)
XLA Modules:
  0.0 490.1 jit_solution(10576941725036796267)
XLA Ops:
  35.6 6.2 %collective-permute-done.3.refs_1_ = bf16[512,384]{1,0:T(8,128)(2,1)S(1)} collective-permute-done((bf16[512,384]{1,0:T(8,128)(2,1)}, bf16[512,384]{1,0:T(8,128)(2,1)S(1)}, u32[]{:S(2)}, u32[]{:S(2)}) %collective-permute-start.3) | collective-permute-done | bytes 393248 | tf_op jit(solution)/shard_map/ppermute | solution.py:93
  50.5 25.7 %all-gather.7.cloned.1.call-done.refs_1_.refs_3_ = bf16[2048,256]{1,0:T(8,128)(2,1)} async-done(((bf16[512,256]{1,0:T(8,128)(2,1)}), bf16[2048,256]{1,0:T(8,128)(2,1)}) %all-gather.7.cloned.1.call-update) | async-done | bytes 1048592 | tf_op jit(solution)/shard_map/all_gather | solution.py:864
  79.5 11.2 %collective-permute-done.11.refs_2_ = bf16[512,512]{1,0:T(8,128)(2,1)S(1)} collective-permute-done((bf16[512,512]{1,0:T(8,128)(2,1)}, bf16[512,512]{1,0:T(8,128)(2,1)S(1)}, u32[]{:S(2)}, u32[]{:S(2)}) %collective-permute-start.11) | collective-permute-done | bytes 524320 | tf_op jit(solution)/shard_map/ppermute | solution.py:93
  92.9 7.2 %collective-permute-done.12.refs_3_ = bf16[512,384]{1,0:T(8,128)(2,1)S(1)} collective-permute-done((bf16[512,384]{1,0:T(8,128)(2,1)S(1)}, bf16[512,384]{1,0:T(8,128)(2,1)S(1)}, u32[]{:S(2)}, u32[]{:S(2)}) %collective-permute-start.12) | collective-permute-done | bytes 393248 | tf_op jit(solution)/shard_map/ppermute | solution.py:93
  100.9 5.8 %fusion = (f32[2048,128]{1,0:T(8,128)}, f32[2048,128]{1,0:T(8,128)}, f32[2048,128]{1,0:T(8,128)}) fusion(f32[128]{0:T(128)S(1)} %fusion.12, f32[2048]{0:T(1024)S(1)} %get-tuple-element.207, pred[128]{0:T(512)(128)(4,1)S(1)} %get-tuple-element.211, pred[128]{0:T(512)(128)(4,1)S(1)} %get-tuple-element.212, pred[128]{0:T(512)(128)(4,1)S(1)} %broadcast_compare_fusion.1), kind=kLoop, calls=%fused_computation.7 | loop fusion | flops 1310720 | bytes 3154816 | tf_op jit(solution)/shard_map/jit(_where)/select_n | solution.py:62
  117.3 14.1 %shard_map.205 = (f32[2048,512]{1,0:T(8,128)}, bf16[2048,512]{1,0:T(8,128)(2,1)}, bf16[2048,128]{1,0:T(8,128)(2,1)S(1)}, bf16[2048,128]{1,0:T(8,128)(2,1)S(1)}, bf16[2048,128]{1,0:T(8,128)(2,1)S(1)}) custom-call(bf16[2048,256]{1,0:T(8,128)(2,1)S(1)} %copy-done, bf16[2048,256]{1,0:T(8,128)(2,1)S(1)} %copy-done.1, ...), custom_call_target="tpu_custom_call" | custom-call | flops 7516192768 | bytes 18874368 | tf_op jit(solution)/shard_map/pallas_call | solution.py:201
  139.8 11.3 %all-gather.9.cloned.1.call-done.refs_2_.refs_0_.refs_8_ = bf16[2048,256]{1,0:T(8,128)(2,1)} async-done(((bf16[512,256]{1,0:T(8,128)(2,1)}), bf16[2048,256]{1,0:T(8,128)(2,1)}) %all-gather.9.cloned.1.call-update) | async-done | bytes 1048592 | tf_op jit(solution)/shard_map/all_gather | solution.py:871
  153.1 12.0 %shard_map.206 = (bf16[2048,128]{1,0:T(8,128)(2,1)}, f32[2048,128]{1,0:T(8,128)}, f32[2,2048]{1,0:T(2,128)}) custom-call(s32[4]{0:T(128)} %and_select_fusion.lowest_ref, bf16[2048,128]{1,0:T(8,128)(2,1)} %copy-done.6, bf16[2048,128]{1,0:T(8,128)(2,1)} %copy-done.7, bf16[2048,128]{1,0:T(8,128)(2,1)} %copy-done.8, s32[1,2048]{1,0:T(1,128)} %subtract_subtract_fusion.begin_ref), custom_call_target="tpu_custom_call" | custom-call | flops 1073741824 | bytes 3145728 | tf_op jit(solution)/shard_map/pallas_call | solution.py:684
  167.6 9.9 %collective-permute-done.19.refs_3_.refs_1_.refs_9_ = bf16[2048,256]{1,0:T(8,128)(2,1)} collective-permute-done((bf16[2048,256]{1,0:T(8,128)(2,1)}, bf16[2048,256]{1,0:T(8,128)(2,1)}, u32[]{:S(2)}, u32[]{:S(2)}) %collective-permute-start.19) | collective-permute-done | bytes 1048608 | tf_op jit(solution)/shard_map/ppermute | solution.py:93
  177.5 5.2 %collective-permute-done.18.refs_7_.refs_10_ = bf16[640,512]{1,0:T(8,128)(2,1)} collective-permute-done((bf16[640,512]{1,0:T(8,128)(2,1)}, bf16[640,512]{1,0:T(8,128)(2,1)}, u32[]{:S(2)}, u32[]{:S(2)}) %collective-permute-start.18) | collective-permute-done | bytes 655392 | tf_op jit(solution)/shard_map/ppermute | solution.py:93
  183.2 9.6 %shard_map.208 = (bf16[1024,512]{1,0:T(8,128)(2,1)}, bf16[1024,512]{1,0:T(8,128)(2,1)}, bf16[2048,512]{1,0:T(8,128)(2,1)}) custom-call(bf16[2048,512]{1,0:T(8,128)(2,1)} %get-tuple-element.102.refs_0_, bf16[2048,128]{1,0:T(8,128)(2,1)} %get-tuple-element.107.refs_1_.refs_6_, bf16[2048,512]{1,0:T(8,128)(2,1)} %collective-permute-done.15.refs_2_.refs_1_, ...), custom_call_target="tpu_custom_call" | custom-call | flops 5368709120 | bytes 9437184 | tf_op jit(solution)/shard_map/pallas_call | solution.py:374
  192.8 9.4 %shard_map.209 = (bf16[4,256,512]{2,1,0:T(8,128)(2,1)}, bf16[4,256,512]{2,1,0:T(8,128)(2,1)}) custom-call(s32[1]{0:T(128)} %bitcast.15.half_ref, bf16[2048,512]{1,0:T(8,128)(2,1)} %get-tuple-element.102.refs_0_, bf16[2048,512]{1,0:T(8,128)(2,1)} %collective-permute-done.15.refs_2_.refs_1_, ...), custom_call_target="tpu_custom_call" | custom-call | flops 4294967296 | bytes 16777216 | tf_op jit(solution)/shard_map/pallas_call | solution.py:464
  202.3 13.5 %shard_map.210 = (bf16[2048,512]{1,0:T(8,128)(2,1)}, bf16[2048,128]{1,0:T(8,128)(2,1)}, f32[1,512]{1,0:T(1,128)}) custom-call(bf16[2048,256]{1,0:T(8,128)(2,1)} %all-gather.9.cloned.1.call-done.refs_2_.refs_0_.refs_8_, bf16[2048,256]{1,0:T(8,128)(2,1)} %collective-permute-done.19.refs_3_.refs_1_.refs_9_, ...), custom_call_target="tpu_custom_call" | custom-call | flops 5368709120 | bytes 14680064 | tf_op jit(solution)/shard_map/pallas_call | solution.py:263
  216.4 25.2 %collective-permute-done.26 = bf16[1024,512]{1,0:T(8,128)(2,1)S(1)} collective-permute-done((bf16[1024,512]{1,0:T(8,128)(2,1)}, bf16[1024,512]{1,0:T(8,128)(2,1)S(1)}, u32[]{:S(2)}, u32[]{:S(2)}) %collective-permute-start.26) | collective-permute-done | bytes 1048608 | tf_op jit(solution)/shard_map/ppermute | solution.py:93
  244.1 9.4 %shard_map.212 = (bf16[4,256,512]{2,1,0:T(8,128)(2,1)}, bf16[4,256,512]{2,1,0:T(8,128)(2,1)}) custom-call(s32[1]{0:T(128)} %bitcast.15.half_ref, bf16[2048,256]{1,0:T(8,128)(2,1)} %all-gather.5.cloned.1.call-done.refs_0_.refs_2_, bf16[2048,256]{1,0:T(8,128)(2,1)} %all-gather.7.cloned.1.call-done.refs_1_.refs_3_, ...), custom_call_target="tpu_custom_call" | custom-call | flops 4294967296 | bytes 16777216 | tf_op jit(solution)/shard_map/pallas_call | solution.py:464
  253.5 17.9 %shard_map.213 = (bf16[2048,384]{1,0:T(8,128)(2,1)}, f32[1,384]{1,0:T(1,128)}) custom-call(s32[4]{0:T(128)} %and_select_fusion.lowest_ref, bf16[2048,128]{1,0:T(8,128)(2,1)} %copy-done.6, bf16[2048,128]{1,0:T(8,128)(2,1)} %copy-done.7, bf16[2048,128]{1,0:T(8,128)(2,1)} %copy-done.8, s32[1,2048]{1,0:T(1,128)} %subtract_subtract_fusion.begin_ref, ...), custom_call_target="tpu_custom_call" | custom-call | flops 2684354560 | bytes 4194304 | tf_op jit(solution)/shard_map/pallas_call | solution.py:789
  272.9 24.4 %collective-permute-done.29.received_ref = bf16[4,256,512]{2,1,0:T(8,128)(2,1)} collective-permute-done((bf16[4,256,512]{2,1,0:T(8,128)(2,1)}, bf16[4,256,512]{2,1,0:T(8,128)(2,1)}, u32[]{:S(2)}, u32[]{:S(2)}) %collective-permute-start.29) | collective-permute-done | bytes 1048608 | tf_op jit(solution)/shard_map/ppermute | solution.py:93
  299.9 12.4 %shard_map.215 = (bf16[1024,512]{1,0:T(8,128)(2,1)}, bf16[1024,512]{1,0:T(8,128)(2,1)}, bf16[2048,512]{1,0:T(8,128)(2,1)}) custom-call(bf16[2048,512]{1,0:T(8,128)(2,1)} %get-tuple-element.128.refs_4_.refs_0_, bf16[2048,384]{1,0:T(8,128)(2,1)} %get-tuple-element.144.refs_1_.refs_0_, bf16[2048,512]{1,0:T(8,128)(2,1)} %collective-permute-done.28.refs_5_.refs_2_, ...), custom_call_target="tpu_custom_call" | custom-call | flops 7516192768 | bytes 11534336 | tf_op jit(solution)/shard_map/pallas_call | solution.py:374
  314.1 24.1 %collective-permute-done.31 = bf16[1024,512]{1,0:T(8,128)(2,1)S(1)} collective-permute-done((bf16[1024,512]{1,0:T(8,128)(2,1)S(1)}, bf16[1024,512]{1,0:T(8,128)(2,1)S(1)}, u32[]{:S(2)}, u32[]{:S(2)}) %collective-permute-start.31) | collective-permute-done | bytes 1048608 | tf_op jit(solution)/shard_map/ppermute | solution.py:93
  342.1 10.7 %shard_map.218 = (bf16[4,512,256]{2,1,0:T(8,128)(2,1)}, bf16[4,512,256]{2,1,0:T(8,128)(2,1)}) custom-call(s32[1]{0:T(128)} %bitcast.15.half_ref, bf16[2048,384]{1,0:T(8,128)(2,1)} %get-tuple-element.144.refs_1_.refs_0_, bf16[2048,384]{1,0:T(8,128)(2,1)} %collective-permute-done.30.refs_3_.refs_1_, ...), custom_call_target="tpu_custom_call" | custom-call | flops 4294967296 | bytes 16777216 | tf_op jit(solution)/shard_map/pallas_call | solution.py:464
  355.4 11.6 %collective-permute-done.43.received_ref = bf16[4,256,512]{2,1,0:T(8,128)(2,1)} collective-permute-done((bf16[4,256,512]{2,1,0:T(8,128)(2,1)}, bf16[4,256,512]{2,1,0:T(8,128)(2,1)}, u32[]{:S(2)}, u32[]{:S(2)}) %collective-permute-start.43) | collective-permute-done | bytes 1048608 | tf_op jit(solution)/shard_map/ppermute | solution.py:93
  370.2 19.2 %collective-permute-done.38.received_ref = bf16[4,512,256]{2,1,0:T(8,128)(2,1)} collective-permute-done((bf16[4,512,256]{2,1,0:T(8,128)(2,1)}, bf16[4,512,256]{2,1,0:T(8,128)(2,1)}, u32[]{:S(2)}, u32[]{:S(2)}) %collective-permute-start.38) | collective-permute-done | bytes 1048608 | tf_op jit(solution)/shard_map/ppermute | solution.py:93
  395.7 14.1 %collective-permute-done.42 = f32[1,896]{1,0:T(1,128)S(1)} collective-permute-done((f32[1,896]{1,0:T(1,128)S(1)}, f32[1,896]{1,0:T(1,128)S(1)}, u32[]{:S(2)}, u32[]{:S(2)}) %collective-permute-start.42) | collective-permute-done | bytes 3616 | tf_op jit(solution)/shard_map/ppermute | solution.py:93
  441.1 16.8 %reduce-scatter.5.cloned.1.call-done.first_ref = bf16[256,512]{1,0:T(8,128)(2,1)} async-done(((bf16[1024,512]{1,0:T(8,128)(2,1)}), bf16[256,512]{1,0:T(8,128)(2,1)}) %reduce-scatter.5.cloned.1.call-update) | async-done | bytes 262160 | tf_op jit(solution)/shard_map/reduce_scatter | solution.py:939
  (203 shorter events, 148.9 us)
Async XLA Ops:
  7.2 41.0 %all-gather.5.cloned.1.call-start = ((), (), s32[]{:S(2)}) async-start(), calls=%async_computation.4 | async-start | bytes 1310720 | tf_op jit(solution)/shard_map/all_gather | solution.py:863
  16.7 59.4 %all-gather.7.cloned.1.call-start = ((), (), s32[]{:S(2)}) async-start(), calls=%async_computation.5 | async-start | bytes 1310720 | tf_op jit(solution)/shard_map/all_gather | solution.py:864
  20.7 119.0 %all-gather.11.cloned.1.call-start = ((), (), s32[]{:S(2)}) async-start(), calls=%async_computation.7 | async-start | bytes 2621440 | tf_op jit(solution)/shard_map/all_gather | solution.py:872
  50.5 100.6 %all-gather.9.cloned.1.call-start = ((), (), s32[]{:S(2)}) async-start(), calls=%async_computation.6 | async-start | bytes 1310720 | tf_op jit(solution)/shard_map/all_gather | solution.py:871
  79.5 30.2 %collective-permute-start.13 = (bf16[512,896]{1,0:T(8,128)(2,1)}, bf16[512,896]{1,0:T(8,128)(2,1)}, u32[]{:S(2)}, u32[]{:S(2)}) collective-permute-start(bf16[512,896]{1,0:T(8,128)(2,1)} %get-tuple-element.100.refs_5_), channel_id=1, source_target_pairs={{0,1},{1,0},{2,3},{3,2},{4,5},{5,4},{6,7},{7,6},{8,9},{9,8},{10,11... | collective-permute-start | bytes 2752520 | tf_op jit(solution)/shard_map/ppermute | solution.py:93
  110.1 284.6 %reduce-scatter.11.cloned.1.call-start = ((), (), s32[]{:S(2)}) async-start(), calls=%async_computation.11 | async-start | bytes 2621440 | tf_op jit(solution)/shard_map/reduce_scatter | solution.py:959
  133.7 49.0 %collective-permute-start.15 = (bf16[2048,512]{1,0:T(8,128)(2,1)}, bf16[2048,512]{1,0:T(8,128)(2,1)}, u32[]{:S(2)}, u32[]{:S(2)}) collective-permute-start(bf16[2048,512]{1,0:T(8,128)(2,1)} %get-tuple-element.102.refs_0_), channel_id=1, source_target_pairs={{0,1},{1,0},{2,3},{3,2},{4,5},{5,4},{6,7},{7,6},{8,9},{9,8},{10,11... | collective-permute-start | bytes 6291464 | tf_op jit(solution)/shard_map/ppermute | solution.py:93
  139.7 62.5 %collective-permute-start.22 = (bf16[2048,512]{1,0:T(8,128)(2,1)}, bf16[2048,512]{1,0:T(8,128)(2,1)}, u32[]{:S(2)}, u32[]{:S(2)}) collective-permute-start(bf16[2048,512]{1,0:T(8,128)(2,1)} %all-gather.11.cloned.1.call-done.refs_4_.refs_2_.refs_10_), channel_id=1, source_target_pairs={{0,1},{1,0},{2,3},{3,2},{4,5},{5,4},{6,7},{7,6},{8,9},{9,8},{10,11... | collective-permute-start | bytes 6291464 | tf_op jit(solution)/shard_map/ppermute | solution.py:93
  167.5 34.7 %collective-permute-start.20 = (bf16[2048,256]{1,0:T(8,128)(2,1)}, bf16[2048,256]{1,0:T(8,128)(2,1)}, u32[]{:S(2)}, u32[]{:S(2)}) collective-permute-start(bf16[2048,256]{1,0:T(8,128)(2,1)} %all-gather.9.cloned.1.call-done.refs_2_.refs_0_.refs_8_), channel_id=1, source_target_pairs={{0,1},{1,0},{2,3},{3,2},{4,5},{5,4},{6,7},{7,6},{8,9},{9,8},{10,11... | collective-permute-start | bytes 3145736 | tf_op jit(solution)/shard_map/ppermute | solution.py:93
  215.7 28.4 %collective-permute-start.28 = (bf16[2048,512]{1,0:T(8,128)(2,1)}, bf16[2048,512]{1,0:T(8,128)(2,1)}, u32[]{:S(2)}, u32[]{:S(2)}) collective-permute-start(bf16[2048,512]{1,0:T(8,128)(2,1)} %get-tuple-element.128.refs_4_.refs_0_), channel_id=1, source_target_pairs={{0,1},{1,0},{2,3},{3,2},{4,5},{5,4},{6,7},{7,6},{8,9},{9,8},{10,11... | collective-permute-start | bytes 6291464 | tf_op jit(solution)/shard_map/ppermute | solution.py:93
  271.4 28.5 %collective-permute-start.30 = (bf16[2048,384]{1,0:T(8,128)(2,1)}, bf16[2048,384]{1,0:T(8,128)(2,1)}, u32[]{:S(2)}, u32[]{:S(2)}) collective-permute-start(bf16[2048,384]{1,0:T(8,128)(2,1)} %get-tuple-element.144.refs_1_.refs_0_), channel_id=1, source_target_pairs={{0,1},{1,0},{2,3},{3,2},{4,5},{5,4},{6,7},{7,6},{8,9},{9,8},{10,11... | collective-permute-start | bytes 4718600 | tf_op jit(solution)/shard_map/ppermute | solution.py:93
  312.4 106.0 %reduce-scatter.9.cloned.1.call-start = ((), (), s32[]{:S(2)}) async-start(), calls=%async_computation.10 | async-start | bytes 1310720 | tf_op jit(solution)/shard_map/reduce_scatter | solution.py:975
  339.5 89.5 %reduce-scatter.7.cloned.1.call-start = ((), (), s32[]{:S(2)}) async-start(), calls=%async_computation.9 | async-start | bytes 2621440 | tf_op jit(solution)/shard_map/reduce_scatter | solution.py:917
  340.3 117.6 %reduce-scatter.5.cloned.1.call-start = ((), (), s32[]{:S(2)}) async-start(), calls=%async_computation.8 | async-start | bytes 1310720 | tf_op jit(solution)/shard_map/reduce_scatter | solution.py:939
  352.8 36.7 %collective-permute-start.38 = (bf16[4,512,256]{2,1,0:T(8,128)(2,1)}, bf16[4,512,256]{2,1,0:T(8,128)(2,1)}, u32[]{:S(2)}, u32[]{:S(2)}) collective-permute-start(bf16[4,512,256]{2,1,0:T(8,128)(2,1)} %get-tuple-element.146), channel_id=1, source_target_pairs={{0,16},{16,0},{1,17},{17,1},{2,18},{18,2},{3,19},{19,3},{4,20},{20... | collective-permute-start | bytes 3145736 | tf_op jit(solution)/shard_map/ppermute | solution.py:93
  353.3 39.3 %collective-permute-start.47 = (bf16[2,256,512]{2,1,0:T(8,128)(2,1)}, bf16[2,256,512]{2,1,0:T(8,128)(2,1)}, u32[]{:S(2)}, u32[]{:S(2)}) collective-permute-start(bf16[2,256,512]{2,1,0:T(8,128)(2,1)} %get-tuple-element.159), channel_id=1, source_target_pairs={{0,2},{1,3},{2,0},{3,1},{4,6},{5,7},{6,4},{7,5},{8,10},{9,11},{10,... | collective-permute-start | bytes 1572872 | tf_op jit(solution)/shard_map/ppermute | solution.py:93
  354.0 56.4 %collective-permute-start.48 = (bf16[2,256,512]{2,1,0:T(8,128)(2,1)}, bf16[2,256,512]{2,1,0:T(8,128)(2,1)}, u32[]{:S(2)}, u32[]{:S(2)}) collective-permute-start(bf16[2,256,512]{2,1,0:T(8,128)(2,1)} %get-tuple-element.137.refs_0_), channel_id=1, source_target_pairs={{0,16},{16,0},{1,17},{17,1},{2,18},{18,2},{3,19},{19,3},{4,20},{20... | collective-permute-start | bytes 1572872 | tf_op jit(solution)/shard_map/ppermute | solution.py:93
  369.7 43.9 %collective-permute-start.44 = (bf16[2,256,512]{2,1,0:T(8,128)(2,1)}, bf16[2,256,512]{2,1,0:T(8,128)(2,1)}, u32[]{:S(2)}, u32[]{:S(2)}) collective-permute-start(bf16[2,256,512]{2,1,0:T(8,128)(2,1)} %get-tuple-element.157), channel_id=1, source_target_pairs={{0,2},{1,3},{2,0},{3,1},{4,6},{5,7},{6,4},{7,5},{8,10},{9,11},{10,... | collective-permute-start | bytes 1572872 | tf_op jit(solution)/shard_map/ppermute | solution.py:93
  392.6 28.8 %collective-permute-start.49 = (bf16[2,256,512]{2,1,0:T(8,128)(2,1)}, bf16[2,256,512]{2,1,0:T(8,128)(2,1)}, u32[]{:S(2)}, u32[]{:S(2)}) collective-permute-start(bf16[2,256,512]{2,1,0:T(8,128)(2,1)} %collective-permute-done.47.refs_1_), channel_id=1, source_target_pairs={{0,16},{16,0},{1,17},{17,1},{2,18},{18,2},{3,19},{19,3},{4,20},{20... | collective-permute-start | bytes 1572872 | tf_op jit(solution)/shard_map/ppermute | solution.py:93
  413.6 51.0 %collective-permute-start.46 = (bf16[2,256,512]{2,1,0:T(8,128)(2,1)}, bf16[2,256,512]{2,1,0:T(8,128)(2,1)}, u32[]{:S(2)}, u32[]{:S(2)}) collective-permute-start(bf16[2,256,512]{2,1,0:T(8,128)(2,1)} %collective-permute-done.44.refs_1_), channel_id=1, source_target_pairs={{0,16},{16,0},{1,17},{17,1},{2,18},{18,2},{3,19},{19,3},{4,20},{20... | collective-permute-start | bytes 1572872 | tf_op jit(solution)/shard_map/ppermute | solution.py:93
  414.2 54.8 %collective-permute-start.40 = (bf16[2,512,256]{2,1,0:T(8,128)(2,1)}, bf16[2,512,256]{2,1,0:T(8,128)(2,1)}, u32[]{:S(2)}, u32[]{:S(2)}) collective-permute-start(bf16[2,512,256]{2,1,0:T(8,128)(2,1)} %get-tuple-element.147.refs_0_), channel_id=1, source_target_pairs={{0,16},{16,0},{1,17},{17,1},{2,18},{18,2},{3,19},{19,3},{4,20},{20... | collective-permute-start | bytes 1572872 | tf_op jit(solution)/shard_map/ppermute | solution.py:93
  416.3 52.6 %collective-permute-start.41 = (bf16[2,512,256]{2,1,0:T(8,128)(2,1)}, bf16[2,512,256]{2,1,0:T(8,128)(2,1)}, u32[]{:S(2)}, u32[]{:S(2)}) collective-permute-start(bf16[2,512,256]{2,1,0:T(8,128)(2,1)} %collective-permute-done.39.refs_1_), channel_id=1, source_target_pairs={{0,16},{16,0},{1,17},{17,1},{2,18},{18,2},{3,19},{19,3},{4,20},{20... | collective-permute-start | bytes 1572872 | tf_op jit(solution)/shard_map/ppermute | solution.py:93
  433.9 44.7 %collective-permute-start.34 = (f32[2,512]{1,0:T(2,128)S(1)}, f32[2,512]{1,0:T(2,128)S(1)}, u32[]{:S(2)}, u32[]{:S(2)}) collective-permute-start(f32[2,512]{1,0:T(2,128)S(1)} %add.106), channel_id=1, source_target_pairs={{0,2},{1,3},{2,0},{3,1},{4,6},{5,7},{6,4},{7,5},{8,10},{9,11},{10,... | collective-permute-start | bytes 12296 | tf_op jit(solution)/shard_map/ppermute | solution.py:93
  438.8 43.8 %collective-permute-start.37 = (f32[3,512]{1,0:T(4,128)S(1)}, f32[3,512]{1,0:T(4,128)S(1)}, u32[]{:S(2)}, u32[]{:S(2)}) collective-permute-start(f32[3,512]{1,0:T(4,128)S(1)} %add.109), channel_id=1, source_target_pairs={{0,16},{16,0},{1,17},{17,1},{2,18},{18,2},{3,19},{19,3},{4,20},{20... | collective-permute-start | bytes 18440 | tf_op jit(solution)/shard_map/ppermute | solution.py:93
  (52 other events, 782.0 us)
Sparse Core Ops, SparseCore 0:
  16.9 29.7 all-gather.4
  48.8 27.3 all-gather.6
  77.7 45.0 all-gather.10
  124.2 26.7 all-gather.8
  312.5 42.0 reduce-scatter.10
  357.4 26.4 reduce-scatter.8
  386.8 42.2 reduce-scatter.6
  431.4 26.4 reduce-scatter.4
